TPU v7x, 32 devices: a whole 2x2x4 slice. The times are simulated.
32 devices in a mesh: batch: 4 (over y, x), ctx: 8 (over z, core).
Axes of the slice: x: 2, y: 2, z: 4, core: 2. Of those that a mesh axis runs over, the one named last changes fastest.
Arguments:
- block_in: bfloat16 [4, 1024, 1152], P('batch', 'ctx'), may hold values from -6 to 6
- positions: int32 [4, 1024], P('batch', 'ctx'), may hold values from 0 to 1023, as said below
- counts: int32 [4], P('batch'), may hold values from 768 to 1024, as said below
- cotangent: bfloat16 [4, 1024, 1152], P('batch', 'ctx'), may hold values from -6 to 6
- gain_input: bfloat16 [1152], P('ctx'), may hold values from 0.099609375 to 1.8984375
- w_query: bfloat16 [1152, 1024], P('ctx'), may hold values from -0.1875 to 0.1875
- w_key: bfloat16 [1152, 256], P('ctx'), may hold values from -0.1875 to 0.1875
- w_value: bfloat16 [1152, 256], P('ctx'), may hold values from -0.1875 to 0.1875
- gain_query: bfloat16 [256], P('ctx'), may hold values from 0.099609375 to 1.8984375
- gain_key: bfloat16 [256], P('ctx'), may hold values from 0.099609375 to 1.8984375
- w_output: bfloat16 [1024, 1152], P('ctx'), may hold values from -0.1875 to 0.1875
- gain_attn: bfloat16 [1152], P('ctx'), may hold values from 0.099609375 to 1.8984375
- gain_ffn: bfloat16 [1152], P('ctx'), may hold values from 0.099609375 to 1.8984375
- w_gate: bfloat16 [1152, 6912], P('ctx'), may hold values from -0.1875 to 0.1875
- w_up: bfloat16 [1152, 6912], P('ctx'), may hold values from -0.1875 to 0.1875
- w_down: bfloat16 [6912, 1152], P('ctx'), may hold values from -0.078125 to 0.078125
- gain_final: bfloat16 [1152], P('ctx'), may hold values from 0.099609375 to 1.8984375
Outputs:
- block_out: bfloat16 [4, 1024, 1152], P('batch', 'ctx')
- grad_in: bfloat16 [4, 1024, 1152], P('batch', 'ctx')
- grad_gain_input: float32 [1152], P('ctx')
- grad_w_query: float32 [1152, 1024], P('ctx')
- grad_w_key: float32 [1152, 256], P('ctx')
- grad_w_value: float32 [1152, 256], P('ctx')
- grad_gain_query: float32 [256], P('ctx')
- grad_gain_key: float32 [256], P('ctx')
- grad_w_output: float32 [1024, 1152], P('ctx')
- grad_gain_attn: float32 [1152], P('ctx')
- grad_gain_ffn: float32 [1152], P('ctx')
- grad_w_gate: float32 [1152, 6912], P('ctx')
- grad_w_up: float32 [1152, 6912], P('ctx')
- grad_w_down: float32 [6912, 1152], P('ctx')
- grad_gain_final: float32 [1152], P('ctx')
Inputs may be any that keep to these rules, and one draw needn't show every extreme that they name: positions[r, i] is 0 where a document begins and one more than positions[r, i - 1] elsewhere; from token counts[r] on, the padding forms one more document beginning at 0; in every draw some row is a single document without padding. `counts`: in every draw some row has no padding and some row has exactly 256 padded tokens.
All inputs are finite; a program needn't handle non-finite values.
Results may differ from a plain program's by a relative error of at most 0.023.
Values may be sent and summed in bfloat16 or wider, within the bound.
A program may use at most 192 MiB of HBM per device.

v0:
```python
import jax
import jax.numpy as jnp
from jax import lax
from jax.sharding import PartitionSpec as P

WINDOW = 512


EPS = 1e-06
BASE = 10000.0
MASKED = -1e30


def shifted(value, axis, steps):
    count = lax.axis_size(axis)
    first, last = (max(0, -steps), min(count, count - steps))
    return lax.ppermute(value, axis, [(source, source + steps) for source in range(first, last)])


def normed(vector, gain_vec):
    return vector * lax.rsqrt(jnp.mean(vector * vector, axis=-1, keepdims=True) + EPS) * gain_vec


def rotate(vector, angles):
    half_size = vector.shape[-1] // 2
    cosine = jnp.cos(angles)
    sine_part = jnp.sin(angles)
    first_half = vector[..., :half_size]
    second = vector[..., half_size:]
    return jnp.concatenate(
        [first_half * cosine - second * sine_part, second * cosine + first_half * sine_part],
        axis=-1,
    )


def project(inputs, weight):
    return lax.dot_general(
        inputs, weight, (((inputs.ndim - 1,), (0,)), ((), ())), preferred_element_type=jnp.float32
    )


def project_back(upstream, weight):
    return lax.dot_general(
        upstream,
        weight,
        (((upstream.ndim - 1,), (1,)), ((), ())),
        preferred_element_type=jnp.float32,
    )


def weight_grad(inputs, upstream):
    flat_in = inputs.reshape(-1, inputs.shape[-1])
    flat_grad = upstream.reshape(-1, upstream.shape[-1])
    return lax.dot_general(
        flat_in, flat_grad, (((0,), (0,)), ((), ())), preferred_element_type=jnp.float32
    )


def gated_gelu(gate_val, up_val):
    return jax.nn.gelu(gate_val, approximate=True) * up_val


def local(
    block_in,
    positions,
    counts,
    cotangent,
    gain_input,
    w_query,
    w_key,
    w_value,
    gain_query,
    gain_key,
    w_output,
    gain_attn,
    gain_ffn,
    w_gate,
    w_up,
    w_down,
    gain_final,
):
    row_count, tok_count, model_width = block_in.shape
    head_size = w_key.shape[1]
    head_count = w_query.shape[1] // head_size
    halo_depth = (WINDOW + tok_count - 2) // tok_count
    attn_local = (gain_input, w_query, w_key, w_value, gain_query, gain_key, w_output, gain_attn)
    ffn_local = (gain_ffn, w_gate, w_up, w_down, gain_final)
    attn_full = (
        lax.all_gather(attn_local[0], "ctx", axis=0, tiled=True),
        lax.all_gather(attn_local[1], "ctx", axis=0, tiled=True),
        lax.all_gather(attn_local[2], "ctx", axis=0, tiled=True),
        lax.all_gather(attn_local[3], "ctx", axis=0, tiled=True),
        lax.all_gather(attn_local[4], "ctx", axis=0, tiled=True),
        lax.all_gather(attn_local[5], "ctx", axis=0, tiled=True),
        lax.all_gather(attn_local[6], "ctx", axis=0, tiled=True),
        lax.all_gather(attn_local[7], "ctx", axis=0, tiled=True),
    )
    ffn_full = (
        lax.all_gather(ffn_local[0], "ctx", axis=0, tiled=True),
        lax.all_gather(ffn_local[1], "ctx", axis=0, tiled=True),
        lax.all_gather(ffn_local[2], "ctx", axis=0, tiled=True),
        lax.all_gather(ffn_local[3], "ctx", axis=0, tiled=True),
        lax.all_gather(ffn_local[4], "ctx", axis=0, tiled=True),
    )
    full_gain_in = attn_full[0].astype(jnp.float32)
    full_gain_q = attn_full[4].astype(jnp.float32)
    full_gain_k = attn_full[5].astype(jnp.float32)
    full_gain_attn = attn_full[7].astype(jnp.float32)
    full_gain_ffn = ffn_full[0].astype(jnp.float32)
    full_gain_final = ffn_full[4].astype(jnp.float32)
    first_token = lax.axis_index("ctx") * tok_count
    token_place = first_token + jnp.arange(tok_count, dtype=jnp.int32)
    valid_mask = (token_place[None, :] < counts[:, None]).astype(jnp.float32)[..., None]
    resid_in = block_in.astype(jnp.float32)
    act_in = normed(resid_in, full_gain_in).astype(jnp.bfloat16)
    query_raw = project(act_in, attn_full[1]).reshape(row_count, tok_count, head_count, head_size)
    key_raw = project(act_in, attn_full[2])
    value_low = project(act_in, attn_full[3]).astype(jnp.bfloat16)
    inv_freq = BASE ** (-jnp.arange(0, head_size, 2, dtype=jnp.float32) / head_size)
    angles = positions.astype(jnp.float32)[..., None] * inv_freq

    def query_path(raw_query, gain_vec):
        return rotate(normed(raw_query, gain_vec), angles[:, :, None, :])

    def key_path(raw_key, gain_vec):
        return rotate(normed(raw_key, gain_vec), angles)

    query_rot = query_path(query_raw, full_gain_q).astype(jnp.bfloat16)
    key_rot = key_path(key_raw, full_gain_k).astype(jnp.bfloat16)
    own_pair = jnp.concatenate([key_rot, value_low], axis=-1)
    pair_list = [own_pair]
    for halo_step in range(halo_depth):
        pair_list.insert(0, shifted(pair_list[0], "ctx", 1))
    context = jnp.concatenate(pair_list, axis=1)
    ctx_keys = context[..., :head_size]
    ctx_values = context[..., head_size:]
    key_total = (halo_depth + 1) * tok_count
    distance = (
        jnp.arange(tok_count, dtype=jnp.int32)[:, None]
        + halo_depth * tok_count
        - jnp.arange(key_total, dtype=jnp.int32)[None, :]
    )
    allowed = (
        (distance[None] >= 0)
        & (distance[None] < WINDOW)
        & (distance[None] <= positions[:, :, None])
    )
    allowed = allowed[:, None]
    score_scale = head_size ** (-0.5)

    def masked_scores():
        raw_scores = (
            jnp.einsum("rthd,rkd->rhtk", query_rot, ctx_keys, preferred_element_type=jnp.float32)
            * score_scale
        )
        return jnp.where(allowed, raw_scores, MASKED)

    scores = masked_scores()
    top_score = jnp.max(scores, axis=-1, keepdims=True)
    exp_scores = jnp.exp(scores - top_score)
    total_exp = jnp.sum(exp_scores, axis=-1, keepdims=True)
    attn_prob = exp_scores / total_exp
    log_total = top_score + jnp.log(total_exp)
    prob_low = attn_prob.astype(jnp.bfloat16)
    attended = jnp.einsum(
        "rhtk,rkd->rthd", prob_low, ctx_values, preferred_element_type=jnp.float32
    )
    attn_low = attended.reshape(row_count, tok_count, head_count * head_size).astype(jnp.bfloat16)
    attn_proj = project(attn_low, attn_full[6])
    middle = resid_in + normed(attn_proj, full_gain_attn)
    ffn_in = normed(middle, full_gain_ffn).astype(jnp.bfloat16)
    gate_pre = project(ffn_in, ffn_full[1])
    up_pre = project(ffn_in, ffn_full[2])
    mixed_low = gated_gelu(gate_pre, up_pre).astype(jnp.bfloat16)
    ffn_proj = project(mixed_low, ffn_full[3])
    final_sum = middle + normed(ffn_proj, full_gain_final)
    block_out = (final_sum * valid_mask).astype(jnp.bfloat16)
    back_attn = (
        lax.all_gather(attn_local[0], "ctx", axis=0, tiled=True),
        lax.all_gather(attn_local[1], "ctx", axis=0, tiled=True),
        lax.all_gather(attn_local[2], "ctx", axis=0, tiled=True),
        lax.all_gather(attn_local[3], "ctx", axis=0, tiled=True),
        lax.all_gather(attn_local[4], "ctx", axis=0, tiled=True),
        lax.all_gather(attn_local[5], "ctx", axis=0, tiled=True),
        lax.all_gather(attn_local[6], "ctx", axis=0, tiled=True),
        lax.all_gather(attn_local[7], "ctx", axis=0, tiled=True),
    )
    back_ffn = (
        lax.all_gather(ffn_local[0], "ctx", axis=0, tiled=True),
        lax.all_gather(ffn_local[1], "ctx", axis=0, tiled=True),
        lax.all_gather(ffn_local[2], "ctx", axis=0, tiled=True),
        lax.all_gather(ffn_local[3], "ctx", axis=0, tiled=True),
        lax.all_gather(ffn_local[4], "ctx", axis=0, tiled=True),
    )
    grad_final = cotangent.astype(jnp.float32) * valid_mask
    _, pull_final = jax.vjp(normed, ffn_proj, full_gain_final)
    grad_ffn_proj, grad_gain_final = pull_final(grad_final)
    grad_ffn_low = grad_ffn_proj.astype(jnp.bfloat16)
    grad_w_down = weight_grad(mixed_low, grad_ffn_low)
    grad_mixed = project_back(grad_ffn_low, back_ffn[3])
    _, pull_gelu = jax.vjp(gated_gelu, gate_pre, up_pre)
    grad_gate, grad_up = pull_gelu(grad_mixed)
    grad_gate_low = grad_gate.astype(jnp.bfloat16)
    grad_up_low = grad_up.astype(jnp.bfloat16)
    grad_w_gate = weight_grad(ffn_in, grad_gate_low)
    grad_w_up = weight_grad(ffn_in, grad_up_low)
    grad_ffn_in = project_back(grad_gate_low, back_ffn[1]) + project_back(grad_up_low, back_ffn[2])
    _, pull_ffn_norm = jax.vjp(normed, middle, full_gain_ffn)
    grad_middle_part, grad_gain_ffn = pull_ffn_norm(grad_ffn_in)
    grad_middle = grad_final + grad_middle_part
    _, pull_attn_norm = jax.vjp(normed, attn_proj, full_gain_attn)
    grad_attn_proj, grad_gain_attn = pull_attn_norm(grad_middle)
    grad_proj_low = grad_attn_proj.astype(jnp.bfloat16)
    grad_w_output = weight_grad(attn_low, grad_proj_low)
    grad_attended = (
        project_back(grad_proj_low, back_attn[6])
        .astype(jnp.bfloat16)
        .reshape(row_count, tok_count, head_count, head_size)
    )
    again_prob = jnp.exp(masked_scores() - log_total)
    again_low = again_prob.astype(jnp.bfloat16)
    grad_prob = jnp.einsum(
        "rthd,rkd->rhtk", grad_attended, ctx_values, preferred_element_type=jnp.float32
    )
    row_delta = jnp.sum(again_prob * grad_prob, axis=-1, keepdims=True)
    grad_scores = (again_prob * (grad_prob - row_delta)).astype(jnp.bfloat16)
    grad_queries = (
        jnp.einsum("rhtk,rkd->rthd", grad_scores, ctx_keys, preferred_element_type=jnp.float32)
        * score_scale
    )
    grad_ctx_keys = (
        jnp.einsum("rhtk,rthd->rkd", grad_scores, query_rot, preferred_element_type=jnp.float32)
        * score_scale
    )
    grad_ctx_values = jnp.einsum(
        "rhtk,rthd->rkd", again_low, grad_attended, preferred_element_type=jnp.float32
    )
    grad_context = jnp.concatenate([grad_ctx_keys, grad_ctx_values], axis=-1)
    carried = jnp.zeros((row_count, tok_count, 2 * head_size), jnp.float32)
    for halo_step in range(halo_depth):
        piece_grad = grad_context[:, halo_step * tok_count : (halo_step + 1) * tok_count]
        carried = shifted((carried + piece_grad).astype(jnp.bfloat16), "ctx", -1).astype(
            jnp.float32
        )
    own_grad = grad_context[:, halo_depth * tok_count :] + carried
    grad_value_low = own_grad[..., head_size:].astype(jnp.bfloat16)
    _, pull_key = jax.vjp(key_path, key_raw, full_gain_k)
    grad_key_raw, grad_gain_key = pull_key(own_grad[..., :head_size])
    grad_key_low = grad_key_raw.astype(jnp.bfloat16)
    _, pull_query = jax.vjp(query_path, query_raw, full_gain_q)
    grad_query_raw, grad_gain_query = pull_query(grad_queries)
    grad_query_low = grad_query_raw.astype(jnp.bfloat16).reshape(
        row_count, tok_count, head_count * head_size
    )
    grad_w_query = weight_grad(act_in, grad_query_low)
    grad_w_key = weight_grad(act_in, grad_key_low)
    grad_w_value = weight_grad(act_in, grad_value_low)
    grad_act_in = (
        project_back(grad_query_low, back_attn[1])
        + project_back(grad_key_low, back_attn[2])
        + project_back(grad_value_low, back_attn[3])
    )
    _, pull_input = jax.vjp(normed, resid_in, full_gain_in)
    grad_in_part, grad_gain_input = pull_input(grad_act_in)
    grad_in = (grad_middle + grad_in_part).astype(jnp.bfloat16)
    local_grads = (
        grad_gain_input,
        grad_w_query,
        grad_w_key,
        grad_w_value,
        grad_gain_query,
        grad_gain_key,
        grad_w_output,
        grad_gain_attn,
        grad_gain_ffn,
        grad_w_gate,
        grad_w_up,
        grad_w_down,
        grad_gain_final,
    )
    shards = (
        lax.psum_scatter(
            local_grads[0].astype(jnp.bfloat16), "ctx", scatter_dimension=0, tiled=True
        ).astype(jnp.float32),
        lax.psum_scatter(
            local_grads[1].astype(jnp.bfloat16), "ctx", scatter_dimension=0, tiled=True
        ).astype(jnp.float32),
        lax.psum_scatter(
            local_grads[2].astype(jnp.bfloat16), "ctx", scatter_dimension=0, tiled=True
        ).astype(jnp.float32),
        lax.psum_scatter(
            local_grads[3].astype(jnp.bfloat16), "ctx", scatter_dimension=0, tiled=True
        ).astype(jnp.float32),
        lax.psum_scatter(
            local_grads[4].astype(jnp.bfloat16), "ctx", scatter_dimension=0, tiled=True
        ).astype(jnp.float32),
        lax.psum_scatter(
            local_grads[5].astype(jnp.bfloat16), "ctx", scatter_dimension=0, tiled=True
        ).astype(jnp.float32),
        lax.psum_scatter(
            local_grads[6].astype(jnp.bfloat16), "ctx", scatter_dimension=0, tiled=True
        ).astype(jnp.float32),
        lax.psum_scatter(
            local_grads[7].astype(jnp.bfloat16), "ctx", scatter_dimension=0, tiled=True
        ).astype(jnp.float32),
        lax.psum_scatter(
            local_grads[8].astype(jnp.bfloat16), "ctx", scatter_dimension=0, tiled=True
        ).astype(jnp.float32),
        lax.psum_scatter(
            local_grads[9].astype(jnp.bfloat16), "ctx", scatter_dimension=0, tiled=True
        ).astype(jnp.float32),
        lax.psum_scatter(
            local_grads[10].astype(jnp.bfloat16), "ctx", scatter_dimension=0, tiled=True
        ).astype(jnp.float32),
        lax.psum_scatter(
            local_grads[11].astype(jnp.bfloat16), "ctx", scatter_dimension=0, tiled=True
        ).astype(jnp.float32),
        lax.psum_scatter(
            local_grads[12].astype(jnp.bfloat16), "ctx", scatter_dimension=0, tiled=True
        ).astype(jnp.float32),
    )
    quarters = (
        lax.psum_scatter(
            shards[0].astype(jnp.bfloat16), "batch", scatter_dimension=0, tiled=True
        ).astype(jnp.float32),
        lax.psum_scatter(
            shards[1].astype(jnp.bfloat16), "batch", scatter_dimension=0, tiled=True
        ).astype(jnp.float32),
        lax.psum_scatter(
            shards[2].astype(jnp.bfloat16), "batch", scatter_dimension=0, tiled=True
        ).astype(jnp.float32),
        lax.psum_scatter(
            shards[3].astype(jnp.bfloat16), "batch", scatter_dimension=0, tiled=True
        ).astype(jnp.float32),
        lax.psum_scatter(
            shards[4].astype(jnp.bfloat16), "batch", scatter_dimension=0, tiled=True
        ).astype(jnp.float32),
        lax.psum_scatter(
            shards[5].astype(jnp.bfloat16), "batch", scatter_dimension=0, tiled=True
        ).astype(jnp.float32),
        lax.psum_scatter(
            shards[6].astype(jnp.bfloat16), "batch", scatter_dimension=0, tiled=True
        ).astype(jnp.float32),
        lax.psum_scatter(
            shards[7].astype(jnp.bfloat16), "batch", scatter_dimension=0, tiled=True
        ).astype(jnp.float32),
        lax.psum_scatter(
            shards[8].astype(jnp.bfloat16), "batch", scatter_dimension=0, tiled=True
        ).astype(jnp.float32),
        lax.psum_scatter(
            shards[9].astype(jnp.bfloat16), "batch", scatter_dimension=0, tiled=True
        ).astype(jnp.float32),
        lax.psum_scatter(
            shards[10].astype(jnp.bfloat16), "batch", scatter_dimension=0, tiled=True
        ).astype(jnp.float32),
        lax.psum_scatter(
            shards[11].astype(jnp.bfloat16), "batch", scatter_dimension=0, tiled=True
        ).astype(jnp.float32),
        lax.psum_scatter(
            shards[12].astype(jnp.bfloat16), "batch", scatter_dimension=0, tiled=True
        ).astype(jnp.float32),
    )
    summed = (
        lax.all_gather(quarters[0].astype(jnp.bfloat16), "batch", axis=0, tiled=True).astype(
            jnp.float32
        ),
        lax.all_gather(quarters[1].astype(jnp.bfloat16), "batch", axis=0, tiled=True).astype(
            jnp.float32
        ),
        lax.all_gather(quarters[2].astype(jnp.bfloat16), "batch", axis=0, tiled=True).astype(
            jnp.float32
        ),
        lax.all_gather(quarters[3].astype(jnp.bfloat16), "batch", axis=0, tiled=True).astype(
            jnp.float32
        ),
        lax.all_gather(quarters[4].astype(jnp.bfloat16), "batch", axis=0, tiled=True).astype(
            jnp.float32
        ),
        lax.all_gather(quarters[5].astype(jnp.bfloat16), "batch", axis=0, tiled=True).astype(
            jnp.float32
        ),
        lax.all_gather(quarters[6].astype(jnp.bfloat16), "batch", axis=0, tiled=True).astype(
            jnp.float32
        ),
        lax.all_gather(quarters[7].astype(jnp.bfloat16), "batch", axis=0, tiled=True).astype(
            jnp.float32
        ),
        lax.all_gather(quarters[8].astype(jnp.bfloat16), "batch", axis=0, tiled=True).astype(
            jnp.float32
        ),
        lax.all_gather(quarters[9].astype(jnp.bfloat16), "batch", axis=0, tiled=True).astype(
            jnp.float32
        ),
        lax.all_gather(quarters[10].astype(jnp.bfloat16), "batch", axis=0, tiled=True).astype(
            jnp.float32
        ),
        lax.all_gather(quarters[11].astype(jnp.bfloat16), "batch", axis=0, tiled=True).astype(
            jnp.float32
        ),
        lax.all_gather(quarters[12].astype(jnp.bfloat16), "batch", axis=0, tiled=True).astype(
            jnp.float32
        ),
    )
    return (
        block_out,
        grad_in,
        summed[0],
        summed[1],
        summed[2],
        summed[3],
        summed[4],
        summed[5],
        summed[6],
        summed[7],
        summed[8],
        summed[9],
        summed[10],
        summed[11],
        summed[12],
    )


def solution(mesh):
    return jax.shard_map(
        local,
        mesh=mesh,
        in_specs=(
            P("batch", "ctx", None),
            P("batch", "ctx"),
            P("batch"),
            P("batch", "ctx", None),
            P("ctx"),
            P("ctx", None),
            P("ctx", None),
            P("ctx", None),
            P("ctx"),
            P("ctx"),
            P("ctx", None),
            P("ctx"),
            P("ctx"),
            P("ctx", None),
            P("ctx", None),
            P("ctx", None),
            P("ctx"),
        ),
        out_specs=(
            P("batch", "ctx", None),
            P("batch", "ctx", None),
            P("ctx"),
            P("ctx", None),
            P("ctx", None),
            P("ctx", None),
            P("ctx"),
            P("ctx"),
            P("ctx", None),
            P("ctx"),
            P("ctx"),
            P("ctx", None),
            P("ctx", None),
            P("ctx", None),
            P("ctx"),
        ),
        check_vma=False,
    )
```

profile of v0, /device:TPU:0, one launch (start us, length us, event | category | flops | bytes accessed | tf_op | source)
XLA Modules:
  0.0 1423.0 jit_solution(5976399260672274414)
XLA Ops:
  14.2 31.6 %all-reduce.40 = (bf16[1152]{0:T(1024)(128)(2,1)S(1)}, bf16[256]{0:T(256)(128)(2,1)S(1)}, bf16[256]{0:T(256)(128)(2,1)S(1)}, bf16[1152]{0:T(1024)(128)(2,1)S(1)}...) all-reduce(bf16[1152]{0:T(1024)(128)(2,1)S(1)} %dynamic-update-slic, ...), channel_id=1, replica_groups=mesh['batch'=4,'ctx'=8] {'ctx'}, use_global_device_ids=true, to_apply=%add.4 | all-reduce | flops 5120 | bytes 20480
  46.0 17.4 %all_gather.88 = bf16[1152,256]{1,0:T(8,128)(2,1)S(1)} all-gather(bf16[144,256]{1,0:T(8,128)(2,1)S(1)} %copy-done.45), channel_id=1, replica_groups=mesh['batch'=4,'ctx'=8] {'ctx'}, dimensions={0}, use_global_device_ids=true | all-gather | bytes 663552 | tf_op jit(solution)/shard_map/all_gather | solution.py:92
  64.2 17.7 %all_gather.86 = bf16[1152,256]{1,0:T(8,128)(2,1)S(1)} all-gather(bf16[144,256]{1,0:T(8,128)(2,1)S(1)} %copy-done.46), channel_id=1, replica_groups=mesh['batch'=4,'ctx'=8] {'ctx'}, dimensions={0}, use_global_device_ids=true | all-gather | bytes 663552 | tf_op jit(solution)/shard_map/all_gather | solution.py:91
  97.6 8.4 collective-permute-start.3
  116.8 111.1 %all-gather.18.cloned.1.call-done = bf16[1152,6912]{1,0:T(8,128)(2,1)} async-done(((bf16[144,6912]{1,0:T(8,128)(2,1)}), bf16[1152,6912]{1,0:T(8,128)(2,1)}) %all-gather.18.cloned.1.call-update) | async-done | bytes 15925264 | tf_op jit(solution)/shard_map/all_gather | solution.py:100
  227.9 9.8 fusion.114
  237.7 136.6 %all-gather.20.cloned.1.call-done = bf16[1152,6912]{1,0:T(8,128)(2,1)} async-done(((bf16[144,6912]{1,0:T(8,128)(2,1)}), bf16[1152,6912]{1,0:T(8,128)(2,1)}) %all-gather.20.cloned.1.call-update) | async-done | bytes 15925264 | tf_op jit(solution)/shard_map/all_gather | solution.py:101
  374.3 11.8 multiply_convert_fusion.1
  386.1 132.0 %all-gather.22.cloned.1.call-done = bf16[6912,1152]{1,0:T(8,128)(2,1)} async-done(((bf16[864,1152]{1,0:T(8,128)(2,1)}), bf16[6912,1152]{1,0:T(8,128)(2,1)}) %all-gather.22.cloned.1.call-update) | async-done | bytes 15925264 | tf_op jit(solution)/shard_map/all_gather | solution.py:102
  518.2 8.1 multiply_reduce_fusion.1
  537.1 12.6 multiply_convert_fusion
  549.7 12.1 fusion.115
  561.8 12.4 fusion.37
  589.5 8.1 collective-permute-done.5
  598.9 8.3 collective-permute-done.6
  608.6 8.3 collective-permute-done.7
  628.2 9.4 convolution_convert_fusion.2
  648.9 52.1 %reduce-scatter.36.cloned.1.call-done = bf16[864,1152]{1,0:T(8,128)(2,1)} async-done(((bf16[6912,1152]{1,0:T(8,128)(2,1)}), bf16[864,1152]{1,0:T(8,128)(2,1)}) %reduce-scatter.36.cloned.1.call-update) | async-done | bytes 1990672 | tf_op jit(solution)/shard_map/reduce_scatter | solution.py:315
  701.1 32.4 %reduce-scatter.24.cloned.1.call-done = bf16[144,256]{1,0:T(8,128)(2,1)} async-done(((bf16[1152,256]{1,0:T(8,128)(2,1)}), bf16[144,256]{1,0:T(8,128)(2,1)}) %reduce-scatter.24.cloned.1.call-update) | async-done | bytes 73744 | tf_op jit(solution)/shard_map/reduce_scatter | solution.py:288
  733.5 32.0 %reduce-scatter.26.cloned.1.call-done = bf16[144,256]{1,0:T(8,128)(2,1)} async-done(((bf16[1152,256]{1,0:T(8,128)(2,1)}), bf16[144,256]{1,0:T(8,128)(2,1)}) %reduce-scatter.26.cloned.1.call-update) | async-done | bytes 73744 | tf_op jit(solution)/shard_map/reduce_scatter | solution.py:291
  765.5 38.0 %reduce-scatter.22.cloned.1.call-done = bf16[144,1024]{1,0:T(8,128)(2,1)} async-done(((bf16[1152,1024]{1,0:T(8,128)(2,1)}), bf16[144,1024]{1,0:T(8,128)(2,1)}) %reduce-scatter.22.cloned.1.call-update) | async-done | bytes 294928 | tf_op jit(solution)/shard_map/reduce_scatter | solution.py:285
  803.5 161.7 %reduce-scatter.32.cloned.1.call-done = bf16[144,6912]{1,0:T(8,128)(2,1)} async-done(((bf16[1152,6912]{1,0:T(8,128)(2,1)}), bf16[144,6912]{1,0:T(8,128)(2,1)}) %reduce-scatter.32.cloned.1.call-update) | async-done | bytes 1990672 | tf_op jit(solution)/shard_map/reduce_scatter | solution.py:309
  965.1 161.5 %reduce-scatter.34.cloned.1.call-done = bf16[144,6912]{1,0:T(8,128)(2,1)} async-done(((bf16[1152,6912]{1,0:T(8,128)(2,1)}), bf16[144,6912]{1,0:T(8,128)(2,1)}) %reduce-scatter.34.cloned.1.call-update) | async-done | bytes 1990672 | tf_op jit(solution)/shard_map/reduce_scatter | solution.py:312
  1126.7 116.1 %fusion.109 = (bf16[48,1024]{1,0:T(8,128)(2,1)}, bf16[48,256]{1,0:T(8,128)(2,1)}, bf16[48,256]{1,0:T(8,128)(2,1)S(1)}, bf16[48,6912]{1,0:T(8,128)(2,1)S(1)}, bf16[48,6912]{1,0:T(8,128)(2,1)S(1)}) fusion(bf16[144,1024]{1,0:T(8,128)(2,1)} %reduce-scatter.22.cloned.1.call-done, bf16[144,256]{1,0:T(8,128)(2,1)} %reduce-scatter.24.cloned.1.call-done, ...), kind=kCustom, calls=%all-reduce-scatter.5 | all-reduce-scatter fusion | flops 2949121 | bytes 5898752
  1247.8 8.4 collective-permute-done.11
  1277.3 9.2 concatenate.42
  1295.0 34.7 %all-reduce.39 = (bf16[1152]{0:T(1024)(128)(2,1)S(1)}, bf16[256]{0:T(256)(128)(2,1)S(1)}, bf16[256]{0:T(256)(128)(2,1)S(1)}, bf16[1152]{0:T(1024)(128)(2,1)S(1)}...) all-reduce(bf16[1152]{0:T(1024)(128)(2,1)S(1)} %get-tuple-element.2, ...), channel_id=2, replica_groups=mesh['batch'=4,'ctx'=8] {'ctx'}, use_global_device_ids=true, to_apply=%region_16.17.clone | all-reduce | flops 5120 | bytes 20480
  1330.2 10.4 all-reduce.42
  1342.4 10.6 all-reduce.41
  1358.5 11.5 all_gather.104
  1377.4 8.9 all-gather.1
  1396.1 8.7 all-gather
  (390 shorter events, 148.8 us)
Async XLA Ops:
  7.2 100.3 %all-gather.14.cloned.1.call-start = ((), (), s32[]{:S(2)}) async-start(), calls=%async_computation.9 | async-start | bytes 2654208 | tf_op jit(solution)/shard_map/all_gather | solution.py:90
  7.9 104.4 %all-gather.16.cloned.1.call-start = ((), (), s32[]{:S(2)}) async-start(), calls=%async_computation.10 | async-start | bytes 2654208 | tf_op jit(solution)/shard_map/all_gather | solution.py:95
  8.7 219.2 %all-gather.18.cloned.1.call-start = ((), (), s32[]{:S(2)}) async-start(), calls=%async_computation.11 | async-start | bytes 17915904 | tf_op jit(solution)/shard_map/all_gather | solution.py:100
  9.5 364.8 %all-gather.20.cloned.1.call-start = ((), (), s32[]{:S(2)}) async-start(), calls=%async_computation.12 | async-start | bytes 17915904 | tf_op jit(solution)/shard_map/all_gather | solution.py:101
  10.1 508.0 %all-gather.22.cloned.1.call-start = ((), (), s32[]{:S(2)}) async-start(), calls=%async_computation.13 | async-start | bytes 17915904 | tf_op jit(solution)/shard_map/all_gather | solution.py:102
  10.7 690.3 %reduce-scatter.36.cloned.1.call-start = ((), (), s32[]{:S(2)}) async-start(), calls=%async_computation.21 | async-start | bytes 17915904 | tf_op jit(solution)/shard_map/reduce_scatter | solution.py:315
  83.7 3.2 collective-permute-start
  86.9 3.8 collective-permute-start.1
  90.7 6.9 collective-permute-start.2
  97.6 9.8 collective-permute-start.3
  115.9 121.8 %copy-start.60 = (f32[128]{0:T(128)}, f32[128]{0:T(128)S(1)}, u32[]{:S(2)}) copy-start(f32[128]{0:T(128)S(1)} %fusion.94) | copy-start | bytes 1540
  116.8 120.9 %copy-start.10 = (bf16[128,1152]{1,0:T(8,128)(2,1)}, bf16[128,1152]{1,0:T(8,128)(2,1)S(1)}, u32[]{:S(2)}) copy-start(bf16[128,1152]{1,0:T(8,128)(2,1)S(1)} %fusion.51) | copy-start | bytes 884740
  536.4 197.1 %reduce-scatter.24.cloned.1.call-start = ((), (), s32[]{:S(2)}) async-start(), calls=%async_computation.15 | async-start | bytes 663552 | tf_op jit(solution)/shard_map/reduce_scatter | solution.py:288
  584.9 3.2 collective-permute-start.4
  588.2 9.4 collective-permute-start.5
  597.6 9.6 collective-permute-start.6
  607.3 9.6 collective-permute-start.7
  620.7 144.8 %reduce-scatter.26.cloned.1.call-start = ((), (), s32[]{:S(2)}) async-start(), calls=%async_computation.16 | async-start | bytes 663552 | tf_op jit(solution)/shard_map/reduce_scatter | solution.py:291
  623.0 180.5 %reduce-scatter.22.cloned.1.call-start = ((), (), s32[]{:S(2)}) async-start(), calls=%async_computation.14 | async-start | bytes 2654208 | tf_op jit(solution)/shard_map/reduce_scatter | solution.py:285
  628.2 337.0 %reduce-scatter.32.cloned.1.call-start = ((), (), s32[]{:S(2)}) async-start(), calls=%async_computation.19 | async-start | bytes 17915904 | tf_op jit(solution)/shard_map/reduce_scatter | solution.py:309
  637.7 489.0 %reduce-scatter.34.cloned.1.call-start = ((), (), s32[]{:S(2)}) async-start(), calls=%async_computation.20 | async-start | bytes 17915904 | tf_op jit(solution)/shard_map/reduce_scatter | solution.py:312
  645.7 602.1 %reduce-scatter.28.cloned.1.call-start = ((), (), s32[]{:S(2)}) async-start(), calls=%async_computation.17 | async-start | bytes 2654208 | tf_op jit(solution)/shard_map/reduce_scatter | solution.py:300
  648.9 639.8 %reduce-scatter.38.cloned.1.call-start = ((), (), s32[]{:S(2)}) async-start(), calls=%async_computation.25 | async-start | bytes 2488320
  701.0 657.5 %reduce-scatter.30.cloned.1.call-start = ((), (), s32[]{:S(2)}) async-start(), calls=%async_computation.18 | async-start | bytes 368640 | tf_op jit(solution)/shard_map/reduce_scatter | solution.py:341
  1242.9 13.3 collective-permute-start.11
  1247.8 157.9 %all-gather.26.cloned.1.call-start = ((), (), s32[]{:S(2)}) async-start(), calls=%async_computation.23 | async-start | bytes 2764800 | tf_op jit(solution)/shard_map/all_gather | solution.py:391
  1264.4 144.7 %all-gather.28.cloned.1.call-start = ((), (), s32[]{:S(2)}) async-start(), calls=%async_computation.24 | async-start | bytes 2764800 | tf_op jit(solution)/shard_map/all_gather | solution.py:394
  1264.6 12.8 collective-permute-start.12
  1288.6 123.9 %all-gather.24.cloned.1.call-start = ((), (), s32[]{:S(2)}) async-start(), calls=%async_computation.22 | async-start | bytes 2488320 | tf_op jit(solution)/shard_map/all_gather | solution.py:397
  1357.2 20.0 %collective-permute-start.9 = (bf16[36,256]{1,0:T(8,128)(2,1)S(1)}, bf16[36,256]{1,0:T(8,128)(2,1)S(1)}, u32[]{:S(2)}, u32[]{:S(2)}) collective-permute-start(bf16[36,256]{1,0:T(8,128)(2,1)S(1)} %slice.69), channel_id=1, source_target_pairs={{0,8},{8,16},{16,24},{1,9},{9,17},{17,25},{2,10},{10,18},{18,26},{... | collective-permute-start | bytes 55304
  1370.9 24.9 %collective-permute-start.8 = (bf16[36,1024]{1,0:T(8,128)(2,1)S(1)}, bf16[36,1024]{1,0:T(8,128)(2,1)S(1)}, u32[]{:S(2)}, u32[]{:S(2)}) collective-permute-start(bf16[36,1024]{1,0:T(8,128)(2,1)S(1)} %slice.68), channel_id=1, source_target_pairs={{0,8},{8,16},{16,24},{1,9},{9,17},{17,25},{2,10},{10,18},{18,26},{... | collective-permute-start | bytes 221192
  1373.6 13.4 collective-permute-start.10
  (89 other events, 1116.4 us)
Sparse Core Ops, SparseCore 0:
  9.6 34.6 all-gather.13
  46.0 36.0 all-gather.15
  83.7 144.1 all-gather.17
  229.4 144.8 all-gather.19
  375.8 142.2 all-gather.21
  536.5 164.4 reduce-scatter.35
  703.8 29.6 reduce-scatter.23
  735.8 29.6 reduce-scatter.25
  768.4 35.0 reduce-scatter.21
  805.7 159.4 reduce-scatter.31
  967.5 159.1 reduce-scatter.33
  1129.4 35.5 reduce-scatter.27
  1168.0 49.5 reduce-scatter.37
  1247.9 23.0 reduce-scatter.29
  1273.2 37.7 all-gather.25
  1312.8 36.4 all-gather.27
  1351.0 38.1 all-gather.23
where the time goes:
time: 1430 us; the launch traced here: 1420 us
  waiting for transfers between devices  906 us (63%)
  blocking collectives  276 us (19%)
  matrix products  113 us (8%)
  local copies, waits for them, and re-layouts  45.2 us (3%)
  starting transfers between devices  42.6 us (3%)
  between operations  22.2 us (2%)
  other arithmetic  18 us (1%)
    unnamed x5, blocking collectives  203 us
    reduce_scatter x1, waiting for transfers between devices, local(): lax.psum_scatter(local_grads[9].astype(jnp.bfloat16), 'ctx', scatter_dime...  162 us
    reduce_scatter x1, waiting for transfers between devices, local(): lax.psum_scatter(local_grads[10].astype(jnp.bfloat16), 'ctx', scatter_dim...  162 us
    all_gather x1, waiting for transfers between devices, local(): lax.all_gather(ffn_local[2], 'ctx', axis=0, tiled=True)  137 us
    all_gather x1, waiting for transfers between devices, local(): lax.all_gather(ffn_local[3], 'ctx', axis=0, tiled=True)  132 us
    all_gather x1, waiting for transfers between devices, local(): lax.all_gather(ffn_local[1], 'ctx', axis=0, tiled=True)  111 us
    reduce_scatter x1, waiting for transfers between devices, local(): lax.psum_scatter(local_grads[11].astype(jnp.bfloat16), 'ctx', scatter_dim...  52.1 us
    dot_general x7, matrix products, project_back(): lax.dot_general(upstream, weight, (((upstream.ndim - 1,), (1,)), ((), ())...  40.4 us
  transfers between devices with their start and end apart: 30, of which 18 were waited for; matrix products, arithmetic and copies ran while one was open for 18% of the time, Pallas kernels for 0%

commit v1 on v0

v1 whole, which is shorter than its diff:
```python
import functools

import jax
import jax.numpy as jnp
from jax import lax
from jax.experimental import pallas as pl
from jax.experimental.pallas import tpu as pltpu
from jax.sharding import PartitionSpec as P

WINDOW = 512


EPS = 1e-06
BASE = 10000.0
MASKED = -1e30
BF16 = jnp.bfloat16
F32 = jnp.float32
MESH = pl.DeviceIdType.MESH


def normed(vector, gain_vec):
    return vector * lax.rsqrt(jnp.mean(vector * vector, axis=-1, keepdims=True) + EPS) * gain_vec


def rotate(vector, angles):
    half_size = vector.shape[-1] // 2
    cosine = jnp.cos(angles)
    sine_part = jnp.sin(angles)
    first_half = vector[..., :half_size]
    second = vector[..., half_size:]
    return jnp.concatenate(
        [first_half * cosine - second * sine_part, second * cosine + first_half * sine_part],
        axis=-1,
    )


def project(inputs, weight):
    return lax.dot_general(inputs, weight, (((1,), (0,)), ((), ())), preferred_element_type=F32)


def project_back(upstream, weight):
    return lax.dot_general(upstream, weight, (((1,), (1,)), ((), ())), preferred_element_type=F32)


def weight_grad(inputs, upstream):
    return lax.dot_general(inputs, upstream, (((0,), (0,)), ((), ())), preferred_element_type=F32)


def gated_gelu(gate_val, up_val):
    return jax.nn.gelu(gate_val, approximate=True) * up_val


def batch_kernel(size, kinds, *refs):
    count = len(kinds)
    sources, results = refs[:count], refs[count : 2 * count]
    send_sem, recv_sem, own_sem = refs[2 * count :]
    me = lax.axis_index("batch")
    barrier = pltpu.get_barrier_semaphore()
    for step in range(1, size):
        pl.semaphore_signal(
            barrier, inc=1, device_id={"batch": lax.rem(me + step, size)}, device_id_type=MESH
        )
    pl.semaphore_wait(barrier, size - 1)
    copies = []
    for step in range(1, size):
        peer = lax.rem(me + step, size)
        for item in range(count):
            source = sources[item].at[peer] if kinds[item] else sources[item]
            copies.append(
                pltpu.make_async_remote_copy(
                    src_ref=source,
                    dst_ref=results[item].at[me],
                    send_sem=send_sem.at[item, step - 1],
                    recv_sem=recv_sem.at[item, step - 1],
                    device_id={"batch": peer},
                    device_id_type=MESH,
                )
            )
    for copy in copies:
        copy.start()
    own = []
    for item in range(count):
        source = sources[item].at[me] if kinds[item] else sources[item]
        own.append(pltpu.make_async_copy(source, results[item].at[me], own_sem.at[item]))
    for copy in own:
        copy.start()
    for copy in own:
        copy.wait()
    for copy in copies:
        copy.wait()


def batch_exchange(name, collective_id, size, whole=(), slots=()):
    arrays = list(whole) + list(slots)
    kinds = [0] * len(whole) + [1] * len(slots)
    count = len(arrays)
    shapes = [
        jax.ShapeDtypeStruct(a.shape if k else (size, *a.shape), a.dtype)
        for a, k in zip(arrays, kinds)
    ]
    return pl.pallas_call(
        functools.partial(batch_kernel, size, kinds),
        name=name,
        out_shape=shapes,
        in_specs=[pl.BlockSpec(memory_space=pltpu.VMEM)] * count,
        out_specs=[pl.BlockSpec(memory_space=pltpu.VMEM)] * count,
        scratch_shapes=[
            pltpu.SemaphoreType.DMA((count, size - 1)),
            pltpu.SemaphoreType.DMA((count, size - 1)),
            pltpu.SemaphoreType.DMA((count,)),
        ],
        compiler_params=pltpu.CompilerParams(collective_id=collective_id, has_side_effects=True),
    )(*arrays)


def halo_kernel(size, depth, direction, source_ref, result_ref, send_sem, recv_sem):
    me = lax.axis_index("ctx")
    barrier = pltpu.get_barrier_semaphore()
    for step in range(1, depth + 1):
        giver = me - direction * step

        @pl.when((giver >= 0) & (giver < size))
        def _():
            pl.semaphore_signal(barrier, inc=1, device_id={"ctx": giver}, device_id_type=MESH)

    takers = jnp.minimum(depth, size - 1 - me) if direction > 0 else jnp.minimum(depth, me)

    @pl.when(takers > 0)
    def _():
        pl.semaphore_wait(barrier, takers)

    def copy(step):
        slot = depth - step
        source = source_ref if direction > 0 else source_ref.at[slot]
        return pltpu.make_async_remote_copy(
            src_ref=source,
            dst_ref=result_ref.at[slot],
            send_sem=send_sem.at[step - 1],
            recv_sem=recv_sem.at[step - 1],
            device_id={"ctx": jnp.clip(me + direction * step, 0, size - 1)},
            device_id_type=MESH,
        )

    for step in range(depth, 0, -1):
        taker = me + direction * step

        @pl.when((taker >= 0) & (taker < size))
        def _():
            copy(step).start()

    for step in range(1, depth + 1):
        taker = me + direction * step
        giver = me - direction * step

        @pl.when((giver < 0) | (giver >= size))
        def _():
            result_ref[depth - step] = jnp.zeros(result_ref.shape[1:], result_ref.dtype)

        @pl.when((giver >= 0) & (giver < size))
        def _():
            copy(step).wait_recv()

        @pl.when((taker >= 0) & (taker < size))
        def _():
            copy(step).wait_send()


def halo_exchange(name, collective_id, size, depth, direction, block):
    return pl.pallas_call(
        functools.partial(halo_kernel, size, depth, direction),
        name=name,
        out_shape=jax.ShapeDtypeStruct((depth, *block.shape[-2:]), block.dtype),
        in_specs=[pl.BlockSpec(memory_space=pltpu.VMEM)],
        out_specs=pl.BlockSpec(memory_space=pltpu.VMEM),
        scratch_shapes=[pltpu.SemaphoreType.DMA((depth,)), pltpu.SemaphoreType.DMA((depth,))],
        compiler_params=pltpu.CompilerParams(collective_id=collective_id, has_side_effects=True),
    )(block)


def gathered(shard):
    return lax.all_gather(shard, "ctx", axis=0, tiled=True)


def scattered(whole):
    return lax.psum_scatter(whole.astype(BF16), "ctx", scatter_dimension=0, tiled=True)


def local(
    n_batch,
    n_ctx,
    block_in,
    positions,
    counts,
    cotangent,
    gain_input,
    w_query,
    w_key,
    w_value,
    gain_query,
    gain_key,
    w_output,
    gain_attn,
    gain_ffn,
    w_gate,
    w_up,
    w_down,
    gain_final,
):
    block_in = block_in[0]
    positions = positions[0]
    cotangent = cotangent[0]
    tok_count, model_width = block_in.shape
    width_shard = w_query.shape[0]
    query_width = w_query.shape[1]
    head_size = w_key.shape[1]
    head_count = query_width // head_size
    hidden = w_gate.shape[1]
    hidden_shard = w_down.shape[0]
    piece = hidden_shard // n_batch
    hidden_part = piece * n_ctx
    halo_depth = (WINDOW + tok_count - 2) // tok_count
    batch_at = lax.axis_index("batch")
    ctx_at = lax.axis_index("ctx")
    all_tok = n_batch * tok_count

    gains = jnp.concatenate(
        [gain_input, gain_attn, gain_ffn, gain_final, gain_query, gain_key]
    )
    gains_all = lax.all_gather(gains, "ctx", axis=0).astype(F32)

    def gain_at(start, length):
        return gains_all[:, start : start + length].reshape(1, -1)

    head_shard = gain_query.shape[0]
    full_gain_in = gain_at(0, width_shard)
    full_gain_attn = gain_at(width_shard, width_shard)
    full_gain_ffn = gain_at(2 * width_shard, width_shard)
    full_gain_final = gain_at(3 * width_shard, width_shard)
    full_gain_q = gain_at(4 * width_shard, head_shard)
    full_gain_k = gain_at(4 * width_shard + head_shard, head_shard)

    def own_columns(weight):
        parts = weight.reshape(width_shard, n_ctx, n_batch, piece)
        mine = lax.dynamic_index_in_dim(parts, batch_at, axis=2, keepdims=False)
        return mine.reshape(width_shard, hidden_part)

    wide_qkv = gathered(jnp.concatenate([w_query, w_key, w_value], axis=1))
    full_output = gathered(w_output)
    part_gate = gathered(own_columns(w_gate))
    part_up = gathered(own_columns(w_up))
    part_down = gathered(lax.dynamic_slice_in_dim(w_down, batch_at * piece, piece, 0))

    first_token = ctx_at * tok_count
    token_place = first_token + jnp.arange(tok_count, dtype=jnp.int32)
    valid_mask = (token_place < counts[0]).astype(F32)[:, None]
    resid_in = block_in.astype(F32)
    act_in = normed(resid_in, full_gain_in).astype(BF16)
    qkv_raw = project(act_in, wide_qkv)
    query_raw = qkv_raw[:, :query_width].reshape(tok_count, head_count, head_size)
    key_raw = qkv_raw[:, query_width : query_width + head_size]
    value_low = qkv_raw[:, query_width + head_size :].astype(BF16)
    inv_freq = BASE ** (-jnp.arange(0, head_size, 2, dtype=F32) / head_size)
    angles = positions.astype(F32)[:, None] * inv_freq

    def query_path(raw_query, gain_vec):
        return rotate(normed(raw_query, gain_vec), angles[:, None, :])

    def key_path(raw_key, gain_vec):
        return rotate(normed(raw_key, gain_vec), angles)

    query_rot = query_path(query_raw, full_gain_q).astype(BF16)
    key_rot = key_path(key_raw, full_gain_k).astype(BF16)
    own_pair = jnp.concatenate([key_rot, value_low], axis=-1)
    halo = halo_exchange("halo_out", 1, n_ctx, halo_depth, 1, own_pair)
    context = jnp.concatenate([halo.reshape(halo_depth * tok_count, -1), own_pair], axis=0)
    ctx_keys = context[:, :head_size]
    ctx_values = context[:, head_size:]
    key_total = (halo_depth + 1) * tok_count
    distance = (
        jnp.arange(tok_count, dtype=jnp.int32)[:, None]
        + halo_depth * tok_count
        - jnp.arange(key_total, dtype=jnp.int32)[None, :]
    )
    allowed = (distance >= 0) & (distance < WINDOW) & (distance <= positions[:, None])
    score_scale = head_size ** (-0.5)
    raw_scores = jnp.einsum("thd,kd->htk", query_rot, ctx_keys, preferred_element_type=F32)
    scores = jnp.where(allowed[None], raw_scores * score_scale, MASKED)
    exp_scores = jnp.exp(scores - jnp.max(scores, axis=-1, keepdims=True))
    attn_prob = exp_scores / jnp.sum(exp_scores, axis=-1, keepdims=True)
    prob_low = attn_prob.astype(BF16)
    attended = jnp.einsum("htk,kd->thd", prob_low, ctx_values, preferred_element_type=F32)
    attn_low = attended.reshape(tok_count, query_width).astype(BF16)
    attn_proj = project(attn_low, full_output)
    middle = resid_in + normed(attn_proj, full_gain_attn)
    ffn_in = normed(middle, full_gain_ffn).astype(BF16)

    ffn_in_all, act_in_all, attn_all = batch_exchange(
        "gather_in", 2, n_batch, whole=(ffn_in, act_in, attn_low)
    )
    ffn_in_all = ffn_in_all.reshape(all_tok, model_width)
    act_in_all = act_in_all.reshape(all_tok, model_width)
    attn_all = attn_all.reshape(all_tok, query_width)
    gate_pre = project(ffn_in_all, part_gate)
    up_pre = project(ffn_in_all, part_up)
    mixed_low = gated_gelu(gate_pre, up_pre).astype(BF16)
    proj_part = project(mixed_low, part_down).astype(BF16)
    (proj_parts,) = batch_exchange(
        "sum_out", 3, n_batch, slots=(proj_part.reshape(n_batch, tok_count, model_width),)
    )
    ffn_proj = jnp.sum(proj_parts.astype(F32), axis=0)
    final_sum = middle + normed(ffn_proj, full_gain_final)
    block_out = (final_sum * valid_mask).astype(BF16)

    grad_final = cotangent.astype(F32) * valid_mask
    _, pull_final = jax.vjp(normed, ffn_proj, full_gain_final)
    grad_ffn_proj, grad_gain_final = pull_final(grad_final)
    (grad_ffn_low,) = batch_exchange("gather_grad", 4, n_batch, whole=(grad_ffn_proj.astype(BF16),))
    grad_ffn_low = grad_ffn_low.reshape(all_tok, model_width)
    grad_w_down = scattered(weight_grad(mixed_low, grad_ffn_low))
    grad_mixed = project_back(grad_ffn_low, part_down)
    _, pull_gelu = jax.vjp(gated_gelu, gate_pre, up_pre)
    grad_gate, grad_up = pull_gelu(grad_mixed)
    grad_gate_low = grad_gate.astype(BF16)
    grad_up_low = grad_up.astype(BF16)
    grad_w_gate = scattered(weight_grad(ffn_in_all, grad_gate_low))
    grad_w_up = scattered(weight_grad(ffn_in_all, grad_up_low))
    back_part = project_back(grad_gate_low, part_gate) + project_back(grad_up_low, part_up)
    (back_parts,) = batch_exchange(
        "sum_back", 5, n_batch, slots=(back_part.astype(BF16).reshape(n_batch, tok_count, model_width),)
    )
    grad_ffn_in = jnp.sum(back_parts.astype(F32), axis=0)
    _, pull_ffn_norm = jax.vjp(normed, middle, full_gain_ffn)
    grad_middle_part, grad_gain_ffn = pull_ffn_norm(grad_ffn_in)
    grad_middle = grad_final + grad_middle_part
    _, pull_attn_norm = jax.vjp(normed, attn_proj, full_gain_attn)
    grad_attn_proj, grad_gain_attn = pull_attn_norm(grad_middle)

    grad_proj_low = grad_attn_proj.astype(BF16)
    grad_attended = (
        project_back(grad_proj_low, full_output)
        .astype(BF16)
        .reshape(tok_count, head_count, head_size)
    )
    grad_prob = jnp.einsum("thd,kd->htk", grad_attended, ctx_values, preferred_element_type=F32)
    row_delta = jnp.sum(attn_prob * grad_prob, axis=-1, keepdims=True)
    grad_scores = (attn_prob * (grad_prob - row_delta)).astype(BF16)
    grad_queries = (
        jnp.einsum("htk,kd->thd", grad_scores, ctx_keys, preferred_element_type=F32) * score_scale
    )
    grad_ctx_keys = (
        jnp.einsum("htk,thd->kd", grad_scores, query_rot, preferred_element_type=F32) * score_scale
    )
    grad_ctx_values = jnp.einsum("htk,thd->kd", prob_low, grad_attended, preferred_element_type=F32)
    grad_context = jnp.concatenate([grad_ctx_keys, grad_ctx_values], axis=-1)
    halo_rows = halo_depth * tok_count
    returned = halo_exchange(
        "halo_back",
        6,
        n_ctx,
        halo_depth,
        -1,
        grad_context[:halo_rows].astype(BF16).reshape(halo_depth, tok_count, 2 * head_size),
    )
    own_grad = grad_context[halo_rows:] + jnp.sum(returned.astype(F32), axis=0)
    grad_value_low = own_grad[:, head_size:].astype(BF16)
    _, pull_key = jax.vjp(key_path, key_raw, full_gain_k)
    grad_key_raw, grad_gain_key = pull_key(own_grad[:, :head_size])
    _, pull_query = jax.vjp(query_path, query_raw, full_gain_q)
    grad_query_raw, grad_gain_query = pull_query(grad_queries)
    grad_qkv_low = jnp.concatenate(
        [
            grad_query_raw.astype(BF16).reshape(tok_count, query_width),
            grad_key_raw.astype(BF16),
            grad_value_low,
        ],
        axis=1,
    )
    grad_act_in = project_back(grad_qkv_low, wide_qkv)
    _, pull_input = jax.vjp(normed, resid_in, full_gain_in)
    grad_in_part, grad_gain_input = pull_input(grad_act_in)
    grad_in = (grad_middle + grad_in_part).astype(BF16)

    def column_slots(upstream):
        return upstream.reshape(tok_count, n_batch, -1).transpose(1, 0, 2)

    qkv_slots, proj_slots = batch_exchange(
        "spread_grads",
        7,
        n_batch,
        slots=(column_slots(grad_qkv_low), column_slots(grad_proj_low)),
    )
    grad_w_output = scattered(weight_grad(attn_all, proj_slots.reshape(all_tok, -1)))
    grad_w_qkv = scattered(weight_grad(act_in_all, qkv_slots.reshape(all_tok, -1)))
    gain_rows = jnp.concatenate(
        [
            grad.reshape(n_ctx, -1)
            for grad in (
                grad_gain_input,
                grad_gain_attn,
                grad_gain_ffn,
                grad_gain_final,
                grad_gain_query,
                grad_gain_key,
            )
        ],
        axis=1,
    )
    gain_sums = lax.psum(gain_rows, ("batch", "ctx"))
    gain_mine = lax.dynamic_index_in_dim(gain_sums, ctx_at, axis=0, keepdims=False)

    (down_all,) = batch_exchange("spread_down", 8, n_batch, whole=(grad_w_down,))
    (gate_all,) = batch_exchange("spread_gate", 9, n_batch, whole=(grad_w_gate,))
    (up_all,) = batch_exchange("spread_up", 10, n_batch, whole=(grad_w_up,))
    qkv_all, output_all = batch_exchange(
        "spread_attn", 11, n_batch, whole=(grad_w_qkv, grad_w_output)
    )

    def columns_back(pieces):
        return pieces.astype(F32).transpose(1, 0, 2).reshape(pieces.shape[1], -1)

    def hidden_back(pieces):
        parts = pieces.reshape(n_batch, width_shard, n_ctx, piece)
        return parts.transpose(1, 2, 0, 3).reshape(width_shard, hidden).astype(F32)

    grad_qkv_shard = columns_back(qkv_all)
    return (
        block_out[None],
        grad_in[None],
        gain_mine[:width_shard],
        grad_qkv_shard[:, :query_width],
        grad_qkv_shard[:, query_width : query_width + head_size],
        grad_qkv_shard[:, query_width + head_size :],
        gain_mine[4 * width_shard : 4 * width_shard + head_shard],
        gain_mine[4 * width_shard + head_shard :],
        columns_back(output_all),
        gain_mine[width_shard : 2 * width_shard],
        gain_mine[2 * width_shard : 3 * width_shard],
        hidden_back(gate_all),
        hidden_back(up_all),
        down_all.reshape(hidden_shard, model_width).astype(F32),
        gain_mine[3 * width_shard : 4 * width_shard],
    )


def solution(mesh):
    matrix = P("ctx", None)
    vector = P("ctx")
    tokens = P("batch", "ctx", None)
    return jax.shard_map(
        functools.partial(local, mesh.shape["batch"], mesh.shape["ctx"]),
        mesh=mesh,
        in_specs=(
            tokens,
            P("batch", "ctx"),
            P("batch"),
            tokens,
            vector,
            matrix,
            matrix,
            matrix,
            vector,
            vector,
            matrix,
            vector,
            vector,
            matrix,
            matrix,
            matrix,
            vector,
        ),
        out_specs=(
            tokens,
            tokens,
            vector,
            matrix,
            matrix,
            matrix,
            vector,
            vector,
            matrix,
            vector,
            vector,
            matrix,
            matrix,
            matrix,
            vector,
        ),
        check_vma=False,
    )
```

time: 1430 us -> 627 us (0.44)
  waiting for transfers between devices: 906 us -> 112 us
  Pallas kernels: 0 us -> 238 us
  blocking collectives: 276 us -> 59.4 us
  local copies, waits for them, and re-layouts: 45.2 us -> 91.9 us
  starting transfers between devices: 42.6 us -> 0.88 us
  matrix products: 113 us -> 77.7 us
    reduce_scatter x8 -> x4, waiting for transfers between devices: 478 us -> 29.5 us  [scattered(): lax.psum_scatter(whole.astype(BF16), 'ctx', scatter_dimension=0, tiled=True)]
    all_gather x8 -> x5, waiting for transfers between devices: 380 us -> 79.4 us  [gathered(): return lax.all_gather(shard, 'ctx', axis=0, tiled=True)]
    pallas_call x0 -> x11, Pallas kernels: none -> 238 us  [the longest x9 204 us: batch_exchange(): pl.pallas_call(functools.partial(batch_kernel, size, kinds), name=name, o...]
    unnamed x5 -> x0, blocking collectives: 203 us -> none
    all_gather x6 -> x1, blocking collectives: 72.1 us -> 15.4 us  [local(): gains_all = lax.all_gather(gains, 'ctx', axis=0).astype(F32)]
    psum x0 -> x1, blocking collectives: none -> 44 us  [local(): gain_sums = lax.psum(gain_rows, ('batch', 'ctx'))]
    dot_general x27 -> x20, matrix products: 113 us -> 76.1 us  [the longest x5 27.4 us: project(): lax.dot_general(inputs, weight, (((1,), (0,)), ((), ())), preferred_eleme...]
    convert_element_type x6 -> x11, local copies, waits for them, and re-layouts: 9.17 us -> 43.4 us  [the longest x6 40.9 us: hidden_back(): return parts.transpose(1, 2, 0, 3).reshape(width_shard, hidden).astype(F32)]
  transfers between devices with their start and end apart: 30 -> 10, of which waited for: 18 -> 6; matrix products, arithmetic and copies ran while one was open for 18% -> 22% of each run, Pallas kernels for 0% -> 21%
where the time goes in v1:
time: 627 us; the launch traced here: 620 us
  Pallas kernels  238 us (38%)
  waiting for transfers between devices  112 us (18%)
  local copies, waits for them, and re-layouts  91.9 us (15%)
  matrix products  77.7 us (12%)
  blocking collectives  59.4 us (9%)
  other arithmetic  23.5 us (4%)
  between operations  16.1 us (3%)
    pallas_call x9, Pallas kernels, batch_exchange(): pl.pallas_call(functools.partial(batch_kernel, size, kinds), name=name, o...  204 us
    all_gather x5, waiting for transfers between devices, gathered(): return lax.all_gather(shard, 'ctx', axis=0, tiled=True)  79.4 us
    psum x1, blocking collectives, local(): gain_sums = lax.psum(gain_rows, ('batch', 'ctx'))  44 us
    convert_element_type x6, local copies, waits for them, and re-layouts, hidden_back(): return parts.transpose(1, 2, 0, 3).reshape(width_shard, hidden).astype(F32)  40.9 us
    pallas_call x2, Pallas kernels, halo_exchange(): pl.pallas_call(functools.partial(halo_kernel, size, depth, direction), na...  34.1 us
    reduce_scatter x4, waiting for transfers between devices, scattered(): lax.psum_scatter(whole.astype(BF16), 'ctx', scatter_dimension=0, tiled=True)  29.5 us
    dot_general x5, matrix products, project(): lax.dot_general(inputs, weight, (((1,), (0,)), ((), ())), preferred_eleme...  27.4 us
    dot_general x5, matrix products, weight_grad(): lax.dot_general(inputs, upstream, (((0,), (0,)), ((), ())), preferred_ele...  22.3 us
  transfers between devices with their start and end apart: 10, of which 6 were waited for; matrix products, arithmetic and copies ran while one was open for 22% of the time, Pallas kernels for 21%

profile of v1, /device:TPU:0, one launch (start us, length us, event | category | flops | bytes accessed | tf_op | source)
XLA Modules:
  0.0 620.1 jit_solution(10459625732277025458)
XLA Ops:
  10.0 10.0 %reshape.361 = bf16[144,8,4,216]{3,2,1,0:T(4,128)(2,1)} reshape(bf16[144,6912]{1,0:T(8,128)(2,1)} %param.30) | data formatting | bytes 3981312 | tf_op jit(solution)/shard_map/reshape | solution.py:243
  20.0 5.7 dynamic-slice_reduce_fusion.1
  27.6 10.0 %reshape.363 = bf16[144,8,4,216]{3,2,1,0:T(4,128)(2,1)} reshape(bf16[144,6912]{1,0:T(8,128)(2,1)} %param.31) | data formatting | bytes 3981312 | tf_op jit(solution)/shard_map/reshape | solution.py:243
  45.8 15.4 %all-gather.1 = bf16[8,1,640]{2,1,0:T(2,128)(2,1)S(1)} all-gather(bf16[1,1,640]{2,1,0:T(2,128)(2,1)S(1)} %reshape.397), channel_id=2, replica_groups=mesh['batch'=4,'ctx'=8] {'ctx'}, dimensions={0}, use_global_device_ids=true | all-gather | bytes 11520 | tf_op jit(solution)/shard_map/all_gather | solution.py:229
  67.7 21.3 %halo_out.1 = bf16[4,128,512]{2,1,0:T(8,128)(2,1)} custom-call(bf16[128,512]{1,0:T(8,128)(2,1)} %pad_maximum_fusion.6.source_ref), custom_call_target="tpu_custom_call" | custom-call | tf_op jit(solution)/shard_map/halo_out/pallas_call | solution.py:169
  97.2 44.0 %gather_in.1 = (bf16[4,128,1152]{2,1,0:T(8,128)(2,1)}, bf16[4,128,1152]{2,1,0:T(8,128)(2,1)}, bf16[4,128,1024]{2,1,0:T(8,128)(2,1)}) custom-call(bf16[128,1152]{1,0:T(8,128)(2,1)} %multiply_convert_fusion.4.refs_0_, bf16[128,1152]{1,0:T(8,128)(2,1)} %copy-done.5, bf16[128,1024]{1,0:T(8,128)(2,1)} %copy.201.refs_2_), custom_call_target="tpu_custom_call" | custom-call | tf_op jit(solution)/shard_map/gather_in/pallas_call | solution.py:101
  144.1 6.8 %fusion.85 = f32[512,1728]{0,1:T(8,128)} fusion(bf16[512,1152]{1,0:T(8,128)(2,1)} %bitcast.202, bf16[1152,1728]{1,0:T(8,128)(2,1)} %all-gather.12.cloned.1.call-done), kind=kOutput, calls=%fused_computation.185 | convolution fusion | flops 2038431744 | bytes 8699904 | tf_op jit(solution)/shard_map/dot_general | solution.py:38
  150.9 40.4 %all-gather.14.cloned.1.call-done = bf16[1152,1728]{1,0:T(8,128)(2,1)} async-done(((bf16[144,1728]{1,0:T(8,128)(2,1)}), bf16[1152,1728]{1,0:T(8,128)(2,1)}) %all-gather.14.cloned.1.call-update) | async-done | bytes 3981328 | tf_op jit(solution)/shard_map/all_gather | solution.py:181
  191.3 9.3 %multiply_convert_fusion.1 = (bf16[512,1728]{0,1:T(8,128)(2,1)}, f32[512,1728]{0,1:T(8,128)}) fusion(f32[512,1728]{0,1:T(8,128)} %fusion.85, bf16[512,1152]{1,0:T(8,128)(2,1)} %bitcast.203, bf16[1152,1728]{1,0:T(8,128)(2,1)} %all-gather.14.cloned.1.call-done), kind=kOutput, calls=%fused_computation.14 | convolution fusion | flops 2047279104 | bytes 14008320 | tf_op jit(solution)/shard_map/dot_general | solution.py:38
  200.6 36.2 %all-gather.16.cloned.1.call-done = bf16[1728,1152]{1,0:T(8,128)(2,1)} async-done(((bf16[216,1152]{1,0:T(8,128)(2,1)}), bf16[1728,1152]{1,0:T(8,128)(2,1)}) %all-gather.16.cloned.1.call-update) | async-done | bytes 3981328 | tf_op jit(solution)/shard_map/all_gather | solution.py:181
  236.8 6.3 %convolution_convert_fusion.3 = bf16[512,1152]{1,0:T(8,128)(2,1)} fusion(bf16[512,1728]{0,1:T(8,128)(2,1)} %get-tuple-element.138, bf16[1728,1152]{1,0:T(8,128)(2,1)} %all-gather.16.cloned.1.call-done), kind=kOutput, calls=%fused_computation.18 | convolution fusion | flops 2039021568 | bytes 6930432 | tf_op jit(solution)/shard_map/dot_general | solution.py:38
  243.1 18.9 %sum_out.1 = bf16[4,128,1152]{2,1,0:T(8,128)(2,1)} custom-call(bf16[4,128,1152]{2,1,0:T(8,128)(2,1)} %bitcast.187), custom_call_target="tpu_custom_call" | custom-call | tf_op jit(solution)/shard_map/sum_out/pallas_call | solution.py:101
  265.1 18.2 %gather_grad.1 = bf16[4,128,1152]{2,1,0:T(8,128)(2,1)} custom-call(bf16[128,1152]{1,0:T(8,128)(2,1)} %get-tuple-element.112.refs_0_), custom_call_target="tpu_custom_call" | custom-call | tf_op jit(solution)/shard_map/gather_grad/pallas_call | solution.py:101
  283.3 9.7 %multiply_convert_fusion = (bf16[512,1728]{0,1:T(8,128)(2,1)S(1)}, bf16[512,1728]{0,1:T(8,128)(2,1)S(1)}) fusion(f32[512,1728]{0,1:T(8,128)} %fusion.85, f32[512,1728]{0,1:T(8,128)} %get-tuple-element.139, bf16[512,1152]{1,0:T(8,128)(2,1)} %bitcast.184, bf16[1728,1152]{1,0:T(8,128)(2,1)} %all-gather.16.cloned.1.call-done), kind=kOutput, calls=%fused_computation.13 | convolution fusion | flops 2059665408 | bytes 15777792 | tf_op jit(solution)/shard_map/dot_general | solution.py:42
  300.2 17.2 %sum_back.1 = bf16[4,128,1152]{2,1,0:T(8,128)(2,1)} custom-call(bf16[4,128,1152]{2,1,0:T(8,128)(2,1)} %bitcast.186), custom_call_target="tpu_custom_call" | custom-call | tf_op jit(solution)/shard_map/sum_back/pallas_call | solution.py:101
  328.4 12.8 %halo_back.1 = bf16[4,128,512]{2,1,0:T(8,128)(2,1)} custom-call(bf16[4,128,512]{2,1,0:T(8,128)(2,1)} %bitcast.179), custom_call_target="tpu_custom_call" | custom-call | tf_op jit(solution)/shard_map/halo_back/pallas_call | solution.py:169
  350.3 14.2 %spread_grads.1 = (bf16[4,128,384]{2,1,0:T(8,128)(2,1)}, bf16[4,128,288]{2,1,0:T(8,128)(2,1)}) custom-call(bf16[4,128,384]{2,1,0:T(8,128)(2,1)} %bitcast.181, bf16[4,128,288]{2,1,0:T(8,128)(2,1)} %bitcast.183), custom_call_target="tpu_custom_call" | custom-call | tf_op jit(solution)/shard_map/spread_grads/pallas_call | solution.py:101
  370.5 5.9 convolution_convert_fusion.2
  376.4 5.9 convolution_convert_fusion.1
  383.6 5.9 convolution_convert_fusion
  394.3 44.0 %psum.7 = f32[8,640]{1,0:T(8,128)S(1)} all-reduce(f32[8,640]{1,0:T(8,128)S(1)} %concatenate.35), channel_id=1, replica_groups=mesh['batch'=4,'ctx'=8] {'batch','ctx'}, use_global_device_ids=true, to_apply=%region_24.25 | all-reduce | flops 5120 | bytes 40960 | tf_op jit(solution)/shard_map/psum | solution.py:408
  440.4 14.1 %spread_attn.1 = (bf16[4,144,384]{2,1,0:T(8,128)(2,1)}, bf16[4,128,288]{2,1,0:T(8,128)(2,1)}) custom-call(bf16[144,384]{1,0:T(8,128)(2,1)} %reduce-scatter.8.cloned.1.call-done.refs_0_, bf16[128,288]{1,0:T(8,128)(2,1)} %reduce-scatter.10.cloned.1.call-done.refs_1_), custom_call_target="tpu_custom_call" | custom-call | tf_op jit(solution)/shard_map/spread_attn/pallas_call | solution.py:101
  458.7 25.9 %reduce-scatter.12.cloned.1.call-done.refs_0_ = bf16[144,1728]{1,0:T(8,128)(2,1)} async-done(((bf16[1152,1728]{1,0:T(8,128)(2,1)}), bf16[144,1728]{1,0:T(8,128)(2,1)}) %reduce-scatter.12.cloned.1.call-update) | async-done | bytes 497680 | tf_op jit(solution)/shard_map/reduce_scatter | solution.py:185
  484.6 26.1 %spread_gate.1 = bf16[4,144,1728]{2,1,0:T(8,128)(2,1)} custom-call(bf16[144,1728]{1,0:T(8,128)(2,1)} %reduce-scatter.12.cloned.1.call-done.refs_0_), custom_call_target="tpu_custom_call" | custom-call | tf_op jit(solution)/shard_map/spread_gate/pallas_call | solution.py:101
  510.6 6.2 %reshape.393 = f32[4,144,8,216]{3,2,1,0:T(8,128)} reshape(bf16[4,144,1728]{2,1,0:T(8,128)(2,1)} %spread_gate.1) | data formatting | bytes 5971968 | tf_op jit(solution)/shard_map/convert_element_type | solution.py:423
  516.9 7.5 %copy.185 = f32[144,8,4,216]{3,2,1,0:T(4,128)} copy(f32[144,8,4,216]{3,1,0,2:T(8,128)} %bitcast.171) | data formatting | bytes 7962624 | tf_op jit(solution)/shard_map/convert_element_type | solution.py:423
  524.4 6.6 %reshape.388 = f32[144,6912]{1,0:T(8,128)} reshape(f32[144,8,4,216]{3,2,1,0:T(4,128)} %copy.185) | data formatting | bytes 7962624 | tf_op jit(solution)/shard_map/convert_element_type | solution.py:423
  534.7 26.1 %spread_up.1 = bf16[4,144,1728]{2,1,0:T(8,128)(2,1)} custom-call(bf16[144,1728]{1,0:T(8,128)(2,1)} %reduce-scatter.14.cloned.1.call-done.refs_0_), custom_call_target="tpu_custom_call" | custom-call | tf_op jit(solution)/shard_map/spread_up/pallas_call | solution.py:101
  560.8 6.3 %reshape.394 = f32[4,144,8,216]{3,2,1,0:T(8,128)} reshape(bf16[4,144,1728]{2,1,0:T(8,128)(2,1)} %spread_up.1) | data formatting | bytes 5971968 | tf_op jit(solution)/shard_map/convert_element_type | solution.py:423
  567.1 7.6 %copy.186 = f32[144,8,4,216]{3,2,1,0:T(4,128)} copy(f32[144,8,4,216]{3,1,0,2:T(8,128)} %bitcast.172) | data formatting | bytes 7962624 | tf_op jit(solution)/shard_map/convert_element_type | solution.py:423
  574.8 6.5 %reshape.389 = f32[144,6912]{1,0:T(8,128)} reshape(f32[144,8,4,216]{3,2,1,0:T(4,128)} %copy.186) | data formatting | bytes 7962624 | tf_op jit(solution)/shard_map/convert_element_type | solution.py:423
  583.9 25.4 %spread_down.1 = bf16[4,216,1152]{2,1,0:T(8,128)(2,1)} custom-call(bf16[216,1152]{1,0:T(8,128)(2,1)} %reduce-scatter.16.cloned.1.call-done.refs_0_), custom_call_target="tpu_custom_call" | custom-call | tf_op jit(solution)/shard_map/spread_down/pallas_call | solution.py:101
  (233 shorter events, 87.8 us)
Async XLA Ops:
  7.2 37.5 %copy-start = (bf16[864,1152]{1,0:T(8,128)(2,1)S(1)}, bf16[864,1152]{1,0:T(8,128)(2,1)}, u32[]{:S(2)}) copy-start(bf16[864,1152]{1,0:T(8,128)(2,1)} %param.32) | copy-start | bytes 5971972
  7.2 56.3 %all-gather.8.cloned.1.call-start = ((), (), s32[]{:S(2)}) async-start(), calls=%async_computation.5 | async-start | bytes 3981312 | tf_op jit(solution)/shard_map/all_gather | solution.py:181
  9.2 84.6 %all-gather.10.cloned.1.call-start = ((), (), s32[]{:S(2)}) async-start(), calls=%async_computation.6 | async-start | bytes 2654208 | tf_op jit(solution)/shard_map/all_gather | solution.py:181
  10.0 134.1 %all-gather.12.cloned.1.call-start = ((), (), s32[]{:S(2)}) async-start(), calls=%async_computation.7 | async-start | bytes 4644864 | tf_op jit(solution)/shard_map/all_gather | solution.py:181
  27.1 164.2 %all-gather.14.cloned.1.call-start = ((), (), s32[]{:S(2)}) async-start(), calls=%async_computation.8 | async-start | bytes 4644864 | tf_op jit(solution)/shard_map/all_gather | solution.py:181
  43.1 19.4 %copy-start.3 = (bf16[1,128,1152]{2,1,0:T(8,128)(2,1)S(1)}, bf16[1,128,1152]{2,1,0:T(8,128)(2,1)}, u32[]{:S(2)}) copy-start(bf16[1,128,1152]{2,1,0:T(8,128)(2,1)} %param.17) | copy-start | bytes 884740
  43.2 20.0 %copy-start.41 = (s32[1,128]{1,0:T(1,128)S(1)}, s32[1,128]{1,0:T(1,128)}, u32[]{:S(2)}) copy-start(s32[1,128]{1,0:T(1,128)} %param.18) | copy-start | bytes 1540
  44.6 192.2 %all-gather.16.cloned.1.call-start = ((), (), s32[]{:S(2)}) async-start(), calls=%async_computation.9 | async-start | bytes 4478976 | tf_op jit(solution)/shard_map/all_gather | solution.py:181
  45.5 394.9 %reduce-scatter.10.cloned.1.call-start = ((), (), s32[]{:S(2)}) async-start(), calls=%async_computation.11 | async-start | bytes 884736 | tf_op jit(solution)/shard_map/reduce_scatter | solution.py:185
  45.7 20.9 %copy-start.25 = (f32[128]{0:T(128)}, f32[128]{0:T(128)S(1)}, u32[]{:S(2)}) copy-start(f32[128]{0:T(128)S(1)} %multiply_power_fusion) | copy-start | bytes 1540
  63.2 3.1 copy-start.29
  63.2 3.4 copy-start.27
  63.3 28.7 %copy-start.24 = (pred[128,640]{0,1:T(8,128)(4,1)}, pred[128,640]{0,1:T(8,128)(4,1)S(1)}, u32[]{:S(2)}) copy-start(pred[128,640]{0,1:T(8,128)(4,1)S(1)} %fusion.44) | copy-start | bytes 245764
  66.3 23.2 %copy-start.4 = (f32[128,1536]{1,0:T(8,128)}, f32[128,1536]{1,0:T(8,128)S(1)}, u32[]{:S(2)}) copy-start(f32[128,1536]{1,0:T(8,128)S(1)} %fusion.84) | copy-start | bytes 2359300
  66.5 22.8 %copy-start.33 = (f32[128]{0:T(128)}, f32[128]{0:T(128)S(1)}, u32[]{:S(2)}) copy-start(f32[128]{0:T(128)S(1)} %multiply_reduce_fusion.12) | copy-start | bytes 1540
  67.0 23.3 %copy-start.15 = (f32[128,128]{1,0:T(8,128)}, f32[128,128]{1,0:T(8,128)S(1)}, u32[]{:S(2)}) copy-start(f32[128,128]{1,0:T(8,128)S(1)} %get-tuple-element.130) | copy-start | bytes 196612
  67.0 23.3 %copy-start.17 = (f32[128,128]{1,0:T(8,128)}, f32[128,128]{1,0:T(8,128)S(1)}, u32[]{:S(2)}) copy-start(f32[128,128]{1,0:T(8,128)S(1)} %get-tuple-element.131) | copy-start | bytes 196612
  243.1 20.5 %copy-start.6 = (bf16[1,128,1152]{2,1,0:T(8,128)(2,1)S(1)}, bf16[1,128,1152]{2,1,0:T(8,128)(2,1)}, u32[]{:S(2)}) copy-start(bf16[1,128,1152]{2,1,0:T(8,128)(2,1)} %param.20) | copy-start | bytes 884740
  283.3 9.7 %copy-start.42 = (bf16[1152,1728]{1,0:T(8,128)(2,1)S(1)}, bf16[1152,1728]{1,0:T(8,128)(2,1)}, u32[]{:S(2)}) copy-start(bf16[1152,1728]{1,0:T(8,128)(2,1)} %all-gather.12.cloned.1.call-done) | copy-start | bytes 11943940
  293.0 3.4 copy-start.43
  328.4 15.0 %copy-start.26 = (f32[128]{0:T(128)S(1)}, f32[128]{0:T(128)}, u32[]{:S(2)}) copy-start(f32[128]{0:T(128)} %copy-done.25) | copy-start | bytes 1540
  328.4 15.0 %copy-start.28 = (f32[128]{0:T(128)S(1)}, f32[128]{0:T(128)}, u32[]{:S(2)}) copy-start(f32[128]{0:T(128)} %copy-done.27) | copy-start | bytes 1540
  342.4 3.2 copy-start.34
  343.4 3.4 copy-start.16
  348.2 16.3 %copy-start.14 = (bf16[4,128,1024]{2,1,0:T(8,128)(2,1)S(1)}, bf16[4,128,1024]{2,1,0:T(8,128)(2,1)}, u32[]{:S(2)}) copy-start(bf16[4,128,1024]{2,1,0:T(8,128)(2,1)} %get-tuple-element.25) | copy-start | bytes 3145732
  367.2 3.2 copy-start.44
  367.3 73.2 %reduce-scatter.8.cloned.1.call-start = ((), (), s32[]{:S(2)}) async-start(), calls=%async_computation.10 | async-start | bytes 995328 | tf_op jit(solution)/shard_map/reduce_scatter | solution.py:185
  370.4 114.1 %reduce-scatter.12.cloned.1.call-start = ((), (), s32[]{:S(2)}) async-start(), calls=%async_computation.12 | async-start | bytes 4644864 | tf_op jit(solution)/shard_map/reduce_scatter | solution.py:185
  376.4 158.3 %reduce-scatter.14.cloned.1.call-start = ((), (), s32[]{:S(2)}) async-start(), calls=%async_computation.13 | async-start | bytes 4644864 | tf_op jit(solution)/shard_map/reduce_scatter | solution.py:185
  382.3 201.6 %reduce-scatter.16.cloned.1.call-start = ((), (), s32[]{:S(2)}) async-start(), calls=%async_computation.14 | async-start | bytes 4478976
  390.3 49.2 %copy-start.32 = (f32[128]{0:T(128)S(1)}, f32[128]{0:T(128)}, u32[]{:S(2)}) copy-start(f32[128]{0:T(128)} %copy-done.31) | copy-start | bytes 1540
  583.9 29.1 %copy-start.1 = (bf16[864,1152]{1,0:T(8,128)(2,1)S(1)}, bf16[864,1152]{1,0:T(8,128)(2,1)}, u32[]{:S(2)}) copy-start(bf16[864,1152]{1,0:T(8,128)(2,1)} %param.32) | copy-start | bytes 5971972
  (26 other events, 49.1 us)
Sparse Core Ops, SparseCore 0:
  10.2 44.1 all-gather.7
  56.1 35.8 all-gather.9
  94.2 49.8 all-gather.11
  146.2 45.1 all-gather.13
  192.8 43.9 all-gather.15
  367.4 34.3 reduce-scatter.9
  404.0 30.7 reduce-scatter.7
  437.1 47.3 reduce-scatter.11
  486.9 47.7 reduce-scatter.13
  537.4 46.4 reduce-scatter.15

commit v2 on v1

--- a/solution.py
+++ b/solution.py
@@ -177,6 +177,207 @@
     )(block)
 
 
+def pick_kernel(n_batch, n_ctx, piece, gate_ref, up_ref, gate_out, up_out):
+    me = lax.axis_index("batch")
+    for spot in range(n_batch):
+
+        @pl.when(me == spot)
+        def _():
+            for shard in range(n_ctx):
+                start = (shard * n_batch + spot) * piece
+                place = pl.ds(shard * piece, piece)
+                gate_out[:, place] = gate_ref[:, start : start + piece]
+                up_out[:, place] = up_ref[:, start : start + piece]
+
+
+def pick_columns(n_batch, n_ctx, piece, w_gate, w_up):
+    rows = w_gate.shape[0]
+    block = 48 if rows % 48 == 0 else rows
+    spec = pl.BlockSpec((block, w_gate.shape[1]), lambda i: (i, 0))
+    out_spec = pl.BlockSpec((block, n_ctx * piece), lambda i: (i, 0))
+    out = jax.ShapeDtypeStruct((rows, n_ctx * piece), w_gate.dtype)
+    return pl.pallas_call(
+        functools.partial(pick_kernel, n_batch, n_ctx, piece),
+        name="pick_columns",
+        grid=(rows // block,),
+        out_shape=(out, out),
+        in_specs=[spec, spec],
+        out_specs=[out_spec, out_spec],
+    )(w_gate, w_up)
+
+
+def place_kernel(n_batch, n_ctx, piece, parts_ref, out_ref):
+    for shard in range(n_ctx):
+        for spot in range(n_batch):
+            start = (shard * n_batch + spot) * piece
+            out_ref[:, start : start + piece] = parts_ref[
+                spot, :, shard * piece : (shard + 1) * piece
+            ].astype(F32)
+
+
+def place_columns(name, n_batch, n_ctx, piece, parts):
+    rows = parts.shape[1]
+    block = 48 if rows % 48 == 0 else rows
+    hidden = n_batch * n_ctx * piece
+    return pl.pallas_call(
+        functools.partial(place_kernel, n_batch, n_ctx, piece),
+        name=name,
+        grid=(rows // block,),
+        out_shape=jax.ShapeDtypeStruct((rows, hidden), F32),
+        in_specs=[pl.BlockSpec((n_batch, block, n_ctx * piece), lambda i: (0, i, 0))],
+        out_specs=pl.BlockSpec((block, hidden), lambda i: (i, 0)),
+    )(parts)
+
+
+def weights_kernel(n_batch, n_ctx, qkv_ref, proj_ref, gain_ref, qkv_all, proj_all, gain_all, *sems):
+    send_far, recv_far, send_side, recv_side, send_near, recv_near, own_sem = sems
+    spot = lax.axis_index("batch")
+    me = lax.axis_index("ctx")
+    n_chip = n_ctx // 2
+    chip, core = me // 2, lax.rem(me, 2)
+    near = {"ctx": me + 1 - 2 * core}
+    barrier = pltpu.get_barrier_semaphore()
+
+    def far_at(step):
+        return {"ctx": 2 * lax.rem(chip + step, n_chip) + core}
+
+    def side_at(step):
+        return {"batch": lax.rem(spot + step, n_batch)}
+
+    peers = [near]
+    peers += [far_at(step) for step in range(1, n_chip)]
+    peers += [side_at(step) for step in range(1, n_batch)]
+    for peer in peers:
+        pl.semaphore_signal(barrier, inc=1, device_id=peer, device_id_type=MESH)
+    pl.semaphore_wait(barrier, len(peers))
+
+    def remote(source, target, send, recv, peer):
+        return pltpu.make_async_remote_copy(
+            src_ref=source,
+            dst_ref=target,
+            send_sem=send,
+            recv_sem=recv,
+            device_id=peer,
+            device_id_type=MESH,
+        )
+
+    waits = []
+    far = []
+    for step in range(1, n_chip):
+        triple = [
+            remote(source, target, send_far.at[step - 1, item], recv_far.at[step - 1, item], far_at(step))
+            for item, (source, target) in enumerate(
+                (
+                    (qkv_ref.at[spot], qkv_all.at[spot, me]),
+                    (proj_ref.at[spot], proj_all.at[me, spot]),
+                    (gain_ref, gain_all.at[me]),
+                )
+            )
+        ]
+        for copy in triple:
+            copy.start()
+        far.append(triple)
+    own = [
+        pltpu.make_async_copy(qkv_ref, qkv_all.at[:, me], own_sem.at[0]),
+        pltpu.make_async_copy(proj_ref, proj_all.at[me], own_sem.at[1]),
+        pltpu.make_async_copy(gain_ref, gain_all.at[me], own_sem.at[2]),
+    ]
+    for copy in own:
+        copy.start()
+    first = n_chip - 1
+    pairs = [
+        remote(source, target, send_near.at[first, 0, item], recv_near.at[first, 0, item], near)
+        for item, (source, target) in enumerate(
+            (
+                (qkv_ref, qkv_all.at[:, me]),
+                (proj_ref, proj_all.at[me]),
+                (gain_ref, gain_all.at[me]),
+            )
+        )
+    ]
+    for copy in pairs:
+        copy.start()
+    waits += pairs
+
+    def hand_near(step, turn):
+        origin = 2 * lax.rem(chip + n_chip - step, n_chip) + core
+        quarter = lax.rem(spot + n_batch - turn, n_batch)
+        blocks = [qkv_all.at[quarter, origin], proj_all.at[origin, quarter]]
+        blocks += [gain_all.at[origin]] if turn == 0 else []
+        for item, block in enumerate(blocks):
+            copy = remote(
+                block,
+                block,
+                send_near.at[step - 1, turn, item],
+                recv_near.at[step - 1, turn, item],
+                near,
+            )
+            copy.start()
+            waits.append(copy)
+
+    side = []
+    for step in range(1, n_chip):
+        for copy in far[step - 1]:
+            copy.wait_recv()
+        origin = 2 * lax.rem(chip + n_chip - step, n_chip) + core
+        for turn in range(1, n_batch):
+            pair = [
+                remote(
+                    block,
+                    block,
+                    send_side.at[step - 1, turn - 1, item],
+                    recv_side.at[step - 1, turn - 1, item],
+                    side_at(turn),
+                )
+                for item, block in enumerate((qkv_all.at[spot, origin], proj_all.at[origin, spot]))
+            ]
+            for copy in pair:
+                copy.start()
+            side.append((step, turn, pair))
+        hand_near(step, 0)
+    for step, turn, pair in side:
+        for copy in pair:
+            copy.wait_recv()
+        hand_near(step, turn)
+    for copy in waits:
+        copy.wait()
+    for copy in own:
+        copy.wait()
+    for triple in far:
+        for copy in triple:
+            copy.wait_send()
+    for _, _, pair in side:
+        for copy in pair:
+            copy.wait_send()
+
+
+def gather_weights(n_batch, n_ctx, qkv, proj, gains):
+    n_chip = n_ctx // 2
+    dma = pltpu.SemaphoreType.DMA
+    vmem = pl.BlockSpec(memory_space=pltpu.VMEM)
+    return pl.pallas_call(
+        functools.partial(weights_kernel, n_batch, n_ctx),
+        name="gather_weights",
+        out_shape=(
+            jax.ShapeDtypeStruct((n_batch, n_ctx, *qkv.shape[1:]), qkv.dtype),
+            jax.ShapeDtypeStruct((n_ctx, *proj.shape), proj.dtype),
+            jax.ShapeDtypeStruct((n_ctx, *gains.shape), gains.dtype),
+        ),
+        in_specs=[vmem] * 3,
+        out_specs=[vmem] * 3,
+        scratch_shapes=[
+            dma((n_chip - 1, 3)),
+            dma((n_chip - 1, 3)),
+            dma((n_chip - 1, n_batch - 1, 2)),
+            dma((n_chip - 1, n_batch - 1, 2)),
+            dma((n_chip, n_batch, 3)),
+            dma((n_chip, n_batch, 3)),
+            dma((3,)),
+        ],
+        compiler_params=pltpu.CompilerParams(collective_id=12, has_side_effects=True),
+    )(qkv, proj, gains)
+
+
 def gathered(shard):
     return lax.all_gather(shard, "ctx", axis=0, tiled=True)
 
@@ -214,10 +415,8 @@
     query_width = w_query.shape[1]
     head_size = w_key.shape[1]
     head_count = query_width // head_size
-    hidden = w_gate.shape[1]
     hidden_shard = w_down.shape[0]
     piece = hidden_shard // n_batch
-    hidden_part = piece * n_ctx
     halo_depth = (WINDOW + tok_count - 2) // tok_count
     batch_at = lax.axis_index("batch")
     ctx_at = lax.axis_index("ctx")
@@ -226,7 +425,20 @@
     gains = jnp.concatenate(
         [gain_input, gain_attn, gain_ffn, gain_final, gain_query, gain_key]
     )
-    gains_all = lax.all_gather(gains, "ctx", axis=0).astype(F32)
+    slots_of = query_width + 2 * head_size
+    quarter = slots_of // n_batch
+    qkv_full, proj_full, gains_all = gather_weights(
+        n_batch,
+        n_ctx,
+        jnp.concatenate([w_query, w_key, w_value], axis=1)
+        .reshape(width_shard, n_batch, quarter)
+        .transpose(1, 0, 2),
+        w_output.reshape(n_batch, -1, model_width),
+        gains[None],
+    )
+    qkv_full = qkv_full.reshape(n_batch, model_width, quarter)
+    full_output = proj_full.reshape(query_width, model_width)
+    gains_all = gains_all[:, 0].astype(F32)
 
     def gain_at(start, length):
         return gains_all[:, start : start + length].reshape(1, -1)
@@ -239,23 +451,17 @@
     full_gain_q = gain_at(4 * width_shard, head_shard)
     full_gain_k = gain_at(4 * width_shard + head_shard, head_shard)
 
-    def own_columns(weight):
-        parts = weight.reshape(width_shard, n_ctx, n_batch, piece)
-        mine = lax.dynamic_index_in_dim(parts, batch_at, axis=2, keepdims=False)
-        return mine.reshape(width_shard, hidden_part)
-
-    wide_qkv = gathered(jnp.concatenate([w_query, w_key, w_value], axis=1))
-    full_output = gathered(w_output)
-    part_gate = gathered(own_columns(w_gate))
-    part_up = gathered(own_columns(w_up))
     part_down = gathered(lax.dynamic_slice_in_dim(w_down, batch_at * piece, piece, 0))
+    own_gate, own_up = pick_columns(n_batch, n_ctx, piece, w_gate, w_up)
+    part_gate = gathered(own_gate)
+    part_up = gathered(own_up)
 
     first_token = ctx_at * tok_count
     token_place = first_token + jnp.arange(tok_count, dtype=jnp.int32)
     valid_mask = (token_place < counts[0]).astype(F32)[:, None]
     resid_in = block_in.astype(F32)
     act_in = normed(resid_in, full_gain_in).astype(BF16)
-    qkv_raw = project(act_in, wide_qkv)
+    qkv_raw = jnp.concatenate([project(act_in, qkv_full[i]) for i in range(n_batch)], axis=1)
     query_raw = qkv_raw[:, :query_width].reshape(tok_count, head_count, head_size)
     key_raw = qkv_raw[:, query_width : query_width + head_size]
     value_low = qkv_raw[:, query_width + head_size :].astype(BF16)
@@ -316,18 +522,26 @@
     grad_ffn_proj, grad_gain_final = pull_final(grad_final)
     (grad_ffn_low,) = batch_exchange("gather_grad", 4, n_batch, whole=(grad_ffn_proj.astype(BF16),))
     grad_ffn_low = grad_ffn_low.reshape(all_tok, model_width)
-    grad_w_down = scattered(weight_grad(mixed_low, grad_ffn_low))
+    down_grad = weight_grad(mixed_low, grad_ffn_low).astype(BF16)
+    down_grad, grad_ffn_low = lax.optimization_barrier((down_grad, grad_ffn_low))
+    grad_w_down = scattered(down_grad)
     grad_mixed = project_back(grad_ffn_low, part_down)
     _, pull_gelu = jax.vjp(gated_gelu, gate_pre, up_pre)
     grad_gate, grad_up = pull_gelu(grad_mixed)
     grad_gate_low = grad_gate.astype(BF16)
     grad_up_low = grad_up.astype(BF16)
-    grad_w_gate = scattered(weight_grad(ffn_in_all, grad_gate_low))
-    grad_w_up = scattered(weight_grad(ffn_in_all, grad_up_low))
     back_part = project_back(grad_gate_low, part_gate) + project_back(grad_up_low, part_up)
     (back_parts,) = batch_exchange(
         "sum_back", 5, n_batch, slots=(back_part.astype(BF16).reshape(n_batch, tok_count, model_width),)
     )
+    back_parts, grad_gate_low, grad_up_low = lax.optimization_barrier(
+        (back_parts, grad_gate_low, grad_up_low)
+    )
+    gate_grad = weight_grad(ffn_in_all, grad_gate_low).astype(BF16)
+    up_grad = weight_grad(ffn_in_all, grad_up_low).astype(BF16)
+    back_parts, gate_grad, up_grad = lax.optimization_barrier((back_parts, gate_grad, up_grad))
+    grad_w_gate = scattered(gate_grad)
+    grad_w_up = scattered(up_grad)
     grad_ffn_in = jnp.sum(back_parts.astype(F32), axis=0)
     _, pull_ffn_norm = jax.vjp(normed, middle, full_gain_ffn)
     grad_middle_part, grad_gain_ffn = pull_ffn_norm(grad_ffn_in)
@@ -375,7 +589,10 @@
         ],
         axis=1,
     )
-    grad_act_in = project_back(grad_qkv_low, wide_qkv)
+    grad_act_in = sum(
+        project_back(grad_qkv_low[:, i * quarter : (i + 1) * quarter], qkv_full[i])
+        for i in range(n_batch)
+    )
     _, pull_input = jax.vjp(normed, resid_in, full_gain_in)
     grad_in_part, grad_gain_input = pull_input(grad_act_in)
     grad_in = (grad_middle + grad_in_part).astype(BF16)
@@ -383,14 +600,6 @@
     def column_slots(upstream):
         return upstream.reshape(tok_count, n_batch, -1).transpose(1, 0, 2)
 
-    qkv_slots, proj_slots = batch_exchange(
-        "spread_grads",
-        7,
-        n_batch,
-        slots=(column_slots(grad_qkv_low), column_slots(grad_proj_low)),
-    )
-    grad_w_output = scattered(weight_grad(attn_all, proj_slots.reshape(all_tok, -1)))
-    grad_w_qkv = scattered(weight_grad(act_in_all, qkv_slots.reshape(all_tok, -1)))
     gain_rows = jnp.concatenate(
         [
             grad.reshape(n_ctx, -1)
@@ -405,24 +614,48 @@
         ],
         axis=1,
     )
-    gain_sums = lax.psum(gain_rows, ("batch", "ctx"))
-    gain_mine = lax.dynamic_index_in_dim(gain_sums, ctx_at, axis=0, keepdims=False)
+    gain_parts, qkv_slots, proj_slots = batch_exchange(
+        "spread_grads",
+        7,
+        n_batch,
+        whole=(gain_rows,),
+        slots=(column_slots(grad_qkv_low), column_slots(grad_proj_low)),
+    )
+    proj_rows = w_output.shape[0]
+    gain_count = gain_rows.shape[1]
+    gain_lines = -(-gain_count // quarter)
+    used = width_shard + proj_rows + gain_lines
+    lines = -(-used // 16) * 16
+    grad_w_output = weight_grad(attn_all, proj_slots.reshape(all_tok, -1)).astype(BF16)
+    grad_w_qkv = weight_grad(act_in_all, qkv_slots.reshape(all_tok, -1)).astype(BF16)
+    output_part = model_width // n_batch
+    gain_sum = jnp.sum(gain_parts, axis=0).astype(BF16)
+    packed = jnp.concatenate(
+        [
+            grad_w_qkv.reshape(n_ctx, width_shard, quarter),
+            jnp.pad(
+                grad_w_output.reshape(n_ctx, proj_rows, output_part),
+                ((0, 0), (0, 0), (0, quarter - output_part)),
+            ),
+            jnp.pad(gain_sum, ((0, 0), (0, gain_lines * quarter - gain_count))).reshape(
+                n_ctx, gain_lines, quarter
+            ),
+            jnp.zeros((n_ctx, lines - used, quarter), BF16),
+        ],
+        axis=1,
+    )
+    attn_sum = scattered(packed.reshape(n_ctx * lines, quarter))
 
     (down_all,) = batch_exchange("spread_down", 8, n_batch, whole=(grad_w_down,))
     (gate_all,) = batch_exchange("spread_gate", 9, n_batch, whole=(grad_w_gate,))
     (up_all,) = batch_exchange("spread_up", 10, n_batch, whole=(grad_w_up,))
-    qkv_all, output_all = batch_exchange(
-        "spread_attn", 11, n_batch, whole=(grad_w_qkv, grad_w_output)
-    )
+    (attn_grads,) = batch_exchange("spread_attn", 11, n_batch, whole=(attn_sum,))
+    gain_mine = attn_grads[0, width_shard + proj_rows : used].reshape(-1).astype(F32)
 
     def columns_back(pieces):
         return pieces.astype(F32).transpose(1, 0, 2).reshape(pieces.shape[1], -1)
 
-    def hidden_back(pieces):
-        parts = pieces.reshape(n_batch, width_shard, n_ctx, piece)
-        return parts.transpose(1, 2, 0, 3).reshape(width_shard, hidden).astype(F32)
-
-    grad_qkv_shard = columns_back(qkv_all)
+    grad_qkv_shard = columns_back(attn_grads[:, :width_shard])
     return (
         block_out[None],
         grad_in[None],
@@ -431,12 +664,12 @@
         grad_qkv_shard[:, query_width : query_width + head_size],
         grad_qkv_shard[:, query_width + head_size :],
         gain_mine[4 * width_shard : 4 * width_shard + head_shard],
-        gain_mine[4 * width_shard + head_shard :],
-        columns_back(output_all),
+        gain_mine[4 * width_shard + head_shard : gain_count],
+        columns_back(attn_grads[:, width_shard : width_shard + proj_rows, :output_part]),
         gain_mine[width_shard : 2 * width_shard],
         gain_mine[2 * width_shard : 3 * width_shard],
-        hidden_back(gate_all),
-        hidden_back(up_all),
+        place_columns("place_gate", n_batch, n_ctx, piece, gate_all),
+        place_columns("place_up", n_batch, n_ctx, piece, up_all),
         down_all.reshape(hidden_shard, model_width).astype(F32),
         gain_mine[3 * width_shard : 4 * width_shard],
     )

time: 627 us -> 579 us (0.923)
  Pallas kernels: 238 us -> 312 us
  local copies, waits for them, and re-layouts: 91.9 us -> 22.1 us
  blocking collectives: 59.4 us -> 0 us
    all_gather x5 -> x3, waiting for transfers between devices: 79.4 us -> 7.44 us  [gathered(): return lax.all_gather(shard, 'ctx', axis=0, tiled=True)]
    pallas_call x0 -> x4, Pallas kernels: none -> 62.3 us  [the longest x1 49.1 us: gather_weights(): pl.pallas_call(functools.partial(weights_kernel, n_batch, n_ctx), name='g...]
    reduce_scatter x4 -> x3, waiting for transfers between devices: 29.5 us -> 86.2 us  [scattered(): lax.psum_scatter(whole.astype(BF16), 'ctx', scatter_dimension=0, tiled=True)]
    psum x1 -> x0, blocking collectives: 44 us -> none  [local(): gain_sums = lax.psum(gain_rows, ('batch', 'ctx'))]
    convert_element_type x7 -> x1, local copies, waits for them, and re-layouts: 42.1 us -> 0.01 us  [local(): attn_grads[0, width_shard + proj_rows:used].reshape(-1).astype(F32)]
    reshape x4 -> x3, local copies, waits for them, and re-layouts: 22.8 us -> 1.18 us  [the longest x1 0.81 us: local(): qkv_full, proj_full, gains_all = gather_weights(n_batch, n_ctx, jnp.conca...]
    unnamed x11 -> x8, waiting for transfers between devices: 3.45 us -> 21.3 us
    all_gather x1 -> x0, blocking collectives: 15.4 us -> none  [local(): gains_all = lax.all_gather(gains, 'ctx', axis=0).astype(F32)]
  transfers between devices with their start and end apart: 10 -> 7, of which waited for: 6 -> 5; matrix products, arithmetic and copies ran while one was open for 22% -> 8% of each run, Pallas kernels for 21% -> 33%
where the time goes in v2:
time: 579 us; the launch traced here: 571 us
  Pallas kernels  312 us (54%)
  waiting for transfers between devices  115 us (20%)
  matrix products  80 us (14%)
  other arithmetic  25.4 us (4%)
  local copies, waits for them, and re-layouts  22.1 us (4%)
  between operations  16.4 us (3%)
    pallas_call x9, Pallas kernels, batch_exchange(): pl.pallas_call(functools.partial(batch_kernel, size, kinds), name=name, o...  202 us
    reduce_scatter x3, waiting for transfers between devices, scattered(): lax.psum_scatter(whole.astype(BF16), 'ctx', scatter_dimension=0, tiled=True)  86.2 us
    pallas_call x1, Pallas kernels, gather_weights(): pl.pallas_call(functools.partial(weights_kernel, n_batch, n_ctx), name='g...  49.1 us
    pallas_call x2, Pallas kernels, halo_exchange(): pl.pallas_call(functools.partial(halo_kernel, size, depth, direction), na...  47 us
    dot_general x8, matrix products, project(): lax.dot_general(inputs, weight, (((1,), (0,)), ((), ())), preferred_eleme...  28.7 us
    dot_general x5, matrix products, weight_grad(): lax.dot_general(inputs, upstream, (((0,), (0,)), ((), ())), preferred_ele...  22.5 us
    unnamed x8, waiting for transfers between devices  21.3 us
    dot_general x8, matrix products, project_back(): lax.dot_general(upstream, weight, (((1,), (1,)), ((), ())), preferred_ele...  21.1 us
  transfers between devices with their start and end apart: 7, of which 5 were waited for; matrix products, arithmetic and copies ran while one was open for 8% of the time, Pallas kernels for 33%

profile of v2, /device:TPU:0, one launch (start us, length us, event | category | flops | bytes accessed | tf_op | source)
XLA Modules:
  0.0 570.9 jit_solution(8539151272279689346)
XLA Ops:
  7.2 4.2 pick_columns.1
  14.8 49.1 %gather_weights.1 = (bf16[4,8,144,384]{3,2,1,0:T(8,128)(2,1)}, bf16[8,4,32,1152]{3,2,1,0:T(8,128)(2,1)}, bf16[8,1,640]{2,1,0:T(2,128)(2,1)}) custom-call(bf16[4,144,384]{2,1,0:T(8,128)(2,1)} %bitcast.236, bf16[4,32,1152]{2,1,0:T(8,128)(2,1)} %bitcast.249, bf16[1,640]{1,0:T(2,128)(2,1)} %broadcast_in_dim.34.gain_ref), custom_call_target="tpu_custom_call" | custom-call | tf_op jit(solution)/shard_map/gather_weights/pallas_call | solution.py:358
  65.0 3.6 fusion.107
  71.7 24.5 %halo_out.1 = bf16[4,128,512]{2,1,0:T(8,128)(2,1)} custom-call(bf16[128,512]{1,0:T(8,128)(2,1)} %pad_maximum_fusion.9.source_ref), custom_call_target="tpu_custom_call" | custom-call | tf_op jit(solution)/shard_map/halo_out/pallas_call | solution.py:169
  109.8 44.5 %gather_in.1 = (bf16[4,128,1152]{2,1,0:T(8,128)(2,1)}, bf16[4,128,1152]{2,1,0:T(8,128)(2,1)}, bf16[4,128,1024]{2,1,0:T(8,128)(2,1)}) custom-call(bf16[128,1152]{1,0:T(8,128)(2,1)} %multiply_convert_fusion.4.refs_0_, bf16[128,1152]{1,0:T(8,128)(2,1)} %get-tuple-element.144.refs_1_, bf16[128,1024]{1,0:T(8,128)(2,1)} %copy.203.refs_2_), custom_call_target="tpu_custom_call" | custom-call | tf_op jit(solution)/shard_map/gather_in/pallas_call | solution.py:101
  154.4 6.8 %fusion.114 = f32[512,1728]{0,1:T(8,128)} fusion(bf16[512,1152]{1,0:T(8,128)(2,1)} %bitcast.255, bf16[1152,1728]{1,0:T(8,128)(2,1)} %all-gather.4.cloned.1.call-done), kind=kOutput, calls=%fused_computation.213 | convolution fusion | flops 2038431744 | bytes 8699904 | tf_op jit(solution)/shard_map/dot_general | solution.py:38
  161.2 9.4 %multiply_convert_fusion.1 = (bf16[512,1728]{0,1:T(8,128)(2,1)}, f32[512,1728]{0,1:T(8,128)}) fusion(f32[512,1728]{0,1:T(8,128)} %fusion.114, bf16[512,1152]{1,0:T(8,128)(2,1)} %bitcast.256, bf16[1152,1728]{1,0:T(8,128)(2,1)} %all-gather.6.cloned.1.call-done), kind=kOutput, calls=%fused_computation.16 | convolution fusion | flops 2047279104 | bytes 14008320 | tf_op jit(solution)/shard_map/dot_general | solution.py:38
  170.6 7.4 %all-gather.8.cloned.1.call-done = bf16[1728,1152]{1,0:T(8,128)(2,1)} async-done(((bf16[216,1152]{1,0:T(8,128)(2,1)}), bf16[1728,1152]{1,0:T(8,128)(2,1)}) %all-gather.8.cloned.1.call-update) | async-done | bytes 3981328 | tf_op jit(solution)/shard_map/all_gather | solution.py:382
  178.0 6.3 %convolution_convert_fusion.3 = bf16[512,1152]{1,0:T(8,128)(2,1)} fusion(bf16[512,1728]{0,1:T(8,128)(2,1)} %get-tuple-element.169, bf16[1728,1152]{1,0:T(8,128)(2,1)} %all-gather.8.cloned.1.call-done), kind=kOutput, calls=%fused_computation.22 | convolution fusion | flops 2039021568 | bytes 6930432 | tf_op jit(solution)/shard_map/dot_general | solution.py:38
  184.3 18.9 %sum_out.1 = bf16[4,128,1152]{2,1,0:T(8,128)(2,1)} custom-call(bf16[4,128,1152]{2,1,0:T(8,128)(2,1)} %bitcast.244), custom_call_target="tpu_custom_call" | custom-call | tf_op jit(solution)/shard_map/sum_out/pallas_call | solution.py:101
  206.3 18.3 %gather_grad.1 = bf16[4,128,1152]{2,1,0:T(8,128)(2,1)} custom-call(bf16[128,1152]{1,0:T(8,128)(2,1)} %get-tuple-element.142.refs_0_), custom_call_target="tpu_custom_call" | custom-call | tf_op jit(solution)/shard_map/gather_grad/pallas_call | solution.py:101
  224.6 6.2 %convolution_convert_fusion.2 = bf16[1728,1152]{1,0:T(8,128)(2,1)} fusion(bf16[512,1728]{0,1:T(8,128)(2,1)} %get-tuple-element.169, bf16[512,1152]{1,0:T(8,128)(2,1)} %bitcast.241), kind=kOutput, calls=%fused_computation.3 | convolution fusion | flops 2040422400 | bytes 6930432 | tf_op jit(solution)/shard_map/dot_general | solution.py:46
  230.8 9.7 %multiply_convert_fusion = (bf16[512,1728]{0,1:T(8,128)(2,1)S(1)}, bf16[512,1728]{0,1:T(8,128)(2,1)S(1)}) fusion(f32[512,1728]{0,1:T(8,128)} %fusion.114, f32[512,1728]{0,1:T(8,128)} %get-tuple-element.170, bf16[512,1152]{1,0:T(8,128)(2,1)} %bitcast.242, bf16[1728,1152]{1,0:T(8,128)(2,1)} %all-gather.8.cloned.1.call-done), kind=kOutput, calls=%fused_computation.15 | convolution fusion | flops 2059665408 | bytes 15777792 | tf_op jit(solution)/shard_map/dot_general | solution.py:42
  240.5 2.6 fusion.115
  243.9 3.7 fusion.10
  247.6 17.1 %sum_back.1 = bf16[4,128,1152]{2,1,0:T(8,128)(2,1)} custom-call(bf16[4,128,1152]{2,1,0:T(8,128)(2,1)} %bitcast.243), custom_call_target="tpu_custom_call" | custom-call | tf_op jit(solution)/shard_map/sum_back/pallas_call | solution.py:101
  264.8 6.2 %convolution_convert_fusion.1 = bf16[1152,1728]{1,0:T(8,128)(2,1)} fusion(bf16[512,1152]{1,0:T(8,128)(2,1)} %bitcast.257, bf16[512,1728]{0,1:T(8,128)(2,1)} %copy-done.66), kind=kOutput, calls=%fused_computation.2 | convolution fusion | flops 2040422400 | bytes 6930432 | tf_op jit(solution)/shard_map/dot_general | solution.py:46
  271.0 6.1 %convolution_convert_fusion = bf16[1152,1728]{1,0:T(8,128)(2,1)} fusion(bf16[512,1152]{1,0:T(8,128)(2,1)} %bitcast.258, bf16[512,1728]{0,1:T(8,128)(2,1)} %copy-done.65), kind=kOutput, calls=%fused_computation.1 | convolution fusion | flops 2040422400 | bytes 6930432 | tf_op jit(solution)/shard_map/dot_general | solution.py:46
  282.0 2.7 convolution_bitcast_fusion.3
  288.6 22.5 %halo_back.1 = bf16[4,128,512]{2,1,0:T(8,128)(2,1)} custom-call(bf16[4,128,512]{2,1,0:T(8,128)(2,1)} %bitcast.234), custom_call_target="tpu_custom_call" | custom-call | tf_op jit(solution)/shard_map/halo_back/pallas_call | solution.py:169
  325.9 14.6 %spread_grads.1 = (f32[4,8,640]{2,1,0:T(8,128)}, bf16[4,128,384]{2,1,0:T(8,128)(2,1)}, bf16[4,128,288]{2,1,0:T(8,128)(2,1)}) custom-call(f32[8,640]{1,0:T(8,128)} %concatenate.54.refs_0_, bf16[4,128,384]{2,1,0:T(8,128)(2,1)} %bitcast.238, bf16[4,128,288]{2,1,0:T(8,128)(2,1)} %bitcast.240), custom_call_target="tpu_custom_call" | custom-call | tf_op jit(solution)/shard_map/spread_grads/pallas_call | solution.py:101
  350.0 35.8 %reduce-scatter.7.cloned.1.call-done.refs_0_ = bf16[288,384]{1,0:T(8,128)(2,1)} async-done(((bf16[2304,384]{1,0:T(8,128)(2,1)}), bf16[288,384]{1,0:T(8,128)(2,1)}) %reduce-scatter.7.cloned.1.call-update) | async-done | bytes 221200 | tf_op jit(solution)/shard_map/reduce_scatter | solution.py:386
  385.8 11.5 %spread_attn.1 = bf16[4,288,384]{2,1,0:T(8,128)(2,1)} custom-call(bf16[288,384]{1,0:T(8,128)(2,1)} %reduce-scatter.7.cloned.1.call-done.refs_0_), custom_call_target="tpu_custom_call" | custom-call | tf_op jit(solution)/shard_map/spread_attn/pallas_call | solution.py:101
  404.4 30.9 %reduce-scatter.9.cloned.1.call-done.refs_0_ = bf16[144,1728]{1,0:T(8,128)(2,1)} async-done(((bf16[1152,1728]{1,0:T(8,128)(2,1)}), bf16[144,1728]{1,0:T(8,128)(2,1)}) %reduce-scatter.9.cloned.1.call-update) | async-done | bytes 497680 | tf_op jit(solution)/shard_map/reduce_scatter | solution.py:386
  435.3 26.1 %spread_gate.1.parts_ref = bf16[4,144,1728]{2,1,0:T(8,128)(2,1)} custom-call(bf16[144,1728]{1,0:T(8,128)(2,1)} %reduce-scatter.9.cloned.1.call-done.refs_0_), custom_call_target="tpu_custom_call" | custom-call | tf_op jit(solution)/shard_map/spread_gate/pallas_call | solution.py:101
  461.4 4.5 place_gate.1
  465.9 19.4 %reduce-scatter.11.cloned.1.call-done.refs_0_ = bf16[144,1728]{1,0:T(8,128)(2,1)} async-done(((bf16[1152,1728]{1,0:T(8,128)(2,1)}), bf16[144,1728]{1,0:T(8,128)(2,1)}) %reduce-scatter.11.cloned.1.call-update) | async-done | bytes 497680 | tf_op jit(solution)/shard_map/reduce_scatter | solution.py:386
  485.3 26.0 %spread_up.1.parts_ref = bf16[4,144,1728]{2,1,0:T(8,128)(2,1)} custom-call(bf16[144,1728]{1,0:T(8,128)(2,1)} %reduce-scatter.11.cloned.1.call-done.refs_0_), custom_call_target="tpu_custom_call" | custom-call | tf_op jit(solution)/shard_map/spread_up/pallas_call | solution.py:101
  511.4 4.5 place_up.1
  515.8 18.8 %reduce-scatter.13.cloned.1.call-done.refs_0_ = bf16[216,1152]{1,0:T(8,128)(2,1)} async-done(((bf16[1728,1152]{1,0:T(8,128)(2,1)}), bf16[216,1152]{1,0:T(8,128)(2,1)}) %reduce-scatter.13.cloned.1.call-update) | async-done | bytes 497680
  534.7 25.4 %spread_down.1 = bf16[4,216,1152]{2,1,0:T(8,128)(2,1)} custom-call(bf16[216,1152]{1,0:T(8,128)(2,1)} %reduce-scatter.13.cloned.1.call-done.refs_0_), custom_call_target="tpu_custom_call" | custom-call | tf_op jit(solution)/shard_map/spread_down/pallas_call | solution.py:101
  560.1 3.8 bitcast_convert_fusion
  (267 shorter events, 63.3 us)
Async XLA Ops:
  7.2 5.2 copy-start
  7.2 147.2 %all-gather.4.cloned.1.call-start = ((), (), s32[]{:S(2)}) async-start(), calls=%async_computation.4 | async-start | bytes 4644864 | tf_op jit(solution)/shard_map/all_gather | solution.py:382
  11.5 149.7 %all-gather.6.cloned.1.call-start = ((), (), s32[]{:S(2)}) async-start(), calls=%async_computation.5 | async-start | bytes 4644864 | tf_op jit(solution)/shard_map/all_gather | solution.py:382
  12.3 165.7 %all-gather.8.cloned.1.call-start = ((), (), s32[]{:S(2)}) async-start(), calls=%async_computation.6 | async-start | bytes 4478976 | tf_op jit(solution)/shard_map/all_gather | solution.py:382
  13.2 372.6 %reduce-scatter.7.cloned.1.call-start = ((), (), s32[]{:S(2)}) async-start(), calls=%async_computation.7 | async-start | bytes 1990656 | tf_op jit(solution)/shard_map/reduce_scatter | solution.py:386
  65.0 3.7 copy-start.2
  69.5 28.4 %copy-start.35 = (f32[256]{0:T(256)}, f32[256]{0:T(256)S(1)}, u32[]{:S(2)}) copy-start(f32[256]{0:T(256)S(1)} %mul.601) | copy-start | bytes 3076
  69.5 28.4 %copy-start.45 = (f32[128]{0:T(128)}, f32[128]{0:T(128)S(1)}, u32[]{:S(2)}) copy-start(f32[128]{0:T(128)S(1)} %multiply_power_fusion) | copy-start | bytes 1540
  70.0 27.9 %copy-start.11 = (f32[128,256]{1,0:T(8,128)}, f32[128,256]{1,0:T(8,128)S(1)}, u32[]{:S(2)}) copy-start(f32[128,256]{1,0:T(8,128)S(1)} %get-tuple-element.129) | copy-start | bytes 393220
  70.1 29.5 %copy-start.47 = (f32[128]{0:T(128)}, f32[128]{0:T(128)S(1)}, u32[]{:S(2)}) copy-start(f32[128]{0:T(128)S(1)} %bitcast_convert_fusion.1) | copy-start | bytes 1540
  70.1 29.5 %copy-start.39 = (f32[128]{0:T(128)}, f32[128]{0:T(128)S(1)}, u32[]{:S(2)}) copy-start(f32[128]{0:T(128)S(1)} %fusion.84) | copy-start | bytes 1540
  71.1 29.6 %copy-start.17 = (f32[128,128]{1,0:T(8,128)}, f32[128,128]{1,0:T(8,128)S(1)}, u32[]{:S(2)}) copy-start(f32[128,128]{1,0:T(8,128)S(1)} %get-tuple-element.162) | copy-start | bytes 196612
  96.4 4.2 copy-start.37
  107.9 53.3 %copy-start.60 = (f32[128]{0:T(128)}, f32[128]{0:T(128)S(1)}, u32[]{:S(2)}) copy-start(f32[128]{0:T(128)S(1)} %get-tuple-element.167) | copy-start | bytes 1540
  184.3 20.6 %copy-start.8 = (bf16[1,128,1152]{2,1,0:T(8,128)(2,1)S(1)}, bf16[1,128,1152]{2,1,0:T(8,128)(2,1)}, u32[]{:S(2)}) copy-start(bf16[1,128,1152]{2,1,0:T(8,128)(2,1)} %param.20) | copy-start | bytes 884740
  230.8 9.7 %copy-start.62 = (bf16[1152,1728]{1,0:T(8,128)(2,1)S(1)}, bf16[1152,1728]{1,0:T(8,128)(2,1)}, u32[]{:S(2)}) copy-start(bf16[1152,1728]{1,0:T(8,128)(2,1)} %all-gather.4.cloned.1.call-done) | copy-start | bytes 11943940
  240.5 3.4 copy-start.63
  288.6 24.6 %copy-start.46 = (f32[128]{0:T(128)S(1)}, f32[128]{0:T(128)}, u32[]{:S(2)}) copy-start(f32[128]{0:T(128)} %copy-done.45) | copy-start | bytes 1540
  288.6 24.6 %copy-start.48 = (f32[128]{0:T(128)S(1)}, f32[128]{0:T(128)}, u32[]{:S(2)}) copy-start(f32[128]{0:T(128)} %copy-done.47) | copy-start | bytes 1540
  312.3 4.4 copy-start.38
  313.2 4.2 copy-start.34
  317.8 3.4 copy-start.12
  317.9 3.4 copy-start.19
  317.9 3.4 copy-start.20
  317.9 3.4 copy-start.36
  317.9 3.5 copy-start.52
  317.9 3.8 copy-start.18
  317.9 3.9 copy-start.5
  346.8 88.5 %reduce-scatter.9.cloned.1.call-start = ((), (), s32[]{:S(2)}) async-start(), calls=%async_computation.8 | async-start | bytes 4644864 | tf_op jit(solution)/shard_map/reduce_scatter | solution.py:386
  347.4 137.9 %reduce-scatter.11.cloned.1.call-start = ((), (), s32[]{:S(2)}) async-start(), calls=%async_computation.9 | async-start | bytes 4644864 | tf_op jit(solution)/shard_map/reduce_scatter | solution.py:386
  348.0 186.7 %reduce-scatter.13.cloned.1.call-start = ((), (), s32[]{:S(2)}) async-start(), calls=%async_computation.10 | async-start | bytes 4478976
  534.7 29.1 %copy-start.1 = (bf16[864,1152]{1,0:T(8,128)(2,1)S(1)}, bf16[864,1152]{1,0:T(8,128)(2,1)}, u32[]{:S(2)}) copy-start(bf16[864,1152]{1,0:T(8,128)(2,1)} %param.32) | copy-start | bytes 5971972
  (42 other events, 76.2 us)
Sparse Core Ops, SparseCore 0:
  11.6 62.0 all-gather.3
  75.9 48.0 all-gather.5
  126.2 51.7 all-gather.7
  346.9 38.8 reduce-scatter.6
  388.0 47.2 reduce-scatter.8
  437.5 47.7 reduce-scatter.10
  488.2 46.4 reduce-scatter.12

commit v3 on v2

--- a/solution.py
+++ b/solution.py
@@ -90,7 +90,7 @@
         copy.wait()
 
 
-def batch_exchange(name, collective_id, size, whole=(), slots=()):
+def batch_exchange(collective_id, size, whole=(), slots=()):
     arrays = list(whole) + list(slots)
     kinds = [0] * len(whole) + [1] * len(slots)
     count = len(arrays)
@@ -100,13 +100,82 @@
     ]
     return pl.pallas_call(
         functools.partial(batch_kernel, size, kinds),
-        name=name,
         out_shape=shapes,
         in_specs=[pl.BlockSpec(memory_space=pltpu.VMEM)] * count,
         out_specs=[pl.BlockSpec(memory_space=pltpu.VMEM)] * count,
         scratch_shapes=[
             pltpu.SemaphoreType.DMA((count, size - 1)),
             pltpu.SemaphoreType.DMA((count, size - 1)),
+            pltpu.SemaphoreType.DMA((count,)),
+        ],
+        compiler_params=pltpu.CompilerParams(collective_id=collective_id, has_side_effects=True),
+    )(*arrays)
+
+
+def square_kernel(count, *refs):
+    sources, results = refs[:count], refs[count : 2 * count]
+    send_sem, recv_sem, own_sem = refs[2 * count :]
+    me = lax.axis_index("batch")
+    across = me + 1 - 2 * lax.rem(me, 2)
+    along = lax.rem(me + 2, 4)
+    barrier = pltpu.get_barrier_semaphore()
+    for peer in (across, along):
+        pl.semaphore_signal(barrier, inc=1, device_id={"batch": peer}, device_id_type=MESH)
+    pl.semaphore_wait(barrier, 2)
+
+    def remote(source, target, item, turn, peer):
+        copy = pltpu.make_async_remote_copy(
+            src_ref=source,
+            dst_ref=target,
+            send_sem=send_sem.at[item, turn],
+            recv_sem=recv_sem.at[item, turn],
+            device_id={"batch": peer},
+            device_id_type=MESH,
+        )
+        copy.start()
+        return copy
+
+    firsts = [
+        [
+            remote(sources[item], results[item].at[me], item, turn, peer)
+            for turn, peer in enumerate((across, along))
+        ]
+        for item in range(count)
+    ]
+    own = [
+        pltpu.make_async_copy(sources[item], results[item].at[me], own_sem.at[item])
+        for item in range(count)
+    ]
+    for copy in own:
+        copy.start()
+    seconds = []
+    for item in range(count):
+        columns = sources[item].shape[-1]
+        cut = columns // 256 * 128
+        halves = (pl.ds(0, cut), pl.ds(cut, columns - cut))
+        for turn, (giver, taker) in enumerate(((across, along), (along, across))):
+            firsts[item][turn].wait_recv()
+            block = results[item].at[giver, :, halves[turn]]
+            seconds.append(remote(block, block, item, 2 + turn, taker))
+    for copy in own:
+        copy.wait()
+    for copy in seconds:
+        copy.wait()
+    for pair in firsts:
+        for copy in pair:
+            copy.wait_send()
+
+
+def square_gather(collective_id, *arrays):
+    count = len(arrays)
+    return pl.pallas_call(
+        functools.partial(square_kernel, count),
+        out_shape=[jax.ShapeDtypeStruct((4, *a.shape), a.dtype) for a in arrays],
+        in_specs=[pl.BlockSpec(memory_space=pltpu.VMEM)] * count,
+        out_specs=[pl.BlockSpec(memory_space=pltpu.VMEM)] * count,
+        scratch_shapes=[
+            pltpu.SemaphoreType.DMA((count, 4)),
+            pltpu.SemaphoreType.DMA((count, 4)),
             pltpu.SemaphoreType.DMA((count,)),
         ],
         compiler_params=pltpu.CompilerParams(collective_id=collective_id, has_side_effects=True),
@@ -165,10 +234,9 @@
             copy(step).wait_send()
 
 
-def halo_exchange(name, collective_id, size, depth, direction, block):
+def halo_exchange(collective_id, size, depth, direction, block):
     return pl.pallas_call(
         functools.partial(halo_kernel, size, depth, direction),
-        name=name,
         out_shape=jax.ShapeDtypeStruct((depth, *block.shape[-2:]), block.dtype),
         in_specs=[pl.BlockSpec(memory_space=pltpu.VMEM)],
         out_specs=pl.BlockSpec(memory_space=pltpu.VMEM),
@@ -177,55 +245,60 @@
     )(block)
 
 
-def pick_kernel(n_batch, n_ctx, piece, gate_ref, up_ref, gate_out, up_out):
+def pick_kernel(n_batch, n_ctx, piece, padded, gate_ref, up_ref, out_ref):
     me = lax.axis_index("batch")
+    out_ref[...] = jnp.zeros_like(out_ref)
     for spot in range(n_batch):
 
         @pl.when(me == spot)
         def _():
             for shard in range(n_ctx):
                 start = (shard * n_batch + spot) * piece
-                place = pl.ds(shard * piece, piece)
-                gate_out[:, place] = gate_ref[:, start : start + piece]
-                up_out[:, place] = up_ref[:, start : start + piece]
-
-
-def pick_columns(n_batch, n_ctx, piece, w_gate, w_up):
-    rows = w_gate.shape[0]
-    block = 48 if rows % 48 == 0 else rows
-    spec = pl.BlockSpec((block, w_gate.shape[1]), lambda i: (i, 0))
-    out_spec = pl.BlockSpec((block, n_ctx * piece), lambda i: (i, 0))
-    out = jax.ShapeDtypeStruct((rows, n_ctx * piece), w_gate.dtype)
+                for half, ref in enumerate((gate_ref, up_ref)):
+                    place = (half * n_ctx + shard) * padded
+                    out_ref[:, place : place + piece] = ref[:, start : start + piece]
+
+
+def row_block(rows):
+    return 48 if rows % 48 == 0 else rows
+
+
+def pick_columns(n_batch, n_ctx, piece, padded, w_gate, w_up):
+    rows, hidden = w_gate.shape
+    block = row_block(rows)
+    spec = pl.BlockSpec((block, hidden), lambda i: (i, 0))
     return pl.pallas_call(
-        functools.partial(pick_kernel, n_batch, n_ctx, piece),
+        functools.partial(pick_kernel, n_batch, n_ctx, piece, padded),
         name="pick_columns",
         grid=(rows // block,),
-        out_shape=(out, out),
+        out_shape=jax.ShapeDtypeStruct((rows, 2 * n_ctx * padded), w_gate.dtype),
         in_specs=[spec, spec],
-        out_specs=[out_spec, out_spec],
+        out_specs=pl.BlockSpec((block, 2 * n_ctx * padded), lambda i: (i, 0)),
     )(w_gate, w_up)
 
 
-def place_kernel(n_batch, n_ctx, piece, parts_ref, out_ref):
+def place_kernel(n_batch, n_ctx, piece, padded, parts_ref, gate_ref, up_ref):
     for shard in range(n_ctx):
         for spot in range(n_batch):
             start = (shard * n_batch + spot) * piece
-            out_ref[:, start : start + piece] = parts_ref[
-                spot, :, shard * piece : (shard + 1) * piece
-            ].astype(F32)
-
-
-def place_columns(name, n_batch, n_ctx, piece, parts):
+            for half, ref in enumerate((gate_ref, up_ref)):
+                place = (half * n_ctx + shard) * padded
+                ref[:, start : start + piece] = parts_ref[spot, :, place : place + piece].astype(F32)
+
+
+def place_columns(n_batch, n_ctx, piece, padded, parts):
     rows = parts.shape[1]
-    block = 48 if rows % 48 == 0 else rows
+    block = row_block(rows)
     hidden = n_batch * n_ctx * piece
+    spec = pl.BlockSpec((block, hidden), lambda i: (i, 0))
+    out = jax.ShapeDtypeStruct((rows, hidden), F32)
     return pl.pallas_call(
-        functools.partial(place_kernel, n_batch, n_ctx, piece),
-        name=name,
+        functools.partial(place_kernel, n_batch, n_ctx, piece, padded),
+        name="place_columns",
         grid=(rows // block,),
-        out_shape=jax.ShapeDtypeStruct((rows, hidden), F32),
-        in_specs=[pl.BlockSpec((n_batch, block, n_ctx * piece), lambda i: (0, i, 0))],
-        out_specs=pl.BlockSpec((block, hidden), lambda i: (i, 0)),
+        out_shape=(out, out),
+        in_specs=[pl.BlockSpec((n_batch, block, 2 * n_ctx * padded), lambda i: (0, i, 0))],
+        out_specs=[spec, spec],
     )(parts)
 
 
@@ -383,7 +456,7 @@
 
 
 def scattered(whole):
-    return lax.psum_scatter(whole.astype(BF16), "ctx", scatter_dimension=0, tiled=True)
+    return lax.psum_scatter(whole, "ctx", scatter_dimension=0, tiled=True)
 
 
 def local(
@@ -417,6 +490,8 @@
     head_count = query_width // head_size
     hidden_shard = w_down.shape[0]
     piece = hidden_shard // n_batch
+    hidden_part = -(-piece * n_ctx // 128) * 128
+    padded = hidden_part // n_ctx
     halo_depth = (WINDOW + tok_count - 2) // tok_count
     batch_at = lax.axis_index("batch")
     ctx_at = lax.axis_index("ctx")
@@ -451,10 +526,9 @@
     full_gain_q = gain_at(4 * width_shard, head_shard)
     full_gain_k = gain_at(4 * width_shard + head_shard, head_shard)
 
-    part_down = gathered(lax.dynamic_slice_in_dim(w_down, batch_at * piece, piece, 0))
-    own_gate, own_up = pick_columns(n_batch, n_ctx, piece, w_gate, w_up)
-    part_gate = gathered(own_gate)
-    part_up = gathered(own_up)
+    part_both = gathered(pick_columns(n_batch, n_ctx, piece, padded, w_gate, w_up))
+    own_down = lax.dynamic_slice_in_dim(w_down, batch_at * piece, piece, 0)
+    part_down = gathered(jnp.pad(own_down, ((0, padded - piece), (0, 0))))
 
     first_token = ctx_at * tok_count
     token_place = first_token + jnp.arange(tok_count, dtype=jnp.int32)
@@ -477,7 +551,7 @@
     query_rot = query_path(query_raw, full_gain_q).astype(BF16)
     key_rot = key_path(key_raw, full_gain_k).astype(BF16)
     own_pair = jnp.concatenate([key_rot, value_low], axis=-1)
-    halo = halo_exchange("halo_out", 1, n_ctx, halo_depth, 1, own_pair)
+    halo = halo_exchange(1, n_ctx, halo_depth, 1, own_pair)
     context = jnp.concatenate([halo.reshape(halo_depth * tok_count, -1), own_pair], axis=0)
     ctx_keys = context[:, :head_size]
     ctx_values = context[:, head_size:]
@@ -500,18 +574,14 @@
     middle = resid_in + normed(attn_proj, full_gain_attn)
     ffn_in = normed(middle, full_gain_ffn).astype(BF16)
 
-    ffn_in_all, act_in_all, attn_all = batch_exchange(
-        "gather_in", 2, n_batch, whole=(ffn_in, act_in, attn_low)
-    )
+    (ffn_in_all,) = square_gather(2, ffn_in)
     ffn_in_all = ffn_in_all.reshape(all_tok, model_width)
-    act_in_all = act_in_all.reshape(all_tok, model_width)
-    attn_all = attn_all.reshape(all_tok, query_width)
-    gate_pre = project(ffn_in_all, part_gate)
-    up_pre = project(ffn_in_all, part_up)
+    both_pre = project(ffn_in_all, part_both)
+    gate_pre, up_pre = both_pre[:, :hidden_part], both_pre[:, hidden_part:]
     mixed_low = gated_gelu(gate_pre, up_pre).astype(BF16)
     proj_part = project(mixed_low, part_down).astype(BF16)
     (proj_parts,) = batch_exchange(
-        "sum_out", 3, n_batch, slots=(proj_part.reshape(n_batch, tok_count, model_width),)
+        3, n_batch, slots=(proj_part.reshape(n_batch, tok_count, model_width),)
     )
     ffn_proj = jnp.sum(proj_parts.astype(F32), axis=0)
     final_sum = middle + normed(ffn_proj, full_gain_final)
@@ -520,7 +590,7 @@
     grad_final = cotangent.astype(F32) * valid_mask
     _, pull_final = jax.vjp(normed, ffn_proj, full_gain_final)
     grad_ffn_proj, grad_gain_final = pull_final(grad_final)
-    (grad_ffn_low,) = batch_exchange("gather_grad", 4, n_batch, whole=(grad_ffn_proj.astype(BF16),))
+    (grad_ffn_low,) = square_gather(4, grad_ffn_proj.astype(BF16))
     grad_ffn_low = grad_ffn_low.reshape(all_tok, model_width)
     down_grad = weight_grad(mixed_low, grad_ffn_low).astype(BF16)
     down_grad, grad_ffn_low = lax.optimization_barrier((down_grad, grad_ffn_low))
@@ -528,20 +598,15 @@
     grad_mixed = project_back(grad_ffn_low, part_down)
     _, pull_gelu = jax.vjp(gated_gelu, gate_pre, up_pre)
     grad_gate, grad_up = pull_gelu(grad_mixed)
-    grad_gate_low = grad_gate.astype(BF16)
-    grad_up_low = grad_up.astype(BF16)
-    back_part = project_back(grad_gate_low, part_gate) + project_back(grad_up_low, part_up)
+    grad_both_low = jnp.concatenate([grad_gate, grad_up], axis=1).astype(BF16)
+    back_part = project_back(grad_both_low, part_both).astype(BF16)
     (back_parts,) = batch_exchange(
-        "sum_back", 5, n_batch, slots=(back_part.astype(BF16).reshape(n_batch, tok_count, model_width),)
-    )
-    back_parts, grad_gate_low, grad_up_low = lax.optimization_barrier(
-        (back_parts, grad_gate_low, grad_up_low)
-    )
-    gate_grad = weight_grad(ffn_in_all, grad_gate_low).astype(BF16)
-    up_grad = weight_grad(ffn_in_all, grad_up_low).astype(BF16)
-    back_parts, gate_grad, up_grad = lax.optimization_barrier((back_parts, gate_grad, up_grad))
-    grad_w_gate = scattered(gate_grad)
-    grad_w_up = scattered(up_grad)
+        5, n_batch, slots=(back_part.reshape(n_batch, tok_count, model_width),)
+    )
+    back_parts, grad_both_low = lax.optimization_barrier((back_parts, grad_both_low))
+    both_grad = weight_grad(ffn_in_all, grad_both_low).astype(BF16)
+    back_parts, both_grad = lax.optimization_barrier((back_parts, both_grad))
+    grad_w_both = scattered(both_grad)
     grad_ffn_in = jnp.sum(back_parts.astype(F32), axis=0)
     _, pull_ffn_norm = jax.vjp(normed, middle, full_gain_ffn)
     grad_middle_part, grad_gain_ffn = pull_ffn_norm(grad_ffn_in)
@@ -568,7 +633,6 @@
     grad_context = jnp.concatenate([grad_ctx_keys, grad_ctx_values], axis=-1)
     halo_rows = halo_depth * tok_count
     returned = halo_exchange(
-        "halo_back",
         6,
         n_ctx,
         halo_depth,
@@ -614,13 +678,14 @@
         ],
         axis=1,
     )
-    gain_parts, qkv_slots, proj_slots = batch_exchange(
-        "spread_grads",
+    gain_parts, act_in_all, attn_all, qkv_slots, proj_slots = batch_exchange(
         7,
         n_batch,
-        whole=(gain_rows,),
+        whole=(gain_rows, act_in, attn_low),
         slots=(column_slots(grad_qkv_low), column_slots(grad_proj_low)),
     )
+    act_in_all = act_in_all.reshape(all_tok, model_width)
+    attn_all = attn_all.reshape(all_tok, query_width)
     proj_rows = w_output.shape[0]
     gain_count = gain_rows.shape[1]
     gain_lines = -(-gain_count // quarter)
@@ -646,10 +711,10 @@
     )
     attn_sum = scattered(packed.reshape(n_ctx * lines, quarter))
 
-    (down_all,) = batch_exchange("spread_down", 8, n_batch, whole=(grad_w_down,))
-    (gate_all,) = batch_exchange("spread_gate", 9, n_batch, whole=(grad_w_gate,))
-    (up_all,) = batch_exchange("spread_up", 10, n_batch, whole=(grad_w_up,))
-    (attn_grads,) = batch_exchange("spread_attn", 11, n_batch, whole=(attn_sum,))
+    (down_all,) = square_gather(8, grad_w_down)
+    (both_all,) = square_gather(9, grad_w_both)
+    (attn_grads,) = square_gather(11, attn_sum)
+    grad_gate_shard, grad_up_shard = place_columns(n_batch, n_ctx, piece, padded, both_all)
     gain_mine = attn_grads[0, width_shard + proj_rows : used].reshape(-1).astype(F32)
 
     def columns_back(pieces):
@@ -668,9 +733,9 @@
         columns_back(attn_grads[:, width_shard : width_shard + proj_rows, :output_part]),
         gain_mine[width_shard : 2 * width_shard],
         gain_mine[2 * width_shard : 3 * width_shard],
-        place_columns("place_gate", n_batch, n_ctx, piece, gate_all),
-        place_columns("place_up", n_batch, n_ctx, piece, up_all),
-        down_all.reshape(hidden_shard, model_width).astype(F32),
+        grad_gate_shard,
+        grad_up_shard,
+        down_all[:, :piece].reshape(hidden_shard, model_width).astype(F32),
         gain_mine[3 * width_shard : 4 * width_shard],
     )
 
@@ -679,8 +744,12 @@
     matrix = P("ctx", None)
     vector = P("ctx")
     tokens = P("batch", "ctx", None)
+
+    def step(*arrays):
+        return local(mesh.shape["batch"], mesh.shape["ctx"], *arrays)
+
     return jax.shard_map(
-        functools.partial(local, mesh.shape["batch"], mesh.shape["ctx"]),
+        step,
         mesh=mesh,
         in_specs=(
             tokens,

time: 579 us -> 586 us (1.012)
  waiting for transfers between devices: 115 us -> 156 us
  Pallas kernels: 312 us -> 280 us
    reduce_scatter x3, waiting for transfers between devices: 86.2 us -> 129 us  [scattered(): return lax.psum_scatter(whole, 'ctx', scatter_dimension=0, tiled=True)]
    pallas_call x14 -> x12, Pallas kernels: 263 us -> 231 us  [the longest x5 103 us: square_gather(): pl.pallas_call(functools.partial(square_kernel, count), out_shape=[jax.Sh...]
    unnamed x8 -> x5, waiting for transfers between devices: 21.3 us -> 1.1 us
    all_gather x3 -> x2, waiting for transfers between devices: 7.44 us -> 26 us  [gathered(): return lax.all_gather(shard, 'ctx', axis=0, tiled=True)]
    dot_general x8 -> x7, matrix products: 28.7 us -> 20.6 us  [project(): lax.dot_general(inputs, weight, (((1,), (0,)), ((), ())), preferred_eleme...]
    dot_general x8 -> x7, matrix products: 21.1 us -> 23.7 us  [project_back(): lax.dot_general(upstream, weight, (((1,), (1,)), ((), ())), preferred_ele...]
    dot_general x5 -> x4, matrix products: 22.5 us -> 20.2 us  [weight_grad(): lax.dot_general(inputs, upstream, (((0,), (0,)), ((), ())), preferred_ele...]
  transfers between devices with their start and end apart: 7 -> 5, of which waited for: 5 -> 4; matrix products, arithmetic and copies ran while one was open for 8% -> 8% of each run, Pallas kernels for 33% -> 22%
where the time goes in v3:
time: 586 us; the launch traced here: 581 us
  Pallas kernels  280 us (48%)
  waiting for transfers between devices  156 us (27%)
  matrix products  74.5 us (13%)
  other arithmetic  28.8 us (5%)
  local copies, waits for them, and re-layouts  25.5 us (4%)
  between operations  15.9 us (3%)
    reduce_scatter x3, waiting for transfers between devices, scattered(): return lax.psum_scatter(whole, 'ctx', scatter_dimension=0, tiled=True)  129 us
    pallas_call x5, Pallas kernels, square_gather(): pl.pallas_call(functools.partial(square_kernel, count), out_shape=[jax.Sh...  103 us
    pallas_call x3, Pallas kernels, batch_exchange(): pl.pallas_call(functools.partial(batch_kernel, size, kinds), out_shape=sh...  75.9 us
    pallas_call x1, Pallas kernels, gather_weights(): pl.pallas_call(functools.partial(weights_kernel, n_batch, n_ctx), name='g...  48.5 us
    pallas_call x2, Pallas kernels, halo_exchange(): pl.pallas_call(functools.partial(halo_kernel, size, depth, direction), ou...  41.9 us
    all_gather x2, waiting for transfers between devices, gathered(): return lax.all_gather(shard, 'ctx', axis=0, tiled=True)  26 us
    dot_general x7, matrix products, project_back(): lax.dot_general(upstream, weight, (((1,), (1,)), ((), ())), preferred_ele...  23.7 us
    dot_general x7, matrix products, project(): lax.dot_general(inputs, weight, (((1,), (0,)), ((), ())), preferred_eleme...  20.6 us
  transfers between devices with their start and end apart: 5, of which 4 were waited for; matrix products, arithmetic and copies ran while one was open for 8% of the time, Pallas kernels for 22%

profile of v3, /device:TPU:0, one launch (start us, length us, event | category | flops | bytes accessed | tf_op | source)
XLA Modules:
  0.0 580.8 jit_solution(16756508418186042773)
XLA Ops:
  7.2 3.9 pick_columns.1
  13.9 48.5 %gather_weights.1 = (bf16[4,8,144,384]{3,2,1,0:T(8,128)(2,1)}, bf16[8,4,32,1152]{3,2,1,0:T(8,128)(2,1)}, bf16[8,1,640]{2,1,0:T(2,128)(2,1)}) custom-call(bf16[4,144,384]{2,1,0:T(8,128)(2,1)} %bitcast.228, bf16[4,32,1152]{2,1,0:T(8,128)(2,1)} %bitcast.243, bf16[1,640]{1,0:T(2,128)(2,1)} %broadcast_in_dim.34.gain_ref), custom_call_target="tpu_custom_call" | custom-call | tf_op jit(solution)/shard_map/gather_weights/pallas_call | solution.py:431
  63.4 3.6 fusion.106
  69.4 29.1 %shard_map.280 = bf16[4,128,512]{2,1,0:T(8,128)(2,1)} custom-call(bf16[128,512]{1,0:T(8,128)(2,1)} %pad_maximum_fusion.10.source_ref), custom_call_target="tpu_custom_call" | custom-call | tf_op jit(solution)/shard_map/pallas_call | solution.py:238
  103.9 2.7 fusion.112
  106.6 2.0 convolution_convert_fusion.5
  109.5 2.3 multiply_reduce_fusion.7
  112.9 14.3 %shard_map.281 = bf16[4,128,1152]{2,1,0:T(8,128)(2,1)} custom-call(bf16[128,1152]{1,0:T(8,128)(2,1)} %multiply_convert_fusion.4.refs_0_), custom_call_target="tpu_custom_call" | custom-call | tf_op jit(solution)/shard_map/pallas_call | solution.py:171
  128.6 8.1 %fusion.113 = f32[512,3584]{1,0:T(8,128)S(1)} fusion(bf16[512,1152]{1,0:T(8,128)(2,1)} %bitcast.233, bf16[1152,3584]{1,0:T(8,128)(2,1)} %all-gather.3.cloned.1.call-done), kind=kOutput, calls=%fused_computation.212 | convolution fusion | flops 4227858432 | bytes 16777216 | tf_op jit(solution)/shard_map/dot_general | solution.py:38
  136.8 3.0 copy-done.6
  139.8 2.5 multiply_convert_fusion.1
  142.3 26.0 %all-gather.5.cloned.1.call-done = bf16[1792,1152]{1,0:T(8,128)(2,1)} async-done(((bf16[224,1152]{1,0:T(8,128)(2,1)}), bf16[1792,1152]{1,0:T(8,128)(2,1)}) %all-gather.5.cloned.1.call-update) | async-done | bytes 4128784 | tf_op jit(solution)/shard_map/all_gather | solution.py:455
  168.3 6.3 %convolution_convert_fusion.2 = bf16[512,1152]{1,0:T(8,128)(2,1)} fusion(bf16[512,1792]{1,0:T(8,128)(2,1)} %multiply_convert_fusion.1, bf16[1792,1152]{1,0:T(8,128)(2,1)} %all-gather.5.cloned.1.call-done), kind=kOutput, calls=%fused_computation.20 | convolution fusion | flops 2114519040 | bytes 7143424 | tf_op jit(solution)/shard_map/dot_general | solution.py:38
  174.5 18.8 %shard_map.282 = bf16[4,128,1152]{2,1,0:T(8,128)(2,1)} custom-call(bf16[4,128,1152]{2,1,0:T(8,128)(2,1)} %bitcast.238), custom_call_target="tpu_custom_call" | custom-call | tf_op jit(solution)/shard_map/pallas_call | solution.py:101
  196.5 16.0 %shard_map.283 = bf16[4,128,1152]{2,1,0:T(8,128)(2,1)} custom-call(bf16[128,1152]{1,0:T(8,128)(2,1)} %get-tuple-element.136.refs_0_), custom_call_target="tpu_custom_call" | custom-call | tf_op jit(solution)/shard_map/pallas_call | solution.py:171
  212.5 6.4 %convolution_convert_fusion.1 = bf16[1792,1152]{1,0:T(8,128)(2,1)} fusion(bf16[512,1792]{1,0:T(8,128)(2,1)} %multiply_convert_fusion.1, bf16[512,1152]{1,0:T(8,128)(2,1)} %bitcast.235), kind=kOutput, calls=%fused_computation.2 | convolution fusion | flops 2115993600 | bytes 7143424 | tf_op jit(solution)/shard_map/dot_general | solution.py:46
  218.8 9.3 %fusion.7 = (bf16[512,1792]{1,0:T(8,128)(2,1)S(1)}, bf16[512,1792]{1,0:T(8,128)(2,1)S(1)}) fusion(f32[512,3584]{1,0:T(8,128)} %copy-done.6, bf16[512,1152]{1,0:T(8,128)(2,1)} %bitcast.236, bf16[1792,1152]{1,0:T(8,128)(2,1)} %all-gather.5.cloned.1.call-done), kind=kOutput, calls=%fused_computation.13 | convolution fusion | flops 2135949312 | bytes 16318464 | tf_op jit(solution)/shard_map/dot_general | solution.py:42
  228.1 2.1 pad_maximum_fusion
  230.2 9.3 %convolution_convert_fusion.3 = bf16[512,1152]{1,0:T(8,128)(2,1)} fusion(bf16[1152,3584]{1,0:T(8,128)(2,1)} %all-gather.3.cloned.1.call-done, bf16[512,1792]{1,0:T(8,128)(2,1)S(1)} %get-tuple-element.125, bf16[512,1792]{1,0:T(8,128)(2,1)S(1)} %get-tuple-element.124), kind=kOutput, calls=%fused_computation.22 | convolution fusion | flops 4235788288 | bytes 13107200 | tf_op jit(solution)/shard_map/dot_general | solution.py:42
  239.5 16.2 %shard_map.284 = bf16[4,128,1152]{2,1,0:T(8,128)(2,1)} custom-call(bf16[4,128,1152]{2,1,0:T(8,128)(2,1)} %bitcast.237), custom_call_target="tpu_custom_call" | custom-call | tf_op jit(solution)/shard_map/pallas_call | solution.py:101
  255.8 10.1 %convolution_convert_fusion = bf16[1152,3584]{1,0:T(8,128)(2,1)} fusion(bf16[512,1152]{1,0:T(8,128)(2,1)} %bitcast.234, bf16[512,3584]{1,0:T(8,128)(2,1)} %pad_maximum_fusion), kind=kOutput, calls=%fused_computation.1 | convolution fusion | flops 4231987200 | bytes 13107200 | tf_op jit(solution)/shard_map/dot_general | solution.py:46
  272.1 2.8 convolution_bitcast_fusion.3
  278.9 12.7 %shard_map.285 = bf16[4,128,512]{2,1,0:T(8,128)(2,1)} custom-call(bf16[4,128,512]{2,1,0:T(8,128)(2,1)} %bitcast.226), custom_call_target="tpu_custom_call" | custom-call | tf_op jit(solution)/shard_map/pallas_call | solution.py:238
  306.6 40.8 %shard_map.286 = (f32[4,8,640]{2,1,0:T(8,128)}, bf16[4,128,1152]{2,1,0:T(8,128)(2,1)}, bf16[4,128,1024]{2,1,0:T(8,128)(2,1)}, bf16[4,128,384]{2,1,0:T(8,128)(2,1)}, bf16[4,128,288]{2,1,0:T(8,128)(2,1)}) custom-call(f32[8,640]{1,0:T(8,128)} %concatenate.59.refs_0_, bf16[128,1152]{1,0:T(8,128)(2,1)} %get-tuple-element.138.refs_1_, ...), custom_call_target="tpu_custom_call" | custom-call | tf_op jit(solution)/shard_map/pallas_call | solution.py:101
  354.7 36.9 %reduce-scatter.4.cloned.1.call-done.refs_0_ = bf16[288,384]{1,0:T(8,128)(2,1)} async-done(((bf16[2304,384]{1,0:T(8,128)(2,1)}), bf16[288,384]{1,0:T(8,128)(2,1)}) %reduce-scatter.4.cloned.1.call-update) | async-done | bytes 221200 | tf_op jit(solution)/shard_map/reduce_scatter | solution.py:459
  391.5 13.8 %shard_map.287 = bf16[4,288,384]{2,1,0:T(8,128)(2,1)} custom-call(bf16[288,384]{1,0:T(8,128)(2,1)} %reduce-scatter.4.cloned.1.call-done.refs_0_), custom_call_target="tpu_custom_call" | custom-call | tf_op jit(solution)/shard_map/pallas_call | solution.py:171
  412.5 28.4 %reduce-scatter.8.cloned.1.call-done.refs_0_ = bf16[224,1152]{1,0:T(8,128)(2,1)} async-done(((bf16[1792,1152]{1,0:T(8,128)(2,1)}), bf16[224,1152]{1,0:T(8,128)(2,1)}) %reduce-scatter.8.cloned.1.call-update) | async-done | bytes 516112 | tf_op jit(solution)/shard_map/reduce_scatter | solution.py:459
  440.9 21.1 %shard_map.289 = bf16[4,224,1152]{2,1,0:T(8,128)(2,1)} custom-call(bf16[224,1152]{1,0:T(8,128)(2,1)} %reduce-scatter.8.cloned.1.call-done.refs_0_), custom_call_target="tpu_custom_call" | custom-call | tf_op jit(solution)/shard_map/pallas_call | solution.py:171
  463.6 2.3 bitcast_convert_fusion
  466.0 63.9 %reduce-scatter.6.cloned.1.call-done.refs_0_ = bf16[144,3584]{1,0:T(8,128)(2,1)} async-done(((bf16[1152,3584]{1,0:T(8,128)(2,1)}), bf16[144,3584]{1,0:T(8,128)(2,1)}) %reduce-scatter.6.cloned.1.call-update) | async-done | bytes 1032208 | tf_op jit(solution)/shard_map/reduce_scatter | solution.py:459
  529.9 38.0 %shard_map.288.parts_ref = bf16[4,144,3584]{2,1,0:T(8,128)(2,1)} custom-call(bf16[144,3584]{1,0:T(8,128)(2,1)} %reduce-scatter.6.cloned.1.call-done.refs_0_), custom_call_target="tpu_custom_call" | custom-call | tf_op jit(solution)/shard_map/pallas_call | solution.py:171
  567.9 6.1 %place_columns.1 = (f32[144,6912]{1,0:T(8,128)}, f32[144,6912]{1,0:T(8,128)}) custom-call(bf16[4,144,3584]{2,1,0:T(8,128)(2,1)} %shard_map.288.parts_ref), custom_call_target="tpu_custom_call" | custom-call | tf_op jit(solution)/shard_map/place_columns/pallas_call | solution.py:295
  (247 shorter events, 57.4 us)
Async XLA Ops:
  7.2 4.2 copy-start
  7.2 121.4 %all-gather.3.cloned.1.call-start = ((), (), s32[]{:S(2)}) async-start(), calls=%async_computation.3 | async-start | bytes 9289728 | tf_op jit(solution)/shard_map/all_gather | solution.py:455
  11.3 157.0 %all-gather.5.cloned.1.call-start = ((), (), s32[]{:S(2)}) async-start(), calls=%async_computation.4 | async-start | bytes 4644864 | tf_op jit(solution)/shard_map/all_gather | solution.py:455
  12.3 379.3 %reduce-scatter.4.cloned.1.call-start = ((), (), s32[]{:S(2)}) async-start(), calls=%async_computation.5 | async-start | bytes 1990656 | tf_op jit(solution)/shard_map/reduce_scatter | solution.py:459
  63.4 3.7 copy-start.2
  67.0 31.6 %copy-start.4 = (bf16[1,8,144,384]{3,2,1,0:T(8,128)(2,1)}, bf16[1,8,144,384]{3,2,1,0:T(8,128)(2,1)S(1)}, u32[]{:S(2)}) copy-start(bf16[1,8,144,384]{3,2,1,0:T(8,128)(2,1)S(1)} %get-tuple-element.129) | copy-start | bytes 2654212
  68.2 33.7 %copy-start.50 = (f32[128]{0:T(128)}, f32[128]{0:T(128)S(1)}, u32[]{:S(2)}) copy-start(f32[128]{0:T(128)S(1)} %get-tuple-element.122) | copy-start | bytes 1540
  68.3 33.6 %copy-start.33 = (f32[256]{0:T(256)}, f32[256]{0:T(256)S(1)}, u32[]{:S(2)}) copy-start(f32[256]{0:T(256)S(1)} %mul.601) | copy-start | bytes 3076
  68.3 33.6 %copy-start.44 = (f32[128]{0:T(128)}, f32[128]{0:T(128)S(1)}, u32[]{:S(2)}) copy-start(f32[128]{0:T(128)S(1)} %multiply_power_fusion) | copy-start | bytes 1540
  68.3 30.3 %copy-start.46 = (f32[128]{0:T(128)}, f32[128]{0:T(128)S(1)}, u32[]{:S(2)}) copy-start(f32[128]{0:T(128)S(1)} %bitcast_convert_fusion.1) | copy-start | bytes 1540
  68.3 33.6 %copy-start.38 = (f32[128]{0:T(128)}, f32[128]{0:T(128)S(1)}, u32[]{:S(2)}) copy-start(f32[128]{0:T(128)S(1)} %fusion.83) | copy-start | bytes 1540
  98.7 5.0 copy-start.35
  102.5 4.1 copy-start.31
  103.9 4.7 copy-start.18
  103.9 4.7 copy-start.21
  111.8 155.8 %copy-start.37 = (f32[128]{0:T(128)}, f32[128]{0:T(128)S(1)}, u32[]{:S(2)}) copy-start(f32[128]{0:T(128)S(1)} %fusion.84) | copy-start | bytes 1540
  136.8 3.0 copy-start.6
  174.5 20.5 %copy-start.9 = (bf16[1,128,1152]{2,1,0:T(8,128)(2,1)S(1)}, bf16[1,128,1152]{2,1,0:T(8,128)(2,1)}, u32[]{:S(2)}) copy-start(bf16[1,128,1152]{2,1,0:T(8,128)(2,1)} %param.20) | copy-start | bytes 884740
  278.0 15.7 %copy-start.45 = (f32[128]{0:T(128)S(1)}, f32[128]{0:T(128)}, u32[]{:S(2)}) copy-start(f32[128]{0:T(128)} %copy-done.44) | copy-start | bytes 1540
  278.0 15.7 %copy-start.47 = (f32[128]{0:T(128)S(1)}, f32[128]{0:T(128)}, u32[]{:S(2)}) copy-start(f32[128]{0:T(128)} %copy-done.46) | copy-start | bytes 1540
  291.6 4.7 copy-start.36
  292.8 4.3 copy-start.32
  297.3 3.5 copy-start.16
  297.3 3.5 copy-start.17
  297.3 3.5 copy-start.34
  297.3 3.5 copy-start.39
  297.4 3.7 copy-start.51
  297.5 3.7 copy-start.15
  297.6 3.8 copy-start.5
  353.5 87.4 %reduce-scatter.8.cloned.1.call-start = ((), (), s32[]{:S(2)}) async-start(), calls=%async_computation.7 | async-start | bytes 4644864 | tf_op jit(solution)/shard_map/reduce_scatter | solution.py:459
  354.1 175.8 %reduce-scatter.6.cloned.1.call-start = ((), (), s32[]{:S(2)}) async-start(), calls=%async_computation.6 | async-start | bytes 9289728 | tf_op jit(solution)/shard_map/reduce_scatter | solution.py:459
  529.9 44.2 %copy-start.1 = (bf16[864,1152]{1,0:T(8,128)(2,1)S(1)}, bf16[864,1152]{1,0:T(8,128)(2,1)}, u32[]{:S(2)}) copy-start(bf16[864,1152]{1,0:T(8,128)(2,1)} %param.32) | copy-start | bytes 5971972
  (34 other events, 61.8 us)
Sparse Core Ops, SparseCore 0:
  11.3 97.3 all-gather.2
  110.9 57.2 all-gather.4
  353.6 37.8 reduce-scatter.3
  393.7 47.1 reduce-scatter.7
  443.1 86.7 reduce-scatter.5

commit v4 on v3

--- a/solution.py
+++ b/solution.py
@@ -277,28 +277,24 @@
     )(w_gate, w_up)
 
 
-def place_kernel(n_batch, n_ctx, piece, padded, parts_ref, gate_ref, up_ref):
+def place_kernel(n_batch, n_ctx, piece, padded, parts_ref, out_ref):
     for shard in range(n_ctx):
         for spot in range(n_batch):
             start = (shard * n_batch + spot) * piece
-            for half, ref in enumerate((gate_ref, up_ref)):
-                place = (half * n_ctx + shard) * padded
-                ref[:, start : start + piece] = parts_ref[spot, :, place : place + piece].astype(F32)
+            place = shard * padded
+            out_ref[:, start : start + piece] = parts_ref[spot, :, place : place + piece].astype(F32)
 
 
 def place_columns(n_batch, n_ctx, piece, padded, parts):
     rows = parts.shape[1]
     block = row_block(rows)
     hidden = n_batch * n_ctx * piece
-    spec = pl.BlockSpec((block, hidden), lambda i: (i, 0))
-    out = jax.ShapeDtypeStruct((rows, hidden), F32)
     return pl.pallas_call(
         functools.partial(place_kernel, n_batch, n_ctx, piece, padded),
-        name="place_columns",
         grid=(rows // block,),
-        out_shape=(out, out),
-        in_specs=[pl.BlockSpec((n_batch, block, 2 * n_ctx * padded), lambda i: (0, i, 0))],
-        out_specs=[spec, spec],
+        out_shape=jax.ShapeDtypeStruct((rows, hidden), F32),
+        in_specs=[pl.BlockSpec((n_batch, block, n_ctx * padded), lambda i: (0, i, 0))],
+        out_specs=pl.BlockSpec((block, hidden), lambda i: (i, 0)),
     )(parts)
 
 
@@ -579,6 +575,11 @@
     both_pre = project(ffn_in_all, part_both)
     gate_pre, up_pre = both_pre[:, :hidden_part], both_pre[:, hidden_part:]
     mixed_low = gated_gelu(gate_pre, up_pre).astype(BF16)
+    mixed_low, act_in_late, attn_late = lax.optimization_barrier((mixed_low, act_in, attn_low))
+    act_in_all, attn_all = square_gather(13, act_in_late, attn_late)
+    mixed_low, act_in_all, attn_all = lax.optimization_barrier((mixed_low, act_in_all, attn_all))
+    act_in_all = act_in_all.reshape(all_tok, model_width)
+    attn_all = attn_all.reshape(all_tok, query_width)
     proj_part = project(mixed_low, part_down).astype(BF16)
     (proj_parts,) = batch_exchange(
         3, n_batch, slots=(proj_part.reshape(n_batch, tok_count, model_width),)
@@ -598,15 +599,21 @@
     grad_mixed = project_back(grad_ffn_low, part_down)
     _, pull_gelu = jax.vjp(gated_gelu, gate_pre, up_pre)
     grad_gate, grad_up = pull_gelu(grad_mixed)
-    grad_both_low = jnp.concatenate([grad_gate, grad_up], axis=1).astype(BF16)
+    grad_gate_low = grad_gate.astype(BF16)
+    grad_up_low = grad_up.astype(BF16)
+    grad_both_low = jnp.concatenate([grad_gate_low, grad_up_low], axis=1)
     back_part = project_back(grad_both_low, part_both).astype(BF16)
     (back_parts,) = batch_exchange(
         5, n_batch, slots=(back_part.reshape(n_batch, tok_count, model_width),)
     )
-    back_parts, grad_both_low = lax.optimization_barrier((back_parts, grad_both_low))
-    both_grad = weight_grad(ffn_in_all, grad_both_low).astype(BF16)
-    back_parts, both_grad = lax.optimization_barrier((back_parts, both_grad))
-    grad_w_both = scattered(both_grad)
+    back_parts, grad_gate_low, grad_up_low = lax.optimization_barrier(
+        (back_parts, grad_gate_low, grad_up_low)
+    )
+    gate_grad = weight_grad(ffn_in_all, grad_gate_low).astype(BF16)
+    up_grad = weight_grad(ffn_in_all, grad_up_low).astype(BF16)
+    back_parts, gate_grad, up_grad = lax.optimization_barrier((back_parts, gate_grad, up_grad))
+    grad_w_gate = scattered(gate_grad)
+    grad_w_up = scattered(up_grad)
     grad_ffn_in = jnp.sum(back_parts.astype(F32), axis=0)
     _, pull_ffn_norm = jax.vjp(normed, middle, full_gain_ffn)
     grad_middle_part, grad_gain_ffn = pull_ffn_norm(grad_ffn_in)
@@ -678,14 +685,12 @@
         ],
         axis=1,
     )
-    gain_parts, act_in_all, attn_all, qkv_slots, proj_slots = batch_exchange(
+    gain_parts, qkv_slots, proj_slots = batch_exchange(
         7,
         n_batch,
-        whole=(gain_rows, act_in, attn_low),
+        whole=(gain_rows,),
         slots=(column_slots(grad_qkv_low), column_slots(grad_proj_low)),
     )
-    act_in_all = act_in_all.reshape(all_tok, model_width)
-    attn_all = attn_all.reshape(all_tok, query_width)
     proj_rows = w_output.shape[0]
     gain_count = gain_rows.shape[1]
     gain_lines = -(-gain_count // quarter)
@@ -711,10 +716,9 @@
     )
     attn_sum = scattered(packed.reshape(n_ctx * lines, quarter))
 
-    (down_all,) = square_gather(8, grad_w_down)
-    (both_all,) = square_gather(9, grad_w_both)
+    down_all, gate_all = square_gather(8, grad_w_down, grad_w_gate)
+    (up_all,) = square_gather(9, grad_w_up)
     (attn_grads,) = square_gather(11, attn_sum)
-    grad_gate_shard, grad_up_shard = place_columns(n_batch, n_ctx, piece, padded, both_all)
     gain_mine = attn_grads[0, width_shard + proj_rows : used].reshape(-1).astype(F32)
 
     def columns_back(pieces):
@@ -733,8 +737,8 @@
         columns_back(attn_grads[:, width_shard : width_shard + proj_rows, :output_part]),
         gain_mine[width_shard : 2 * width_shard],
         gain_mine[2 * width_shard : 3 * width_shard],
-        grad_gate_shard,
-        grad_up_shard,
+        place_columns(n_batch, n_ctx, piece, padded, gate_all),
+        place_columns(n_batch, n_ctx, piece, padded, up_all),
         down_all[:, :piece].reshape(hidden_shard, model_width).astype(F32),
         gain_mine[3 * width_shard : 4 * width_shard],
     )

time: 586 us -> 562 us (0.959)
  waiting for transfers between devices: 156 us -> 129 us
    pallas_call x3, Pallas kernels: 75.9 us -> 49.2 us  [batch_exchange(): pl.pallas_call(functools.partial(batch_kernel, size, kinds), out_shape=sh...]
    pallas_call x5 -> x6, Pallas kernels: 103 us -> 127 us  [square_gather(): pl.pallas_call(functools.partial(square_kernel, count), out_shape=[jax.Sh...]
    all_gather x2, waiting for transfers between devices: 26 us -> 6.89 us  [gathered(): return lax.all_gather(shard, 'ctx', axis=0, tiled=True)]
    reduce_scatter x3 -> x4, waiting for transfers between devices: 129 us -> 121 us  [scattered(): return lax.psum_scatter(whole, 'ctx', scatter_dimension=0, tiled=True)]
    pallas_call x2, Pallas kernels: 41.9 us -> 48.2 us  [halo_exchange(): pl.pallas_call(functools.partial(halo_kernel, size, depth, direction), ou...]
    dot_general x4 -> x5, matrix products: 20.2 us -> 22.6 us  [weight_grad(): lax.dot_general(inputs, upstream, (((0,), (0,)), ((), ())), preferred_ele...]
  transfers between devices with their start and end apart: 5 -> 6, of which waited for: 4 -> 5; matrix products, arithmetic and copies ran while one was open for 8% -> 7% of each run, Pallas kernels for 22% -> 31%
where the time goes in v4:
time: 562 us; the launch traced here: 557 us
  Pallas kernels  285 us (51%)
  waiting for transfers between devices  129 us (23%)
  matrix products  75.7 us (13%)
  other arithmetic  27 us (5%)
  local copies, waits for them, and re-layouts  23.5 us (4%)
  between operations  16.3 us (3%)
    pallas_call x6, Pallas kernels, square_gather(): pl.pallas_call(functools.partial(square_kernel, count), out_shape=[jax.Sh...  127 us
    reduce_scatter x4, waiting for transfers between devices, scattered(): return lax.psum_scatter(whole, 'ctx', scatter_dimension=0, tiled=True)  121 us
    pallas_call x3, Pallas kernels, batch_exchange(): pl.pallas_call(functools.partial(batch_kernel, size, kinds), out_shape=sh...  49.2 us
    pallas_call x1, Pallas kernels, gather_weights(): pl.pallas_call(functools.partial(weights_kernel, n_batch, n_ctx), name='g...  48.5 us
    pallas_call x2, Pallas kernels, halo_exchange(): pl.pallas_call(functools.partial(halo_kernel, size, depth, direction), ou...  48.2 us
    dot_general x7, matrix products, project_back(): lax.dot_general(upstream, weight, (((1,), (1,)), ((), ())), preferred_ele...  25.1 us
    dot_general x5, matrix products, weight_grad(): lax.dot_general(inputs, upstream, (((0,), (0,)), ((), ())), preferred_ele...  22.6 us
    dot_general x7, matrix products, project(): lax.dot_general(inputs, weight, (((1,), (0,)), ((), ())), preferred_eleme...  20.3 us
  transfers between devices with their start and end apart: 6, of which 5 were waited for; matrix products, arithmetic and copies ran while one was open for 7% of the time, Pallas kernels for 31%

profile of v4, /device:TPU:0, one launch (start us, length us, event | category | flops | bytes accessed | tf_op | source)
XLA Modules:
  0.0 557.1 jit_solution(10376846192089333858)
XLA Ops:
  7.2 3.9 pick_columns.1
  13.9 48.5 %gather_weights.1 = (bf16[4,8,144,384]{3,2,1,0:T(8,128)(2,1)}, bf16[8,4,32,1152]{3,2,1,0:T(8,128)(2,1)}, bf16[8,1,640]{2,1,0:T(2,128)(2,1)}) custom-call(bf16[4,144,384]{2,1,0:T(8,128)(2,1)} %bitcast.230, bf16[4,32,1152]{2,1,0:T(8,128)(2,1)} %bitcast.246, bf16[1,640]{1,0:T(2,128)(2,1)} %broadcast_in_dim.34.gain_ref), custom_call_target="tpu_custom_call" | custom-call | tf_op jit(solution)/shard_map/gather_weights/pallas_call | solution.py:427
  63.4 3.6 fusion.114
  69.8 29.1 %shard_map.280 = bf16[4,128,512]{2,1,0:T(8,128)(2,1)} custom-call(bf16[128,512]{1,0:T(8,128)(2,1)} %pad_maximum_fusion.9.source_ref), custom_call_target="tpu_custom_call" | custom-call | tf_op jit(solution)/shard_map/pallas_call | solution.py:238
  106.9 2.3 multiply_reduce_fusion.7
  111.0 14.3 %shard_map.281 = bf16[4,128,1152]{2,1,0:T(8,128)(2,1)} custom-call(bf16[128,1152]{1,0:T(8,128)(2,1)} %multiply_convert_fusion.4.refs_0_), custom_call_target="tpu_custom_call" | custom-call | tf_op jit(solution)/shard_map/pallas_call | solution.py:171
  126.7 7.8 %fusion.121 = f32[512,3584]{1,0:T(8,128)S(1)} fusion(bf16[512,1152]{1,0:T(8,128)(2,1)} %bitcast.235, bf16[1152,3584]{1,0:T(8,128)(2,1)} %all-gather.3.cloned.1.call-done), kind=kOutput, calls=%fused_computation.217 | convolution fusion | flops 4227858432 | bytes 16777216 | tf_op jit(solution)/shard_map/dot_general | solution.py:38
  134.6 3.0 multiply_convert_fusion.1
  138.1 23.2 %shard_map.282 = (bf16[4,128,1152]{2,1,0:T(8,128)(2,1)}, bf16[4,128,1024]{2,1,0:T(8,128)(2,1)}) custom-call(bf16[128,1152]{1,0:T(8,128)(2,1)} %get-tuple-element.43.refs_0_, bf16[128,1024]{1,0:T(8,128)(2,1)} %copy.191.refs_1_), custom_call_target="tpu_custom_call" | custom-call | tf_op jit(solution)/shard_map/pallas_call | solution.py:171
  161.4 6.9 %all-gather.5.cloned.1.call-done = bf16[1792,1152]{1,0:T(8,128)(2,1)} async-done(((bf16[224,1152]{1,0:T(8,128)(2,1)}), bf16[1792,1152]{1,0:T(8,128)(2,1)}) %all-gather.5.cloned.1.call-update) | async-done | bytes 4128784 | tf_op jit(solution)/shard_map/all_gather | solution.py:451
  168.3 6.3 %convolution_convert_fusion.3 = bf16[512,1152]{1,0:T(8,128)(2,1)} fusion(bf16[512,1792]{1,0:T(8,128)(2,1)} %multiply_convert_fusion.1, bf16[1792,1152]{1,0:T(8,128)(2,1)} %all-gather.5.cloned.1.call-done), kind=kOutput, calls=%fused_computation.25 | convolution fusion | flops 2114519040 | bytes 7143424 | tf_op jit(solution)/shard_map/dot_general | solution.py:38
  174.5 18.8 %shard_map.283 = bf16[4,128,1152]{2,1,0:T(8,128)(2,1)} custom-call(bf16[4,128,1152]{2,1,0:T(8,128)(2,1)} %bitcast.241), custom_call_target="tpu_custom_call" | custom-call | tf_op jit(solution)/shard_map/pallas_call | solution.py:101
  196.5 16.0 %shard_map.284 = bf16[4,128,1152]{2,1,0:T(8,128)(2,1)} custom-call(bf16[128,1152]{1,0:T(8,128)(2,1)} %get-tuple-element.152.refs_0_), custom_call_target="tpu_custom_call" | custom-call | tf_op jit(solution)/shard_map/pallas_call | solution.py:171
  212.5 6.4 %convolution_convert_fusion.2 = bf16[1792,1152]{1,0:T(8,128)(2,1)} fusion(bf16[512,1792]{1,0:T(8,128)(2,1)} %multiply_convert_fusion.1, bf16[512,1152]{1,0:T(8,128)(2,1)} %bitcast.238), kind=kOutput, calls=%fused_computation.3 | convolution fusion | flops 2115993600 | bytes 7143424 | tf_op jit(solution)/shard_map/dot_general | solution.py:46
  218.9 9.3 %fusion.7 = (bf16[512,1792]{1,0:T(8,128)(2,1)S(1)}, bf16[512,1792]{1,0:T(8,128)(2,1)S(1)}) fusion(f32[512,3584]{1,0:T(8,128)} %copy-done.6, bf16[512,1152]{1,0:T(8,128)(2,1)} %bitcast.239, bf16[1792,1152]{1,0:T(8,128)(2,1)} %all-gather.5.cloned.1.call-done), kind=kOutput, calls=%fused_computation.14 | convolution fusion | flops 2135949312 | bytes 16318464 | tf_op jit(solution)/shard_map/dot_general | solution.py:42
  228.2 10.6 %fusion.14 = bf16[512,1152]{1,0:T(8,128)(2,1)} fusion(bf16[1152,3584]{1,0:T(8,128)(2,1)} %all-gather.3.cloned.1.call-done, bf16[512,1792]{1,0:T(8,128)(2,1)S(1)} %get-tuple-element.51, bf16[512,1792]{1,0:T(8,128)(2,1)S(1)} %get-tuple-element.50), kind=kOutput, calls=%fused_computation.24 | convolution fusion | flops 4235788288 | bytes 13107200 | tf_op jit(solution)/shard_map/dot_general | solution.py:42
  238.8 16.2 %shard_map.285 = bf16[4,128,1152]{2,1,0:T(8,128)(2,1)} custom-call(bf16[4,128,1152]{2,1,0:T(8,128)(2,1)} %bitcast.240), custom_call_target="tpu_custom_call" | custom-call | tf_op jit(solution)/shard_map/pallas_call | solution.py:101
  255.1 6.2 %convolution_convert_fusion.1 = bf16[1152,1792]{1,0:T(8,128)(2,1)} fusion(bf16[512,1152]{1,0:T(8,128)(2,1)} %bitcast.236, bf16[512,1792]{1,0:T(8,128)(2,1)} %copy-done.65), kind=kOutput, calls=%fused_computation.2 | convolution fusion | flops 2115993600 | bytes 7143424 | tf_op jit(solution)/shard_map/dot_general | solution.py:46
  261.2 6.1 %convolution_convert_fusion = bf16[1152,1792]{1,0:T(8,128)(2,1)} fusion(bf16[512,1152]{1,0:T(8,128)(2,1)} %bitcast.237, bf16[512,1792]{1,0:T(8,128)(2,1)} %copy-done.64), kind=kOutput, calls=%fused_computation.1 | convolution fusion | flops 2115993600 | bytes 7143424 | tf_op jit(solution)/shard_map/dot_general | solution.py:46
  272.2 2.7 convolution_bitcast_fusion.3
  278.9 19.1 %shard_map.286 = bf16[4,128,512]{2,1,0:T(8,128)(2,1)} custom-call(bf16[4,128,512]{2,1,0:T(8,128)(2,1)} %bitcast.228), custom_call_target="tpu_custom_call" | custom-call | tf_op jit(solution)/shard_map/pallas_call | solution.py:238
  312.7 14.1 %shard_map.287 = (f32[4,8,640]{2,1,0:T(8,128)}, bf16[4,128,384]{2,1,0:T(8,128)(2,1)}, bf16[4,128,288]{2,1,0:T(8,128)(2,1)}) custom-call(f32[8,640]{1,0:T(8,128)} %concatenate.58.refs_0_, bf16[4,128,384]{2,1,0:T(8,128)(2,1)} %bitcast.232, bf16[4,128,288]{2,1,0:T(8,128)(2,1)} %bitcast.234), custom_call_target="tpu_custom_call" | custom-call | tf_op jit(solution)/shard_map/pallas_call | solution.py:101
  336.3 35.1 %reduce-scatter.5.cloned.1.call-done.refs_0_ = bf16[288,384]{1,0:T(8,128)(2,1)} async-done(((bf16[2304,384]{1,0:T(8,128)(2,1)}), bf16[288,384]{1,0:T(8,128)(2,1)}) %reduce-scatter.5.cloned.1.call-update) | async-done | bytes 221200 | tf_op jit(solution)/shard_map/reduce_scatter | solution.py:455
  371.5 14.0 %shard_map.288 = bf16[4,288,384]{2,1,0:T(8,128)(2,1)} custom-call(bf16[288,384]{1,0:T(8,128)(2,1)} %reduce-scatter.5.cloned.1.call-done.refs_0_), custom_call_target="tpu_custom_call" | custom-call | tf_op jit(solution)/shard_map/pallas_call | solution.py:171
  392.6 28.5 %reduce-scatter.7.cloned.1.call-done.refs_0_ = bf16[224,1152]{1,0:T(8,128)(2,1)} async-done(((bf16[1792,1152]{1,0:T(8,128)(2,1)}), bf16[224,1152]{1,0:T(8,128)(2,1)}) %reduce-scatter.7.cloned.1.call-update) | async-done | bytes 516112 | tf_op jit(solution)/shard_map/reduce_scatter | solution.py:455
  421.0 50.0 %reduce-scatter.9.cloned.1.call-done.refs_1_ = bf16[144,1792]{1,0:T(8,128)(2,1)} async-done(((bf16[1152,1792]{1,0:T(8,128)(2,1)}), bf16[144,1792]{1,0:T(8,128)(2,1)}) %reduce-scatter.9.cloned.1.call-update) | async-done | bytes 516112 | tf_op jit(solution)/shard_map/reduce_scatter | solution.py:455
  471.0 38.6 %shard_map.289 = (bf16[4,224,1152]{2,1,0:T(8,128)(2,1)}, bf16[4,144,1792]{2,1,0:T(8,128)(2,1)}) custom-call(bf16[224,1152]{1,0:T(8,128)(2,1)} %reduce-scatter.7.cloned.1.call-done.refs_0_, bf16[144,1792]{1,0:T(8,128)(2,1)} %reduce-scatter.9.cloned.1.call-done.refs_1_), custom_call_target="tpu_custom_call" | custom-call | tf_op jit(solution)/shard_map/pallas_call | solution.py:171
  509.6 4.3 shard_map.290
  514.0 7.0 %reduce-scatter.11.cloned.1.call-done.refs_0_ = bf16[144,1792]{1,0:T(8,128)(2,1)} async-done(((bf16[1152,1792]{1,0:T(8,128)(2,1)}), bf16[144,1792]{1,0:T(8,128)(2,1)}) %reduce-scatter.11.cloned.1.call-update) | async-done | bytes 516112 | tf_op jit(solution)/shard_map/reduce_scatter | solution.py:455
  521.0 20.5 %shard_map.291.parts_ref = bf16[4,144,1792]{2,1,0:T(8,128)(2,1)} custom-call(bf16[144,1792]{1,0:T(8,128)(2,1)} %reduce-scatter.11.cloned.1.call-done.refs_0_), custom_call_target="tpu_custom_call" | custom-call | tf_op jit(solution)/shard_map/pallas_call | solution.py:171
  541.5 4.3 shard_map.292
  547.7 2.3 bitcast_convert_fusion
  (263 shorter events, 61.6 us)
Async XLA Ops:
  7.2 4.1 copy-start
  7.2 119.5 %all-gather.3.cloned.1.call-start = ((), (), s32[]{:S(2)}) async-start(), calls=%async_computation.4 | async-start | bytes 9289728 | tf_op jit(solution)/shard_map/all_gather | solution.py:451
  11.2 157.0 %all-gather.5.cloned.1.call-start = ((), (), s32[]{:S(2)}) async-start(), calls=%async_computation.5 | async-start | bytes 4644864 | tf_op jit(solution)/shard_map/all_gather | solution.py:451
  12.3 359.2 %reduce-scatter.5.cloned.1.call-start = ((), (), s32[]{:S(2)}) async-start(), calls=%async_computation.6 | async-start | bytes 1990656 | tf_op jit(solution)/shard_map/reduce_scatter | solution.py:455
  63.4 3.7 copy-start.2
  68.1 32.4 %copy-start.12 = (f32[128,256]{1,0:T(8,128)}, f32[128,256]{1,0:T(8,128)S(1)}, u32[]{:S(2)}) copy-start(f32[128,256]{1,0:T(8,128)S(1)} %get-tuple-element.139) | copy-start | bytes 393220
  68.2 34.0 %copy-start.36 = (f32[256]{0:T(256)}, f32[256]{0:T(256)S(1)}, u32[]{:S(2)}) copy-start(f32[256]{0:T(256)S(1)} %mul.601) | copy-start | bytes 3076
  68.2 30.7 %copy-start.46 = (f32[128]{0:T(128)}, f32[128]{0:T(128)S(1)}, u32[]{:S(2)}) copy-start(f32[128]{0:T(128)S(1)} %multiply_power_fusion) | copy-start | bytes 1540
  68.2 34.0 %copy-start.48 = (f32[128]{0:T(128)}, f32[128]{0:T(128)S(1)}, u32[]{:S(2)}) copy-start(f32[128]{0:T(128)S(1)} %bitcast_convert_fusion.1) | copy-start | bytes 1540
  68.3 33.9 %copy-start.40 = (f32[128]{0:T(128)}, f32[128]{0:T(128)S(1)}, u32[]{:S(2)}) copy-start(f32[128]{0:T(128)S(1)} %fusion.90) | copy-start | bytes 1540
  69.1 34.2 %copy-start.18 = (f32[128,128]{1,0:T(8,128)}, f32[128,128]{1,0:T(8,128)S(1)}, u32[]{:S(2)}) copy-start(f32[128,128]{1,0:T(8,128)S(1)} %get-tuple-element.172) | copy-start | bytes 196612
  99.0 4.1 copy-start.38
  109.1 16.2 %copy-start.61 = (f32[128]{0:T(128)}, f32[128]{0:T(128)S(1)}, u32[]{:S(2)}) copy-start(f32[128]{0:T(128)S(1)} %get-tuple-element.177) | copy-start | bytes 1540
  134.6 3.6 copy-start.6
  174.5 20.5 %copy-start.9 = (bf16[1,128,1152]{2,1,0:T(8,128)(2,1)S(1)}, bf16[1,128,1152]{2,1,0:T(8,128)(2,1)}, u32[]{:S(2)}) copy-start(bf16[1,128,1152]{2,1,0:T(8,128)(2,1)} %param.20) | copy-start | bytes 884740
  228.2 10.7 %copy-start.64 = (bf16[512,1792]{1,0:T(8,128)(2,1)}, bf16[512,1792]{1,0:T(8,128)(2,1)S(1)}, u32[]{:S(2)}) copy-start(bf16[512,1792]{1,0:T(8,128)(2,1)S(1)} %get-tuple-element.51) | copy-start | bytes 5505028
  228.2 10.6 %copy-start.65 = (bf16[512,1792]{1,0:T(8,128)(2,1)}, bf16[512,1792]{1,0:T(8,128)(2,1)S(1)}, u32[]{:S(2)}) copy-start(bf16[512,1792]{1,0:T(8,128)(2,1)S(1)} %get-tuple-element.50) | copy-start | bytes 5505028
  278.9 21.2 %copy-start.47 = (f32[128]{0:T(128)S(1)}, f32[128]{0:T(128)}, u32[]{:S(2)}) copy-start(f32[128]{0:T(128)} %copy-done.46) | copy-start | bytes 1540
  278.9 21.2 %copy-start.49 = (f32[128]{0:T(128)S(1)}, f32[128]{0:T(128)}, u32[]{:S(2)}) copy-start(f32[128]{0:T(128)} %copy-done.48) | copy-start | bytes 1540
  299.1 4.4 copy-start.39
  300.1 4.2 copy-start.35
  304.7 3.4 copy-start.13
  304.7 3.4 copy-start.20
  304.7 3.4 copy-start.21
  304.7 3.4 copy-start.37
  304.7 3.5 copy-start.53
  304.7 3.8 copy-start.19
  304.7 3.9 copy-start.5
  333.2 87.9 %reduce-scatter.7.cloned.1.call-start = ((), (), s32[]{:S(2)}) async-start(), calls=%async_computation.7 | async-start | bytes 4644864 | tf_op jit(solution)/shard_map/reduce_scatter | solution.py:455
  333.7 137.3 %reduce-scatter.9.cloned.1.call-start = ((), (), s32[]{:S(2)}) async-start(), calls=%async_computation.8 | async-start | bytes 4644864 | tf_op jit(solution)/shard_map/reduce_scatter | solution.py:455
  334.3 186.6 %reduce-scatter.11.cloned.1.call-start = ((), (), s32[]{:S(2)}) async-start(), calls=%async_computation.9 | async-start | bytes 4644864 | tf_op jit(solution)/shard_map/reduce_scatter | solution.py:455
  545.8 4.2 copy-start.1
  (40 other events, 63.9 us)
Sparse Core Ops, SparseCore 0:
  11.3 97.3 all-gather.2
  110.9 57.2 all-gather.4
  333.3 38.1 reduce-scatter.4
  373.6 47.3 reduce-scatter.6
  423.2 47.7 reduce-scatter.8
  473.2 47.7 reduce-scatter.10

commit v5 on v4

--- a/solution.py
+++ b/solution.py
@@ -182,6 +182,240 @@
     )(*arrays)
 
 
+def turn_kernel(
+    mixed_ref,
+    down_ref,
+    middle_ref,
+    upstream_ref,
+    valid_ref,
+    gain_ref,
+    out_ref,
+    grads_ref,
+    gain_grad_ref,
+    part_ref,
+    taken_ref,
+    send_sem,
+    recv_sem,
+    pass_sem,
+    take_sem,
+):
+    me = lax.axis_index("batch")
+    across = me + 1 - 2 * lax.rem(me, 2)
+    along = lax.rem(me + 2, 4)
+    corner = lax.rem(across + 2, 4)
+    order = (corner, across, along)
+    tok_count = middle_ref.shape[0]
+    barrier = pltpu.get_barrier_semaphore()
+    for peer in order:
+        pl.semaphore_signal(barrier, inc=1, device_id={"batch": peer}, device_id_type=MESH)
+    pl.semaphore_wait(barrier, 3)
+
+    def product(place):
+        rows = pl.ds(pl.multiple_of(place * tok_count, tok_count), tok_count)
+        return jnp.dot(mixed_ref[rows, :], down_ref[...], preferred_element_type=F32)
+
+    copies = [
+        pltpu.make_async_remote_copy(
+            src_ref=part_ref.at[turn],
+            dst_ref=taken_ref.at[turn],
+            send_sem=send_sem.at[turn],
+            recv_sem=recv_sem.at[turn],
+            device_id={"batch": peer},
+            device_id_type=MESH,
+        )
+        for turn, peer in enumerate(order)
+    ]
+    for turn, peer in enumerate(order):
+        part_ref[turn] = product(peer).astype(BF16)
+        if turn > 0:
+            copies[turn - 1].start()
+    total = product(me)
+    copies[2].start()
+    for turn in range(3):
+        copies[turn].wait_recv()
+        total = total + taken_ref[turn].astype(F32)
+    gain = gain_ref[...]
+    valid = valid_ref[...]
+    scale = lax.rsqrt(jnp.mean(total * total, axis=-1, keepdims=True) + EPS)
+    upstream = upstream_ref[...].astype(F32) * valid
+    gained = upstream * gain
+    back = scale * gained - total * (
+        scale * scale * scale * jnp.mean(total * gained, axis=-1, keepdims=True)
+    )
+    grads_ref[me] = back.astype(BF16)
+    unit = total * scale
+    out_ref[...] = ((middle_ref[...] + unit * gain) * valid).astype(BF16)
+    gain_grad_ref[...] = jnp.sum(upstream * unit, axis=0, keepdims=True)
+
+    def remote(block, turn, peer):
+        copy = pltpu.make_async_remote_copy(
+            src_ref=block,
+            dst_ref=block,
+            send_sem=pass_sem.at[turn],
+            recv_sem=take_sem.at[turn],
+            device_id={"batch": peer},
+            device_id_type=MESH,
+        )
+        copy.start()
+        return copy
+
+    firsts = [remote(grads_ref.at[me], turn, peer) for turn, peer in enumerate((across, along))]
+    columns = grads_ref.shape[-1]
+    cut = columns // 256 * 128
+    halves = (pl.ds(0, cut), pl.ds(cut, columns - cut))
+    seconds = []
+    for turn, (giver, taker) in enumerate(((across, along), (along, across))):
+        firsts[turn].wait_recv()
+        seconds.append(remote(grads_ref.at[giver, :, halves[turn]], 2 + turn, taker))
+    for copy in seconds:
+        copy.wait()
+    for copy in firsts + copies:
+        copy.wait_send()
+
+
+def turn_round(mixed, down, middle, upstream, valid, gain):
+    tok_count, width = middle.shape
+    dma = pltpu.SemaphoreType.DMA
+    vmem = pl.BlockSpec(memory_space=pltpu.VMEM)
+    flops = 2 * mixed.shape[0] * mixed.shape[1] * width
+    return pl.pallas_call(
+        turn_kernel,
+        name="turn_round",
+        out_shape=(
+            jax.ShapeDtypeStruct((tok_count, width), BF16),
+            jax.ShapeDtypeStruct((4, tok_count, width), BF16),
+            jax.ShapeDtypeStruct((1, width), F32),
+        ),
+        in_specs=[vmem] * 6,
+        out_specs=[vmem] * 3,
+        scratch_shapes=[
+            pltpu.VMEM((3, tok_count, width), BF16),
+            pltpu.VMEM((3, tok_count, width), BF16),
+            dma((3,)),
+            dma((3,)),
+            dma((4,)),
+            dma((4,)),
+        ],
+        cost_estimate=pl.CostEstimate(flops=flops, bytes_accessed=8 << 20, transcendentals=0),
+        compiler_params=pltpu.CompilerParams(collective_id=3, has_side_effects=True),
+    )(mixed, down, middle, upstream, valid, gain)
+
+
+def product_kernel(left_ref, right_ref, out_ref):
+    out_ref[...] = jnp.dot(left_ref[...], right_ref[...], preferred_element_type=F32).astype(BF16)
+
+
+def product_low(tile, left, right):
+    rows, depth = left.shape
+    columns = right.shape[1]
+    return pl.pallas_call(
+        product_kernel,
+        grid=(columns // tile,),
+        out_shape=jax.ShapeDtypeStruct((rows, columns), BF16),
+        in_specs=[
+            pl.BlockSpec((rows, depth), lambda i: (0, 0)),
+            pl.BlockSpec((depth, tile), lambda i: (0, i)),
+        ],
+        out_specs=pl.BlockSpec((rows, tile), lambda i: (0, i)),
+        cost_estimate=pl.CostEstimate(
+            flops=2 * rows * depth * columns, bytes_accessed=8 << 20, transcendentals=0
+        ),
+    )(left, right)
+
+
+def mix_kernel(tokens_ref, w_gate_ref, w_up_ref, gate_ref, up_ref, mixed_ref, turned_ref):
+    gate = project(tokens_ref[...], w_gate_ref[...])
+    up = project(tokens_ref[...], w_up_ref[...])
+    gate_ref[...] = gate
+    up_ref[...] = up
+    mixed = gated_gelu(gate, up)
+    mixed_ref[...] = mixed.astype(BF16)
+    turned_ref[...] = mixed.T.astype(BF16)
+
+
+def hidden_mix(tile, tokens, both_weights):
+    count, width = tokens.shape
+    hidden = both_weights.shape[1] // 2
+    steps = hidden // tile
+    wide = jax.ShapeDtypeStruct((count, hidden), F32)
+    column = pl.BlockSpec((count, tile), lambda i: (0, i))
+    return pl.pallas_call(
+        mix_kernel,
+        name="hidden_mix",
+        grid=(steps,),
+        out_shape=(
+            wide,
+            wide,
+            jax.ShapeDtypeStruct((count, hidden), BF16),
+            jax.ShapeDtypeStruct((hidden, count), BF16),
+        ),
+        in_specs=[
+            pl.BlockSpec((count, width), lambda i: (0, 0)),
+            pl.BlockSpec((width, tile), lambda i: (0, i)),
+            pl.BlockSpec((width, tile), lambda i: (0, i + steps)),
+        ],
+        out_specs=[column, column, column, pl.BlockSpec((tile, count), lambda i: (i, 0))],
+        cost_estimate=pl.CostEstimate(
+            flops=4 * count * hidden * width, bytes_accessed=24 << 20, transcendentals=0
+        ),
+    )(tokens, both_weights, both_weights)
+
+
+def back_kernel(
+    upstream_ref, down_ref, gate_ref, up_ref, w_gate_ref, w_up_ref, gate_out, up_out, back_ref, total
+):
+    step = pl.program_id(0)
+    grad_mixed = project_back(upstream_ref[...], down_ref[...])
+    _, pull_gelu = jax.vjp(gated_gelu, gate_ref[...], up_ref[...])
+    grad_gate, grad_up = pull_gelu(grad_mixed)
+    grad_gate, grad_up = grad_gate.astype(BF16), grad_up.astype(BF16)
+    gate_out[...] = grad_gate
+    up_out[...] = grad_up
+    part = project_back(grad_gate, w_gate_ref[...]) + project_back(grad_up, w_up_ref[...])
+
+    @pl.when(step == 0)
+    def _():
+        total[...] = part
+
+    @pl.when(step > 0)
+    def _():
+        total[...] += part
+
+    @pl.when(step == pl.num_programs(0) - 1)
+    def _():
+        back_ref[...] = total[...].astype(BF16)
+
+
+def hidden_back(tile, upstream, down, gate_pre, up_pre, both_weights):
+    tokens, width = upstream.shape
+    hidden = down.shape[0]
+    count = hidden // tile
+    low = jax.ShapeDtypeStruct((tokens, hidden), BF16)
+    return pl.pallas_call(
+        back_kernel,
+        name="hidden_back",
+        grid=(count,),
+        out_shape=(low, low, jax.ShapeDtypeStruct((tokens, width), BF16)),
+        in_specs=[
+            pl.BlockSpec((tokens, width), lambda i: (0, 0)),
+            pl.BlockSpec((tile, width), lambda i: (i, 0)),
+            pl.BlockSpec((tokens, tile), lambda i: (0, i)),
+            pl.BlockSpec((tokens, tile), lambda i: (0, i)),
+            pl.BlockSpec((width, tile), lambda i: (0, i)),
+            pl.BlockSpec((width, tile), lambda i: (0, i + count)),
+        ],
+        out_specs=[
+            pl.BlockSpec((tokens, tile), lambda i: (0, i)),
+            pl.BlockSpec((tokens, tile), lambda i: (0, i)),
+            pl.BlockSpec((tokens, width), lambda i: (0, 0)),
+        ],
+        scratch_shapes=[pltpu.VMEM((tokens, width), F32)],
+        cost_estimate=pl.CostEstimate(
+            flops=6 * tokens * hidden * width, bytes_accessed=24 << 20, transcendentals=0
+        ),
+    )(upstream, down, gate_pre, up_pre, both_weights, both_weights)
+
+
 def halo_kernel(size, depth, direction, source_ref, result_ref, send_sem, recv_sem):
     me = lax.axis_index("ctx")
     barrier = pltpu.get_barrier_semaphore()
@@ -260,7 +494,7 @@
 
 
 def row_block(rows):
-    return 48 if rows % 48 == 0 else rows
+    return 16 if rows % 16 == 0 else rows
 
 
 def pick_columns(n_batch, n_ctx, piece, padded, w_gate, w_up):
@@ -572,45 +806,35 @@
 
     (ffn_in_all,) = square_gather(2, ffn_in)
     ffn_in_all = ffn_in_all.reshape(all_tok, model_width)
-    both_pre = project(ffn_in_all, part_both)
-    gate_pre, up_pre = both_pre[:, :hidden_part], both_pre[:, hidden_part:]
-    mixed_low = gated_gelu(gate_pre, up_pre).astype(BF16)
+    gate_pre, up_pre, mixed_low, mixed_turned = hidden_mix(256, ffn_in_all, part_both)
     mixed_low, act_in_late, attn_late = lax.optimization_barrier((mixed_low, act_in, attn_low))
     act_in_all, attn_all = square_gather(13, act_in_late, attn_late)
-    mixed_low, act_in_all, attn_all = lax.optimization_barrier((mixed_low, act_in_all, attn_all))
+    ffn_in_turned = ffn_in_all.T
+    mixed_low, act_in_all, attn_all, mixed_turned, ffn_in_turned = lax.optimization_barrier(
+        (mixed_low, act_in_all, attn_all, mixed_turned, ffn_in_turned)
+    )
     act_in_all = act_in_all.reshape(all_tok, model_width)
     attn_all = attn_all.reshape(all_tok, query_width)
-    proj_part = project(mixed_low, part_down).astype(BF16)
-    (proj_parts,) = batch_exchange(
-        3, n_batch, slots=(proj_part.reshape(n_batch, tok_count, model_width),)
-    )
-    ffn_proj = jnp.sum(proj_parts.astype(F32), axis=0)
-    final_sum = middle + normed(ffn_proj, full_gain_final)
-    block_out = (final_sum * valid_mask).astype(BF16)
+    block_out, grad_ffn_low, grad_gain_final = turn_round(
+        mixed_low, part_down, middle, cotangent, valid_mask, full_gain_final
+    )
 
     grad_final = cotangent.astype(F32) * valid_mask
-    _, pull_final = jax.vjp(normed, ffn_proj, full_gain_final)
-    grad_ffn_proj, grad_gain_final = pull_final(grad_final)
-    (grad_ffn_low,) = square_gather(4, grad_ffn_proj.astype(BF16))
     grad_ffn_low = grad_ffn_low.reshape(all_tok, model_width)
-    down_grad = weight_grad(mixed_low, grad_ffn_low).astype(BF16)
+    down_grad = product_low(384, mixed_turned, grad_ffn_low)
     down_grad, grad_ffn_low = lax.optimization_barrier((down_grad, grad_ffn_low))
     grad_w_down = scattered(down_grad)
-    grad_mixed = project_back(grad_ffn_low, part_down)
-    _, pull_gelu = jax.vjp(gated_gelu, gate_pre, up_pre)
-    grad_gate, grad_up = pull_gelu(grad_mixed)
-    grad_gate_low = grad_gate.astype(BF16)
-    grad_up_low = grad_up.astype(BF16)
-    grad_both_low = jnp.concatenate([grad_gate_low, grad_up_low], axis=1)
-    back_part = project_back(grad_both_low, part_both).astype(BF16)
+    grad_gate_low, grad_up_low, back_part = hidden_back(
+        256, grad_ffn_low, part_down, gate_pre, up_pre, part_both
+    )
     (back_parts,) = batch_exchange(
         5, n_batch, slots=(back_part.reshape(n_batch, tok_count, model_width),)
     )
     back_parts, grad_gate_low, grad_up_low = lax.optimization_barrier(
         (back_parts, grad_gate_low, grad_up_low)
     )
-    gate_grad = weight_grad(ffn_in_all, grad_gate_low).astype(BF16)
-    up_grad = weight_grad(ffn_in_all, grad_up_low).astype(BF16)
+    gate_grad = product_low(256, ffn_in_turned, grad_gate_low)
+    up_grad = product_low(256, ffn_in_turned, grad_up_low)
     back_parts, gate_grad, up_grad = lax.optimization_barrier((back_parts, gate_grad, up_grad))
     grad_w_gate = scattered(gate_grad)
     grad_w_up = scattered(up_grad)

time: 562 us -> 563 us (level)
  Pallas kernels: 285 us -> 351 us
  matrix products: 75.7 us -> 19.4 us
  waiting for transfers between devices: 129 us -> 120 us
  local copies, waits for them, and re-layouts: 23.5 us -> 29.6 us
    pallas_call x0 -> x6, Pallas kernels: none -> 91 us  [the longest x1 36.5 us: turn_round(): pl.pallas_call(turn_kernel, name='turn_round', out_shape=(jax.ShapeDtypeS...]
    dot_general x7 -> x5, matrix products: 25.1 us -> 3.86 us  [project_back(): lax.dot_general(upstream, weight, (((1,), (1,)), ((), ())), preferred_ele...]
    dot_general x5 -> x2, matrix products: 22.6 us -> 3.97 us  [weight_grad(): lax.dot_general(inputs, upstream, (((0,), (0,)), ((), ())), preferred_ele...]
    pallas_call x3 -> x2, Pallas kernels: 49.2 us -> 30.8 us  [batch_exchange(): pl.pallas_call(functools.partial(batch_kernel, size, kinds), out_shape=sh...]
    dot_general x7 -> x5, matrix products: 20.3 us -> 3.87 us  [project(): lax.dot_general(inputs, weight, (((1,), (0,)), ((), ())), preferred_eleme...]
    pallas_call x6 -> x5, Pallas kernels: 127 us -> 111 us  [square_gather(): pl.pallas_call(functools.partial(square_kernel, count), out_shape=[jax.Sh...]
    reduce_scatter x4, waiting for transfers between devices: 121 us -> 114 us  [scattered(): return lax.psum_scatter(whole, 'ctx', scatter_dimension=0, tiled=True)]
  transfers between devices with their start and end apart: 6 -> 6, of which waited for: 5 -> 5; matrix products, arithmetic and copies ran while one was open for 7% -> 6% of each run, Pallas kernels for 31% -> 33%
where the time goes in v5:
time: 563 us; the launch traced here: 560 us
  Pallas kernels  351 us (62%)
  waiting for transfers between devices  120 us (21%)
  local copies, waits for them, and re-layouts  29.6 us (5%)
  other arithmetic  23.2 us (4%)
  matrix products  19.4 us (3%)
  between operations  15.9 us (3%)
    reduce_scatter x4, waiting for transfers between devices, scattered(): return lax.psum_scatter(whole, 'ctx', scatter_dimension=0, tiled=True)  114 us
    pallas_call x5, Pallas kernels, square_gather(): pl.pallas_call(functools.partial(square_kernel, count), out_shape=[jax.Sh...  111 us
    pallas_call x2, Pallas kernels, halo_exchange(): pl.pallas_call(functools.partial(halo_kernel, size, depth, direction), ou...  49.2 us
    pallas_call x1, Pallas kernels, gather_weights(): pl.pallas_call(functools.partial(weights_kernel, n_batch, n_ctx), name='g...  48.5 us
    pallas_call x1, Pallas kernels, turn_round(): pl.pallas_call(turn_kernel, name='turn_round', out_shape=(jax.ShapeDtypeS...  36.5 us
    pallas_call x2, Pallas kernels, batch_exchange(): pl.pallas_call(functools.partial(batch_kernel, size, kinds), out_shape=sh...  30.8 us
    pallas_call x3, Pallas kernels, product_low(): pl.pallas_call(product_kernel, grid=(columns // tile,), out_shape=jax.Sha...  21.5 us
    pallas_call x1, Pallas kernels, hidden_back(): pl.pallas_call(back_kernel, name='hidden_back', grid=(count,), out_shape=...  21 us
  transfers between devices with their start and end apart: 6, of which 5 were waited for; matrix products, arithmetic and copies ran while one was open for 6% of the time, Pallas kernels for 33%

profile of v5, /device:TPU:0, one launch (start us, length us, event | category | flops | bytes accessed | tf_op | source)
XLA Modules:
  0.0 559.7 jit_solution(10237223663326576893)
XLA Ops:
  7.2 6.6 %pick_columns.1 = bf16[144,3584]{1,0:T(8,128)(2,1)} custom-call(bf16[144,6912]{1,0:T(8,128)(2,1)} %gate_ref.1, bf16[144,6912]{1,0:T(8,128)(2,1)} %up_ref.1), custom_call_target="tpu_custom_call" | custom-call | tf_op jit(solution)/shard_map/pick_columns/pallas_call | solution.py:504
  16.5 48.5 %gather_weights.1 = (bf16[4,8,144,384]{3,2,1,0:T(8,128)(2,1)}, bf16[8,4,32,1152]{3,2,1,0:T(8,128)(2,1)}, bf16[8,1,640]{2,1,0:T(2,128)(2,1)}) custom-call(bf16[4,144,384]{2,1,0:T(8,128)(2,1)} %bitcast.215, bf16[4,32,1152]{2,1,0:T(8,128)(2,1)} %bitcast.230, bf16[1,640]{1,0:T(2,128)(2,1)} %broadcast_in_dim.32.gain_ref), custom_call_target="tpu_custom_call" | custom-call | tf_op jit(solution)/shard_map/gather_weights/pallas_call | solution.py:661
  66.1 2.3 fusion.91
  73.5 28.9 %shard_map.280 = bf16[4,128,512]{2,1,0:T(8,128)(2,1)} custom-call(bf16[128,512]{1,0:T(8,128)(2,1)} %pad_maximum_fusion.9.source_ref), custom_call_target="tpu_custom_call" | custom-call | tf_op jit(solution)/shard_map/pallas_call | solution.py:472
  107.5 2.3 multiply_reduce_fusion.6
  111.8 14.3 %shard_map.281 = bf16[4,128,1152]{2,1,0:T(8,128)(2,1)} custom-call(bf16[128,1152]{1,0:T(8,128)(2,1)} %multiply_convert_fusion.1.refs_0_), custom_call_target="tpu_custom_call" | custom-call | tf_op jit(solution)/shard_map/pallas_call | solution.py:171
  126.1 2.4 copy.203
  131.1 11.9 %hidden_mix.1 = (f32[512,1792]{1,0:T(8,128)}, f32[512,1792]{1,0:T(8,128)}, bf16[512,1792]{1,0:T(8,128)(2,1)}, bf16[1792,512]{1,0:T(8,128)(2,1)}) custom-call(bf16[512,1152]{1,0:T(8,128)(2,1)} %bitcast.193, bf16[1152,3584]{1,0:T(8,128)(2,1)} %all-gather.3.cloned.1.call-done.w_gate_ref.w_up_ref, bf16[1152,3584]{1,0:T(8,128)(2,1)} %all-gather.3.cloned.1.call-done.w_gate_ref.w_up_ref), custom_call_target="tpu_custom_call" | custom-call | flops 4227858432 | bytes 25165824 | tf_op jit(solution)/shard_map/hidden_mix/pallas_call | solution.py:342
  143.0 23.6 %shard_map.282 = (bf16[4,128,1152]{2,1,0:T(8,128)(2,1)}, bf16[4,128,1024]{2,1,0:T(8,128)(2,1)}) custom-call(bf16[128,1152]{1,0:T(8,128)(2,1)} %get-tuple-element.56.refs_0_, bf16[128,1024]{1,0:T(8,128)(2,1)} %copy.202.refs_1_), custom_call_target="tpu_custom_call" | custom-call | tf_op jit(solution)/shard_map/pallas_call | solution.py:171
  166.6 4.4 all-gather.5.cloned.1.call-done.down_ref
  171.0 36.5 %turn_round.1 = (bf16[128,1152]{1,0:T(8,128)(2,1)}, bf16[4,128,1152]{2,1,0:T(8,128)(2,1)}, f32[1,1152]{1,0:T(1,128)}) custom-call(bf16[512,1792]{1,0:T(8,128)(2,1)} %get-tuple-element.61.mixed_ref, bf16[1792,1152]{1,0:T(8,128)(2,1)} %all-gather.5.cloned.1.call-done.down_ref, f32[128,1152]{1,0:T(8,128)} %copy-done.3, bf16[128,1152]{1,0:T(8,128)(2,1)} %bitcast.229, ...), custom_call_target="tpu_custom_call" | custom-call | flops 2113929216 | bytes 8388608 | tf_op jit(solution)/shard_map/turn_round/pallas_call | solution.py:281
  207.6 6.3 %shard_map.283 = bf16[1792,1152]{1,0:T(8,128)(2,1)} custom-call(bf16[1792,512]{1,0:T(8,128)(2,1)} %get-tuple-element.63.left_ref, bf16[512,1152]{1,0:T(8,128)(2,1)} %bitcast.220), custom_call_target="tpu_custom_call" | custom-call | flops 2113929216 | bytes 8388608 | tf_op jit(solution)/shard_map/pallas_call | solution.py:311
  213.9 21.0 %hidden_back.1 = (bf16[512,1792]{1,0:T(8,128)(2,1)}, bf16[512,1792]{1,0:T(8,128)(2,1)}, bf16[512,1152]{1,0:T(8,128)(2,1)}) custom-call(bf16[512,1152]{1,0:T(8,128)(2,1)} %bitcast.221, bf16[1792,1152]{1,0:T(8,128)(2,1)} %all-gather.5.cloned.1.call-done.down_ref, f32[512,1792]{1,0:T(8,128)} %get-tuple-element.66.gate_ref, ...), custom_call_target="tpu_custom_call" | custom-call | flops 6341787648 | bytes 25165824 | tf_op jit(solution)/shard_map/hidden_back/pallas_call | solution.py:394
  234.9 16.7 %shard_map.284 = bf16[4,128,1152]{2,1,0:T(8,128)(2,1)} custom-call(bf16[4,128,1152]{2,1,0:T(8,128)(2,1)} %bitcast.224), custom_call_target="tpu_custom_call" | custom-call | tf_op jit(solution)/shard_map/pallas_call | solution.py:101
  251.6 7.6 %shard_map.286 = bf16[1152,1792]{1,0:T(8,128)(2,1)} custom-call(bf16[1152,512]{1,0:T(8,128)(2,1)} %bitcast.222, bf16[512,1792]{1,0:T(8,128)(2,1)} %get-tuple-element.74.right_ref), custom_call_target="tpu_custom_call" | custom-call | flops 2113929216 | bytes 8388608 | tf_op jit(solution)/shard_map/pallas_call | solution.py:311
  259.2 7.6 %shard_map.285 = bf16[1152,1792]{1,0:T(8,128)(2,1)} custom-call(bf16[1152,512]{1,0:T(8,128)(2,1)} %bitcast.223, bf16[512,1792]{1,0:T(8,128)(2,1)} %get-tuple-element.73.right_ref), custom_call_target="tpu_custom_call" | custom-call | flops 2113929216 | bytes 8388608 | tf_op jit(solution)/shard_map/pallas_call | solution.py:311
  271.9 2.7 convolution_bitcast_fusion.3
  274.5 1.8 multiply_reduce_fusion
  279.2 20.3 %shard_map.287 = bf16[4,128,512]{2,1,0:T(8,128)(2,1)} custom-call(bf16[4,128,512]{2,1,0:T(8,128)(2,1)} %bitcast.213), custom_call_target="tpu_custom_call" | custom-call | tf_op jit(solution)/shard_map/pallas_call | solution.py:472
  316.0 14.1 %shard_map.288 = (f32[4,8,640]{2,1,0:T(8,128)}, bf16[4,128,384]{2,1,0:T(8,128)(2,1)}, bf16[4,128,288]{2,1,0:T(8,128)(2,1)}) custom-call(f32[8,640]{1,0:T(8,128)} %concatenate.54.refs_0_, bf16[4,128,384]{2,1,0:T(8,128)(2,1)} %bitcast.217, bf16[4,128,288]{2,1,0:T(8,128)(2,1)} %bitcast.219), custom_call_target="tpu_custom_call" | custom-call | tf_op jit(solution)/shard_map/pallas_call | solution.py:101
  330.1 1.9 fusion.11
  332.5 2.1 fusion.3
  334.6 1.8 fusion.6
  339.6 35.6 %reduce-scatter.5.cloned.1.call-done.refs_0_ = bf16[288,384]{1,0:T(8,128)(2,1)} async-done(((bf16[2304,384]{1,0:T(8,128)(2,1)}), bf16[288,384]{1,0:T(8,128)(2,1)}) %reduce-scatter.5.cloned.1.call-update) | async-done | bytes 221200 | tf_op jit(solution)/shard_map/reduce_scatter | solution.py:689
  375.2 13.8 %shard_map.289 = bf16[4,288,384]{2,1,0:T(8,128)(2,1)} custom-call(bf16[288,384]{1,0:T(8,128)(2,1)} %reduce-scatter.5.cloned.1.call-done.refs_0_), custom_call_target="tpu_custom_call" | custom-call | tf_op jit(solution)/shard_map/pallas_call | solution.py:171
  396.1 28.4 %reduce-scatter.9.cloned.1.call-done.refs_1_ = bf16[144,1792]{1,0:T(8,128)(2,1)} async-done(((bf16[1152,1792]{1,0:T(8,128)(2,1)}), bf16[144,1792]{1,0:T(8,128)(2,1)}) %reduce-scatter.9.cloned.1.call-update) | async-done | bytes 516112 | tf_op jit(solution)/shard_map/reduce_scatter | solution.py:689
  424.5 50.0 %reduce-scatter.7.cloned.1.call-done.refs_0_ = bf16[224,1152]{1,0:T(8,128)(2,1)} async-done(((bf16[1792,1152]{1,0:T(8,128)(2,1)}), bf16[224,1152]{1,0:T(8,128)(2,1)}) %reduce-scatter.7.cloned.1.call-update) | async-done | bytes 516112 | tf_op jit(solution)/shard_map/reduce_scatter | solution.py:689
  474.4 38.6 %shard_map.290 = (bf16[4,224,1152]{2,1,0:T(8,128)(2,1)}, bf16[4,144,1792]{2,1,0:T(8,128)(2,1)}) custom-call(bf16[224,1152]{1,0:T(8,128)(2,1)} %reduce-scatter.7.cloned.1.call-done.refs_0_, bf16[144,1792]{1,0:T(8,128)(2,1)} %reduce-scatter.9.cloned.1.call-done.refs_1_), custom_call_target="tpu_custom_call" | custom-call | tf_op jit(solution)/shard_map/pallas_call | solution.py:171
  514.8 7.1 %shard_map.291 = f32[144,6912]{1,0:T(8,128)} custom-call(bf16[4,144,1792]{2,1,0:T(8,128)(2,1)} %get-tuple-element.84.parts_ref), custom_call_target="tpu_custom_call" | custom-call | tf_op jit(solution)/shard_map/pallas_call | solution.py:526
  521.9 2.3 bitcast_convert_fusion
  524.4 20.5 %shard_map.292.parts_ref = bf16[4,144,1792]{2,1,0:T(8,128)(2,1)} custom-call(bf16[144,1792]{1,0:T(8,128)(2,1)} %reduce-scatter.11.cloned.1.call-done.refs_0_), custom_call_target="tpu_custom_call" | custom-call | tf_op jit(solution)/shard_map/pallas_call | solution.py:171
  544.9 7.2 %shard_map.293 = f32[144,6912]{1,0:T(8,128)} custom-call(bf16[4,144,1792]{2,1,0:T(8,128)(2,1)} %shard_map.292.parts_ref), custom_call_target="tpu_custom_call" | custom-call | tf_op jit(solution)/shard_map/pallas_call | solution.py:526
  (249 shorter events, 54.7 us)
Async XLA Ops:
  7.2 6.8 %copy-start = (bf16[864,1152]{1,0:T(8,128)(2,1)S(1)}, bf16[864,1152]{1,0:T(8,128)(2,1)}, u32[]{:S(2)}) copy-start(bf16[864,1152]{1,0:T(8,128)(2,1)} %param.32) | copy-start | bytes 5971972
  7.2 123.9 %all-gather.3.cloned.1.call-start = ((), (), s32[]{:S(2)}) async-start(), calls=%async_computation.4 | async-start | bytes 9289728 | tf_op jit(solution)/shard_map/all_gather | solution.py:685
  13.9 157.2 %all-gather.5.cloned.1.call-start = ((), (), s32[]{:S(2)}) async-start(), calls=%async_computation.5 | async-start | bytes 4644864 | tf_op jit(solution)/shard_map/all_gather | solution.py:685
  14.9 51.0 %copy-start.2 = (bf16[1,128,1152]{2,1,0:T(8,128)(2,1)S(1)}, bf16[1,128,1152]{2,1,0:T(8,128)(2,1)}, u32[]{:S(2)}) copy-start(bf16[1,128,1152]{2,1,0:T(8,128)(2,1)} %param.17) | copy-start | bytes 884740
  14.9 360.3 %reduce-scatter.5.cloned.1.call-start = ((), (), s32[]{:S(2)}) async-start(), calls=%async_computation.6 | async-start | bytes 1990656 | tf_op jit(solution)/shard_map/reduce_scatter | solution.py:689
  66.0 2.4 copy-start.50
  71.0 32.6 %copy-start.39 = (f32[128,4]{0,1:T(4,128)}, f32[128,4]{0,1:T(4,128)S(1)}, u32[]{:S(2)}) copy-start(f32[128,4]{0,1:T(4,128)S(1)} %copy.156) | copy-start | bytes 6148
  71.2 32.6 %copy-start.43 = (f32[256]{0:T(256)}, f32[256]{0:T(256)S(1)}, u32[]{:S(2)}) copy-start(f32[256]{0:T(256)S(1)} %mul.493) | copy-start | bytes 3076
  71.9 30.5 %copy-start.45 = (f32[128]{0:T(128)}, f32[128]{0:T(128)S(1)}, u32[]{:S(2)}) copy-start(f32[128]{0:T(128)S(1)} %fusion.69) | copy-start | bytes 1540
  72.8 31.2 %copy-start.21 = (f32[128,128]{1,0:T(8,128)}, f32[128,128]{1,0:T(8,128)S(1)}, u32[]{:S(2)}) copy-start(f32[128,128]{1,0:T(8,128)S(1)} %get-tuple-element.190) | copy-start | bytes 196612
  103.7 2.0 copy-start.16
  103.8 1.9 copy-start.36
  104.1 167.7 %copy-start.29 = (bf16[128,4,128]{2,0,1:T(8,128)(2,1)}, bf16[128,4,128]{2,0,1:T(8,128)(2,1)S(1)}, u32[]{:S(2)}) copy-start(bf16[128,4,128]{2,0,1:T(8,128)(2,1)S(1)} %get-tuple-element.171) | copy-start | bytes 393220
  110.9 17.6 %copy-start.3 = (f32[128,1152]{1,0:T(8,128)}, f32[128,1152]{1,0:T(8,128)S(1)}, u32[]{:S(2)}) copy-start(f32[128,1152]{1,0:T(8,128)S(1)} %get-tuple-element.159.middle_ref) | copy-start | bytes 1769476
  268.6 2.2 copy-start.5
  300.6 2.0 copy-start.18
  301.7 2.4 copy-start.42
  301.7 2.4 copy-start.46
  302.7 2.9 copy-start.28
  302.7 2.9 copy-start.53
  302.7 4.7 copy-start.26
  303.1 5.0 copy-start.22
  303.2 5.0 copy-start.44
  309.8 2.5 copy-start.7
  330.1 2.3 copy-start.35
  330.1 2.3 copy-start.61
  332.5 2.1 copy-start.48
  336.4 88.0 %reduce-scatter.9.cloned.1.call-start = ((), (), s32[]{:S(2)}) async-start(), calls=%async_computation.8 | async-start | bytes 4644864 | tf_op jit(solution)/shard_map/reduce_scatter | solution.py:689
  337.0 137.4 %reduce-scatter.7.cloned.1.call-start = ((), (), s32[]{:S(2)}) async-start(), calls=%async_computation.7 | async-start | bytes 4644864 | tf_op jit(solution)/shard_map/reduce_scatter | solution.py:689
  337.6 186.8 %reduce-scatter.11.cloned.1.call-start = ((), (), s32[]{:S(2)}) async-start(), calls=%async_computation.9 | async-start | bytes 4644864 | tf_op jit(solution)/shard_map/reduce_scatter | solution.py:689
  544.9 7.2 %copy-start.33 = (bf16[128,1152]{1,0:T(8,128)(2,1)S(1)}, bf16[128,1152]{1,0:T(8,128)(2,1)}, u32[]{:S(2)}) copy-start(bf16[128,1152]{1,0:T(8,128)(2,1)} %get-tuple-element.62) | copy-start | bytes 884740
  544.9 7.9 %copy-start.1 = (bf16[864,1152]{1,0:T(8,128)(2,1)S(1)}, bf16[864,1152]{1,0:T(8,128)(2,1)}, u32[]{:S(2)}) copy-start(bf16[864,1152]{1,0:T(8,128)(2,1)} %param.32) | copy-start | bytes 5971972
  (36 other events, 39.6 us)
Sparse Core Ops, SparseCore 0:
  14.0 97.3 all-gather.2
  113.6 57.4 all-gather.4
  336.5 38.6 reduce-scatter.4
  377.4 47.0 reduce-scatter.8
  426.6 47.7 reduce-scatter.6
  476.6 47.7 reduce-scatter.10

commit v6 on v5

--- a/solution.py
+++ b/solution.py
@@ -494,7 +494,7 @@
 
 
 def row_block(rows):
-    return 16 if rows % 16 == 0 else rows
+    return 48 if rows % 48 == 0 else rows
 
 
 def pick_columns(n_batch, n_ctx, piece, padded, w_gate, w_up):
@@ -681,6 +681,260 @@
     )(qkv, proj, gains)
 
 
+def tail_kernel(
+    n_ctx,
+    gate_ref,
+    down_ref,
+    up_ref,
+    attn_ref,
+    gate_all,
+    down_all,
+    up_all,
+    attn_all,
+    pair_up,
+    pair_attn,
+    way_up,
+    way_attn,
+    pair_send,
+    pair_recv,
+    way_send,
+    way_recv,
+    side_send,
+    side_recv,
+    own_sem,
+):
+    n_chip = n_ctx // 2
+    spot = lax.axis_index("batch")
+    me = lax.axis_index("ctx")
+    chip, core = me // 2, lax.rem(me, 2)
+    across = {"batch": spot + 1 - 2 * lax.rem(spot, 2)}
+    along = {"batch": lax.rem(spot + 2, 4)}
+    near = {"ctx": me + 1 - 2 * core}
+    beyond = ({"ctx": jnp.minimum(me + 2, n_ctx - 1)}, {"ctx": jnp.maximum(me - 2, 0)})
+    inner = (chip > 0, chip < n_chip - 1)
+    barrier = pltpu.get_barrier_semaphore()
+    for peer in (near, across, along):
+        pl.semaphore_signal(barrier, inc=1, device_id=peer, device_id_type=MESH)
+    for has_giver, giver in zip(inner, (beyond[1], beyond[0])):
+
+        @pl.when(has_giver)
+        def _():
+            pl.semaphore_signal(barrier, inc=1, device_id=giver, device_id_type=MESH)
+
+    pl.semaphore_wait(barrier, 3 + jnp.minimum(chip, 1) + jnp.minimum(n_chip - 1 - chip, 1))
+
+    def remote(source, target, send, recv, peer):
+        return pltpu.make_async_remote_copy(
+            src_ref=source,
+            dst_ref=target,
+            send_sem=send,
+            recv_sem=recv,
+            device_id=peer,
+            device_id_type=MESH,
+        )
+
+    width = up_ref.shape[-1]
+    cut = width // 256 * 128
+    chains = (
+        (up_ref, pair_up, way_up, up_all, pl.ds(0, cut)),
+        (up_ref, pair_up, way_up, up_all, pl.ds(cut, width - cut)),
+        (attn_ref, pair_attn, way_attn, attn_all, pl.ds(0, attn_ref.shape[-1])),
+    )
+    numbers = range(len(chains))
+
+    def pair_copy(number, place):
+        source, pair, _, _, columns = chains[number]
+        return remote(
+            source.at[2 * place + 1 - core, :, columns],
+            pair.at[place, :, columns],
+            pair_send.at[number, place],
+            pair_recv.at[number, place],
+            near,
+        )
+
+    def way_copy(number, direction, step, source):
+        _, _, way, _, columns = chains[number]
+        return remote(
+            source,
+            way.at[direction, step - 1, :, columns],
+            way_send.at[number, direction, step - 1],
+            way_recv.at[number, direction, step - 1],
+            beyond[direction],
+        )
+
+    def passes(direction, step):
+        return chip <= step - 1 if direction == 0 else chip >= n_chip - step
+
+    def bound_for(direction, step):
+        place = chip + n_chip - step if direction == 0 else chip - n_chip + step
+        return jnp.clip(place, 0, n_chip - 1)
+
+    def side_pair(item, sources, target, columns):
+        return [
+            remote(
+                sources,
+                target.at[spot, :, columns],
+                side_send.at[item, turn],
+                side_recv.at[item, turn],
+                peer,
+            )
+            for turn, peer in enumerate((across, along))
+        ]
+
+    def side_pass(item, firsts, target, start, length):
+        half = length // 256 * 128
+        halves = (pl.ds(start, half), pl.ds(start + half, length - half))
+        copies = []
+        for turn, (giver, taker) in enumerate(((across, along), (along, across))):
+            firsts[turn].wait_recv()
+            block = target.at[giver["batch"], :, halves[turn]]
+            copies.append(
+                remote(block, block, side_send.at[item, 2 + turn], side_recv.at[item, 2 + turn], taker)
+            )
+            copies[-1].start()
+        return copies
+
+    for number in numbers:
+        for place in range(n_chip):
+            pair_copy(number, place).start()
+    early = ((gate_ref, gate_all), (down_ref, down_all))
+    side_firsts = []
+    for item, (source, target) in enumerate(early):
+        side_firsts.append(side_pair(item, source, target, pl.ds(0, source.shape[-1])))
+        for copy in side_firsts[-1]:
+            copy.start()
+    own = [
+        pltpu.make_async_copy(source, target.at[spot], own_sem.at[item])
+        for item, (source, target) in enumerate(early)
+    ]
+    for copy in own:
+        copy.start()
+    for _, _, way, _, columns in chains:
+        for direction in range(2):
+
+            @pl.when(jnp.logical_not(inner[direction]))
+            def _():
+                way[direction, n_chip - 2, :, columns] = jnp.zeros(
+                    (way.shape[2], columns.size), way.dtype
+                )
+
+    for number in numbers:
+        source, pair, _, _, columns = chains[number]
+        for place in range(n_chip):
+            pair_copy(number, place).wait_recv()
+            pair[place, :, columns] = (
+                pair[place, :, columns].astype(F32)
+                + source[2 * place + core, :, columns].astype(F32)
+            ).astype(BF16)
+        for direction in range(2):
+
+            @pl.when(passes(direction, 1))
+            def _():
+                place = bound_for(direction, 1)
+                way_copy(number, direction, 1, pair.at[place, :, columns]).start()
+
+    side_seconds = []
+    for step in range(2, n_chip + 1):
+        if step <= 3:
+            item = step - 2
+            target = early[item][1]
+            side_seconds += side_pass(item, side_firsts[item], target, 0, target.shape[-1])
+        if step == n_chip:
+            break
+        for number in numbers:
+            _, pair, way, _, columns = chains[number]
+            for direction in range(2):
+                place = bound_for(direction, step)
+
+                @pl.when(passes(direction, step) & inner[direction])
+                def _():
+                    way_copy(number, direction, step - 1, pair.at[place, :, columns]).wait_recv()
+                    way[direction, step - 2, :, columns] = (
+                        way[direction, step - 2, :, columns].astype(F32)
+                        + pair[place, :, columns].astype(F32)
+                    ).astype(BF16)
+
+            for direction in range(2):
+                place = bound_for(direction, step)
+
+                @pl.when(passes(direction, step) & inner[direction])
+                def _():
+                    way_copy(number, direction, step, way.at[direction, step - 2, :, columns]).start()
+
+                @pl.when(passes(direction, step) & jnp.logical_not(inner[direction]))
+                def _():
+                    way_copy(number, direction, step, pair.at[place, :, columns]).start()
+
+    chain_firsts = []
+    for number in numbers:
+        _, pair, way, target, columns = chains[number]
+        for direction in range(2):
+
+            @pl.when(inner[direction])
+            def _():
+                way_copy(number, direction, n_chip - 1, pair.at[0, :, columns]).wait_recv()
+
+        target[spot, :, columns] = (
+            pair[chip, :, columns].astype(F32)
+            + way[0, n_chip - 2, :, columns].astype(F32)
+            + way[1, n_chip - 2, :, columns].astype(F32)
+        ).astype(BF16)
+        firsts = side_pair(2 + number, target.at[spot, :, columns], target, columns)
+        for copy in firsts:
+            copy.start()
+        chain_firsts.append(firsts)
+    for number in numbers:
+        _, _, _, target, columns = chains[number]
+        side_seconds += side_pass(
+            2 + number, chain_firsts[number], target, columns.start, columns.size
+        )
+    for copy in own:
+        copy.wait()
+    for copy in side_seconds:
+        copy.wait()
+    for firsts in side_firsts + chain_firsts:
+        for copy in firsts:
+            copy.wait_send()
+    for number in numbers:
+        _, pair, _, _, columns = chains[number]
+        for place in range(n_chip):
+            pair_copy(number, place).wait_send()
+        for direction in range(2):
+            for step in range(1, n_chip):
+
+                @pl.when(passes(direction, step))
+                def _():
+                    way_copy(number, direction, step, pair.at[0, :, columns]).wait_send()
+
+
+def tail_round(n_ctx, gate, down, up, attn):
+    n_chip = n_ctx // 2
+    dma = pltpu.SemaphoreType.DMA
+    vmem = pl.BlockSpec(memory_space=pltpu.VMEM)
+    shapes = (gate.shape, down.shape, up.shape[1:], attn.shape[1:])
+    return pl.pallas_call(
+        functools.partial(tail_kernel, n_ctx),
+        name="tail_round",
+        out_shape=[jax.ShapeDtypeStruct((4, *shape), BF16) for shape in shapes],
+        in_specs=[vmem] * 4,
+        out_specs=[vmem] * 4,
+        scratch_shapes=[
+            pltpu.VMEM((n_chip, *up.shape[1:]), BF16),
+            pltpu.VMEM((n_chip, *attn.shape[1:]), BF16),
+            pltpu.VMEM((2, n_chip - 1, *up.shape[1:]), BF16),
+            pltpu.VMEM((2, n_chip - 1, *attn.shape[1:]), BF16),
+            dma((3, n_chip)),
+            dma((3, n_chip)),
+            dma((3, 2, n_chip - 1)),
+            dma((3, 2, n_chip - 1)),
+            dma((5, 4)),
+            dma((5, 4)),
+            dma((2,)),
+        ],
+        compiler_params=pltpu.CompilerParams(collective_id=8, has_side_effects=True),
+    )(gate, down, up, attn)
+
+
 def gathered(shard):
     return lax.all_gather(shard, "ctx", axis=0, tiled=True)
 
@@ -837,7 +1091,6 @@
     up_grad = product_low(256, ffn_in_turned, grad_up_low)
     back_parts, gate_grad, up_grad = lax.optimization_barrier((back_parts, gate_grad, up_grad))
     grad_w_gate = scattered(gate_grad)
-    grad_w_up = scattered(up_grad)
     grad_ffn_in = jnp.sum(back_parts.astype(F32), axis=0)
     _, pull_ffn_norm = jax.vjp(normed, middle, full_gain_ffn)
     grad_middle_part, grad_gain_ffn = pull_ffn_norm(grad_ffn_in)
@@ -938,11 +1191,13 @@
         ],
         axis=1,
     )
-    attn_sum = scattered(packed.reshape(n_ctx * lines, quarter))
-
-    down_all, gate_all = square_gather(8, grad_w_down, grad_w_gate)
-    (up_all,) = square_gather(9, grad_w_up)
-    (attn_grads,) = square_gather(11, attn_sum)
+    gate_all, down_all, up_all, attn_grads = tail_round(
+        n_ctx,
+        grad_w_gate,
+        grad_w_down,
+        up_grad.reshape(n_ctx, width_shard, hidden_part),
+        packed,
+    )
     gain_mine = attn_grads[0, width_shard + proj_rows : used].reshape(-1).astype(F32)
 
     def columns_back(pieces):

time: 563 us -> 486 us (0.86)
  waiting for transfers between devices: 120 us -> 53 us
  Pallas kernels: 351 us -> 338 us
    pallas_call x5 -> x2, Pallas kernels: 111 us -> 37.8 us  [square_gather(): pl.pallas_call(functools.partial(square_kernel, count), out_shape=[jax.Sh...]
    pallas_call x0 -> x1, Pallas kernels: none -> 68.5 us  [tail_round(): pl.pallas_call(functools.partial(tail_kernel, n_ctx), name='tail_round',...]
    reduce_scatter x4 -> x2, waiting for transfers between devices: 114 us -> 48.1 us  [scattered(): return lax.psum_scatter(whole, 'ctx', scatter_dimension=0, tiled=True)]
  transfers between devices with their start and end apart: 6 -> 4, of which waited for: 5 -> 2; matrix products, arithmetic and copies ran while one was open for 6% -> 11% of each run, Pallas kernels for 33% -> 34%
where the time goes in v6:
time: 486 us; the launch traced here: 478 us
  Pallas kernels  338 us (70%)
  waiting for transfers between devices  53 us (11%)
  local copies, waits for them, and re-layouts  28.9 us (6%)
  matrix products  21.3 us (4%)
  other arithmetic  20.3 us (4%)
  between operations  15.6 us (3%)
    pallas_call x1, Pallas kernels, tail_round(): pl.pallas_call(functools.partial(tail_kernel, n_ctx), name='tail_round',...  68.5 us
    pallas_call x2, Pallas kernels, halo_exchange(): pl.pallas_call(functools.partial(halo_kernel, size, depth, direction), ou...  52.8 us
    pallas_call x1, Pallas kernels, gather_weights(): pl.pallas_call(functools.partial(weights_kernel, n_batch, n_ctx), name='g...  48.3 us
    reduce_scatter x2, waiting for transfers between devices, scattered(): return lax.psum_scatter(whole, 'ctx', scatter_dimension=0, tiled=True)  48.1 us
    pallas_call x2, Pallas kernels, square_gather(): pl.pallas_call(functools.partial(square_kernel, count), out_shape=[jax.Sh...  37.8 us
    pallas_call x1, Pallas kernels, turn_round(): pl.pallas_call(turn_kernel, name='turn_round', out_shape=(jax.ShapeDtypeS...  36.5 us
    pallas_call x2, Pallas kernels, batch_exchange(): pl.pallas_call(functools.partial(batch_kernel, size, kinds), out_shape=sh...  27.3 us
    pallas_call x3, Pallas kernels, product_low(): pl.pallas_call(product_kernel, grid=(columns // tile,), out_shape=jax.Sha...  21.6 us
  transfers between devices with their start and end apart: 4, of which 2 were waited for; matrix products, arithmetic and copies ran while one was open for 11% of the time, Pallas kernels for 34%

profile of v6, /device:TPU:0, one launch (start us, length us, event | category | flops | bytes accessed | tf_op | source)
XLA Modules:
  0.0 477.9 jit_solution(5938884345412660546)
XLA Ops:
  7.2 3.9 pick_columns.1
  13.9 48.3 %gather_weights.1 = (bf16[4,8,144,384]{3,2,1,0:T(8,128)(2,1)}, bf16[8,4,32,1152]{3,2,1,0:T(8,128)(2,1)}, bf16[8,1,640]{2,1,0:T(2,128)(2,1)}) custom-call(bf16[4,144,384]{2,1,0:T(8,128)(2,1)} %bitcast.215, bf16[4,32,1152]{2,1,0:T(8,128)(2,1)} %bitcast.230, bf16[1,640]{1,0:T(2,128)(2,1)} %broadcast_in_dim.32.gain_ref), custom_call_target="tpu_custom_call" | custom-call | tf_op jit(solution)/shard_map/gather_weights/pallas_call | solution.py:661
  63.3 2.3 fusion.91
  70.7 29.1 %shard_map.280 = bf16[4,128,512]{2,1,0:T(8,128)(2,1)} custom-call(bf16[128,512]{1,0:T(8,128)(2,1)} %pad_maximum_fusion.9.source_ref), custom_call_target="tpu_custom_call" | custom-call | tf_op jit(solution)/shard_map/pallas_call | solution.py:472
  101.6 1.6 fusion.97
  105.0 2.3 multiply_reduce_fusion.6
  109.3 14.2 %shard_map.281 = bf16[4,128,1152]{2,1,0:T(8,128)(2,1)} custom-call(bf16[128,1152]{1,0:T(8,128)(2,1)} %multiply_convert_fusion.1.refs_0_), custom_call_target="tpu_custom_call" | custom-call | tf_op jit(solution)/shard_map/pallas_call | solution.py:171
  123.5 2.4 copy.203
  127.9 11.9 %hidden_mix.1 = (f32[512,1792]{1,0:T(8,128)}, f32[512,1792]{1,0:T(8,128)}, bf16[512,1792]{1,0:T(8,128)(2,1)}, bf16[1792,512]{1,0:T(8,128)(2,1)}) custom-call(bf16[512,1152]{1,0:T(8,128)(2,1)} %bitcast.193, bf16[1152,3584]{1,0:T(8,128)(2,1)} %all-gather.3.cloned.1.call-done.w_gate_ref.w_up_ref, bf16[1152,3584]{1,0:T(8,128)(2,1)} %all-gather.3.cloned.1.call-done.w_gate_ref.w_up_ref), custom_call_target="tpu_custom_call" | custom-call | flops 4227858432 | bytes 25165824 | tf_op jit(solution)/shard_map/hidden_mix/pallas_call | solution.py:342
  139.8 23.6 %shard_map.282 = (bf16[4,128,1152]{2,1,0:T(8,128)(2,1)}, bf16[4,128,1024]{2,1,0:T(8,128)(2,1)}) custom-call(bf16[128,1152]{1,0:T(8,128)(2,1)} %get-tuple-element.58.refs_0_, bf16[128,1024]{1,0:T(8,128)(2,1)} %copy.202.refs_1_), custom_call_target="tpu_custom_call" | custom-call | tf_op jit(solution)/shard_map/pallas_call | solution.py:171
  163.4 4.9 %all-gather.5.cloned.1.call-done.down_ref = bf16[1792,1152]{1,0:T(8,128)(2,1)} async-done(((bf16[224,1152]{1,0:T(8,128)(2,1)}), bf16[1792,1152]{1,0:T(8,128)(2,1)}) %all-gather.5.cloned.1.call-update) | async-done | bytes 4128784 | tf_op jit(solution)/shard_map/all_gather | solution.py:939
  168.3 36.5 %turn_round.1 = (bf16[128,1152]{1,0:T(8,128)(2,1)}, bf16[4,128,1152]{2,1,0:T(8,128)(2,1)}, f32[1,1152]{1,0:T(1,128)}) custom-call(bf16[512,1792]{1,0:T(8,128)(2,1)} %get-tuple-element.63.mixed_ref, bf16[1792,1152]{1,0:T(8,128)(2,1)} %all-gather.5.cloned.1.call-done.down_ref, f32[128,1152]{1,0:T(8,128)} %copy-done.3, bf16[128,1152]{1,0:T(8,128)(2,1)} %bitcast.229, ...), custom_call_target="tpu_custom_call" | custom-call | flops 2113929216 | bytes 8388608 | tf_op jit(solution)/shard_map/turn_round/pallas_call | solution.py:281
  204.7 6.4 %shard_map.283 = bf16[1792,1152]{1,0:T(8,128)(2,1)} custom-call(bf16[1792,512]{1,0:T(8,128)(2,1)} %get-tuple-element.65.left_ref, bf16[512,1152]{1,0:T(8,128)(2,1)} %bitcast.220), custom_call_target="tpu_custom_call" | custom-call | flops 2113929216 | bytes 8388608 | tf_op jit(solution)/shard_map/pallas_call | solution.py:311
  211.1 21.0 %hidden_back.1 = (bf16[512,1792]{1,0:T(8,128)(2,1)}, bf16[512,1792]{1,0:T(8,128)(2,1)}, bf16[512,1152]{1,0:T(8,128)(2,1)}) custom-call(bf16[512,1152]{1,0:T(8,128)(2,1)} %bitcast.221, bf16[1792,1152]{1,0:T(8,128)(2,1)} %all-gather.5.cloned.1.call-done.down_ref, f32[512,1792]{1,0:T(8,128)} %get-tuple-element.68.gate_ref, ...), custom_call_target="tpu_custom_call" | custom-call | flops 6341787648 | bytes 25165824 | tf_op jit(solution)/shard_map/hidden_back/pallas_call | solution.py:394
  232.1 16.6 %shard_map.284 = bf16[4,128,1152]{2,1,0:T(8,128)(2,1)} custom-call(bf16[4,128,1152]{2,1,0:T(8,128)(2,1)} %bitcast.224), custom_call_target="tpu_custom_call" | custom-call | tf_op jit(solution)/shard_map/pallas_call | solution.py:101
  248.7 7.6 %shard_map.286 = bf16[1152,1792]{1,0:T(8,128)(2,1)} custom-call(bf16[1152,512]{1,0:T(8,128)(2,1)} %bitcast.222, bf16[512,1792]{1,0:T(8,128)(2,1)} %get-tuple-element.76.right_ref), custom_call_target="tpu_custom_call" | custom-call | flops 2113929216 | bytes 8388608 | tf_op jit(solution)/shard_map/pallas_call | solution.py:311
  256.4 7.6 %shard_map.285 = bf16[1152,1792]{1,0:T(8,128)(2,1)} custom-call(bf16[1152,512]{1,0:T(8,128)(2,1)} %bitcast.223, bf16[512,1792]{1,0:T(8,128)(2,1)} %get-tuple-element.75.right_ref), custom_call_target="tpu_custom_call" | custom-call | flops 2113929216 | bytes 8388608 | tf_op jit(solution)/shard_map/pallas_call | solution.py:311
  269.1 2.6 convolution_convert_fusion
  271.9 2.7 convolution_bitcast_fusion.3
  274.6 1.8 multiply_reduce_fusion
  279.3 23.7 %shard_map.287 = bf16[4,128,512]{2,1,0:T(8,128)(2,1)} custom-call(bf16[4,128,512]{2,1,0:T(8,128)(2,1)} %bitcast.213), custom_call_target="tpu_custom_call" | custom-call | tf_op jit(solution)/shard_map/pallas_call | solution.py:472
  309.8 1.6 fusion.50
  316.2 10.7 %shard_map.288 = (f32[4,8,640]{2,1,0:T(8,128)}, bf16[4,128,384]{2,1,0:T(8,128)(2,1)}, bf16[4,128,288]{2,1,0:T(8,128)(2,1)}) custom-call(f32[8,640]{1,0:T(8,128)} %concatenate.54.refs_0_, bf16[4,128,384]{2,1,0:T(8,128)(2,1)} %bitcast.217, bf16[4,128,288]{2,1,0:T(8,128)(2,1)} %bitcast.219), custom_call_target="tpu_custom_call" | custom-call | tf_op jit(solution)/shard_map/pallas_call | solution.py:101
  326.9 1.9 fusion.11
  329.2 2.1 fusion.3
  331.4 1.8 fusion.6.attn_ref
  334.1 48.1 %reduce-scatter.5.cloned.1.call-done.down_ref = bf16[224,1152]{1,0:T(8,128)(2,1)} async-done(((bf16[1792,1152]{1,0:T(8,128)(2,1)}), bf16[224,1152]{1,0:T(8,128)(2,1)}) %reduce-scatter.5.cloned.1.call-update) | async-done | bytes 516112 | tf_op jit(solution)/shard_map/reduce_scatter | solution.py:943
  382.2 68.5 %tail_round.1 = (bf16[4,144,1792]{2,1,0:T(8,128)(2,1)}, bf16[4,224,1152]{2,1,0:T(8,128)(2,1)}, bf16[4,144,1792]{2,1,0:T(8,128)(2,1)}, bf16[4,288,384]{2,1,0:T(8,128)(2,1)}) custom-call(bf16[144,1792]{1,0:T(8,128)(2,1)} %reduce-scatter.3.cloned.1.call-done.gate_ref, bf16[224,1152]{1,0:T(8,128)(2,1)} %reduce-scatter.5.cloned.1.call-done.down_ref, ...), custom_call_target="tpu_custom_call" | custom-call | tf_op jit(solution)/shard_map/tail_round/pallas_call | solution.py:915
  456.5 1.7 slice.172
  458.2 2.3 bitcast_convert_fusion
  460.5 4.3 shard_map.289
  464.8 4.5 shard_map.290
  (249 shorter events, 43.7 us)
Async XLA Ops:
  7.2 4.1 copy-start
  7.2 120.8 %all-gather.3.cloned.1.call-start = ((), (), s32[]{:S(2)}) async-start(), calls=%async_computation.2 | async-start | bytes 9289728 | tf_op jit(solution)/shard_map/all_gather | solution.py:939
  11.2 157.0 %all-gather.5.cloned.1.call-start = ((), (), s32[]{:S(2)}) async-start(), calls=%async_computation.3 | async-start | bytes 4644864 | tf_op jit(solution)/shard_map/all_gather | solution.py:939
  12.3 50.9 %copy-start.2 = (bf16[1,128,1152]{2,1,0:T(8,128)(2,1)S(1)}, bf16[1,128,1152]{2,1,0:T(8,128)(2,1)}, u32[]{:S(2)}) copy-start(bf16[1,128,1152]{2,1,0:T(8,128)(2,1)} %param.17) | copy-start | bytes 884740
  12.3 321.8 %reduce-scatter.3.cloned.1.call-start = ((), (), s32[]{:S(2)}) async-start(), calls=%async_computation.4 | async-start | bytes 4644864 | tf_op jit(solution)/shard_map/reduce_scatter | solution.py:943
  63.3 2.3 copy-start.54
  68.2 32.9 %copy-start.38 = (f32[128,4]{0,1:T(4,128)}, f32[128,4]{0,1:T(4,128)S(1)}, u32[]{:S(2)}) copy-start(f32[128,4]{0,1:T(4,128)S(1)} %copy.156) | copy-start | bytes 6148
  68.4 32.9 %copy-start.42 = (f32[256]{0:T(256)}, f32[256]{0:T(256)S(1)}, u32[]{:S(2)}) copy-start(f32[256]{0:T(256)S(1)} %mul.493) | copy-start | bytes 3076
  68.9 32.2 %copy-start.50 = (f32[128]{0:T(128)}, f32[128]{0:T(128)S(1)}, u32[]{:S(2)}) copy-start(f32[128]{0:T(128)S(1)} %multiply_power_fusion) | copy-start | bytes 1540
  69.6 30.3 %copy-start.44 = (f32[128]{0:T(128)}, f32[128]{0:T(128)S(1)}, u32[]{:S(2)}) copy-start(f32[128]{0:T(128)S(1)} %fusion.69) | copy-start | bytes 1540
  69.6 31.5 %copy-start.52 = (f32[128]{0:T(128)}, f32[128]{0:T(128)S(1)}, u32[]{:S(2)}) copy-start(f32[128]{0:T(128)S(1)} %bitcast_convert_fusion.1) | copy-start | bytes 1540
  70.0 31.4 %copy-start.18 = (f32[128,128]{1,0:T(8,128)}, f32[128,128]{1,0:T(8,128)S(1)}, u32[]{:S(2)}) copy-start(f32[128,128]{1,0:T(8,128)S(1)} %get-tuple-element.193) | copy-start | bytes 196612
  70.0 31.4 %copy-start.20 = (f32[128,128]{1,0:T(8,128)}, f32[128,128]{1,0:T(8,128)S(1)}, u32[]{:S(2)}) copy-start(f32[128,128]{1,0:T(8,128)S(1)} %get-tuple-element.194) | copy-start | bytes 196612
  101.1 2.1 copy-start.13
  108.4 17.6 %copy-start.3 = (f32[128,1152]{1,0:T(8,128)}, f32[128,1152]{1,0:T(8,128)S(1)}, u32[]{:S(2)}) copy-start(f32[128,1152]{1,0:T(8,128)S(1)} %get-tuple-element.163.middle_ref) | copy-start | bytes 1769476
  264.0 118.2 %reduce-scatter.5.cloned.1.call-start = ((), (), s32[]{:S(2)}) async-start(), calls=%async_computation.5 | async-start | bytes 4644864 | tf_op jit(solution)/shard_map/reduce_scatter | solution.py:943
  269.1 2.8 copy-start.14
  269.1 2.8 copy-start.26
  269.1 2.8 copy-start.28
  269.1 2.8 copy-start.49
  303.0 2.2 copy-start.51
  303.0 2.2 copy-start.53
  305.1 2.2 copy-start.15
  305.2 2.1 copy-start.23
  305.2 2.5 copy-start.19
  305.2 2.5 copy-start.21
  308.9 2.5 copy-start.8
  326.8 2.3 copy-start.34
  326.8 2.3 copy-start.55
  326.9 2.4 copy-start.65
  329.2 2.1 copy-start.47
  464.8 6.5 %copy-start.1 = (bf16[864,1152]{1,0:T(8,128)(2,1)S(1)}, bf16[864,1152]{1,0:T(8,128)(2,1)}, u32[]{:S(2)}) copy-start(bf16[864,1152]{1,0:T(8,128)(2,1)} %param.32) | copy-start | bytes 5971972
  (38 other events, 45.4 us)
Sparse Core Ops, SparseCore 0:
  11.3 97.3 all-gather.2
  110.9 57.2 all-gather.4
  264.1 63.9 reduce-scatter.2
  330.2 51.9 reduce-scatter.4

commit v7 on v6

--- a/solution.py
+++ b/solution.py
@@ -416,67 +416,219 @@
     )(upstream, down, gate_pre, up_pre, both_weights, both_weights)
 
 
-def halo_kernel(size, depth, direction, source_ref, result_ref, send_sem, recv_sem):
+def halo_out_kernel(n_chip, source_ref, result_ref, send_sem, recv_sem):
     me = lax.axis_index("ctx")
+    chip, core = me // 2, lax.rem(me, 2)
+    near = {"ctx": me + 1 - 2 * core}
+    after = {"ctx": jnp.minimum(me + 2, 2 * n_chip - 1)}
+    has_after = chip < n_chip - 1
     barrier = pltpu.get_barrier_semaphore()
-    for step in range(1, depth + 1):
-        giver = me - direction * step
-
-        @pl.when((giver >= 0) & (giver < size))
-        def _():
-            pl.semaphore_signal(barrier, inc=1, device_id={"ctx": giver}, device_id_type=MESH)
-
-    takers = jnp.minimum(depth, size - 1 - me) if direction > 0 else jnp.minimum(depth, me)
-
-    @pl.when(takers > 0)
-    def _():
-        pl.semaphore_wait(barrier, takers)
-
-    def copy(step):
-        slot = depth - step
-        source = source_ref if direction > 0 else source_ref.at[slot]
+    pl.semaphore_signal(barrier, inc=1, device_id=near, device_id_type=MESH)
+
+    @pl.when(chip > 0)
+    def _():
+        before = {"ctx": jnp.maximum(me - 2, 0)}
+        pl.semaphore_signal(barrier, inc=1, device_id=before, device_id_type=MESH)
+
+    pl.semaphore_wait(barrier, 1 + jnp.minimum(n_chip - 1 - chip, 1))
+
+    def remote(source, slot, turn, peer):
         return pltpu.make_async_remote_copy(
             src_ref=source,
             dst_ref=result_ref.at[slot],
-            send_sem=send_sem.at[step - 1],
-            recv_sem=recv_sem.at[step - 1],
-            device_id={"ctx": jnp.clip(me + direction * step, 0, size - 1)},
+            send_sem=send_sem.at[turn],
+            recv_sem=recv_sem.at[turn],
+            device_id=peer,
             device_id_type=MESH,
         )
 
-    for step in range(depth, 0, -1):
-        taker = me + direction * step
-
-        @pl.when((taker >= 0) & (taker < size))
-        def _():
-            copy(step).start()
-
-    for step in range(1, depth + 1):
-        taker = me + direction * step
-        giver = me - direction * step
-
-        @pl.when((giver < 0) | (giver >= size))
-        def _():
-            result_ref[depth - step] = jnp.zeros(result_ref.shape[1:], result_ref.dtype)
-
-        @pl.when((giver >= 0) & (giver < size))
-        def _():
-            copy(step).wait_recv()
-
-        @pl.when((taker >= 0) & (taker < size))
-        def _():
-            copy(step).wait_send()
-
-
-def halo_exchange(collective_id, size, depth, direction, block):
+    one_on = remote(source_ref, 2, 0, after)
+    two_on = remote(result_ref.at[2], 0, 1, after)
+    own_near = remote(source_ref, 3, 2, near)
+    before_near = remote(result_ref.at[2], 3 - 2 * (1 - core), 3, near)
+    far_near = remote(result_ref.at[0], 1, 4, near)
+
+    @pl.when(has_after)
+    def _():
+        one_on.start()
+
+    @pl.when(core == 0)
+    def _():
+        own_near.start()
+
+    def blank(slot):
+        result_ref[slot] = jnp.zeros(result_ref.shape[1:], result_ref.dtype)
+
+    @pl.when(chip == 0)
+    def _():
+        blank(2)
+        blank(0)
+        blank(1)
+
+    @pl.when((chip == 0) & (core == 0))
+    def _():
+        blank(3)
+
+    @pl.when(chip == 1)
+    def _():
+        blank(0)
+
+    @pl.when((chip == 1) & (core == 0))
+    def _():
+        blank(1)
+
+    @pl.when(chip > 0)
+    def _():
+        one_on.wait_recv()
+
+    @pl.when((chip > 0) & has_after)
+    def _():
+        two_on.start()
+
+    @pl.when(chip > 0)
+    def _():
+        before_near.start()
+
+    @pl.when(chip > 1)
+    def _():
+        two_on.wait_recv()
+
+    @pl.when((chip > 1) & (core == 1))
+    def _():
+        far_near.start()
+
+    @pl.when(core == 1)
+    def _():
+        own_near.wait_recv()
+
+    @pl.when(core == 0)
+    def _():
+        own_near.wait_send()
+
+    @pl.when(chip > 0)
+    def _():
+        before_near.wait()
+
+    @pl.when((chip > 1) & (core == 0))
+    def _():
+        far_near.wait_recv()
+
+    @pl.when((chip > 1) & (core == 1))
+    def _():
+        far_near.wait_send()
+
+    @pl.when(has_after)
+    def _():
+        one_on.wait_send()
+
+    @pl.when((chip > 0) & has_after)
+    def _():
+        two_on.wait_send()
+
+
+def halo_back_kernel(
+    n_chip, source_ref, result_ref, near_ref, far_ref, way_ref, send_sem, recv_sem
+):
+    me = lax.axis_index("ctx")
+    chip, core = me // 2, lax.rem(me, 2)
+    near = {"ctx": me + 1 - 2 * core}
+    before = {"ctx": jnp.maximum(me - 2, 0)}
+    has_after = chip < n_chip - 1
+    barrier = pltpu.get_barrier_semaphore()
+    pl.semaphore_signal(barrier, inc=1, device_id=near, device_id_type=MESH)
+
+    @pl.when(has_after)
+    def _():
+        after = {"ctx": jnp.minimum(me + 2, 2 * n_chip - 1)}
+        pl.semaphore_signal(barrier, inc=1, device_id=after, device_id_type=MESH)
+
+    pl.semaphore_wait(barrier, 1 + jnp.minimum(chip, 1))
+
+    def remote(source, target, turn, peer):
+        return pltpu.make_async_remote_copy(
+            src_ref=source,
+            dst_ref=target,
+            send_sem=send_sem.at[turn],
+            recv_sem=recv_sem.at[turn],
+            device_id=peer,
+            device_id_type=MESH,
+        )
+
+    to_before = remote(source_ref.at[3 - 2 * core], near_ref.at[0], 0, near)
+    to_other = remote(source_ref.at[1 + 2 * core], near_ref.at[1], 1, near)
+    to_before.start()
+    to_other.start()
+
+    @pl.when((chip == 0) | jnp.logical_not(has_after))
+    def _():
+        way_ref[0] = jnp.zeros(way_ref.shape[1:], way_ref.dtype)
+
+    @pl.when(jnp.logical_not(has_after))
+    def _():
+        way_ref[1] = jnp.zeros(way_ref.shape[1:], way_ref.dtype)
+
+    to_other.wait_recv()
+    theirs = near_ref[1].astype(F32)
+    far_ref[0] = (source_ref[0].astype(F32) + jnp.where(core == 1, theirs, 0.0)).astype(BF16)
+    two_back = remote(far_ref.at[0], way_ref.at[0], 2, before)
+    one_back = remote(far_ref.at[1], way_ref.at[1], 3, before)
+
+    @pl.when(chip > 1)
+    def _():
+        two_back.start()
+
+    to_before.wait_recv()
+    due = source_ref[2].astype(F32) + near_ref[0].astype(F32)
+
+    @pl.when((chip > 0) & has_after)
+    def _():
+        two_back.wait_recv()
+
+    far_ref[1] = (due + way_ref[0].astype(F32)).astype(BF16)
+
+    @pl.when(chip > 0)
+    def _():
+        one_back.start()
+
+    @pl.when(has_after)
+    def _():
+        one_back.wait_recv()
+
+    result_ref[...] = way_ref[1].astype(F32) + jnp.where(core == 0, theirs, 0.0)
+    to_before.wait_send()
+    to_other.wait_send()
+
+    @pl.when(chip > 1)
+    def _():
+        two_back.wait_send()
+
+    @pl.when(chip > 0)
+    def _():
+        one_back.wait_send()
+
+
+def halo_call(collective_id, kernel, n_ctx, block, out_shape, buffers, copies):
+    dma = pltpu.SemaphoreType.DMA
     return pl.pallas_call(
-        functools.partial(halo_kernel, size, depth, direction),
-        out_shape=jax.ShapeDtypeStruct((depth, *block.shape[-2:]), block.dtype),
+        functools.partial(kernel, n_ctx // 2),
+        out_shape=out_shape,
         in_specs=[pl.BlockSpec(memory_space=pltpu.VMEM)],
         out_specs=pl.BlockSpec(memory_space=pltpu.VMEM),
-        scratch_shapes=[pltpu.SemaphoreType.DMA((depth,)), pltpu.SemaphoreType.DMA((depth,))],
+        scratch_shapes=[*buffers, dma((copies,)), dma((copies,))],
         compiler_params=pltpu.CompilerParams(collective_id=collective_id, has_side_effects=True),
     )(block)
+
+
+def halo_out(n_ctx, block):
+    out_shape = jax.ShapeDtypeStruct((4, *block.shape), block.dtype)
+    return halo_call(1, halo_out_kernel, n_ctx, block, out_shape, (), 5)
+
+
+def halo_back(n_ctx, blocks):
+    shape = blocks.shape[1:]
+    buffers = [pltpu.VMEM((2, *shape), blocks.dtype)] * 3
+    out_shape = jax.ShapeDtypeStruct(shape, F32)
+    return halo_call(6, halo_back_kernel, n_ctx, blocks, out_shape, buffers, 4)
 
 
 def pick_kernel(n_batch, n_ctx, piece, padded, gate_ref, up_ref, out_ref):
@@ -977,6 +1129,7 @@
     hidden_part = -(-piece * n_ctx // 128) * 128
     padded = hidden_part // n_ctx
     halo_depth = (WINDOW + tok_count - 2) // tok_count
+    assert halo_depth == 4
     batch_at = lax.axis_index("batch")
     ctx_at = lax.axis_index("ctx")
     all_tok = n_batch * tok_count
@@ -1035,7 +1188,7 @@
     query_rot = query_path(query_raw, full_gain_q).astype(BF16)
     key_rot = key_path(key_raw, full_gain_k).astype(BF16)
     own_pair = jnp.concatenate([key_rot, value_low], axis=-1)
-    halo = halo_exchange(1, n_ctx, halo_depth, 1, own_pair)
+    halo = halo_out(n_ctx, own_pair)
     context = jnp.concatenate([halo.reshape(halo_depth * tok_count, -1), own_pair], axis=0)
     ctx_keys = context[:, :head_size]
     ctx_values = context[:, head_size:]
@@ -1116,14 +1269,11 @@
     grad_ctx_values = jnp.einsum("htk,thd->kd", prob_low, grad_attended, preferred_element_type=F32)
     grad_context = jnp.concatenate([grad_ctx_keys, grad_ctx_values], axis=-1)
     halo_rows = halo_depth * tok_count
-    returned = halo_exchange(
-        6,
+    returned = halo_back(
         n_ctx,
-        halo_depth,
-        -1,
         grad_context[:halo_rows].astype(BF16).reshape(halo_depth, tok_count, 2 * head_size),
     )
-    own_grad = grad_context[halo_rows:] + jnp.sum(returned.astype(F32), axis=0)
+    own_grad = grad_context[halo_rows:] + returned
     grad_value_low = own_grad[:, head_size:].astype(BF16)
     _, pull_key = jax.vjp(key_path, key_raw, full_gain_k)
     grad_key_raw, grad_gain_key = pull_key(own_grad[:, :head_size])

time: 486 us -> 468 us (0.963)
  waiting for transfers between devices: 53 us -> 43.3 us
  Pallas kernels: 338 us -> 331 us
    reduce_scatter x2, waiting for transfers between devices: 48.1 us -> 34.7 us  [scattered(): return lax.psum_scatter(whole, 'ctx', scatter_dimension=0, tiled=True)]
    pallas_call x2, Pallas kernels: 52.8 us -> 42.5 us  [halo_call(): pl.pallas_call(functools.partial(kernel, n_ctx // 2), out_shape=out_shape...]
where the time goes in v7:
time: 468 us; the launch traced here: 460 us
  Pallas kernels  331 us (71%)
  waiting for transfers between devices  43.3 us (9%)
  local copies, waits for them, and re-layouts  29.1 us (6%)
  matrix products  21.2 us (5%)
  other arithmetic  19.2 us (4%)
  between operations  15.6 us (3%)
    pallas_call x1, Pallas kernels, tail_round(): pl.pallas_call(functools.partial(tail_kernel, n_ctx), name='tail_round',...  68.5 us
    pallas_call x1, Pallas kernels, gather_weights(): pl.pallas_call(functools.partial(weights_kernel, n_batch, n_ctx), name='g...  48.4 us
    pallas_call x2, Pallas kernels, halo_call(): pl.pallas_call(functools.partial(kernel, n_ctx // 2), out_shape=out_shape...  42.5 us
    pallas_call x2, Pallas kernels, square_gather(): pl.pallas_call(functools.partial(square_kernel, count), out_shape=[jax.Sh...  37.2 us
    pallas_call x1, Pallas kernels, turn_round(): pl.pallas_call(turn_kernel, name='turn_round', out_shape=(jax.ShapeDtypeS...  36.4 us
    reduce_scatter x2, waiting for transfers between devices, scattered(): return lax.psum_scatter(whole, 'ctx', scatter_dimension=0, tiled=True)  34.7 us
    pallas_call x2, Pallas kernels, batch_exchange(): pl.pallas_call(functools.partial(batch_kernel, size, kinds), out_shape=sh...  31.1 us
    pallas_call x3, Pallas kernels, product_low(): pl.pallas_call(product_kernel, grid=(columns // tile,), out_shape=jax.Sha...  21.6 us
  transfers between devices with their start and end apart: 4, of which 2 were waited for; matrix products, arithmetic and copies ran while one was open for 11% of the time, Pallas kernels for 34%

profile of v7, /device:TPU:0, one launch (start us, length us, event | category | flops | bytes accessed | tf_op | source)
XLA Modules:
  0.0 460.3 jit_solution(8989483758528672188)
XLA Ops:
  7.2 3.9 pick_columns.1
  13.9 48.4 %gather_weights.1 = (bf16[4,8,144,384]{3,2,1,0:T(8,128)(2,1)}, bf16[8,4,32,1152]{3,2,1,0:T(8,128)(2,1)}, bf16[8,1,640]{2,1,0:T(2,128)(2,1)}) custom-call(bf16[4,144,384]{2,1,0:T(8,128)(2,1)} %bitcast.215, bf16[4,32,1152]{2,1,0:T(8,128)(2,1)} %bitcast.230, bf16[1,640]{1,0:T(2,128)(2,1)} %broadcast_in_dim.32.gain_ref), custom_call_target="tpu_custom_call" | custom-call | tf_op jit(solution)/shard_map/gather_weights/pallas_call | solution.py:813
  63.3 2.3 fusion.91
  70.8 17.5 %shard_map.280 = bf16[4,128,512]{2,1,0:T(8,128)(2,1)} custom-call(bf16[128,512]{1,0:T(8,128)(2,1)} %pad_maximum_fusion.9.source_ref), custom_call_target="tpu_custom_call" | custom-call | tf_op jit(solution)/shard_map/pallas_call | solution.py:612
  90.1 1.6 fusion.97
  93.6 2.3 multiply_reduce_fusion.6
  97.9 15.9 %shard_map.281 = bf16[4,128,1152]{2,1,0:T(8,128)(2,1)} custom-call(bf16[128,1152]{1,0:T(8,128)(2,1)} %multiply_convert_fusion.1.refs_0_), custom_call_target="tpu_custom_call" | custom-call | tf_op jit(solution)/shard_map/pallas_call | solution.py:171
  113.8 2.4 copy.203
  118.2 12.1 %hidden_mix.1 = (f32[512,1792]{1,0:T(8,128)}, f32[512,1792]{1,0:T(8,128)}, bf16[512,1792]{1,0:T(8,128)(2,1)}, bf16[1792,512]{1,0:T(8,128)(2,1)}) custom-call(bf16[512,1152]{1,0:T(8,128)(2,1)} %bitcast.193, bf16[1152,3584]{1,0:T(8,128)(2,1)} %all-gather.3.cloned.1.call-done.w_gate_ref.w_up_ref, bf16[1152,3584]{1,0:T(8,128)(2,1)} %all-gather.3.cloned.1.call-done.w_gate_ref.w_up_ref), custom_call_target="tpu_custom_call" | custom-call | flops 4227858432 | bytes 25165824 | tf_op jit(solution)/shard_map/hidden_mix/pallas_call | solution.py:342
  130.3 21.3 %shard_map.282 = (bf16[4,128,1152]{2,1,0:T(8,128)(2,1)}, bf16[4,128,1024]{2,1,0:T(8,128)(2,1)}) custom-call(bf16[128,1152]{1,0:T(8,128)(2,1)} %get-tuple-element.58.refs_0_, bf16[128,1024]{1,0:T(8,128)(2,1)} %copy.202.refs_1_), custom_call_target="tpu_custom_call" | custom-call | tf_op jit(solution)/shard_map/pallas_call | solution.py:171
  151.6 8.2 %all-gather.5.cloned.1.call-done.down_ref = bf16[1792,1152]{1,0:T(8,128)(2,1)} async-done(((bf16[224,1152]{1,0:T(8,128)(2,1)}), bf16[1792,1152]{1,0:T(8,128)(2,1)}) %all-gather.5.cloned.1.call-update) | async-done | bytes 4128784 | tf_op jit(solution)/shard_map/all_gather | solution.py:1091
  159.8 36.4 %turn_round.1 = (bf16[128,1152]{1,0:T(8,128)(2,1)}, bf16[4,128,1152]{2,1,0:T(8,128)(2,1)}, f32[1,1152]{1,0:T(1,128)}) custom-call(bf16[512,1792]{1,0:T(8,128)(2,1)} %get-tuple-element.63.mixed_ref, bf16[1792,1152]{1,0:T(8,128)(2,1)} %all-gather.5.cloned.1.call-done.down_ref, f32[128,1152]{1,0:T(8,128)} %copy-done.3, bf16[128,1152]{1,0:T(8,128)(2,1)} %bitcast.229, ...), custom_call_target="tpu_custom_call" | custom-call | flops 2113929216 | bytes 8388608 | tf_op jit(solution)/shard_map/turn_round/pallas_call | solution.py:281
  196.3 6.4 %shard_map.283 = bf16[1792,1152]{1,0:T(8,128)(2,1)} custom-call(bf16[1792,512]{1,0:T(8,128)(2,1)} %get-tuple-element.65.left_ref, bf16[512,1152]{1,0:T(8,128)(2,1)} %bitcast.220), custom_call_target="tpu_custom_call" | custom-call | flops 2113929216 | bytes 8388608 | tf_op jit(solution)/shard_map/pallas_call | solution.py:311
  202.6 21.0 %hidden_back.1 = (bf16[512,1792]{1,0:T(8,128)(2,1)}, bf16[512,1792]{1,0:T(8,128)(2,1)}, bf16[512,1152]{1,0:T(8,128)(2,1)}) custom-call(bf16[512,1152]{1,0:T(8,128)(2,1)} %bitcast.221, bf16[1792,1152]{1,0:T(8,128)(2,1)} %all-gather.5.cloned.1.call-done.down_ref, f32[512,1792]{1,0:T(8,128)} %get-tuple-element.68.gate_ref, ...), custom_call_target="tpu_custom_call" | custom-call | flops 6341787648 | bytes 25165824 | tf_op jit(solution)/shard_map/hidden_back/pallas_call | solution.py:394
  223.7 16.6 %shard_map.284 = bf16[4,128,1152]{2,1,0:T(8,128)(2,1)} custom-call(bf16[4,128,1152]{2,1,0:T(8,128)(2,1)} %bitcast.224), custom_call_target="tpu_custom_call" | custom-call | tf_op jit(solution)/shard_map/pallas_call | solution.py:101
  240.3 7.6 %shard_map.286 = bf16[1152,1792]{1,0:T(8,128)(2,1)} custom-call(bf16[1152,512]{1,0:T(8,128)(2,1)} %bitcast.222, bf16[512,1792]{1,0:T(8,128)(2,1)} %get-tuple-element.76.right_ref), custom_call_target="tpu_custom_call" | custom-call | flops 2113929216 | bytes 8388608 | tf_op jit(solution)/shard_map/pallas_call | solution.py:311
  247.9 7.6 %shard_map.285 = bf16[1152,1792]{1,0:T(8,128)(2,1)} custom-call(bf16[1152,512]{1,0:T(8,128)(2,1)} %bitcast.223, bf16[512,1792]{1,0:T(8,128)(2,1)} %get-tuple-element.75.right_ref), custom_call_target="tpu_custom_call" | custom-call | flops 2113929216 | bytes 8388608 | tf_op jit(solution)/shard_map/pallas_call | solution.py:311
  260.9 2.6 convolution_convert_fusion
  263.7 2.7 convolution_bitcast_fusion.3
  266.4 1.8 multiply_reduce_fusion
  271.1 25.0 %shard_map.287 = f32[128,512]{1,0:T(8,128)} custom-call(bf16[4,128,512]{2,1,0:T(8,128)(2,1)} %bitcast.213), custom_call_target="tpu_custom_call" | custom-call | tf_op jit(solution)/shard_map/pallas_call | solution.py:612
  301.8 1.6 fusion.50
  308.2 14.4 %shard_map.288 = (f32[4,8,640]{2,1,0:T(8,128)}, bf16[4,128,384]{2,1,0:T(8,128)(2,1)}, bf16[4,128,288]{2,1,0:T(8,128)(2,1)}) custom-call(f32[8,640]{1,0:T(8,128)} %concatenate.54.refs_0_, bf16[4,128,384]{2,1,0:T(8,128)(2,1)} %bitcast.217, bf16[4,128,288]{2,1,0:T(8,128)(2,1)} %bitcast.219), custom_call_target="tpu_custom_call" | custom-call | tf_op jit(solution)/shard_map/pallas_call | solution.py:101
  322.6 1.9 fusion.11
  325.0 2.1 fusion.3
  327.1 1.8 fusion.6.attn_ref
  329.9 34.7 %reduce-scatter.5.cloned.1.call-done.down_ref = bf16[224,1152]{1,0:T(8,128)(2,1)} async-done(((bf16[1792,1152]{1,0:T(8,128)(2,1)}), bf16[224,1152]{1,0:T(8,128)(2,1)}) %reduce-scatter.5.cloned.1.call-update) | async-done | bytes 516112 | tf_op jit(solution)/shard_map/reduce_scatter | solution.py:1095
  364.6 68.5 %tail_round.1 = (bf16[4,144,1792]{2,1,0:T(8,128)(2,1)}, bf16[4,224,1152]{2,1,0:T(8,128)(2,1)}, bf16[4,144,1792]{2,1,0:T(8,128)(2,1)}, bf16[4,288,384]{2,1,0:T(8,128)(2,1)}) custom-call(bf16[144,1792]{1,0:T(8,128)(2,1)} %reduce-scatter.3.cloned.1.call-done.gate_ref, bf16[224,1152]{1,0:T(8,128)(2,1)} %reduce-scatter.5.cloned.1.call-done.down_ref, ...), custom_call_target="tpu_custom_call" | custom-call | tf_op jit(solution)/shard_map/tail_round/pallas_call | solution.py:1067
  438.9 1.7 slice.172
  440.6 2.3 bitcast_convert_fusion
  442.9 4.3 shard_map.289
  447.3 4.5 shard_map.290
  (248 shorter events, 43.0 us)
Async XLA Ops:
  7.2 4.1 copy-start
  7.2 111.0 %all-gather.3.cloned.1.call-start = ((), (), s32[]{:S(2)}) async-start(), calls=%async_computation.2 | async-start | bytes 9289728 | tf_op jit(solution)/shard_map/all_gather | solution.py:1091
  11.2 148.6 %all-gather.5.cloned.1.call-start = ((), (), s32[]{:S(2)}) async-start(), calls=%async_computation.3 | async-start | bytes 4644864 | tf_op jit(solution)/shard_map/all_gather | solution.py:1091
  12.3 50.9 %copy-start.2 = (bf16[1,128,1152]{2,1,0:T(8,128)(2,1)S(1)}, bf16[1,128,1152]{2,1,0:T(8,128)(2,1)}, u32[]{:S(2)}) copy-start(bf16[1,128,1152]{2,1,0:T(8,128)(2,1)} %param.17) | copy-start | bytes 884740
  12.3 317.6 %reduce-scatter.3.cloned.1.call-start = ((), (), s32[]{:S(2)}) async-start(), calls=%async_computation.4 | async-start | bytes 4644864 | tf_op jit(solution)/shard_map/reduce_scatter | solution.py:1095
  63.3 2.3 copy-start.54
  68.3 21.4 %copy-start.38 = (f32[128,4]{0,1:T(4,128)}, f32[128,4]{0,1:T(4,128)S(1)}, u32[]{:S(2)}) copy-start(f32[128,4]{0,1:T(4,128)S(1)} %copy.156) | copy-start | bytes 6148
  68.4 21.4 %copy-start.42 = (f32[256]{0:T(256)}, f32[256]{0:T(256)S(1)}, u32[]{:S(2)}) copy-start(f32[256]{0:T(256)S(1)} %mul.493) | copy-start | bytes 3076
  68.9 20.7 %copy-start.50 = (f32[128]{0:T(128)}, f32[128]{0:T(128)S(1)}, u32[]{:S(2)}) copy-start(f32[128]{0:T(128)S(1)} %multiply_power_fusion) | copy-start | bytes 1540
  69.7 18.7 %copy-start.44 = (f32[128]{0:T(128)}, f32[128]{0:T(128)S(1)}, u32[]{:S(2)}) copy-start(f32[128]{0:T(128)S(1)} %fusion.69) | copy-start | bytes 1540
  69.7 20.0 %copy-start.52 = (f32[128]{0:T(128)}, f32[128]{0:T(128)S(1)}, u32[]{:S(2)}) copy-start(f32[128]{0:T(128)S(1)} %bitcast_convert_fusion.1) | copy-start | bytes 1540
  70.1 19.8 %copy-start.18 = (f32[128,128]{1,0:T(8,128)}, f32[128,128]{1,0:T(8,128)S(1)}, u32[]{:S(2)}) copy-start(f32[128,128]{1,0:T(8,128)S(1)} %get-tuple-element.193) | copy-start | bytes 196612
  70.1 19.8 %copy-start.20 = (f32[128,128]{1,0:T(8,128)}, f32[128,128]{1,0:T(8,128)S(1)}, u32[]{:S(2)}) copy-start(f32[128,128]{1,0:T(8,128)S(1)} %get-tuple-element.194) | copy-start | bytes 196612
  97.0 19.2 %copy-start.3 = (f32[128,1152]{1,0:T(8,128)}, f32[128,1152]{1,0:T(8,128)S(1)}, u32[]{:S(2)}) copy-start(f32[128,1152]{1,0:T(8,128)S(1)} %get-tuple-element.163.middle_ref) | copy-start | bytes 1769476
  255.5 109.1 %reduce-scatter.5.cloned.1.call-start = ((), (), s32[]{:S(2)}) async-start(), calls=%async_computation.5 | async-start | bytes 4644864 | tf_op jit(solution)/shard_map/reduce_scatter | solution.py:1095
  256.1 2.2 copy-start.4
  260.9 2.8 copy-start.14
  260.9 2.8 copy-start.26
  260.9 2.8 copy-start.28
  260.9 2.8 copy-start.49
  271.1 26.1 %copy-start.51 = (f32[128]{0:T(128)S(1)}, f32[128]{0:T(128)}, u32[]{:S(2)}) copy-start(f32[128]{0:T(128)} %copy-done.50) | copy-start | bytes 1540
  271.1 26.1 %copy-start.53 = (f32[128]{0:T(128)S(1)}, f32[128]{0:T(128)}, u32[]{:S(2)}) copy-start(f32[128]{0:T(128)} %copy-done.52) | copy-start | bytes 1540
  297.1 2.2 copy-start.15
  297.2 2.1 copy-start.23
  297.2 2.5 copy-start.19
  297.2 2.5 copy-start.21
  300.9 2.5 copy-start.8
  322.6 2.3 copy-start.34
  322.6 2.3 copy-start.55
  322.6 2.3 copy-start.65
  325.0 2.1 copy-start.47
  447.2 6.5 %copy-start.1 = (bf16[864,1152]{1,0:T(8,128)(2,1)S(1)}, bf16[864,1152]{1,0:T(8,128)(2,1)}, u32[]{:S(2)}) copy-start(bf16[864,1152]{1,0:T(8,128)(2,1)} %param.32) | copy-start | bytes 5971972
  (38 other events, 46.3 us)
Sparse Core Ops, SparseCore 0:
  11.3 95.1 all-gather.2
  108.8 51.0 all-gather.4
  255.7 59.2 reduce-scatter.2
  317.1 47.4 reduce-scatter.4

commit v8 on v7

--- a/solution.py
+++ b/solution.py
@@ -663,25 +663,62 @@
     )(w_gate, w_up)
 
 
-def place_kernel(n_batch, n_ctx, piece, padded, parts_ref, out_ref):
-    for shard in range(n_ctx):
-        for spot in range(n_batch):
-            start = (shard * n_batch + spot) * piece
-            place = shard * padded
-            out_ref[:, start : start + piece] = parts_ref[spot, :, place : place + piece].astype(F32)
-
-
-def place_columns(n_batch, n_ctx, piece, padded, parts):
-    rows = parts.shape[1]
+def finish_kernel(n_batch, n_ctx, piece, padded, proj_part, gate_ref, up_ref, down_ref, attn_ref, *refs):
+    outs, bufs, sems = refs[:8], refs[8:16], refs[16]
+    gate_buf, up_buf, down_buf, query_buf, key_buf, value_buf, proj_buf, gain_buf = bufs
+    copies = [pltpu.make_async_copy(bufs[i], outs[i], sems.at[i]) for i in range(8)]
+    rows = gate_ref.shape[1]
     block = row_block(rows)
-    hidden = n_batch * n_ctx * piece
+
+    for ref, buf, copy in ((gate_ref, gate_buf, copies[0]), (up_ref, up_buf, copies[1])):
+
+        def place_rows(step, carry):
+            lines = pl.ds(pl.multiple_of(step * block, block), block)
+            for shard in range(n_ctx):
+                for spot in range(n_batch):
+                    start = (shard * n_batch + spot) * piece
+                    place = shard * padded
+                    buf[lines, start : start + piece] = ref[
+                        spot, lines, place : place + piece
+                    ].astype(F32)
+            return carry
+
+        lax.fori_loop(0, rows // block, place_rows, 0)
+        copy.start()
+    for spot in range(n_batch):
+        down_buf[spot * piece : (spot + 1) * piece, :] = down_ref[spot, :piece, :].astype(F32)
+    copies[2].start()
+    quarter = attn_ref.shape[-1]
+    proj_rows = proj_buf.shape[0]
+    for spot in range(n_batch):
+        for tile in range(0, quarter, 128):
+            column = spot * quarter + tile
+            for buf in (query_buf, key_buf, value_buf):
+                if 0 <= column < buf.shape[-1]:
+                    buf[:, column : column + 128] = attn_ref[
+                        spot, :rows, tile : tile + 128
+                    ].astype(F32)
+                column -= buf.shape[-1]
+        proj_buf[:, spot * proj_part : (spot + 1) * proj_part] = attn_ref[
+            spot, rows : rows + proj_rows, :proj_part
+        ].astype(F32)
+    gain_buf[...] = attn_ref[0, rows + proj_rows : rows + proj_rows + gain_buf.shape[0], :].astype(F32)
+    for copy in copies[3:]:
+        copy.start()
+    for copy in copies:
+        copy.wait()
+
+
+def finish_round(n_batch, n_ctx, piece, padded, proj_part, gate, up, down, attn, shapes):
+    outs = [jax.ShapeDtypeStruct(shape, F32) for shape in shapes]
     return pl.pallas_call(
-        functools.partial(place_kernel, n_batch, n_ctx, piece, padded),
-        grid=(rows // block,),
-        out_shape=jax.ShapeDtypeStruct((rows, hidden), F32),
-        in_specs=[pl.BlockSpec((n_batch, block, n_ctx * padded), lambda i: (0, i, 0))],
-        out_specs=pl.BlockSpec((block, hidden), lambda i: (i, 0)),
-    )(parts)
+        functools.partial(finish_kernel, n_batch, n_ctx, piece, padded, proj_part),
+        name="finish_round",
+        out_shape=outs,
+        in_specs=[pl.BlockSpec(memory_space=pltpu.VMEM)] * 4,
+        out_specs=[pl.BlockSpec(memory_space=pl.ANY)] * 8,
+        scratch_shapes=[pltpu.VMEM(shape, F32) for shape in shapes] + [pltpu.SemaphoreType.DMA((8,))],
+    )(gate, up, down, attn)
 
 
 def weights_kernel(n_batch, n_ctx, qkv_ref, proj_ref, gain_ref, qkv_all, proj_all, gain_all, *sems):
@@ -1348,27 +1385,45 @@
         up_grad.reshape(n_ctx, width_shard, hidden_part),
         packed,
     )
-    gain_mine = attn_grads[0, width_shard + proj_rows : used].reshape(-1).astype(F32)
-
-    def columns_back(pieces):
-        return pieces.astype(F32).transpose(1, 0, 2).reshape(pieces.shape[1], -1)
-
-    grad_qkv_shard = columns_back(attn_grads[:, :width_shard])
+    shapes = (
+        (width_shard, w_gate.shape[1]),
+        (width_shard, w_gate.shape[1]),
+        (hidden_shard, model_width),
+        (width_shard, query_width),
+        (width_shard, head_size),
+        (width_shard, head_size),
+        (proj_rows, model_width),
+        (gain_lines, quarter),
+    )
+    (
+        grad_gate_shard,
+        grad_up_shard,
+        grad_down_shard,
+        grad_query_shard,
+        grad_key_shard,
+        grad_value_shard,
+        grad_output_shard,
+        gain_block,
+    ) = finish_round(
+        n_batch, n_ctx, piece, padded, output_part, gate_all, up_all, down_all, attn_grads, shapes
+    )
+    gain_mine = gain_block.reshape(-1)
+
     return (
         block_out[None],
         grad_in[None],
         gain_mine[:width_shard],
-        grad_qkv_shard[:, :query_width],
-        grad_qkv_shard[:, query_width : query_width + head_size],
-        grad_qkv_shard[:, query_width + head_size :],
+        grad_query_shard,
+        grad_key_shard,
+        grad_value_shard,
         gain_mine[4 * width_shard : 4 * width_shard + head_shard],
         gain_mine[4 * width_shard + head_shard : gain_count],
-        columns_back(attn_grads[:, width_shard : width_shard + proj_rows, :output_part]),
+        grad_output_shard,
         gain_mine[width_shard : 2 * width_shard],
         gain_mine[2 * width_shard : 3 * width_shard],
-        place_columns(n_batch, n_ctx, piece, padded, gate_all),
-        place_columns(n_batch, n_ctx, piece, padded, up_all),
-        down_all[:, :piece].reshape(hidden_shard, model_width).astype(F32),
+        grad_gate_shard,
+        grad_up_shard,
+        grad_down_shard,
         gain_mine[3 * width_shard : 4 * width_shard],
     )
 

time: 468 us -> 459 us (0.981)
  other arithmetic: 19.2 us -> 14 us
  transfers between devices with their start and end apart: 4 -> 4, of which waited for: 2 -> 2; matrix products, arithmetic and copies ran while one was open for 11% -> 12% of each run, Pallas kernels for 34% -> 34%
where the time goes in v8:
time: 459 us; the launch traced here: 451 us
  Pallas kernels  332 us (72%)
  waiting for transfers between devices  43.3 us (9%)
  local copies, waits for them, and re-layouts  25.1 us (5%)
  matrix products  21.2 us (5%)
  between operations  15.6 us (3%)
  other arithmetic  14 us (3%)
    pallas_call x1, Pallas kernels, tail_round(): pl.pallas_call(functools.partial(tail_kernel, n_ctx), name='tail_round',...  68.5 us
    pallas_call x1, Pallas kernels, gather_weights(): pl.pallas_call(functools.partial(weights_kernel, n_batch, n_ctx), name='g...  48.4 us
    pallas_call x2, Pallas kernels, halo_call(): pl.pallas_call(functools.partial(kernel, n_ctx // 2), out_shape=out_shape...  42.5 us
    pallas_call x2, Pallas kernels, square_gather(): pl.pallas_call(functools.partial(square_kernel, count), out_shape=[jax.Sh...  37.2 us
    pallas_call x1, Pallas kernels, turn_round(): pl.pallas_call(turn_kernel, name='turn_round', out_shape=(jax.ShapeDtypeS...  36.4 us
    reduce_scatter x2, waiting for transfers between devices, scattered(): return lax.psum_scatter(whole, 'ctx', scatter_dimension=0, tiled=True)  34.7 us
    pallas_call x2, Pallas kernels, batch_exchange(): pl.pallas_call(functools.partial(batch_kernel, size, kinds), out_shape=sh...  31.1 us
    pallas_call x3, Pallas kernels, product_low(): pl.pallas_call(product_kernel, grid=(columns // tile,), out_shape=jax.Sha...  21.6 us
  transfers between devices with their start and end apart: 4, of which 2 were waited for; matrix products, arithmetic and copies ran while one was open for 12% of the time, Pallas kernels for 34%

profile of v8, /device:TPU:0, one launch (start us, length us, event | category | flops | bytes accessed | tf_op | source)
XLA Modules:
  0.0 451.2 jit_solution(16251773872811605883)
XLA Ops:
  7.2 3.9 pick_columns.1
  13.9 48.4 %gather_weights.1 = (bf16[4,8,144,384]{3,2,1,0:T(8,128)(2,1)}, bf16[8,4,32,1152]{3,2,1,0:T(8,128)(2,1)}, bf16[8,1,640]{2,1,0:T(2,128)(2,1)}) custom-call(bf16[4,144,384]{2,1,0:T(8,128)(2,1)} %bitcast.202, bf16[4,32,1152]{2,1,0:T(8,128)(2,1)} %bitcast.217, bf16[1,640]{1,0:T(2,128)(2,1)} %broadcast_in_dim.32.gain_ref), custom_call_target="tpu_custom_call" | custom-call | tf_op jit(solution)/shard_map/gather_weights/pallas_call | solution.py:850
  63.3 2.3 fusion.91
  70.8 17.5 %shard_map.280 = bf16[4,128,512]{2,1,0:T(8,128)(2,1)} custom-call(bf16[128,512]{1,0:T(8,128)(2,1)} %pad_maximum_fusion.9.source_ref), custom_call_target="tpu_custom_call" | custom-call | tf_op jit(solution)/shard_map/pallas_call | solution.py:612
  88.5 1.1 maximum_maximum_fusion
  90.1 1.6 fusion.96
  93.6 2.3 multiply_reduce_fusion.6
  96.0 1.0 multiply_reduce_fusion.5
  97.9 15.9 %shard_map.281 = bf16[4,128,1152]{2,1,0:T(8,128)(2,1)} custom-call(bf16[128,1152]{1,0:T(8,128)(2,1)} %multiply_convert_fusion.1.refs_0_), custom_call_target="tpu_custom_call" | custom-call | tf_op jit(solution)/shard_map/pallas_call | solution.py:171
  113.8 2.4 copy.191
  118.2 12.1 %hidden_mix.1 = (f32[512,1792]{1,0:T(8,128)}, f32[512,1792]{1,0:T(8,128)}, bf16[512,1792]{1,0:T(8,128)(2,1)}, bf16[1792,512]{1,0:T(8,128)(2,1)}) custom-call(bf16[512,1152]{1,0:T(8,128)(2,1)} %bitcast.183, bf16[1152,3584]{1,0:T(8,128)(2,1)} %all-gather.3.cloned.1.call-done.w_gate_ref.w_up_ref, bf16[1152,3584]{1,0:T(8,128)(2,1)} %all-gather.3.cloned.1.call-done.w_gate_ref.w_up_ref), custom_call_target="tpu_custom_call" | custom-call | flops 4227858432 | bytes 25165824 | tf_op jit(solution)/shard_map/hidden_mix/pallas_call | solution.py:342
  130.3 21.3 %shard_map.282 = (bf16[4,128,1152]{2,1,0:T(8,128)(2,1)}, bf16[4,128,1024]{2,1,0:T(8,128)(2,1)}) custom-call(bf16[128,1152]{1,0:T(8,128)(2,1)} %get-tuple-element.66.refs_0_, bf16[128,1024]{1,0:T(8,128)(2,1)} %copy.190.refs_1_), custom_call_target="tpu_custom_call" | custom-call | tf_op jit(solution)/shard_map/pallas_call | solution.py:171
  151.6 8.2 %all-gather.5.cloned.1.call-done.down_ref = bf16[1792,1152]{1,0:T(8,128)(2,1)} async-done(((bf16[224,1152]{1,0:T(8,128)(2,1)}), bf16[1792,1152]{1,0:T(8,128)(2,1)}) %all-gather.5.cloned.1.call-update) | async-done | bytes 4128784 | tf_op jit(solution)/shard_map/all_gather | solution.py:1128
  159.8 36.4 %turn_round.1 = (bf16[128,1152]{1,0:T(8,128)(2,1)}, bf16[4,128,1152]{2,1,0:T(8,128)(2,1)}, f32[1,1152]{1,0:T(1,128)}) custom-call(bf16[512,1792]{1,0:T(8,128)(2,1)} %get-tuple-element.71.mixed_ref, bf16[1792,1152]{1,0:T(8,128)(2,1)} %all-gather.5.cloned.1.call-done.down_ref, f32[128,1152]{1,0:T(8,128)} %copy-done.3, bf16[128,1152]{1,0:T(8,128)(2,1)} %bitcast.216, ...), custom_call_target="tpu_custom_call" | custom-call | flops 2113929216 | bytes 8388608 | tf_op jit(solution)/shard_map/turn_round/pallas_call | solution.py:281
  196.3 6.4 %shard_map.283 = bf16[1792,1152]{1,0:T(8,128)(2,1)} custom-call(bf16[1792,512]{1,0:T(8,128)(2,1)} %get-tuple-element.73.left_ref, bf16[512,1152]{1,0:T(8,128)(2,1)} %bitcast.207), custom_call_target="tpu_custom_call" | custom-call | flops 2113929216 | bytes 8388608 | tf_op jit(solution)/shard_map/pallas_call | solution.py:311
  202.6 21.0 %hidden_back.1 = (bf16[512,1792]{1,0:T(8,128)(2,1)}, bf16[512,1792]{1,0:T(8,128)(2,1)}, bf16[512,1152]{1,0:T(8,128)(2,1)}) custom-call(bf16[512,1152]{1,0:T(8,128)(2,1)} %bitcast.208, bf16[1792,1152]{1,0:T(8,128)(2,1)} %all-gather.5.cloned.1.call-done.down_ref, f32[512,1792]{1,0:T(8,128)} %get-tuple-element.76.gate_ref, ...), custom_call_target="tpu_custom_call" | custom-call | flops 6341787648 | bytes 25165824 | tf_op jit(solution)/shard_map/hidden_back/pallas_call | solution.py:394
  223.7 16.6 %shard_map.284 = bf16[4,128,1152]{2,1,0:T(8,128)(2,1)} custom-call(bf16[4,128,1152]{2,1,0:T(8,128)(2,1)} %bitcast.211), custom_call_target="tpu_custom_call" | custom-call | tf_op jit(solution)/shard_map/pallas_call | solution.py:101
  240.3 7.6 %shard_map.286 = bf16[1152,1792]{1,0:T(8,128)(2,1)} custom-call(bf16[1152,512]{1,0:T(8,128)(2,1)} %bitcast.209, bf16[512,1792]{1,0:T(8,128)(2,1)} %get-tuple-element.84.right_ref), custom_call_target="tpu_custom_call" | custom-call | flops 2113929216 | bytes 8388608 | tf_op jit(solution)/shard_map/pallas_call | solution.py:311
  247.9 7.6 %shard_map.285 = bf16[1152,1792]{1,0:T(8,128)(2,1)} custom-call(bf16[1152,512]{1,0:T(8,128)(2,1)} %bitcast.210, bf16[512,1792]{1,0:T(8,128)(2,1)} %get-tuple-element.83.right_ref), custom_call_target="tpu_custom_call" | custom-call | flops 2113929216 | bytes 8388608 | tf_op jit(solution)/shard_map/pallas_call | solution.py:311
  256.8 1.5 convert_reduce_fusion
  260.9 2.6 convolution_convert_fusion
  263.7 2.7 convolution_bitcast_fusion.3
  266.4 1.8 multiply_reduce_fusion
  271.1 25.0 %shard_map.287 = f32[128,512]{1,0:T(8,128)} custom-call(bf16[4,128,512]{2,1,0:T(8,128)(2,1)} %bitcast.200), custom_call_target="tpu_custom_call" | custom-call | tf_op jit(solution)/shard_map/pallas_call | solution.py:612
  301.8 1.6 fusion.50
  308.2 14.4 %shard_map.288 = (f32[4,8,640]{2,1,0:T(8,128)}, bf16[4,128,384]{2,1,0:T(8,128)(2,1)}, bf16[4,128,288]{2,1,0:T(8,128)(2,1)}) custom-call(f32[8,640]{1,0:T(8,128)} %concatenate.54.refs_0_, bf16[4,128,384]{2,1,0:T(8,128)(2,1)} %bitcast.204, bf16[4,128,288]{2,1,0:T(8,128)(2,1)} %bitcast.206), custom_call_target="tpu_custom_call" | custom-call | tf_op jit(solution)/shard_map/pallas_call | solution.py:101
  322.6 1.9 fusion.11
  325.0 2.1 fusion.3
  327.1 1.8 fusion.6.attn_ref
  329.9 34.7 %reduce-scatter.5.cloned.1.call-done.down_ref = bf16[224,1152]{1,0:T(8,128)(2,1)} async-done(((bf16[1792,1152]{1,0:T(8,128)(2,1)}), bf16[224,1152]{1,0:T(8,128)(2,1)}) %reduce-scatter.5.cloned.1.call-update) | async-done | bytes 516112 | tf_op jit(solution)/shard_map/reduce_scatter | solution.py:1132
  364.6 68.5 %tail_round.1 = (bf16[4,144,1792]{2,1,0:T(8,128)(2,1)}, bf16[4,224,1152]{2,1,0:T(8,128)(2,1)}, bf16[4,144,1792]{2,1,0:T(8,128)(2,1)}, bf16[4,288,384]{2,1,0:T(8,128)(2,1)}) custom-call(bf16[144,1792]{1,0:T(8,128)(2,1)} %reduce-scatter.3.cloned.1.call-done.gate_ref, bf16[224,1152]{1,0:T(8,128)(2,1)} %reduce-scatter.5.cloned.1.call-done.down_ref, ...), custom_call_target="tpu_custom_call" | custom-call | tf_op jit(solution)/shard_map/tail_round/pallas_call | solution.py:1104
  433.1 8.9 %finish_round.1 = (f32[144,6912]{1,0:T(8,128)}, f32[144,6912]{1,0:T(8,128)}, f32[864,1152]{1,0:T(8,128)}, f32[144,1024]{1,0:T(8,128)}, f32[144,256]{1,0:T(8,128)...) custom-call(bf16[4,144,1792]{2,1,0:T(8,128)(2,1)} %get-tuple-element.95.gate_ref, ...), custom_call_target="tpu_custom_call" | custom-call | tf_op jit(solution)/shard_map/finish_round/pallas_call | solution.py:714
  (237 shorter events, 34.2 us)
Async XLA Ops:
  7.2 4.1 copy-start
  7.2 111.0 %all-gather.3.cloned.1.call-start = ((), (), s32[]{:S(2)}) async-start(), calls=%async_computation.2 | async-start | bytes 9289728 | tf_op jit(solution)/shard_map/all_gather | solution.py:1128
  11.2 148.6 %all-gather.5.cloned.1.call-start = ((), (), s32[]{:S(2)}) async-start(), calls=%async_computation.3 | async-start | bytes 4644864 | tf_op jit(solution)/shard_map/all_gather | solution.py:1128
  12.3 50.9 %copy-start.2 = (bf16[1,128,1152]{2,1,0:T(8,128)(2,1)S(1)}, bf16[1,128,1152]{2,1,0:T(8,128)(2,1)}, u32[]{:S(2)}) copy-start(bf16[1,128,1152]{2,1,0:T(8,128)(2,1)} %param.17) | copy-start | bytes 884740
  12.3 317.6 %reduce-scatter.3.cloned.1.call-start = ((), (), s32[]{:S(2)}) async-start(), calls=%async_computation.4 | async-start | bytes 4644864 | tf_op jit(solution)/shard_map/reduce_scatter | solution.py:1132
  63.3 2.3 copy-start.54
  68.3 21.4 %copy-start.38 = (f32[128,4]{0,1:T(4,128)}, f32[128,4]{0,1:T(4,128)S(1)}, u32[]{:S(2)}) copy-start(f32[128,4]{0,1:T(4,128)S(1)} %copy.147) | copy-start | bytes 6148
  68.4 21.4 %copy-start.42 = (f32[256]{0:T(256)}, f32[256]{0:T(256)S(1)}, u32[]{:S(2)}) copy-start(f32[256]{0:T(256)S(1)} %mul.493) | copy-start | bytes 3076
  68.9 20.7 %copy-start.50 = (f32[128]{0:T(128)}, f32[128]{0:T(128)S(1)}, u32[]{:S(2)}) copy-start(f32[128]{0:T(128)S(1)} %multiply_power_fusion) | copy-start | bytes 1540
  69.7 18.7 %copy-start.44 = (f32[128]{0:T(128)}, f32[128]{0:T(128)S(1)}, u32[]{:S(2)}) copy-start(f32[128]{0:T(128)S(1)} %fusion.69) | copy-start | bytes 1540
  69.7 20.0 %copy-start.52 = (f32[128]{0:T(128)}, f32[128]{0:T(128)S(1)}, u32[]{:S(2)}) copy-start(f32[128]{0:T(128)S(1)} %bitcast_convert_fusion) | copy-start | bytes 1540
  70.1 19.8 %copy-start.18 = (f32[128,128]{1,0:T(8,128)}, f32[128,128]{1,0:T(8,128)S(1)}, u32[]{:S(2)}) copy-start(f32[128,128]{1,0:T(8,128)S(1)} %get-tuple-element.147) | copy-start | bytes 196612
  70.1 19.8 %copy-start.20 = (f32[128,128]{1,0:T(8,128)}, f32[128,128]{1,0:T(8,128)S(1)}, u32[]{:S(2)}) copy-start(f32[128,128]{1,0:T(8,128)S(1)} %get-tuple-element.148) | copy-start | bytes 196612
  97.0 19.2 %copy-start.3 = (f32[128,1152]{1,0:T(8,128)}, f32[128,1152]{1,0:T(8,128)S(1)}, u32[]{:S(2)}) copy-start(f32[128,1152]{1,0:T(8,128)S(1)} %get-tuple-element.119.middle_ref) | copy-start | bytes 1769476
  255.5 109.1 %reduce-scatter.5.cloned.1.call-start = ((), (), s32[]{:S(2)}) async-start(), calls=%async_computation.5 | async-start | bytes 4644864 | tf_op jit(solution)/shard_map/reduce_scatter | solution.py:1132
  256.1 2.2 copy-start.4
  260.9 2.8 copy-start.14
  260.9 2.8 copy-start.26
  260.9 2.8 copy-start.28
  260.9 2.8 copy-start.49
  271.1 26.1 %copy-start.51 = (f32[128]{0:T(128)S(1)}, f32[128]{0:T(128)}, u32[]{:S(2)}) copy-start(f32[128]{0:T(128)} %copy-done.50) | copy-start | bytes 1540
  271.1 26.1 %copy-start.53 = (f32[128]{0:T(128)S(1)}, f32[128]{0:T(128)}, u32[]{:S(2)}) copy-start(f32[128]{0:T(128)} %copy-done.52) | copy-start | bytes 1540
  297.1 2.2 copy-start.15
  297.2 2.1 copy-start.23
  297.2 2.5 copy-start.19
  297.2 2.5 copy-start.21
  300.9 2.5 copy-start.8
  322.6 2.3 copy-start.34
  322.6 2.3 copy-start.55
  322.6 2.3 copy-start.65
  433.1 10.9 %copy-start.32 = (bf16[128,1152]{1,0:T(8,128)(2,1)S(1)}, bf16[128,1152]{1,0:T(8,128)(2,1)}, u32[]{:S(2)}) copy-start(bf16[128,1152]{1,0:T(8,128)(2,1)} %get-tuple-element.72) | copy-start | bytes 884740
  433.1 11.6 %copy-start.1 = (bf16[864,1152]{1,0:T(8,128)(2,1)S(1)}, bf16[864,1152]{1,0:T(8,128)(2,1)}, u32[]{:S(2)}) copy-start(bf16[864,1152]{1,0:T(8,128)(2,1)} %param.32) | copy-start | bytes 5971972
  (38 other events, 47.3 us)
Sparse Core Ops, SparseCore 0:
  11.3 95.1 all-gather.2
  108.8 51.0 all-gather.4
  255.7 59.2 reduce-scatter.2
  317.1 47.4 reduce-scatter.4

commit v9 on v8

--- a/solution.py
+++ b/solution.py
@@ -8,6 +8,7 @@
 from jax.sharding import PartitionSpec as P
 
 WINDOW = 512
+UP_FIRST = 512
 
 
 EPS = 1e-06
@@ -305,16 +306,17 @@
     out_ref[...] = jnp.dot(left_ref[...], right_ref[...], preferred_element_type=F32).astype(BF16)
 
 
-def product_low(tile, left, right):
+def product_low(tile, left, right, start=0, columns=None):
     rows, depth = left.shape
-    columns = right.shape[1]
+    columns = columns or right.shape[1]
+    skip = start // tile
     return pl.pallas_call(
         product_kernel,
         grid=(columns // tile,),
         out_shape=jax.ShapeDtypeStruct((rows, columns), BF16),
         in_specs=[
             pl.BlockSpec((rows, depth), lambda i: (0, 0)),
-            pl.BlockSpec((depth, tile), lambda i: (0, i)),
+            pl.BlockSpec((depth, tile), lambda i: (0, i + skip)),
         ],
         out_specs=pl.BlockSpec((rows, tile), lambda i: (0, i)),
         cost_estimate=pl.CostEstimate(
@@ -527,9 +529,24 @@
 
 
 def halo_back_kernel(
-    n_chip, source_ref, result_ref, near_ref, far_ref, way_ref, send_sem, recv_sem
+    n_chip,
+    source_ref,
+    shard_ref,
+    result_ref,
+    shards_ref,
+    near_ref,
+    far_ref,
+    way_ref,
+    send_sem,
+    recv_sem,
+    pass_sem,
+    take_sem,
+    own_sem,
 ):
     me = lax.axis_index("ctx")
+    spot = lax.axis_index("batch")
+    across = spot + 1 - 2 * lax.rem(spot, 2)
+    along = lax.rem(spot + 2, 4)
     chip, core = me // 2, lax.rem(me, 2)
     near = {"ctx": me + 1 - 2 * core}
     before = {"ctx": jnp.maximum(me - 2, 0)}
@@ -542,7 +559,21 @@
         after = {"ctx": jnp.minimum(me + 2, 2 * n_chip - 1)}
         pl.semaphore_signal(barrier, inc=1, device_id=after, device_id_type=MESH)
 
-    pl.semaphore_wait(barrier, 1 + jnp.minimum(chip, 1))
+    for peer in (across, along):
+        pl.semaphore_signal(barrier, inc=1, device_id={"batch": peer}, device_id_type=MESH)
+    pl.semaphore_wait(barrier, 3 + jnp.minimum(chip, 1))
+
+    def beside(source, target, turn, peer):
+        copy = pltpu.make_async_remote_copy(
+            src_ref=source,
+            dst_ref=target,
+            send_sem=pass_sem.at[turn],
+            recv_sem=take_sem.at[turn],
+            device_id={"batch": peer},
+            device_id_type=MESH,
+        )
+        copy.start()
+        return copy
 
     def remote(source, target, turn, peer):
         return pltpu.make_async_remote_copy(
@@ -558,6 +589,12 @@
     to_other = remote(source_ref.at[1 + 2 * core], near_ref.at[1], 1, near)
     to_before.start()
     to_other.start()
+    firsts = [
+        beside(shard_ref, shards_ref.at[spot], turn, peer)
+        for turn, peer in enumerate((across, along))
+    ]
+    own = pltpu.make_async_copy(shard_ref, shards_ref.at[spot], own_sem.at[0])
+    own.start()
 
     @pl.when((chip == 0) | jnp.logical_not(has_after))
     def _():
@@ -590,13 +627,25 @@
     def _():
         one_back.start()
 
+    columns = shard_ref.shape[-1]
+    cut = columns // 256 * 128
+    halves = (pl.ds(0, cut), pl.ds(cut, columns - cut))
+    seconds = []
+    for turn, (giver, taker) in enumerate(((across, along), (along, across))):
+        firsts[turn].wait_recv()
+        block = shards_ref.at[giver, :, halves[turn]]
+        seconds.append(beside(block, block, 2 + turn, taker))
+
     @pl.when(has_after)
     def _():
         one_back.wait_recv()
 
     result_ref[...] = way_ref[1].astype(F32) + jnp.where(core == 0, theirs, 0.0)
-    to_before.wait_send()
-    to_other.wait_send()
+    own.wait()
+    for copy in seconds:
+        copy.wait()
+    for copy in firsts + [to_before, to_other]:
+        copy.wait_send()
 
     @pl.when(chip > 1)
     def _():
@@ -607,28 +656,33 @@
         one_back.wait_send()
 
 
-def halo_call(collective_id, kernel, n_ctx, block, out_shape, buffers, copies):
+def halo_call(collective_id, kernel, n_ctx, arrays, out_shape, buffers, counts):
     dma = pltpu.SemaphoreType.DMA
+    vmem = pl.BlockSpec(memory_space=pltpu.VMEM)
     return pl.pallas_call(
         functools.partial(kernel, n_ctx // 2),
         out_shape=out_shape,
-        in_specs=[pl.BlockSpec(memory_space=pltpu.VMEM)],
-        out_specs=pl.BlockSpec(memory_space=pltpu.VMEM),
-        scratch_shapes=[*buffers, dma((copies,)), dma((copies,))],
+        in_specs=[vmem] * len(arrays),
+        out_specs=[vmem] * len(out_shape),
+        scratch_shapes=[*buffers, *(dma((count,)) for count in counts)],
         compiler_params=pltpu.CompilerParams(collective_id=collective_id, has_side_effects=True),
-    )(block)
+    )(*arrays)
 
 
 def halo_out(n_ctx, block):
-    out_shape = jax.ShapeDtypeStruct((4, *block.shape), block.dtype)
-    return halo_call(1, halo_out_kernel, n_ctx, block, out_shape, (), 5)
-
-
-def halo_back(n_ctx, blocks):
+    out_shape = [jax.ShapeDtypeStruct((4, *block.shape), block.dtype)]
+    return halo_call(1, halo_out_kernel, n_ctx, (block,), out_shape, (), (5, 5))[0]
+
+
+def halo_back(n_ctx, blocks, shard):
     shape = blocks.shape[1:]
     buffers = [pltpu.VMEM((2, *shape), blocks.dtype)] * 3
-    out_shape = jax.ShapeDtypeStruct(shape, F32)
-    return halo_call(6, halo_back_kernel, n_ctx, blocks, out_shape, buffers, 4)
+    out_shape = [
+        jax.ShapeDtypeStruct(shape, F32),
+        jax.ShapeDtypeStruct((4, *shard.shape), shard.dtype),
+    ]
+    counts = (4, 4, 4, 4, 1)
+    return halo_call(6, halo_back_kernel, n_ctx, (blocks, shard), out_shape, buffers, counts)
 
 
 def pick_kernel(n_batch, n_ctx, piece, padded, gate_ref, up_ref, out_ref):
@@ -873,11 +927,10 @@
 def tail_kernel(
     n_ctx,
     gate_ref,
-    down_ref,
+    first_ref,
     up_ref,
     attn_ref,
     gate_all,
-    down_all,
     up_all,
     attn_all,
     pair_up,
@@ -929,6 +982,8 @@
         (up_ref, pair_up, way_up, up_all, pl.ds(cut, width - cut)),
         (attn_ref, pair_attn, way_attn, attn_all, pl.ds(0, attn_ref.shape[-1])),
     )
+    offset = first_ref.shape[-1]
+    spread_columns = (pl.ds(offset, cut), pl.ds(offset + cut, width - cut), chains[2][4])
     numbers = range(len(chains))
 
     def pair_copy(number, place):
@@ -986,14 +1041,16 @@
     for number in numbers:
         for place in range(n_chip):
             pair_copy(number, place).start()
-    early = ((gate_ref, gate_all), (down_ref, down_all))
+    early = ((gate_ref, gate_all), (first_ref, up_all))
     side_firsts = []
     for item, (source, target) in enumerate(early):
         side_firsts.append(side_pair(item, source, target, pl.ds(0, source.shape[-1])))
         for copy in side_firsts[-1]:
             copy.start()
     own = [
-        pltpu.make_async_copy(source, target.at[spot], own_sem.at[item])
+        pltpu.make_async_copy(
+            source, target.at[spot, :, pl.ds(0, source.shape[-1])], own_sem.at[item]
+        )
         for item, (source, target) in enumerate(early)
     ]
     for copy in own:
@@ -1026,8 +1083,8 @@
     for step in range(2, n_chip + 1):
         if step <= 3:
             item = step - 2
-            target = early[item][1]
-            side_seconds += side_pass(item, side_firsts[item], target, 0, target.shape[-1])
+            source, target = early[item]
+            side_seconds += side_pass(item, side_firsts[item], target, 0, source.shape[-1])
         if step == n_chip:
             break
         for number in numbers:
@@ -1063,19 +1120,20 @@
             def _():
                 way_copy(number, direction, n_chip - 1, pair.at[0, :, columns]).wait_recv()
 
-        target[spot, :, columns] = (
+        spread = spread_columns[number]
+        target[spot, :, spread] = (
             pair[chip, :, columns].astype(F32)
             + way[0, n_chip - 2, :, columns].astype(F32)
             + way[1, n_chip - 2, :, columns].astype(F32)
         ).astype(BF16)
-        firsts = side_pair(2 + number, target.at[spot, :, columns], target, columns)
+        firsts = side_pair(2 + number, target.at[spot, :, spread], target, spread)
         for copy in firsts:
             copy.start()
         chain_firsts.append(firsts)
     for number in numbers:
-        _, _, _, target, columns = chains[number]
+        target, spread = chains[number][3], spread_columns[number]
         side_seconds += side_pass(
-            2 + number, chain_firsts[number], target, columns.start, columns.size
+            2 + number, chain_firsts[number], target, spread.start, spread.size
         )
     for copy in own:
         copy.wait()
@@ -1096,17 +1154,18 @@
                     way_copy(number, direction, step, pair.at[0, :, columns]).wait_send()
 
 
-def tail_round(n_ctx, gate, down, up, attn):
+def tail_round(n_ctx, gate, first, up, attn):
     n_chip = n_ctx // 2
     dma = pltpu.SemaphoreType.DMA
     vmem = pl.BlockSpec(memory_space=pltpu.VMEM)
-    shapes = (gate.shape, down.shape, up.shape[1:], attn.shape[1:])
+    up_shape = (up.shape[1], first.shape[1] + up.shape[2])
+    shapes = (gate.shape, up_shape, attn.shape[1:])
     return pl.pallas_call(
         functools.partial(tail_kernel, n_ctx),
         name="tail_round",
         out_shape=[jax.ShapeDtypeStruct((4, *shape), BF16) for shape in shapes],
         in_specs=[vmem] * 4,
-        out_specs=[vmem] * 4,
+        out_specs=[vmem] * 3,
         scratch_shapes=[
             pltpu.VMEM((n_chip, *up.shape[1:]), BF16),
             pltpu.VMEM((n_chip, *attn.shape[1:]), BF16),
@@ -1121,7 +1180,7 @@
             dma((2,)),
         ],
         compiler_params=pltpu.CompilerParams(collective_id=8, has_side_effects=True),
-    )(gate, down, up, attn)
+    )(gate, first, up, attn)
 
 
 def gathered(shard):
@@ -1278,8 +1337,12 @@
         (back_parts, grad_gate_low, grad_up_low)
     )
     gate_grad = product_low(256, ffn_in_turned, grad_gate_low)
-    up_grad = product_low(256, ffn_in_turned, grad_up_low)
-    back_parts, gate_grad, up_grad = lax.optimization_barrier((back_parts, gate_grad, up_grad))
+    up_first = product_low(256, ffn_in_turned, grad_up_low, 0, UP_FIRST)
+    up_grad = product_low(256, ffn_in_turned, grad_up_low, UP_FIRST, hidden_part - UP_FIRST)
+    back_parts, gate_grad, up_first, up_grad = lax.optimization_barrier(
+        (back_parts, gate_grad, up_first, up_grad)
+    )
+    grad_up_first = scattered(up_first)
     grad_w_gate = scattered(gate_grad)
     grad_ffn_in = jnp.sum(back_parts.astype(F32), axis=0)
     _, pull_ffn_norm = jax.vjp(normed, middle, full_gain_ffn)
@@ -1306,9 +1369,10 @@
     grad_ctx_values = jnp.einsum("htk,thd->kd", prob_low, grad_attended, preferred_element_type=F32)
     grad_context = jnp.concatenate([grad_ctx_keys, grad_ctx_values], axis=-1)
     halo_rows = halo_depth * tok_count
-    returned = halo_back(
+    returned, down_all = halo_back(
         n_ctx,
         grad_context[:halo_rows].astype(BF16).reshape(halo_depth, tok_count, 2 * head_size),
+        grad_w_down,
     )
     own_grad = grad_context[halo_rows:] + returned
     grad_value_low = own_grad[:, head_size:].astype(BF16)
@@ -1378,11 +1442,11 @@
         ],
         axis=1,
     )
-    gate_all, down_all, up_all, attn_grads = tail_round(
+    gate_all, up_all, attn_grads = tail_round(
         n_ctx,
         grad_w_gate,
-        grad_w_down,
-        up_grad.reshape(n_ctx, width_shard, hidden_part),
+        grad_up_first,
+        up_grad.reshape(n_ctx, width_shard, hidden_part - UP_FIRST),
         packed,
     )
     shapes = (

time: 459 us -> 426 us (0.928)
  waiting for transfers between devices: 43.3 us -> 21.3 us
  Pallas kernels: 332 us -> 321 us
    reduce_scatter x2 -> x3, waiting for transfers between devices: 34.7 us -> 11.9 us  [scattered(): return lax.psum_scatter(whole, 'ctx', scatter_dimension=0, tiled=True)]
    pallas_call x1, Pallas kernels: 68.5 us -> 58.2 us  [tail_round(): pl.pallas_call(functools.partial(tail_kernel, n_ctx), name='tail_round',...]
    pallas_call x3 -> x4, Pallas kernels: 21.6 us -> 23.2 us  [product_low(): pl.pallas_call(product_kernel, grid=(columns // tile,), out_shape=jax.Sha...]
  transfers between devices with their start and end apart: 4 -> 5, of which waited for: 2 -> 2; matrix products, arithmetic and copies ran while one was open for 12% -> 13% of each run, Pallas kernels for 34% -> 49%
where the time goes in v9:
time: 426 us; the launch traced here: 421 us
  Pallas kernels  321 us (75%)
  local copies, waits for them, and re-layouts  24.3 us (6%)
  matrix products  21.9 us (5%)
  waiting for transfers between devices  21.3 us (5%)
  other arithmetic  16 us (4%)
  between operations  15.5 us (4%)
    pallas_call x1, Pallas kernels, tail_round(): pl.pallas_call(functools.partial(tail_kernel, n_ctx), name='tail_round',...  58.2 us
    pallas_call x1, Pallas kernels, gather_weights(): pl.pallas_call(functools.partial(weights_kernel, n_batch, n_ctx), name='g...  48.4 us
    pallas_call x2, Pallas kernels, halo_call(): pl.pallas_call(functools.partial(kernel, n_ctx // 2), out_shape=out_shape...  42 us
    pallas_call x2, Pallas kernels, square_gather(): pl.pallas_call(functools.partial(square_kernel, count), out_shape=[jax.Sh...  37.8 us
    pallas_call x1, Pallas kernels, turn_round(): pl.pallas_call(turn_kernel, name='turn_round', out_shape=(jax.ShapeDtypeS...  36.5 us
    pallas_call x2, Pallas kernels, batch_exchange(): pl.pallas_call(functools.partial(batch_kernel, size, kinds), out_shape=sh...  29.5 us
    pallas_call x4, Pallas kernels, product_low(): pl.pallas_call(product_kernel, grid=(columns // tile,), out_shape=jax.Sha...  23.2 us
    pallas_call x1, Pallas kernels, hidden_back(): pl.pallas_call(back_kernel, name='hidden_back', grid=(count,), out_shape=...  21.2 us
  transfers between devices with their start and end apart: 5, of which 2 were waited for; matrix products, arithmetic and copies ran while one was open for 13% of the time, Pallas kernels for 49%

profile of v9, /device:TPU:0, one launch (start us, length us, event | category | flops | bytes accessed | tf_op | source)
XLA Modules:
  0.0 420.6 jit_solution(6198424918041250964)
XLA Ops:
  7.2 3.9 pick_columns.1
  13.9 48.4 %gather_weights.1 = (bf16[4,8,144,384]{3,2,1,0:T(8,128)(2,1)}, bf16[8,4,32,1152]{3,2,1,0:T(8,128)(2,1)}, bf16[8,1,640]{2,1,0:T(2,128)(2,1)}) custom-call(bf16[4,144,384]{2,1,0:T(8,128)(2,1)} %bitcast.205, bf16[4,32,1152]{2,1,0:T(8,128)(2,1)} %bitcast.218, bf16[1,640]{1,0:T(2,128)(2,1)} %broadcast_in_dim.32.gain_ref), custom_call_target="tpu_custom_call" | custom-call | tf_op jit(solution)/shard_map/gather_weights/pallas_call | solution.py:904
  63.3 2.3 fusion.91
  70.2 17.5 %shard_map.280 = bf16[4,128,512]{2,1,0:T(8,128)(2,1)} custom-call(bf16[128,512]{1,0:T(8,128)(2,1)} %pad_maximum_fusion.9.source_ref), custom_call_target="tpu_custom_call" | custom-call | tf_op jit(solution)/shard_map/pallas_call | solution.py:662
  89.4 1.6 fusion.96
  92.9 2.3 multiply_reduce_fusion.6
  97.1 16.1 %shard_map.281 = bf16[4,128,1152]{2,1,0:T(8,128)(2,1)} custom-call(bf16[128,1152]{1,0:T(8,128)(2,1)} %multiply_convert_fusion.1.refs_0_), custom_call_target="tpu_custom_call" | custom-call | tf_op jit(solution)/shard_map/pallas_call | solution.py:172
  113.1 2.4 copy.191
  117.5 11.8 %hidden_mix.1 = (f32[512,1792]{1,0:T(8,128)}, f32[512,1792]{1,0:T(8,128)}, bf16[512,1792]{1,0:T(8,128)(2,1)}, bf16[1792,512]{1,0:T(8,128)(2,1)}) custom-call(bf16[512,1152]{1,0:T(8,128)(2,1)} %bitcast.184, bf16[1152,3584]{1,0:T(8,128)(2,1)} %all-gather.3.cloned.1.call-done.w_gate_ref.w_up_ref, bf16[1152,3584]{1,0:T(8,128)(2,1)} %all-gather.3.cloned.1.call-done.w_gate_ref.w_up_ref), custom_call_target="tpu_custom_call" | custom-call | flops 4227858432 | bytes 25165824 | tf_op jit(solution)/shard_map/hidden_mix/pallas_call | solution.py:344
  129.3 21.7 %shard_map.282 = (bf16[4,128,1152]{2,1,0:T(8,128)(2,1)}, bf16[4,128,1024]{2,1,0:T(8,128)(2,1)}) custom-call(bf16[128,1152]{1,0:T(8,128)(2,1)} %get-tuple-element.68.refs_0_, bf16[128,1024]{1,0:T(8,128)(2,1)} %copy.190.refs_1_), custom_call_target="tpu_custom_call" | custom-call | tf_op jit(solution)/shard_map/pallas_call | solution.py:172
  151.1 8.8 %all-gather.5.cloned.1.call-done.down_ref = bf16[1792,1152]{1,0:T(8,128)(2,1)} async-done(((bf16[224,1152]{1,0:T(8,128)(2,1)}), bf16[1792,1152]{1,0:T(8,128)(2,1)}) %all-gather.5.cloned.1.call-update) | async-done | bytes 4128784 | tf_op jit(solution)/shard_map/all_gather | solution.py:1187
  159.8 36.5 %turn_round.1 = (bf16[128,1152]{1,0:T(8,128)(2,1)}, bf16[4,128,1152]{2,1,0:T(8,128)(2,1)}, f32[1,1152]{1,0:T(1,128)}) custom-call(bf16[512,1792]{1,0:T(8,128)(2,1)} %get-tuple-element.73.mixed_ref, bf16[1792,1152]{1,0:T(8,128)(2,1)} %all-gather.5.cloned.1.call-done.down_ref, f32[128,1152]{1,0:T(8,128)} %copy-done.3, bf16[128,1152]{1,0:T(8,128)(2,1)} %bitcast.217, ...), custom_call_target="tpu_custom_call" | custom-call | flops 2113929216 | bytes 8388608 | tf_op jit(solution)/shard_map/turn_round/pallas_call | solution.py:282
  196.3 6.3 %shard_map.283 = bf16[1792,1152]{1,0:T(8,128)(2,1)} custom-call(bf16[1792,512]{1,0:T(8,128)(2,1)} %get-tuple-element.75.left_ref, bf16[512,1152]{1,0:T(8,128)(2,1)} %bitcast.210), custom_call_target="tpu_custom_call" | custom-call | flops 2113929216 | bytes 8388608 | tf_op jit(solution)/shard_map/pallas_call | solution.py:313
  203.0 21.2 %hidden_back.1 = (bf16[512,1792]{1,0:T(8,128)(2,1)}, bf16[512,1792]{1,0:T(8,128)(2,1)}, bf16[512,1152]{1,0:T(8,128)(2,1)}) custom-call(bf16[512,1152]{1,0:T(8,128)(2,1)} %bitcast.211, bf16[1792,1152]{1,0:T(8,128)(2,1)} %all-gather.5.cloned.1.call-done.down_ref, f32[512,1792]{1,0:T(8,128)} %get-tuple-element.78.gate_ref, ...), custom_call_target="tpu_custom_call" | custom-call | flops 6341787648 | bytes 25165824 | tf_op jit(solution)/shard_map/hidden_back/pallas_call | solution.py:396
  224.2 16.6 %shard_map.284 = bf16[4,128,1152]{2,1,0:T(8,128)(2,1)} custom-call(bf16[4,128,1152]{2,1,0:T(8,128)(2,1)} %bitcast.212), custom_call_target="tpu_custom_call" | custom-call | tf_op jit(solution)/shard_map/pallas_call | solution.py:102
  240.7 3.2 shard_map.286
  243.9 6.0 %shard_map.287 = bf16[1152,1280]{1,0:T(8,128)(2,1)} custom-call(bf16[1152,512]{1,0:T(8,128)(2,1)} %bitcast.186, bf16[512,1792]{1,0:T(8,128)(2,1)} %get-tuple-element.86.right_ref), custom_call_target="tpu_custom_call" | custom-call | flops 1509949440 | bytes 8388608 | tf_op jit(solution)/shard_map/pallas_call | solution.py:313
  249.9 7.6 %shard_map.285 = bf16[1152,1792]{1,0:T(8,128)(2,1)} custom-call(bf16[1152,512]{1,0:T(8,128)(2,1)} %bitcast.187, bf16[512,1792]{1,0:T(8,128)(2,1)} %get-tuple-element.85.right_ref), custom_call_target="tpu_custom_call" | custom-call | flops 2113929216 | bytes 8388608 | tf_op jit(solution)/shard_map/pallas_call | solution.py:313
  258.8 1.5 convert_reduce_fusion
  262.2 2.6 convolution_convert_fusion
  265.1 1.8 multiply_reduce_fusion
  272.6 3.0 convolution_bitcast_fusion.3
  280.0 24.5 %shard_map.288 = (f32[128,512]{1,0:T(8,128)}, bf16[4,224,1152]{2,1,0:T(8,128)(2,1)}) custom-call(bf16[4,128,512]{2,1,0:T(8,128)(2,1)} %bitcast.203, bf16[224,1152]{1,0:T(8,128)(2,1)} %reduce-scatter.4.cloned.1.call-done.shard_ref), custom_call_target="tpu_custom_call" | custom-call | tf_op jit(solution)/shard_map/pallas_call | solution.py:662
  307.8 1.9 copy.171
  310.2 1.5 fusion.23
  312.5 12.9 %shard_map.289 = (f32[4,8,640]{2,1,0:T(8,128)}, bf16[4,128,384]{2,1,0:T(8,128)(2,1)}, bf16[4,128,288]{2,1,0:T(8,128)(2,1)}) custom-call(f32[8,640]{1,0:T(8,128)} %concatenate.54.refs_0_, bf16[4,128,384]{2,1,0:T(8,128)(2,1)} %bitcast.207, bf16[4,128,288]{2,1,0:T(8,128)(2,1)} %bitcast.209), custom_call_target="tpu_custom_call" | custom-call | tf_op jit(solution)/shard_map/pallas_call | solution.py:102
  325.5 1.5 fusion.11
  327.4 2.2 fusion.3
  329.7 1.8 fusion.6.attn_ref
  331.5 11.9 %reduce-scatter.6.cloned.1.call-done.gate_ref = bf16[144,1792]{1,0:T(8,128)(2,1)} async-done(((bf16[1152,1792]{1,0:T(8,128)(2,1)}), bf16[144,1792]{1,0:T(8,128)(2,1)}) %reduce-scatter.6.cloned.1.call-update) | async-done | bytes 516112 | tf_op jit(solution)/shard_map/reduce_scatter | solution.py:1191
  343.4 58.2 %tail_round.1 = (bf16[4,144,1792]{2,1,0:T(8,128)(2,1)}, bf16[4,144,1792]{2,1,0:T(8,128)(2,1)}, bf16[4,288,384]{2,1,0:T(8,128)(2,1)}) custom-call(bf16[144,1792]{1,0:T(8,128)(2,1)} %reduce-scatter.6.cloned.1.call-done.gate_ref, bf16[144,512]{1,0:T(8,128)(2,1)} %reduce-scatter.8.cloned.1.call-done.first_ref, bf16[8,144,1280]{2,1,0:T(8,128)(2,1)} %bitcast.182, ...), custom_call_target="tpu_custom_call" | custom-call | tf_op jit(solution)/shard_map/tail_round/pallas_call | solution.py:1163
  401.6 8.9 %finish_round.1 = (f32[144,6912]{1,0:T(8,128)}, f32[144,6912]{1,0:T(8,128)}, f32[864,1152]{1,0:T(8,128)}, f32[144,1024]{1,0:T(8,128)}, f32[144,256]{1,0:T(8,128)...) custom-call(bf16[4,144,1792]{2,1,0:T(8,128)(2,1)} %get-tuple-element.99.gate_ref, ...), custom_call_target="tpu_custom_call" | custom-call | tf_op jit(solution)/shard_map/finish_round/pallas_call | solution.py:768
  (217 shorter events, 36.6 us)
Async XLA Ops:
  7.2 4.1 copy-start
  7.2 110.3 %all-gather.3.cloned.1.call-start = ((), (), s32[]{:S(2)}) async-start(), calls=%async_computation.3 | async-start | bytes 9289728 | tf_op jit(solution)/shard_map/all_gather | solution.py:1187
  11.2 148.6 %all-gather.5.cloned.1.call-start = ((), (), s32[]{:S(2)}) async-start(), calls=%async_computation.4 | async-start | bytes 4644864 | tf_op jit(solution)/shard_map/all_gather | solution.py:1187
  12.3 50.9 %copy-start.2 = (bf16[1,128,1152]{2,1,0:T(8,128)(2,1)S(1)}, bf16[1,128,1152]{2,1,0:T(8,128)(2,1)}, u32[]{:S(2)}) copy-start(bf16[1,128,1152]{2,1,0:T(8,128)(2,1)} %param.17) | copy-start | bytes 884740
  12.3 267.7 %reduce-scatter.4.cloned.1.call-start = ((), (), s32[]{:S(2)}) async-start(), calls=%async_computation.5 | async-start | bytes 4644864 | tf_op jit(solution)/shard_map/reduce_scatter | solution.py:1191
  63.3 2.3 copy-start.45
  69.1 19.9 %copy-start.18 = (f32[128,256]{1,0:T(8,128)}, f32[128,256]{1,0:T(8,128)S(1)}, u32[]{:S(2)}) copy-start(f32[128,256]{1,0:T(8,128)S(1)} %get-tuple-element.125) | copy-start | bytes 393220
  69.5 19.8 %copy-start.25 = (f32[128,128]{1,0:T(8,128)}, f32[128,128]{1,0:T(8,128)S(1)}, u32[]{:S(2)}) copy-start(f32[128,128]{1,0:T(8,128)S(1)} %get-tuple-element.151) | copy-start | bytes 196612
  69.6 19.8 %copy-start.27 = (f32[128,128]{1,0:T(8,128)}, f32[128,128]{1,0:T(8,128)S(1)}, u32[]{:S(2)}) copy-start(f32[128,128]{1,0:T(8,128)S(1)} %get-tuple-element.152) | copy-start | bytes 196612
  89.0 3.0 copy-start.20
  96.2 19.4 %copy-start.3 = (f32[128,1152]{1,0:T(8,128)}, f32[128,1152]{1,0:T(8,128)S(1)}, u32[]{:S(2)}) copy-start(f32[128,1152]{1,0:T(8,128)S(1)} %get-tuple-element.123.middle_ref) | copy-start | bytes 1769476
  202.7 128.8 %reduce-scatter.8.cloned.1.call-start = ((), (), s32[]{:S(2)}) async-start(), calls=%async_computation.7 | async-start | bytes 1327104 | tf_op jit(solution)/shard_map/reduce_scatter | solution.py:1191
  257.6 85.8 %reduce-scatter.6.cloned.1.call-start = ((), (), s32[]{:S(2)}) async-start(), calls=%async_computation.6 | async-start | bytes 4644864 | tf_op jit(solution)/shard_map/reduce_scatter | solution.py:1191
  258.2 2.2 copy-start.4
  262.2 2.8 copy-start.21
  268.9 2.6 copy-start.42
  272.6 3.0 copy-start.31
  272.6 3.0 copy-start.33
  276.7 2.0 copy-start.11
  276.7 2.0 copy-start.8
  278.7 25.8 %copy-start.16 = (f32[640,256]{1,0:T(8,128)S(1)}, f32[640,256]{1,0:T(8,128)}, u32[]{:S(2)}) copy-start(f32[640,256]{1,0:T(8,128)} %convolution_bitcast_fusion.3) | copy-start | bytes 1966084
  280.0 24.6 %copy-start.12 = (f32[640,256]{1,0:T(8,128)S(1)}, f32[640,256]{1,0:T(8,128)}, u32[]{:S(2)}) copy-start(f32[640,256]{1,0:T(8,128)} %copy-done.11) | copy-start | bytes 1966084
  305.6 4.1 copy-start.29
  305.6 4.1 copy-start.6
  305.6 4.1 copy-start.17
  310.2 15.3 %copy-start.24 = (bf16[4,128,1024]{2,1,0:T(8,128)(2,1)S(1)}, bf16[4,128,1024]{2,1,0:T(8,128)(2,1)}, u32[]{:S(2)}) copy-start(bf16[4,128,1024]{2,1,0:T(8,128)(2,1)} %get-tuple-element.96) | copy-start | bytes 3145732
  325.4 1.9 copy-start.38
  327.4 2.2 copy-start.43
  401.5 10.9 %copy-start.46 = (f32[128]{0:T(128)S(1)}, f32[128]{0:T(128)}, u32[]{:S(2)}) copy-start(f32[128]{0:T(128)} %copy-done.45) | copy-start | bytes 1540
  401.6 10.9 %copy-start.14 = (f32[128,1152]{1,0:T(8,128)S(1)}, f32[128,1152]{1,0:T(8,128)}, u32[]{:S(2)}) copy-start(f32[128,1152]{1,0:T(8,128)} %copy-done.13) | copy-start | bytes 1769476
  401.6 12.5 %copy-start.1 = (bf16[864,1152]{1,0:T(8,128)(2,1)S(1)}, bf16[864,1152]{1,0:T(8,128)(2,1)}, u32[]{:S(2)}) copy-start(bf16[864,1152]{1,0:T(8,128)(2,1)} %param.32) | copy-start | bytes 5971972
  411.2 2.2 copy-start.36
  (27 other events, 34.1 us)
Sparse Core Ops, SparseCore 0:
  11.3 95.1 all-gather.2
  108.8 51.0 all-gather.4
  202.8 50.9 reduce-scatter.3
  257.7 36.1 reduce-scatter.7
  296.0 47.2 reduce-scatter.5

commit v10 on v9

--- a/solution.py
+++ b/solution.py
@@ -418,6 +418,31 @@
     )(upstream, down, gate_pre, up_pre, both_weights, both_weights)
 
 
+def product_pair_kernel(split, left_ref, first_ref, second_ref, out_ref):
+    right = jnp.where(pl.program_id(0) < split, first_ref[...], second_ref[...])
+    out_ref[...] = jnp.dot(left_ref[...], right, preferred_element_type=F32).astype(BF16)
+
+
+def product_pair(tile, left, first, second, columns):
+    rows, depth = left.shape
+    split = first.shape[1] // tile
+    steps = split + columns // tile
+    return pl.pallas_call(
+        functools.partial(product_pair_kernel, split),
+        grid=(steps,),
+        out_shape=jax.ShapeDtypeStruct((rows, steps * tile), BF16),
+        in_specs=[
+            pl.BlockSpec((rows, depth), lambda i: (0, 0)),
+            pl.BlockSpec((depth, tile), lambda i: (0, jnp.minimum(i, split - 1))),
+            pl.BlockSpec((depth, tile), lambda i: (0, jnp.maximum(i - split, 0))),
+        ],
+        out_specs=pl.BlockSpec((rows, tile), lambda i: (0, i)),
+        cost_estimate=pl.CostEstimate(
+            flops=2 * rows * depth * steps * tile, bytes_accessed=10 << 20, transcendentals=0
+        ),
+    )(left, first, second)
+
+
 def halo_out_kernel(n_chip, source_ref, result_ref, send_sem, recv_sem):
     me = lax.axis_index("ctx")
     chip, core = me // 2, lax.rem(me, 2)
@@ -926,8 +951,7 @@
 
 def tail_kernel(
     n_ctx,
-    gate_ref,
-    first_ref,
+    both_ref,
     up_ref,
     attn_ref,
     gate_all,
@@ -982,7 +1006,8 @@
         (up_ref, pair_up, way_up, up_all, pl.ds(cut, width - cut)),
         (attn_ref, pair_attn, way_attn, attn_all, pl.ds(0, attn_ref.shape[-1])),
     )
-    offset = first_ref.shape[-1]
+    gate_width = gate_all.shape[-1]
+    offset = both_ref.shape[-1] - gate_width
     spread_columns = (pl.ds(offset, cut), pl.ds(offset + cut, width - cut), chains[2][4])
     numbers = range(len(chains))
 
@@ -1041,7 +1066,10 @@
     for number in numbers:
         for place in range(n_chip):
             pair_copy(number, place).start()
-    early = ((gate_ref, gate_all), (first_ref, up_all))
+    early = (
+        (both_ref.at[:, pl.ds(0, gate_width)], gate_all),
+        (both_ref.at[:, pl.ds(gate_width, offset)], up_all),
+    )
     side_firsts = []
     for item, (source, target) in enumerate(early):
         side_firsts.append(side_pair(item, source, target, pl.ds(0, source.shape[-1])))
@@ -1154,17 +1182,17 @@
                     way_copy(number, direction, step, pair.at[0, :, columns]).wait_send()
 
 
-def tail_round(n_ctx, gate, first, up, attn):
+def tail_round(n_ctx, hidden, both, up, attn):
     n_chip = n_ctx // 2
     dma = pltpu.SemaphoreType.DMA
     vmem = pl.BlockSpec(memory_space=pltpu.VMEM)
-    up_shape = (up.shape[1], first.shape[1] + up.shape[2])
-    shapes = (gate.shape, up_shape, attn.shape[1:])
+    wide = (up.shape[1], hidden)
+    shapes = (wide, wide, attn.shape[1:])
     return pl.pallas_call(
         functools.partial(tail_kernel, n_ctx),
         name="tail_round",
         out_shape=[jax.ShapeDtypeStruct((4, *shape), BF16) for shape in shapes],
-        in_specs=[vmem] * 4,
+        in_specs=[vmem] * 3,
         out_specs=[vmem] * 3,
         scratch_shapes=[
             pltpu.VMEM((n_chip, *up.shape[1:]), BF16),
@@ -1180,7 +1208,7 @@
             dma((2,)),
         ],
         compiler_params=pltpu.CompilerParams(collective_id=8, has_side_effects=True),
-    )(gate, first, up, attn)
+    )(both, up, attn)
 
 
 def gathered(shard):
@@ -1336,14 +1364,10 @@
     back_parts, grad_gate_low, grad_up_low = lax.optimization_barrier(
         (back_parts, grad_gate_low, grad_up_low)
     )
-    gate_grad = product_low(256, ffn_in_turned, grad_gate_low)
-    up_first = product_low(256, ffn_in_turned, grad_up_low, 0, UP_FIRST)
+    both_grad = product_pair(256, ffn_in_turned, grad_gate_low, grad_up_low, UP_FIRST)
     up_grad = product_low(256, ffn_in_turned, grad_up_low, UP_FIRST, hidden_part - UP_FIRST)
-    back_parts, gate_grad, up_first, up_grad = lax.optimization_barrier(
-        (back_parts, gate_grad, up_first, up_grad)
-    )
-    grad_up_first = scattered(up_first)
-    grad_w_gate = scattered(gate_grad)
+    back_parts, both_grad, up_grad = lax.optimization_barrier((back_parts, both_grad, up_grad))
+    grad_w_both = scattered(both_grad)
     grad_ffn_in = jnp.sum(back_parts.astype(F32), axis=0)
     _, pull_ffn_norm = jax.vjp(normed, middle, full_gain_ffn)
     grad_middle_part, grad_gain_ffn = pull_ffn_norm(grad_ffn_in)
@@ -1444,8 +1468,8 @@
     )
     gate_all, up_all, attn_grads = tail_round(
         n_ctx,
-        grad_w_gate,
-        grad_up_first,
+        hidden_part,
+        grad_w_both,
         up_grad.reshape(n_ctx, width_shard, hidden_part - UP_FIRST),
         packed,
     )

time: 426 us -> 414 us (0.972)
  waiting for transfers between devices: 21.3 us -> 8.41 us
    reduce_scatter x3 -> x2, waiting for transfers between devices: 11.9 us -> 0.01 us  [scattered(): return lax.psum_scatter(whole, 'ctx', scatter_dimension=0, tiled=True)]
    pallas_call x4 -> x2, Pallas kernels: 23.2 us -> 12.3 us  [product_low(): pl.pallas_call(product_kernel, grid=(columns // tile,), out_shape=jax.Sha...]
    pallas_call x0 -> x1, Pallas kernels: none -> 9.49 us  [product_pair(): pl.pallas_call(functools.partial(product_pair_kernel, split), grid=(steps...]
  transfers between devices with their start and end apart: 5 -> 4, of which waited for: 2 -> 1; matrix products, arithmetic and copies ran while one was open for 13% -> 13% of each run, Pallas kernels for 49% -> 52%
where the time goes in v10:
time: 414 us; the launch traced here: 407 us
  Pallas kernels  322 us (78%)
  matrix products  23.4 us (6%)
  local copies, waits for them, and re-layouts  22.3 us (5%)
  between operations  15.7 us (4%)
  other arithmetic  14.5 us (4%)
  waiting for transfers between devices  8.41 us (2%)
    pallas_call x1, Pallas kernels, tail_round(): pl.pallas_call(functools.partial(tail_kernel, n_ctx), name='tail_round',...  56.3 us
    pallas_call x1, Pallas kernels, gather_weights(): pl.pallas_call(functools.partial(weights_kernel, n_batch, n_ctx), name='g...  48.3 us
    pallas_call x2, Pallas kernels, halo_call(): pl.pallas_call(functools.partial(kernel, n_ctx // 2), out_shape=out_shape...  45 us
    pallas_call x2, Pallas kernels, square_gather(): pl.pallas_call(functools.partial(square_kernel, count), out_shape=[jax.Sh...  37.2 us
    pallas_call x1, Pallas kernels, turn_round(): pl.pallas_call(turn_kernel, name='turn_round', out_shape=(jax.ShapeDtypeS...  36.4 us
    pallas_call x2, Pallas kernels, batch_exchange(): pl.pallas_call(functools.partial(batch_kernel, size, kinds), out_shape=sh...  31 us
    pallas_call x1, Pallas kernels, hidden_back(): pl.pallas_call(back_kernel, name='hidden_back', grid=(count,), out_shape=...  21 us
    pallas_call x2, Pallas kernels, product_low(): pl.pallas_call(product_kernel, grid=(columns // tile,), out_shape=jax.Sha...  12.3 us
  transfers between devices with their start and end apart: 4, of which 1 were waited for; matrix products, arithmetic and copies ran while one was open for 13% of the time, Pallas kernels for 52%

profile of v10, /device:TPU:0, one launch (start us, length us, event | category | flops | bytes accessed | tf_op | source)
XLA Modules:
  0.0 406.8 jit_solution(4876480598031500035)
XLA Ops:
  7.2 3.9 pick_columns.1
  13.9 48.3 %gather_weights.1 = (bf16[4,8,144,384]{3,2,1,0:T(8,128)(2,1)}, bf16[8,4,32,1152]{3,2,1,0:T(8,128)(2,1)}, bf16[8,1,640]{2,1,0:T(2,128)(2,1)}) custom-call(bf16[4,144,384]{2,1,0:T(8,128)(2,1)} %bitcast.204, bf16[4,32,1152]{2,1,0:T(8,128)(2,1)} %bitcast.217, bf16[1,640]{1,0:T(2,128)(2,1)} %broadcast_in_dim.32.gain_ref), custom_call_target="tpu_custom_call" | custom-call | tf_op jit(solution)/shard_map/gather_weights/pallas_call | solution.py:929
  63.3 2.3 fusion.91
  70.7 17.5 %shard_map.280 = bf16[4,128,512]{2,1,0:T(8,128)(2,1)} custom-call(bf16[128,512]{1,0:T(8,128)(2,1)} %pad_maximum_fusion.9.source_ref), custom_call_target="tpu_custom_call" | custom-call | tf_op jit(solution)/shard_map/pallas_call | solution.py:687
  88.5 1.1 maximum_maximum_fusion
  90.0 1.7 fusion.96
  93.6 2.3 multiply_reduce_fusion.6
  97.8 15.9 %shard_map.281 = bf16[4,128,1152]{2,1,0:T(8,128)(2,1)} custom-call(bf16[128,1152]{1,0:T(8,128)(2,1)} %multiply_convert_fusion.1.refs_0_), custom_call_target="tpu_custom_call" | custom-call | tf_op jit(solution)/shard_map/pallas_call | solution.py:172
  113.8 2.4 copy.191
  118.1 12.1 %hidden_mix.1 = (f32[512,1792]{1,0:T(8,128)}, f32[512,1792]{1,0:T(8,128)}, bf16[512,1792]{1,0:T(8,128)(2,1)}, bf16[1792,512]{1,0:T(8,128)(2,1)}) custom-call(bf16[512,1152]{1,0:T(8,128)(2,1)} %bitcast.184, bf16[1152,3584]{1,0:T(8,128)(2,1)} %all-gather.3.cloned.1.call-done.w_gate_ref.w_up_ref, bf16[1152,3584]{1,0:T(8,128)(2,1)} %all-gather.3.cloned.1.call-done.w_gate_ref.w_up_ref), custom_call_target="tpu_custom_call" | custom-call | flops 4227858432 | bytes 25165824 | tf_op jit(solution)/shard_map/hidden_mix/pallas_call | solution.py:344
  130.2 21.3 %shard_map.282 = (bf16[4,128,1152]{2,1,0:T(8,128)(2,1)}, bf16[4,128,1024]{2,1,0:T(8,128)(2,1)}) custom-call(bf16[128,1152]{1,0:T(8,128)(2,1)} %get-tuple-element.67.refs_0_, bf16[128,1024]{1,0:T(8,128)(2,1)} %copy.190.refs_1_), custom_call_target="tpu_custom_call" | custom-call | tf_op jit(solution)/shard_map/pallas_call | solution.py:172
  151.5 8.3 %all-gather.5.cloned.1.call-done.down_ref = bf16[1792,1152]{1,0:T(8,128)(2,1)} async-done(((bf16[224,1152]{1,0:T(8,128)(2,1)}), bf16[1792,1152]{1,0:T(8,128)(2,1)}) %all-gather.5.cloned.1.call-update) | async-done | bytes 4128784 | tf_op jit(solution)/shard_map/all_gather | solution.py:1215
  159.8 36.4 %turn_round.1 = (bf16[128,1152]{1,0:T(8,128)(2,1)}, bf16[4,128,1152]{2,1,0:T(8,128)(2,1)}, f32[1,1152]{1,0:T(1,128)}) custom-call(bf16[512,1792]{1,0:T(8,128)(2,1)} %get-tuple-element.72.mixed_ref, bf16[1792,1152]{1,0:T(8,128)(2,1)} %all-gather.5.cloned.1.call-done.down_ref, f32[128,1152]{1,0:T(8,128)} %copy-done.3, bf16[128,1152]{1,0:T(8,128)(2,1)} %bitcast.216, ...), custom_call_target="tpu_custom_call" | custom-call | flops 2113929216 | bytes 8388608 | tf_op jit(solution)/shard_map/turn_round/pallas_call | solution.py:282
  196.3 6.3 %shard_map.283 = bf16[1792,1152]{1,0:T(8,128)(2,1)} custom-call(bf16[1792,512]{1,0:T(8,128)(2,1)} %get-tuple-element.74.left_ref, bf16[512,1152]{1,0:T(8,128)(2,1)} %bitcast.209), custom_call_target="tpu_custom_call" | custom-call | flops 2113929216 | bytes 8388608 | tf_op jit(solution)/shard_map/pallas_call | solution.py:313
  202.9 21.0 %hidden_back.1 = (bf16[512,1792]{1,0:T(8,128)(2,1)}, bf16[512,1792]{1,0:T(8,128)(2,1)}, bf16[512,1152]{1,0:T(8,128)(2,1)}) custom-call(bf16[512,1152]{1,0:T(8,128)(2,1)} %bitcast.210, bf16[1792,1152]{1,0:T(8,128)(2,1)} %all-gather.5.cloned.1.call-done.down_ref, f32[512,1792]{1,0:T(8,128)} %get-tuple-element.77.gate_ref, ...), custom_call_target="tpu_custom_call" | custom-call | flops 6341787648 | bytes 25165824 | tf_op jit(solution)/shard_map/hidden_back/pallas_call | solution.py:396
  223.9 16.6 %shard_map.284 = bf16[4,128,1152]{2,1,0:T(8,128)(2,1)} custom-call(bf16[4,128,1152]{2,1,0:T(8,128)(2,1)} %bitcast.211), custom_call_target="tpu_custom_call" | custom-call | tf_op jit(solution)/shard_map/pallas_call | solution.py:102
  240.5 6.0 %shard_map.286 = bf16[1152,1280]{1,0:T(8,128)(2,1)} custom-call(bf16[1152,512]{1,0:T(8,128)(2,1)} %bitcast.185, bf16[512,1792]{1,0:T(8,128)(2,1)} %get-tuple-element.85.second_ref.right_ref), custom_call_target="tpu_custom_call" | custom-call | flops 1509949440 | bytes 8388608 | tf_op jit(solution)/shard_map/pallas_call | solution.py:313
  246.6 9.5 %shard_map.285 = bf16[1152,2304]{1,0:T(8,128)(2,1)} custom-call(bf16[1152,512]{1,0:T(8,128)(2,1)} %bitcast.186, bf16[512,1792]{1,0:T(8,128)(2,1)} %get-tuple-element.84.first_ref, bf16[512,1792]{1,0:T(8,128)(2,1)} %get-tuple-element.85.second_ref.right_ref), custom_call_target="tpu_custom_call" | custom-call | flops 2717908992 | bytes 10485760 | tf_op jit(solution)/shard_map/pallas_call | solution.py:430
  256.7 1.5 convert_reduce_fusion
  259.5 2.6 convolution_convert_fusion
  262.3 1.9 multiply_reduce_fusion
  269.2 3.0 convolution_bitcast_fusion.3
  272.2 1.3 fusion.12
  275.4 1.2 convolution_add_fusion.2
  276.6 27.5 %shard_map.287 = (f32[128,512]{1,0:T(8,128)}, bf16[4,224,1152]{2,1,0:T(8,128)(2,1)}) custom-call(bf16[4,128,512]{2,1,0:T(8,128)(2,1)} %bitcast.202, bf16[224,1152]{1,0:T(8,128)(2,1)} %reduce-scatter.3.cloned.1.call-done.shard_ref), custom_call_target="tpu_custom_call" | custom-call | tf_op jit(solution)/shard_map/pallas_call | solution.py:687
  307.7 1.5 convolution_add_fusion.1
  310.7 14.4 %shard_map.288 = (f32[4,8,640]{2,1,0:T(8,128)}, bf16[4,128,384]{2,1,0:T(8,128)(2,1)}, bf16[4,128,288]{2,1,0:T(8,128)(2,1)}) custom-call(f32[8,640]{1,0:T(8,128)} %concatenate.54.refs_0_, bf16[4,128,384]{2,1,0:T(8,128)(2,1)} %bitcast.206, bf16[4,128,288]{2,1,0:T(8,128)(2,1)} %bitcast.208), custom_call_target="tpu_custom_call" | custom-call | tf_op jit(solution)/shard_map/pallas_call | solution.py:102
  325.1 1.9 fusion.11
  327.4 2.2 fusion.3
  329.6 1.8 fusion.6.attn_ref
  332.3 56.3 %tail_round.1 = (bf16[4,144,1792]{2,1,0:T(8,128)(2,1)}, bf16[4,144,1792]{2,1,0:T(8,128)(2,1)}, bf16[4,288,384]{2,1,0:T(8,128)(2,1)}) custom-call(bf16[144,2304]{1,0:T(8,128)(2,1)} %reduce-scatter.5.cloned.1.call-done.both_ref, bf16[8,144,1280]{2,1,0:T(8,128)(2,1)} %bitcast.182, bf16[8,288,384]{2,1,0:T(8,128)(2,1)} %fusion.6.attn_ref), custom_call_target="tpu_custom_call" | custom-call | tf_op jit(solution)/shard_map/tail_round/pallas_call | solution.py:1191
  388.7 8.9 %finish_round.1 = (f32[144,6912]{1,0:T(8,128)}, f32[144,6912]{1,0:T(8,128)}, f32[864,1152]{1,0:T(8,128)}, f32[144,1024]{1,0:T(8,128)}, f32[144,256]{1,0:T(8,128)...) custom-call(bf16[4,144,1792]{2,1,0:T(8,128)(2,1)} %get-tuple-element.97.gate_ref, ...), custom_call_target="tpu_custom_call" | custom-call | tf_op jit(solution)/shard_map/finish_round/pallas_call | solution.py:793
  (243 shorter events, 32.0 us)
Async XLA Ops:
  7.2 4.1 %copy-start = (bf16[864,1152]{1,0:T(8,128)(2,1)S(1)}, bf16[864,1152]{1,0:T(8,128)(2,1)}, u32[]{:S(2)}) copy-start(bf16[864,1152]{1,0:T(8,128)(2,1)} %param.32) | copy-start | bytes 5971972
  7.2 110.9 %all-gather.3.cloned.1.call-start = ((), (), s32[]{:S(2)}) async-start(), calls=%async_computation.2 | async-start | bytes 9289728 | tf_op jit(solution)/shard_map/all_gather | solution.py:1215
  11.2 148.6 %all-gather.5.cloned.1.call-start = ((), (), s32[]{:S(2)}) async-start(), calls=%async_computation.3 | async-start | bytes 4644864 | tf_op jit(solution)/shard_map/all_gather | solution.py:1215
  12.3 50.9 %copy-start.2 = (bf16[1,128,1152]{2,1,0:T(8,128)(2,1)S(1)}, bf16[1,128,1152]{2,1,0:T(8,128)(2,1)}, u32[]{:S(2)}) copy-start(bf16[1,128,1152]{2,1,0:T(8,128)(2,1)} %param.17) | copy-start | bytes 884740
  12.3 264.4 %reduce-scatter.3.cloned.1.call-start = ((), (), s32[]{:S(2)}) async-start(), calls=%async_computation.4 | async-start | bytes 4644864 | tf_op jit(solution)/shard_map/reduce_scatter | solution.py:1219
  63.3 2.3 copy-start.56
  68.2 21.4 %copy-start.37 = (f32[128,4]{0,1:T(4,128)}, f32[128,4]{0,1:T(4,128)S(1)}, u32[]{:S(2)}) copy-start(f32[128,4]{0,1:T(4,128)S(1)} %copy.147) | copy-start | bytes 6148
  68.4 21.4 %copy-start.42 = (f32[256]{0:T(256)}, f32[256]{0:T(256)S(1)}, u32[]{:S(2)}) copy-start(f32[256]{0:T(256)S(1)} %mul.493) | copy-start | bytes 3076
  68.9 19.6 %copy-start.52 = (f32[128]{0:T(128)}, f32[128]{0:T(128)S(1)}, u32[]{:S(2)}) copy-start(f32[128]{0:T(128)S(1)} %multiply_power_fusion) | copy-start | bytes 1540
  69.0 20.6 %copy-start.17 = (f32[128,256]{1,0:T(8,128)}, f32[128,256]{1,0:T(8,128)S(1)}, u32[]{:S(2)}) copy-start(f32[128,256]{1,0:T(8,128)S(1)} %get-tuple-element.123) | copy-start | bytes 393220
  69.6 18.7 %copy-start.44 = (f32[128]{0:T(128)}, f32[128]{0:T(128)S(1)}, u32[]{:S(2)}) copy-start(f32[128]{0:T(128)S(1)} %fusion.69) | copy-start | bytes 1540
  69.6 20.0 %copy-start.54 = (f32[128]{0:T(128)}, f32[128]{0:T(128)S(1)}, u32[]{:S(2)}) copy-start(f32[128]{0:T(128)S(1)} %bitcast_convert_fusion) | copy-start | bytes 1540
  70.0 19.9 %copy-start.22 = (f32[128,128]{1,0:T(8,128)}, f32[128,128]{1,0:T(8,128)S(1)}, u32[]{:S(2)}) copy-start(f32[128,128]{1,0:T(8,128)S(1)} %get-tuple-element.150) | copy-start | bytes 196612
  89.6 3.1 copy-start.19
  96.9 19.2 %copy-start.3 = (f32[128,1152]{1,0:T(8,128)}, f32[128,1152]{1,0:T(8,128)S(1)}, u32[]{:S(2)}) copy-start(f32[128,1152]{1,0:T(8,128)S(1)} %get-tuple-element.121.middle_ref) | copy-start | bytes 1769476
  202.6 129.7 %reduce-scatter.5.cloned.1.call-start = ((), (), s32[]{:S(2)}) async-start(), calls=%async_computation.5 | async-start | bytes 5971968 | tf_op jit(solution)/shard_map/reduce_scatter | solution.py:1219
  256.1 2.2 copy-start.4
  259.5 2.8 copy-start.50
  266.6 2.6 copy-start.51
  267.3 8.1 %copy-start.13 = (bf16[128,4,256]{0,2,1:T(8,128)(2,1)}, bf16[128,4,256]{0,2,1:T(8,128)(2,1)S(1)}, u32[]{:S(2)}) copy-start(bf16[128,4,256]{0,2,1:T(8,128)(2,1)S(1)} %copy.161) | copy-start | bytes 786436
  269.2 3.1 copy-start.12
  269.2 3.1 copy-start.27
  275.4 28.8 %copy-start.16 = (f32[640,256]{1,0:T(8,128)S(1)}, f32[640,256]{1,0:T(8,128)}, u32[]{:S(2)}) copy-start(f32[640,256]{1,0:T(8,128)} %convolution_bitcast_fusion.3) | copy-start | bytes 1966084
  276.6 28.6 %copy-start.53 = (f32[128]{0:T(128)S(1)}, f32[128]{0:T(128)}, u32[]{:S(2)}) copy-start(f32[128]{0:T(128)} %copy-done.52) | copy-start | bytes 1540
  276.6 28.6 %copy-start.55 = (f32[128]{0:T(128)S(1)}, f32[128]{0:T(128)}, u32[]{:S(2)}) copy-start(f32[128]{0:T(128)} %copy-done.54) | copy-start | bytes 1540
  304.2 2.1 copy-start.59
  305.3 2.4 copy-start.6
  325.1 2.3 copy-start.33
  325.1 2.3 copy-start.57
  327.4 2.2 copy-start.47
  388.7 10.9 %copy-start.31 = (bf16[128,1152]{1,0:T(8,128)(2,1)S(1)}, bf16[128,1152]{1,0:T(8,128)(2,1)}, u32[]{:S(2)}) copy-start(bf16[128,1152]{1,0:T(8,128)(2,1)} %get-tuple-element.73) | copy-start | bytes 884740
  388.7 11.6 %copy-start.1 = (bf16[864,1152]{1,0:T(8,128)(2,1)S(1)}, bf16[864,1152]{1,0:T(8,128)(2,1)}, u32[]{:S(2)}) copy-start(bf16[864,1152]{1,0:T(8,128)(2,1)} %param.32) | copy-start | bytes 5971972
  (41 other events, 52.6 us)
Sparse Core Ops, SparseCore 0:
  11.3 95.1 all-gather.2
  108.8 51.0 all-gather.4
  202.7 52.6 reduce-scatter.2
  257.6 68.7 reduce-scatter.4

commit v11 on v10

--- a/solution.py
+++ b/solution.py
@@ -306,17 +306,16 @@
     out_ref[...] = jnp.dot(left_ref[...], right_ref[...], preferred_element_type=F32).astype(BF16)
 
 
-def product_low(tile, left, right, start=0, columns=None):
+def product_low(tile, left, right):
     rows, depth = left.shape
-    columns = columns or right.shape[1]
-    skip = start // tile
+    columns = right.shape[1]
     return pl.pallas_call(
         product_kernel,
         grid=(columns // tile,),
         out_shape=jax.ShapeDtypeStruct((rows, columns), BF16),
         in_specs=[
             pl.BlockSpec((rows, depth), lambda i: (0, 0)),
-            pl.BlockSpec((depth, tile), lambda i: (0, i + skip)),
+            pl.BlockSpec((depth, tile), lambda i: (0, i)),
         ],
         out_specs=pl.BlockSpec((rows, tile), lambda i: (0, i)),
         cost_estimate=pl.CostEstimate(
@@ -418,29 +417,118 @@
     )(upstream, down, gate_pre, up_pre, both_weights, both_weights)
 
 
-def product_pair_kernel(split, left_ref, first_ref, second_ref, out_ref):
-    right = jnp.where(pl.program_id(0) < split, first_ref[...], second_ref[...])
-    out_ref[...] = jnp.dot(left_ref[...], right, preferred_element_type=F32).astype(BF16)
-
-
-def product_pair(tile, left, first, second, columns):
+def multiply_tiles(tile, first, last, left, right, out, target, sems):
+    def step(index, carry):
+        columns = pl.ds(pl.multiple_of(index * tile, tile), tile)
+        out[:, columns] = jnp.dot(
+            left[...], right[:, columns], preferred_element_type=F32
+        ).astype(BF16)
+        pltpu.make_async_copy(out.at[:, columns], target.at[:, columns], sems.at[index]).start()
+        return carry
+
+    lax.fori_loop(first, last, step, 0)
+
+
+def await_tiles(tile, count, out, target, sems):
+    for index in range(count):
+        columns = pl.ds(index * tile, tile)
+        pltpu.make_async_copy(out.at[:, columns], target.at[:, columns], sems.at[index]).wait()
+
+
+def sum_back_kernel(
+    tile,
+    slots_ref,
+    left_ref,
+    gate_ref,
+    up_ref,
+    sum_ref,
+    both_ref,
+    left,
+    right,
+    both,
+    taken_ref,
+    send_sem,
+    recv_sem,
+    load_sem,
+    store_sem,
+):
+    me = lax.axis_index("batch")
+    across = me + 1 - 2 * lax.rem(me, 2)
+    along = lax.rem(me + 2, 4)
+    order = (lax.rem(across + 2, 4), across, along)
+    hidden = gate_ref.shape[1]
+    width = right.shape[1]
+    loads = [
+        pltpu.make_async_copy(left_ref, left, load_sem.at[0]),
+        pltpu.make_async_copy(gate_ref, right.at[:, pl.ds(0, hidden)], load_sem.at[1]),
+        pltpu.make_async_copy(
+            up_ref.at[:, pl.ds(0, width - hidden)],
+            right.at[:, pl.ds(hidden, width - hidden)],
+            load_sem.at[2],
+        ),
+    ]
+    for load in loads:
+        load.start()
+    barrier = pltpu.get_barrier_semaphore()
+    for peer in order:
+        pl.semaphore_signal(barrier, inc=1, device_id={"batch": peer}, device_id_type=MESH)
+    pl.semaphore_wait(barrier, 3)
+    copies = [
+        pltpu.make_async_remote_copy(
+            src_ref=slots_ref.at[peer],
+            dst_ref=taken_ref.at[turn],
+            send_sem=send_sem.at[turn],
+            recv_sem=recv_sem.at[turn],
+            device_id={"batch": peer},
+            device_id_type=MESH,
+        )
+        for turn, peer in enumerate(order)
+    ]
+    for copy in copies:
+        copy.start()
+    for load in loads:
+        load.wait()
+    multiply_tiles(tile, 0, width // tile, left, right, both, both_ref, store_sem)
+    total = slots_ref[me].astype(F32)
+    for turn in range(3):
+        copies[turn].wait_recv()
+        total = total + taken_ref[turn].astype(F32)
+    sum_ref[...] = total
+    for copy in copies:
+        copy.wait_send()
+    await_tiles(tile, width // tile, both, both_ref, store_sem)
+
+
+def sum_back(tile, slots, left, gate, up, columns):
     rows, depth = left.shape
-    split = first.shape[1] // tile
-    steps = split + columns // tile
+    width = gate.shape[1] + columns
+    dma = pltpu.SemaphoreType.DMA
+    vmem = pl.BlockSpec(memory_space=pltpu.VMEM)
+    anywhere = pl.BlockSpec(memory_space=pl.ANY)
     return pl.pallas_call(
-        functools.partial(product_pair_kernel, split),
-        grid=(steps,),
-        out_shape=jax.ShapeDtypeStruct((rows, steps * tile), BF16),
-        in_specs=[
-            pl.BlockSpec((rows, depth), lambda i: (0, 0)),
-            pl.BlockSpec((depth, tile), lambda i: (0, jnp.minimum(i, split - 1))),
-            pl.BlockSpec((depth, tile), lambda i: (0, jnp.maximum(i - split, 0))),
+        functools.partial(sum_back_kernel, tile),
+        name="sum_back",
+        out_shape=[
+            jax.ShapeDtypeStruct(slots.shape[1:], F32),
+            jax.ShapeDtypeStruct((rows, width), BF16),
         ],
-        out_specs=pl.BlockSpec((rows, tile), lambda i: (0, i)),
+        in_specs=[vmem, anywhere, anywhere, anywhere],
+        out_specs=[vmem, anywhere],
+        scratch_shapes=[
+            pltpu.VMEM((rows, depth), BF16),
+            pltpu.VMEM((depth, width), BF16),
+            pltpu.VMEM((rows, width), BF16),
+            pltpu.VMEM((3, *slots.shape[1:]), BF16),
+            dma((3,)),
+            dma((3,)),
+            dma((3,)),
+            dma((width // tile,)),
+        ],
         cost_estimate=pl.CostEstimate(
-            flops=2 * rows * depth * steps * tile, bytes_accessed=10 << 20, transcendentals=0
+            flops=2 * rows * depth * width, bytes_accessed=12 << 20, transcendentals=0
         ),
-    )(left, first, second)
+        compiler_params=pltpu.CompilerParams(collective_id=5, has_side_effects=True),
+    )(slots, left, gate, up)
 
 
 def halo_out_kernel(n_chip, source_ref, result_ref, send_sem, recv_sem):
@@ -554,19 +642,27 @@
 
 
 def halo_back_kernel(
+    tile,
     n_chip,
     source_ref,
     shard_ref,
+    left_ref,
+    up_ref,
     result_ref,
     shards_ref,
+    rest_ref,
     near_ref,
     far_ref,
     way_ref,
+    left,
+    right,
+    rest,
     send_sem,
     recv_sem,
     pass_sem,
     take_sem,
     own_sem,
+    store_sem,
 ):
     me = lax.axis_index("ctx")
     spot = lax.axis_index("batch")
@@ -614,6 +710,16 @@
     to_other = remote(source_ref.at[1 + 2 * core], near_ref.at[1], 1, near)
     to_before.start()
     to_other.start()
+    width = right.shape[1]
+    count = width // tile
+    loads = [
+        pltpu.make_async_copy(left_ref, left, own_sem.at[1]),
+        pltpu.make_async_copy(
+            up_ref.at[:, pl.ds(up_ref.shape[1] - width, width)], right, own_sem.at[2]
+        ),
+    ]
+    for load in loads:
+        load.start()
     firsts = [
         beside(shard_ref, shards_ref.at[spot], turn, peer)
         for turn, peer in enumerate((across, along))
@@ -642,6 +748,10 @@
     to_before.wait_recv()
     due = source_ref[2].astype(F32) + near_ref[0].astype(F32)
 
+    for load in loads:
+        load.wait()
+    multiply_tiles(tile, 0, count // 3, left, right, rest, rest_ref, store_sem)
+
     @pl.when((chip > 0) & has_after)
     def _():
         two_back.wait_recv()
@@ -652,6 +762,7 @@
     def _():
         one_back.start()
 
+    multiply_tiles(tile, count // 3, count, left, right, rest, rest_ref, store_sem)
     columns = shard_ref.shape[-1]
     cut = columns // 256 * 128
     halves = (pl.ds(0, cut), pl.ds(cut, columns - cut))
@@ -671,6 +782,7 @@
         copy.wait()
     for copy in firsts + [to_before, to_other]:
         copy.wait_send()
+    await_tiles(tile, count, rest, rest_ref, store_sem)
 
     @pl.when(chip > 1)
     def _():
@@ -681,14 +793,15 @@
         one_back.wait_send()
 
 
-def halo_call(collective_id, kernel, n_ctx, arrays, out_shape, buffers, counts):
+def halo_call(collective_id, kernel, arrays, in_vmem, out_shape, out_vmem, buffers, counts):
     dma = pltpu.SemaphoreType.DMA
     vmem = pl.BlockSpec(memory_space=pltpu.VMEM)
+    anywhere = pl.BlockSpec(memory_space=pl.ANY)
     return pl.pallas_call(
-        functools.partial(kernel, n_ctx // 2),
+        kernel,
         out_shape=out_shape,
-        in_specs=[vmem] * len(arrays),
-        out_specs=[vmem] * len(out_shape),
+        in_specs=[vmem if i < in_vmem else anywhere for i in range(len(arrays))],
+        out_specs=[vmem if i < out_vmem else anywhere for i in range(len(out_shape))],
         scratch_shapes=[*buffers, *(dma((count,)) for count in counts)],
         compiler_params=pltpu.CompilerParams(collective_id=collective_id, has_side_effects=True),
     )(*arrays)
@@ -696,18 +809,28 @@
 
 def halo_out(n_ctx, block):
     out_shape = [jax.ShapeDtypeStruct((4, *block.shape), block.dtype)]
-    return halo_call(1, halo_out_kernel, n_ctx, (block,), out_shape, (), (5, 5))[0]
-
-
-def halo_back(n_ctx, blocks, shard):
+    kernel = functools.partial(halo_out_kernel, n_ctx // 2)
+    return halo_call(1, kernel, (block,), 1, out_shape, 1, (), (5, 5))[0]
+
+
+def halo_back(tile, n_ctx, blocks, shard, left, up, columns):
     shape = blocks.shape[1:]
+    rows, depth = left.shape
     buffers = [pltpu.VMEM((2, *shape), blocks.dtype)] * 3
+    buffers += [
+        pltpu.VMEM((rows, depth), BF16),
+        pltpu.VMEM((depth, columns), BF16),
+        pltpu.VMEM((rows, columns), BF16),
+    ]
     out_shape = [
         jax.ShapeDtypeStruct(shape, F32),
         jax.ShapeDtypeStruct((4, *shard.shape), shard.dtype),
+        jax.ShapeDtypeStruct((rows, columns), BF16),
     ]
-    counts = (4, 4, 4, 4, 1)
-    return halo_call(6, halo_back_kernel, n_ctx, (blocks, shard), out_shape, buffers, counts)
+    kernel = functools.partial(halo_back_kernel, tile, n_ctx // 2)
+    arrays = (blocks, shard, left, up)
+    counts = (4, 4, 4, 4, 3, columns // tile)
+    return halo_call(6, kernel, arrays, 2, out_shape, 2, buffers, counts)
 
 
 def pick_kernel(n_batch, n_ctx, piece, padded, gate_ref, up_ref, out_ref):
@@ -1358,17 +1481,15 @@
     grad_gate_low, grad_up_low, back_part = hidden_back(
         256, grad_ffn_low, part_down, gate_pre, up_pre, part_both
     )
-    (back_parts,) = batch_exchange(
-        5, n_batch, slots=(back_part.reshape(n_batch, tok_count, model_width),)
-    )
-    back_parts, grad_gate_low, grad_up_low = lax.optimization_barrier(
-        (back_parts, grad_gate_low, grad_up_low)
-    )
-    both_grad = product_pair(256, ffn_in_turned, grad_gate_low, grad_up_low, UP_FIRST)
-    up_grad = product_low(256, ffn_in_turned, grad_up_low, UP_FIRST, hidden_part - UP_FIRST)
-    back_parts, both_grad, up_grad = lax.optimization_barrier((back_parts, both_grad, up_grad))
+    grad_ffn_in, both_grad = sum_back(
+        256,
+        back_part.reshape(n_batch, tok_count, model_width),
+        ffn_in_turned,
+        grad_gate_low,
+        grad_up_low,
+        UP_FIRST,
+    )
     grad_w_both = scattered(both_grad)
-    grad_ffn_in = jnp.sum(back_parts.astype(F32), axis=0)
     _, pull_ffn_norm = jax.vjp(normed, middle, full_gain_ffn)
     grad_middle_part, grad_gain_ffn = pull_ffn_norm(grad_ffn_in)
     grad_middle = grad_final + grad_middle_part
@@ -1393,10 +1514,14 @@
     grad_ctx_values = jnp.einsum("htk,thd->kd", prob_low, grad_attended, preferred_element_type=F32)
     grad_context = jnp.concatenate([grad_ctx_keys, grad_ctx_values], axis=-1)
     halo_rows = halo_depth * tok_count
-    returned, down_all = halo_back(
+    returned, down_all, up_grad = halo_back(
+        256,
         n_ctx,
         grad_context[:halo_rows].astype(BF16).reshape(halo_depth, tok_count, 2 * head_size),
         grad_w_down,
+        ffn_in_turned,
+        grad_up_low,
+        hidden_part - UP_FIRST,
     )
     own_grad = grad_context[halo_rows:] + returned
     grad_value_low = own_grad[:, head_size:].astype(BF16)

time: 414 us -> 403 us (0.973)
  Pallas kernels: 322 us -> 308 us
  waiting for transfers between devices: 8.41 us -> 15 us
    pallas_call x2 -> x1, Pallas kernels: 31 us -> 13.7 us  [batch_exchange(): pl.pallas_call(functools.partial(batch_kernel, size, kinds), out_shape=sh...]
    pallas_call x3, Pallas kernels: 54.5 us -> 61.6 us  [the longest x2 44.9 us: halo_call(): pl.pallas_call(kernel, out_shape=out_shape, in_specs=[vmem if i < in_vmem...]
    reduce_scatter x2, waiting for transfers between devices: 0.01 us -> 6.51 us  [scattered(): return lax.psum_scatter(whole, 'ctx', scatter_dimension=0, tiled=True)]
    pallas_call x2 -> x1, Pallas kernels: 12.3 us -> 6.3 us  [product_low(): pl.pallas_call(product_kernel, grid=(columns // tile,), out_shape=jax.Sha...]
  transfers between devices with their start and end apart: 4 -> 4, of which waited for: 1 -> 2; matrix products, arithmetic and copies ran while one was open for 13% -> 13% of each run, Pallas kernels for 52% -> 49%
where the time goes in v11:
time: 403 us; the launch traced here: 398 us
  Pallas kernels  308 us (76%)
  local copies, waits for them, and re-layouts  23.2 us (6%)
  matrix products  21.3 us (5%)
  between operations  15.5 us (4%)
  waiting for transfers between devices  15 us (4%)
  other arithmetic  14.9 us (4%)
    pallas_call x1, Pallas kernels, tail_round(): pl.pallas_call(functools.partial(tail_kernel, n_ctx), name='tail_round',...  58.1 us
    pallas_call x1, Pallas kernels, gather_weights(): pl.pallas_call(functools.partial(weights_kernel, n_batch, n_ctx), name='g...  48.3 us
    pallas_call x2, Pallas kernels, halo_call(): pl.pallas_call(kernel, out_shape=out_shape, in_specs=[vmem if i < in_vmem...  44.9 us
    pallas_call x2, Pallas kernels, square_gather(): pl.pallas_call(functools.partial(square_kernel, count), out_shape=[jax.Sh...  37.4 us
    pallas_call x1, Pallas kernels, turn_round(): pl.pallas_call(turn_kernel, name='turn_round', out_shape=(jax.ShapeDtypeS...  36.5 us
    pallas_call x1, Pallas kernels, hidden_back(): pl.pallas_call(back_kernel, name='hidden_back', grid=(count,), out_shape=...  21.1 us
    pallas_call x1, Pallas kernels, sum_back(): pl.pallas_call(functools.partial(sum_back_kernel, tile), name='sum_back',...  16.7 us
    pallas_call x1, Pallas kernels, batch_exchange(): pl.pallas_call(functools.partial(batch_kernel, size, kinds), out_shape=sh...  13.7 us
  transfers between devices with their start and end apart: 4, of which 2 were waited for; matrix products, arithmetic and copies ran while one was open for 13% of the time, Pallas kernels for 49%

profile of v11, /device:TPU:0, one launch (start us, length us, event | category | flops | bytes accessed | tf_op | source)
XLA Modules:
  0.0 398.2 jit_solution(4452781678722427474)
XLA Ops:
  7.2 3.9 pick_columns.1
  13.9 48.3 %gather_weights.1 = (bf16[4,8,144,384]{3,2,1,0:T(8,128)(2,1)}, bf16[8,4,32,1152]{3,2,1,0:T(8,128)(2,1)}, bf16[8,1,640]{2,1,0:T(2,128)(2,1)}) custom-call(bf16[4,144,384]{2,1,0:T(8,128)(2,1)} %bitcast.204, bf16[4,32,1152]{2,1,0:T(8,128)(2,1)} %bitcast.216, bf16[1,640]{1,0:T(2,128)(2,1)} %broadcast_in_dim.32.gain_ref), custom_call_target="tpu_custom_call" | custom-call | tf_op jit(solution)/shard_map/gather_weights/pallas_call | solution.py:1052
  63.3 2.3 fusion.91
  70.7 17.5 %shard_map.280 = bf16[4,128,512]{2,1,0:T(8,128)(2,1)} custom-call(bf16[128,512]{1,0:T(8,128)(2,1)} %pad_maximum_fusion.9.source_ref), custom_call_target="tpu_custom_call" | custom-call | tf_op jit(solution)/shard_map/pallas_call | solution.py:800
  88.4 1.1 maximum_maximum_fusion
  89.9 1.6 fusion.96
  91.5 0.9 convolution_convert_fusion.1
  93.3 2.3 multiply_reduce_fusion.6
  95.6 1.0 multiply_reduce_fusion.5
  97.5 16.0 %shard_map.281 = bf16[4,128,1152]{2,1,0:T(8,128)(2,1)} custom-call(bf16[128,1152]{1,0:T(8,128)(2,1)} %multiply_convert_fusion.1.refs_0_), custom_call_target="tpu_custom_call" | custom-call | tf_op jit(solution)/shard_map/pallas_call | solution.py:172
  113.6 2.4 copy.191
  118.0 12.0 %hidden_mix.1 = (f32[512,1792]{1,0:T(8,128)}, f32[512,1792]{1,0:T(8,128)}, bf16[512,1792]{1,0:T(8,128)(2,1)}, bf16[1792,512]{1,0:T(8,128)(2,1)}) custom-call(bf16[512,1152]{1,0:T(8,128)(2,1)} %bitcast.183, bf16[1152,3584]{1,0:T(8,128)(2,1)} %all-gather.3.cloned.1.call-done.w_gate_ref.w_up_ref, bf16[1152,3584]{1,0:T(8,128)(2,1)} %all-gather.3.cloned.1.call-done.w_gate_ref.w_up_ref), custom_call_target="tpu_custom_call" | custom-call | flops 4227858432 | bytes 25165824 | tf_op jit(solution)/shard_map/hidden_mix/pallas_call | solution.py:343
  130.0 21.4 %shard_map.282 = (bf16[4,128,1152]{2,1,0:T(8,128)(2,1)}, bf16[4,128,1024]{2,1,0:T(8,128)(2,1)}) custom-call(bf16[128,1152]{1,0:T(8,128)(2,1)} %get-tuple-element.64.refs_0_, bf16[128,1024]{1,0:T(8,128)(2,1)} %copy.190.refs_1_), custom_call_target="tpu_custom_call" | custom-call | tf_op jit(solution)/shard_map/pallas_call | solution.py:172
  151.4 8.4 %all-gather.5.cloned.1.call-done.down_ref = bf16[1792,1152]{1,0:T(8,128)(2,1)} async-done(((bf16[224,1152]{1,0:T(8,128)(2,1)}), bf16[1792,1152]{1,0:T(8,128)(2,1)}) %all-gather.5.cloned.1.call-update) | async-done | bytes 4128784 | tf_op jit(solution)/shard_map/all_gather | solution.py:1338
  159.8 36.5 %turn_round.1 = (bf16[128,1152]{1,0:T(8,128)(2,1)}, bf16[4,128,1152]{2,1,0:T(8,128)(2,1)}, f32[1,1152]{1,0:T(1,128)}) custom-call(bf16[512,1792]{1,0:T(8,128)(2,1)} %get-tuple-element.69.mixed_ref, bf16[1792,1152]{1,0:T(8,128)(2,1)} %all-gather.5.cloned.1.call-done.down_ref, f32[128,1152]{1,0:T(8,128)} %copy-done.3, bf16[128,1152]{1,0:T(8,128)(2,1)} %bitcast.215, ...), custom_call_target="tpu_custom_call" | custom-call | flops 2113929216 | bytes 8388608 | tf_op jit(solution)/shard_map/turn_round/pallas_call | solution.py:282
  196.3 6.3 %shard_map.283 = bf16[1792,1152]{1,0:T(8,128)(2,1)} custom-call(bf16[1792,512]{1,0:T(8,128)(2,1)} %get-tuple-element.71.left_ref, bf16[512,1152]{1,0:T(8,128)(2,1)} %bitcast.209), custom_call_target="tpu_custom_call" | custom-call | flops 2113929216 | bytes 8388608 | tf_op jit(solution)/shard_map/pallas_call | solution.py:312
  202.9 21.1 %hidden_back.1 = (bf16[512,1792]{1,0:T(8,128)(2,1)}, bf16[512,1792]{1,0:T(8,128)(2,1)}, bf16[512,1152]{1,0:T(8,128)(2,1)}) custom-call(bf16[512,1152]{1,0:T(8,128)(2,1)} %bitcast.210, bf16[1792,1152]{1,0:T(8,128)(2,1)} %all-gather.5.cloned.1.call-done.down_ref, f32[512,1792]{1,0:T(8,128)} %get-tuple-element.74.gate_ref, ...), custom_call_target="tpu_custom_call" | custom-call | flops 6341787648 | bytes 25165824 | tf_op jit(solution)/shard_map/hidden_back/pallas_call | solution.py:395
  224.0 16.7 %sum_back.1 = (f32[128,1152]{1,0:T(8,128)}, bf16[1152,2304]{1,0:T(8,128)(2,1)}) custom-call(bf16[4,128,1152]{2,1,0:T(8,128)(2,1)} %bitcast.223, bf16[1152,512]{1,0:T(8,128)(2,1)} %bitcast.194, bf16[512,1792]{1,0:T(8,128)(2,1)} %get-tuple-element.78.gate_ref, bf16[512,1792]{1,0:T(8,128)(2,1)} %get-tuple-element.79.up_ref), custom_call_target="tpu_custom_call" | custom-call | flops 2717908992 | bytes 12582912 | tf_op jit(solution)/shard_map/sum_back/pallas_call | solution.py:508
  241.7 1.3 multiply_reduce_fusion.1
  244.7 2.7 convolution_convert_fusion
  247.5 1.8 multiply_reduce_fusion
  253.0 3.0 convolution_bitcast_fusion.3
  258.9 1.2 convolution_add_fusion.2
  260.2 27.4 %shard_map.284 = (f32[128,512]{1,0:T(8,128)}, bf16[4,224,1152]{2,1,0:T(8,128)(2,1)}, bf16[1152,1280]{1,0:T(8,128)(2,1)}) custom-call(bf16[4,128,512]{2,1,0:T(8,128)(2,1)} %bitcast.203, bf16[224,1152]{1,0:T(8,128)(2,1)} %reduce-scatter.3.cloned.1.call-done.shard_ref, bf16[1152,512]{1,0:T(8,128)(2,1)} %bitcast.195, bf16[512,1792]{1,0:T(8,128)(2,1)} %get-tuple-element.79.up_ref), custom_call_target="tpu_custom_call" | custom-call | tf_op jit(solution)/shard_map/pallas_call | solution.py:800
  287.6 1.1 fusion.45
  294.4 13.7 %shard_map.285 = (f32[4,8,640]{2,1,0:T(8,128)}, bf16[4,128,384]{2,1,0:T(8,128)(2,1)}, bf16[4,128,288]{2,1,0:T(8,128)(2,1)}) custom-call(f32[8,640]{1,0:T(8,128)} %concatenate.54.refs_0_, bf16[4,128,384]{2,1,0:T(8,128)(2,1)} %bitcast.206, bf16[4,128,288]{2,1,0:T(8,128)(2,1)} %bitcast.208), custom_call_target="tpu_custom_call" | custom-call | tf_op jit(solution)/shard_map/pallas_call | solution.py:102
  308.2 1.9 fusion.11
  310.6 2.1 fusion.3
  312.7 1.8 fusion.6.attn_ref
  315.4 6.5 %reduce-scatter.5.cloned.1.call-done.both_ref = bf16[144,2304]{1,0:T(8,128)(2,1)} async-done(((bf16[1152,2304]{1,0:T(8,128)(2,1)}), bf16[144,2304]{1,0:T(8,128)(2,1)}) %reduce-scatter.5.cloned.1.call-update) | async-done | bytes 663568 | tf_op jit(solution)/shard_map/reduce_scatter | solution.py:1342
  322.0 58.1 %tail_round.1 = (bf16[4,144,1792]{2,1,0:T(8,128)(2,1)}, bf16[4,144,1792]{2,1,0:T(8,128)(2,1)}, bf16[4,288,384]{2,1,0:T(8,128)(2,1)}) custom-call(bf16[144,2304]{1,0:T(8,128)(2,1)} %reduce-scatter.5.cloned.1.call-done.both_ref, bf16[8,144,1280]{2,1,0:T(8,128)(2,1)} %bitcast.201, bf16[8,288,384]{2,1,0:T(8,128)(2,1)} %fusion.6.attn_ref), custom_call_target="tpu_custom_call" | custom-call | tf_op jit(solution)/shard_map/tail_round/pallas_call | solution.py:1314
  380.1 8.9 %finish_round.1 = (f32[144,6912]{1,0:T(8,128)}, f32[144,6912]{1,0:T(8,128)}, f32[864,1152]{1,0:T(8,128)}, f32[144,1024]{1,0:T(8,128)}, f32[144,256]{1,0:T(8,128)...) custom-call(bf16[4,144,1792]{2,1,0:T(8,128)(2,1)} %get-tuple-element.91.gate_ref, ...), custom_call_target="tpu_custom_call" | custom-call | tf_op jit(solution)/shard_map/finish_round/pallas_call | solution.py:916
  (218 shorter events, 31.3 us)
Async XLA Ops:
  7.2 4.1 %copy-start = (bf16[864,1152]{1,0:T(8,128)(2,1)S(1)}, bf16[864,1152]{1,0:T(8,128)(2,1)}, u32[]{:S(2)}) copy-start(bf16[864,1152]{1,0:T(8,128)(2,1)} %param.32) | copy-start | bytes 5971972
  7.2 110.8 %all-gather.3.cloned.1.call-start = ((), (), s32[]{:S(2)}) async-start(), calls=%async_computation.2 | async-start | bytes 9289728 | tf_op jit(solution)/shard_map/all_gather | solution.py:1338
  11.2 148.6 %all-gather.5.cloned.1.call-start = ((), (), s32[]{:S(2)}) async-start(), calls=%async_computation.3 | async-start | bytes 4644864 | tf_op jit(solution)/shard_map/all_gather | solution.py:1338
  12.3 50.9 %copy-start.2 = (bf16[1,128,1152]{2,1,0:T(8,128)(2,1)S(1)}, bf16[1,128,1152]{2,1,0:T(8,128)(2,1)}, u32[]{:S(2)}) copy-start(bf16[1,128,1152]{2,1,0:T(8,128)(2,1)} %param.17) | copy-start | bytes 884740
  12.3 247.9 %reduce-scatter.3.cloned.1.call-start = ((), (), s32[]{:S(2)}) async-start(), calls=%async_computation.4 | async-start | bytes 4644864 | tf_op jit(solution)/shard_map/reduce_scatter | solution.py:1342
  63.3 2.3 copy-start.46
  68.9 19.3 %copy-start.42 = (f32[128]{0:T(128)}, f32[128]{0:T(128)S(1)}, u32[]{:S(2)}) copy-start(f32[128]{0:T(128)S(1)} %multiply_power_fusion) | copy-start | bytes 1540
  69.0 20.5 %copy-start.19 = (f32[128,256]{1,0:T(8,128)}, f32[128,256]{1,0:T(8,128)S(1)}, u32[]{:S(2)}) copy-start(f32[128,256]{1,0:T(8,128)S(1)} %get-tuple-element.117) | copy-start | bytes 393220
  69.5 18.7 %copy-start.35 = (f32[128]{0:T(128)}, f32[128]{0:T(128)S(1)}, u32[]{:S(2)}) copy-start(f32[128]{0:T(128)S(1)} %fusion.69) | copy-start | bytes 1540
  69.5 19.9 %copy-start.44 = (f32[128]{0:T(128)}, f32[128]{0:T(128)S(1)}, u32[]{:S(2)}) copy-start(f32[128]{0:T(128)S(1)} %bitcast_convert_fusion) | copy-start | bytes 1540
  89.5 2.0 copy-start.21
  89.6 1.9 copy-start.31
  91.5 157.9 %copy-start.40 = (f32[4,128]{1,0:T(4,128)}, f32[4,128]{1,0:T(4,128)S(1)}, u32[]{:S(2)}) copy-start(f32[4,128]{1,0:T(4,128)S(1)} %get-tuple-element.147) | copy-start | bytes 6148
  96.6 19.4 %copy-start.3 = (f32[128,1152]{1,0:T(8,128)}, f32[128,1152]{1,0:T(8,128)S(1)}, u32[]{:S(2)}) copy-start(f32[128,1152]{1,0:T(8,128)S(1)} %get-tuple-element.115.middle_ref) | copy-start | bytes 1769476
  202.6 119.3 %reduce-scatter.5.cloned.1.call-start = ((), (), s32[]{:S(2)}) async-start(), calls=%async_computation.5 | async-start | bytes 5971968 | tf_op jit(solution)/shard_map/reduce_scatter | solution.py:1342
  240.7 2.3 copy-start.17
  240.7 2.3 copy-start.26
  244.7 2.9 copy-start.22
  247.5 1.9 copy-start.23
  250.7 2.3 copy-start.41
  253.0 3.0 copy-start.12
  253.0 3.0 copy-start.25
  260.2 27.5 %copy-start.16 = (f32[640,256]{1,0:T(8,128)S(1)}, f32[640,256]{1,0:T(8,128)}, u32[]{:S(2)}) copy-start(f32[640,256]{1,0:T(8,128)} %convolution_bitcast_fusion.3) | copy-start | bytes 1966084
  287.6 2.2 copy-start.49
  288.7 3.8 copy-start.6
  288.7 3.8 copy-start.18
  308.2 2.3 copy-start.30
  308.2 2.3 copy-start.47
  308.2 2.3 copy-start.57
  310.5 2.1 copy-start.38
  380.1 10.9 %copy-start.28 = (bf16[128,1152]{1,0:T(8,128)(2,1)S(1)}, bf16[128,1152]{1,0:T(8,128)(2,1)}, u32[]{:S(2)}) copy-start(bf16[128,1152]{1,0:T(8,128)(2,1)} %get-tuple-element.70) | copy-start | bytes 884740
  380.1 11.6 %copy-start.1 = (bf16[864,1152]{1,0:T(8,128)(2,1)S(1)}, bf16[864,1152]{1,0:T(8,128)(2,1)}, u32[]{:S(2)}) copy-start(bf16[864,1152]{1,0:T(8,128)(2,1)} %param.32) | copy-start | bytes 5971972
  (30 other events, 35.8 us)
Sparse Core Ops, SparseCore 0:
  11.3 95.1 all-gather.2
  108.8 51.0 all-gather.4
  202.8 52.4 reduce-scatter.2
  257.4 64.5 reduce-scatter.4

commit v12 on v11

--- a/solution.py
+++ b/solution.py
@@ -8,7 +8,7 @@
 from jax.sharding import PartitionSpec as P
 
 WINDOW = 512
-UP_FIRST = 512
+UP_FIRST = 256
 
 
 EPS = 1e-06
@@ -211,29 +211,36 @@
         pl.semaphore_signal(barrier, inc=1, device_id={"batch": peer}, device_id_type=MESH)
     pl.semaphore_wait(barrier, 3)
 
-    def product(place):
+    columns = grads_ref.shape[-1]
+    cut = columns // 256 * 128
+    halves = (pl.ds(0, cut), pl.ds(cut, columns - cut))
+
+    def product(place, stretch):
         rows = pl.ds(pl.multiple_of(place * tok_count, tok_count), tok_count)
-        return jnp.dot(mixed_ref[rows, :], down_ref[...], preferred_element_type=F32)
+        return jnp.dot(mixed_ref[rows, :], down_ref[:, stretch], preferred_element_type=F32)
 
     copies = [
         pltpu.make_async_remote_copy(
-            src_ref=part_ref.at[turn],
-            dst_ref=taken_ref.at[turn],
-            send_sem=send_sem.at[turn],
-            recv_sem=recv_sem.at[turn],
+            src_ref=part_ref.at[turn, :, stretch],
+            dst_ref=taken_ref.at[turn, :, stretch],
+            send_sem=send_sem.at[turn, half],
+            recv_sem=recv_sem.at[turn, half],
             device_id={"batch": peer},
             device_id_type=MESH,
         )
         for turn, peer in enumerate(order)
+        for half, stretch in enumerate(halves)
     ]
-    for turn, peer in enumerate(order):
-        part_ref[turn] = product(peer).astype(BF16)
-        if turn > 0:
-            copies[turn - 1].start()
-    total = product(me)
-    copies[2].start()
+    for index in range(len(copies)):
+        turn, stretch = index // 2, halves[index % 2]
+        part_ref[turn, :, stretch] = product(order[turn], stretch).astype(BF16)
+        if index > 0:
+            copies[index - 1].start()
+    total = product(me, pl.ds(0, columns))
+    copies[-1].start()
     for turn in range(3):
-        copies[turn].wait_recv()
+        for copy in copies[2 * turn : 2 * turn + 2]:
+            copy.wait_recv()
         total = total + taken_ref[turn].astype(F32)
     gain = gain_ref[...]
     valid = valid_ref[...]
@@ -261,9 +268,6 @@
         return copy
 
     firsts = [remote(grads_ref.at[me], turn, peer) for turn, peer in enumerate((across, along))]
-    columns = grads_ref.shape[-1]
-    cut = columns // 256 * 128
-    halves = (pl.ds(0, cut), pl.ds(cut, columns - cut))
     seconds = []
     for turn, (giver, taker) in enumerate(((across, along), (along, across))):
         firsts[turn].wait_recv()
@@ -292,8 +296,8 @@
         scratch_shapes=[
             pltpu.VMEM((3, tok_count, width), BF16),
             pltpu.VMEM((3, tok_count, width), BF16),
-            dma((3,)),
-            dma((3,)),
+            dma((3, 2)),
+            dma((3, 2)),
             dma((4,)),
             dma((4,)),
         ],

time: 403 us -> 401 us (level)
  waiting for transfers between devices: 15 us -> 10.8 us
    reduce_scatter x2, waiting for transfers between devices: 6.51 us -> 2.31 us  [scattered(): return lax.psum_scatter(whole, 'ctx', scatter_dimension=0, tiled=True)]
where the time goes in v12:
time: 401 us; the launch traced here: 394 us
  Pallas kernels  308 us (77%)
  local copies, waits for them, and re-layouts  23.2 us (6%)
  matrix products  21.3 us (5%)
  between operations  15.5 us (4%)
  other arithmetic  15 us (4%)
  waiting for transfers between devices  10.8 us (3%)
    pallas_call x1, Pallas kernels, tail_round(): pl.pallas_call(functools.partial(tail_kernel, n_ctx), name='tail_round',...  60.4 us
    pallas_call x1, Pallas kernels, gather_weights(): pl.pallas_call(functools.partial(weights_kernel, n_batch, n_ctx), name='g...  48.3 us
    pallas_call x2, Pallas kernels, halo_call(): pl.pallas_call(kernel, out_shape=out_shape, in_specs=[vmem if i < in_vmem...  42.9 us
    pallas_call x2, Pallas kernels, square_gather(): pl.pallas_call(functools.partial(square_kernel, count), out_shape=[jax.Sh...  37.4 us
    pallas_call x1, Pallas kernels, turn_round(): pl.pallas_call(turn_kernel, name='turn_round', out_shape=(jax.ShapeDtypeS...  35.9 us
    pallas_call x1, Pallas kernels, hidden_back(): pl.pallas_call(back_kernel, name='hidden_back', grid=(count,), out_shape=...  21 us
    pallas_call x1, Pallas kernels, sum_back(): pl.pallas_call(functools.partial(sum_back_kernel, tile), name='sum_back',...  16.6 us
    pallas_call x1, Pallas kernels, batch_exchange(): pl.pallas_call(functools.partial(batch_kernel, size, kinds), out_shape=sh...  14 us
  transfers between devices with their start and end apart: 4, of which 2 were waited for; matrix products, arithmetic and copies ran while one was open for 13% of the time, Pallas kernels for 49%

profile of v12, /device:TPU:0, one launch (start us, length us, event | category | flops | bytes accessed | tf_op | source)
XLA Modules:
  0.0 393.8 jit_solution(4213233913174817679)
XLA Ops:
  7.2 3.9 %pick_columns.1 = bf16[144,3584]{1,0:T(8,128)(2,1)} custom-call(bf16[144,6912]{1,0:T(8,128)(2,1)} %gate_ref.1, bf16[144,6912]{1,0:T(8,128)(2,1)} %up_ref.1), custom_call_target="tpu_custom_call" | custom-call | tf_op jit(solution)/shard_map/pick_columns/pallas_call | solution.py:862
  13.9 48.3 %gather_weights.1 = (bf16[4,8,144,384]{3,2,1,0:T(8,128)(2,1)}, bf16[8,4,32,1152]{3,2,1,0:T(8,128)(2,1)}, bf16[8,1,640]{2,1,0:T(2,128)(2,1)}) custom-call(bf16[4,144,384]{2,1,0:T(8,128)(2,1)} %bitcast.204, bf16[4,32,1152]{2,1,0:T(8,128)(2,1)} %bitcast.216, bf16[1,640]{1,0:T(2,128)(2,1)} %broadcast_in_dim.32.gain_ref), custom_call_target="tpu_custom_call" | custom-call | tf_op jit(solution)/shard_map/gather_weights/pallas_call | solution.py:1056
  63.3 2.3 fusion.91
  70.7 17.5 %shard_map.280 = bf16[4,128,512]{2,1,0:T(8,128)(2,1)} custom-call(bf16[128,512]{1,0:T(8,128)(2,1)} %pad_maximum_fusion.9.source_ref), custom_call_target="tpu_custom_call" | custom-call | tf_op jit(solution)/shard_map/pallas_call | solution.py:804
  88.4 1.1 maximum_maximum_fusion
  89.9 1.6 fusion.96
  91.5 0.9 convolution_convert_fusion.1
  93.3 2.3 multiply_reduce_fusion.6
  95.6 1.0 multiply_reduce_fusion.5
  97.5 16.0 %shard_map.281 = bf16[4,128,1152]{2,1,0:T(8,128)(2,1)} custom-call(bf16[128,1152]{1,0:T(8,128)(2,1)} %multiply_convert_fusion.1.refs_0_), custom_call_target="tpu_custom_call" | custom-call | tf_op jit(solution)/shard_map/pallas_call | solution.py:172
  113.6 2.4 copy.191
  118.0 12.0 %hidden_mix.1 = (f32[512,1792]{1,0:T(8,128)}, f32[512,1792]{1,0:T(8,128)}, bf16[512,1792]{1,0:T(8,128)(2,1)}, bf16[1792,512]{1,0:T(8,128)(2,1)}) custom-call(bf16[512,1152]{1,0:T(8,128)(2,1)} %bitcast.183, bf16[1152,3584]{1,0:T(8,128)(2,1)} %all-gather.3.cloned.1.call-done.w_gate_ref.w_up_ref, bf16[1152,3584]{1,0:T(8,128)(2,1)} %all-gather.3.cloned.1.call-done.w_gate_ref.w_up_ref), custom_call_target="tpu_custom_call" | custom-call | flops 4227858432 | bytes 25165824 | tf_op jit(solution)/shard_map/hidden_mix/pallas_call | solution.py:347
  130.0 21.4 %shard_map.282 = (bf16[4,128,1152]{2,1,0:T(8,128)(2,1)}, bf16[4,128,1024]{2,1,0:T(8,128)(2,1)}) custom-call(bf16[128,1152]{1,0:T(8,128)(2,1)} %get-tuple-element.64.refs_0_, bf16[128,1024]{1,0:T(8,128)(2,1)} %copy.190.refs_1_), custom_call_target="tpu_custom_call" | custom-call | tf_op jit(solution)/shard_map/pallas_call | solution.py:172
  151.4 8.4 %all-gather.5.cloned.1.call-done.down_ref = bf16[1792,1152]{1,0:T(8,128)(2,1)} async-done(((bf16[224,1152]{1,0:T(8,128)(2,1)}), bf16[1792,1152]{1,0:T(8,128)(2,1)}) %all-gather.5.cloned.1.call-update) | async-done | bytes 4128784 | tf_op jit(solution)/shard_map/all_gather | solution.py:1342
  159.8 35.9 %turn_round.1 = (bf16[128,1152]{1,0:T(8,128)(2,1)}, bf16[4,128,1152]{2,1,0:T(8,128)(2,1)}, f32[1,1152]{1,0:T(1,128)}) custom-call(bf16[512,1792]{1,0:T(8,128)(2,1)} %get-tuple-element.69.mixed_ref, bf16[1792,1152]{1,0:T(8,128)(2,1)} %all-gather.5.cloned.1.call-done.down_ref, f32[128,1152]{1,0:T(8,128)} %copy-done.3, bf16[128,1152]{1,0:T(8,128)(2,1)} %bitcast.215, ...), custom_call_target="tpu_custom_call" | custom-call | flops 2113929216 | bytes 8388608 | tf_op jit(solution)/shard_map/turn_round/pallas_call | solution.py:286
  195.7 6.3 %shard_map.283 = bf16[1792,1152]{1,0:T(8,128)(2,1)} custom-call(bf16[1792,512]{1,0:T(8,128)(2,1)} %get-tuple-element.71.left_ref, bf16[512,1152]{1,0:T(8,128)(2,1)} %bitcast.209), custom_call_target="tpu_custom_call" | custom-call | flops 2113929216 | bytes 8388608 | tf_op jit(solution)/shard_map/pallas_call | solution.py:316
  202.3 21.0 %hidden_back.1 = (bf16[512,1792]{1,0:T(8,128)(2,1)}, bf16[512,1792]{1,0:T(8,128)(2,1)}, bf16[512,1152]{1,0:T(8,128)(2,1)}) custom-call(bf16[512,1152]{1,0:T(8,128)(2,1)} %bitcast.210, bf16[1792,1152]{1,0:T(8,128)(2,1)} %all-gather.5.cloned.1.call-done.down_ref, f32[512,1792]{1,0:T(8,128)} %get-tuple-element.74.gate_ref, ...), custom_call_target="tpu_custom_call" | custom-call | flops 6341787648 | bytes 25165824 | tf_op jit(solution)/shard_map/hidden_back/pallas_call | solution.py:399
  223.4 16.6 %sum_back.1 = (f32[128,1152]{1,0:T(8,128)}, bf16[1152,2048]{1,0:T(8,128)(2,1)}) custom-call(bf16[4,128,1152]{2,1,0:T(8,128)(2,1)} %bitcast.223, bf16[1152,512]{1,0:T(8,128)(2,1)} %bitcast.194, bf16[512,1792]{1,0:T(8,128)(2,1)} %get-tuple-element.78.gate_ref, bf16[512,1792]{1,0:T(8,128)(2,1)} %get-tuple-element.79.up_ref), custom_call_target="tpu_custom_call" | custom-call | flops 2415919104 | bytes 12582912 | tf_op jit(solution)/shard_map/sum_back/pallas_call | solution.py:512
  241.1 1.3 multiply_reduce_fusion.1
  244.0 2.6 convolution_convert_fusion
  246.9 1.8 multiply_reduce_fusion
  252.3 3.0 convolution_bitcast_fusion.3
  258.3 1.2 convolution_add_fusion.2
  259.5 25.4 %shard_map.284 = (f32[128,512]{1,0:T(8,128)}, bf16[4,224,1152]{2,1,0:T(8,128)(2,1)}, bf16[1152,1536]{1,0:T(8,128)(2,1)}) custom-call(bf16[4,128,512]{2,1,0:T(8,128)(2,1)} %bitcast.203, bf16[224,1152]{1,0:T(8,128)(2,1)} %reduce-scatter.3.cloned.1.call-done.shard_ref, bf16[1152,512]{1,0:T(8,128)(2,1)} %bitcast.195, bf16[512,1792]{1,0:T(8,128)(2,1)} %get-tuple-element.79.up_ref), custom_call_target="tpu_custom_call" | custom-call | tf_op jit(solution)/shard_map/pallas_call | solution.py:804
  285.0 1.1 fusion.45
  291.8 14.0 %shard_map.285 = (f32[4,8,640]{2,1,0:T(8,128)}, bf16[4,128,384]{2,1,0:T(8,128)(2,1)}, bf16[4,128,288]{2,1,0:T(8,128)(2,1)}) custom-call(f32[8,640]{1,0:T(8,128)} %concatenate.54.refs_0_, bf16[4,128,384]{2,1,0:T(8,128)(2,1)} %bitcast.206, bf16[4,128,288]{2,1,0:T(8,128)(2,1)} %bitcast.208), custom_call_target="tpu_custom_call" | custom-call | tf_op jit(solution)/shard_map/pallas_call | solution.py:102
  305.8 1.9 fusion.11
  308.1 2.1 fusion.3
  310.3 1.8 fusion.6.attn_ref
  313.0 2.3 reduce-scatter.5.cloned.1.call-done.both_ref
  315.3 60.4 %tail_round.1 = (bf16[4,144,1792]{2,1,0:T(8,128)(2,1)}, bf16[4,144,1792]{2,1,0:T(8,128)(2,1)}, bf16[4,288,384]{2,1,0:T(8,128)(2,1)}) custom-call(bf16[144,2048]{1,0:T(8,128)(2,1)} %reduce-scatter.5.cloned.1.call-done.both_ref, bf16[8,144,1536]{2,1,0:T(8,128)(2,1)} %bitcast.200, bf16[8,288,384]{2,1,0:T(8,128)(2,1)} %fusion.6.attn_ref), custom_call_target="tpu_custom_call" | custom-call | tf_op jit(solution)/shard_map/tail_round/pallas_call | solution.py:1318
  375.7 8.9 %finish_round.1 = (f32[144,6912]{1,0:T(8,128)}, f32[144,6912]{1,0:T(8,128)}, f32[864,1152]{1,0:T(8,128)}, f32[144,1024]{1,0:T(8,128)}, f32[144,256]{1,0:T(8,128)...) custom-call(bf16[4,144,1792]{2,1,0:T(8,128)(2,1)} %get-tuple-element.91.gate_ref, ...), custom_call_target="tpu_custom_call" | custom-call | tf_op jit(solution)/shard_map/finish_round/pallas_call | solution.py:920
  (218 shorter events, 31.3 us)
Async XLA Ops:
  7.2 4.1 %copy-start = (bf16[864,1152]{1,0:T(8,128)(2,1)S(1)}, bf16[864,1152]{1,0:T(8,128)(2,1)}, u32[]{:S(2)}) copy-start(bf16[864,1152]{1,0:T(8,128)(2,1)} %param.32) | copy-start | bytes 5971972
  7.2 110.8 %all-gather.3.cloned.1.call-start = ((), (), s32[]{:S(2)}) async-start(), calls=%async_computation.2 | async-start | bytes 9289728 | tf_op jit(solution)/shard_map/all_gather | solution.py:1342
  11.2 148.6 %all-gather.5.cloned.1.call-start = ((), (), s32[]{:S(2)}) async-start(), calls=%async_computation.3 | async-start | bytes 4644864 | tf_op jit(solution)/shard_map/all_gather | solution.py:1342
  12.3 50.9 %copy-start.2 = (bf16[1,128,1152]{2,1,0:T(8,128)(2,1)S(1)}, bf16[1,128,1152]{2,1,0:T(8,128)(2,1)}, u32[]{:S(2)}) copy-start(bf16[1,128,1152]{2,1,0:T(8,128)(2,1)} %param.17) | copy-start | bytes 884740
  12.3 247.2 %reduce-scatter.3.cloned.1.call-start = ((), (), s32[]{:S(2)}) async-start(), calls=%async_computation.4 | async-start | bytes 4644864 | tf_op jit(solution)/shard_map/reduce_scatter | solution.py:1346
  63.3 2.3 copy-start.46
  68.9 19.3 %copy-start.42 = (f32[128]{0:T(128)}, f32[128]{0:T(128)S(1)}, u32[]{:S(2)}) copy-start(f32[128]{0:T(128)S(1)} %multiply_power_fusion) | copy-start | bytes 1540
  69.0 20.5 %copy-start.19 = (f32[128,256]{1,0:T(8,128)}, f32[128,256]{1,0:T(8,128)S(1)}, u32[]{:S(2)}) copy-start(f32[128,256]{1,0:T(8,128)S(1)} %get-tuple-element.117) | copy-start | bytes 393220
  69.5 18.7 %copy-start.35 = (f32[128]{0:T(128)}, f32[128]{0:T(128)S(1)}, u32[]{:S(2)}) copy-start(f32[128]{0:T(128)S(1)} %fusion.69) | copy-start | bytes 1540
  69.5 19.9 %copy-start.44 = (f32[128]{0:T(128)}, f32[128]{0:T(128)S(1)}, u32[]{:S(2)}) copy-start(f32[128]{0:T(128)S(1)} %bitcast_convert_fusion) | copy-start | bytes 1540
  89.5 2.0 copy-start.21
  89.6 1.9 copy-start.31
  91.5 157.2 %copy-start.40 = (f32[4,128]{1,0:T(4,128)}, f32[4,128]{1,0:T(4,128)S(1)}, u32[]{:S(2)}) copy-start(f32[4,128]{1,0:T(4,128)S(1)} %get-tuple-element.147) | copy-start | bytes 6148
  96.6 19.4 %copy-start.3 = (f32[128,1152]{1,0:T(8,128)}, f32[128,1152]{1,0:T(8,128)S(1)}, u32[]{:S(2)}) copy-start(f32[128,1152]{1,0:T(8,128)S(1)} %get-tuple-element.115.middle_ref) | copy-start | bytes 1769476
  202.1 113.3 %reduce-scatter.5.cloned.1.call-start = ((), (), s32[]{:S(2)}) async-start(), calls=%async_computation.5 | async-start | bytes 5308416 | tf_op jit(solution)/shard_map/reduce_scatter | solution.py:1346
  240.0 2.3 copy-start.17
  240.0 2.3 copy-start.26
  244.0 2.9 copy-start.22
  250.0 2.3 copy-start.41
  252.3 3.0 copy-start.12
  252.3 3.0 copy-start.25
  259.5 25.4 %copy-start.16 = (f32[640,256]{1,0:T(8,128)S(1)}, f32[640,256]{1,0:T(8,128)}, u32[]{:S(2)}) copy-start(f32[640,256]{1,0:T(8,128)} %convolution_bitcast_fusion.3) | copy-start | bytes 1966084
  284.9 2.2 copy-start.49
  286.1 3.8 copy-start.6
  286.1 3.8 copy-start.18
  305.8 2.3 copy-start.30
  305.8 2.3 copy-start.47
  305.8 2.4 copy-start.57
  308.1 2.1 copy-start.38
  310.3 1.8 copy-start.14
  375.7 10.9 %copy-start.28 = (bf16[128,1152]{1,0:T(8,128)(2,1)S(1)}, bf16[128,1152]{1,0:T(8,128)(2,1)}, u32[]{:S(2)}) copy-start(bf16[128,1152]{1,0:T(8,128)(2,1)} %get-tuple-element.70) | copy-start | bytes 884740
  375.7 11.6 %copy-start.1 = (bf16[864,1152]{1,0:T(8,128)(2,1)S(1)}, bf16[864,1152]{1,0:T(8,128)(2,1)}, u32[]{:S(2)}) copy-start(bf16[864,1152]{1,0:T(8,128)(2,1)} %param.32) | copy-start | bytes 5971972
  (30 other events, 35.8 us)
Sparse Core Ops, SparseCore 0:
  11.3 95.1 all-gather.2
  108.8 51.0 all-gather.4
  202.2 51.9 reduce-scatter.2
  256.3 58.9 reduce-scatter.4

commit v13 on v12

--- a/solution.py
+++ b/solution.py
@@ -216,31 +216,45 @@
     halves = (pl.ds(0, cut), pl.ds(cut, columns - cut))
 
     def product(place, stretch):
-        rows = pl.ds(pl.multiple_of(place * tok_count, tok_count), tok_count)
+        start = (place // 2) * 2 * tok_count
+        rows = pl.ds(pl.multiple_of(start, 2 * tok_count), 2 * tok_count)
         return jnp.dot(mixed_ref[rows, :], down_ref[:, stretch], preferred_element_type=F32)
 
     copies = [
         pltpu.make_async_remote_copy(
-            src_ref=part_ref.at[turn, :, stretch],
+            src_ref=part_ref.at[base + lax.rem(peer, 2), :, stretch],
             dst_ref=taken_ref.at[turn, :, stretch],
             send_sem=send_sem.at[turn, half],
             recv_sem=recv_sem.at[turn, half],
             device_id={"batch": peer},
             device_id_type=MESH,
         )
-        for turn, peer in enumerate(order)
         for half, stretch in enumerate(halves)
+        for turn, (peer, base) in enumerate(((corner, 0), (along, 0), (across, 2)))
     ]
-    for index in range(len(copies)):
-        turn, stretch = index // 2, halves[index % 2]
-        part_ref[turn, :, stretch] = product(order[turn], stretch).astype(BF16)
-        if index > 0:
-            copies[index - 1].start()
-    total = product(me, pl.ds(0, columns))
-    copies[-1].start()
+
+    def multiply(place, base, half):
+        both = product(place, halves[half])
+        for row in range(2):
+            block = both[row * tok_count : (row + 1) * tok_count]
+            part_ref[base + row, :, halves[half]] = block.astype(BF16)
+        upper = jnp.broadcast_to(lax.rem(me, 2) == 0, (tok_count, both.shape[1]))
+        return jnp.where(upper, both[:tok_count], both[tok_count:])
+
+    multiply(along, 0, 0)
+    multiply(along, 0, 1)
+    copies[0].start()
+    copies[1].start()
+    own_first = multiply(me, 2, 0)
+    copies[3].start()
+    copies[4].start()
+    own_second = multiply(me, 2, 1)
+    copies[2].start()
+    total = jnp.concatenate([own_first, own_second], axis=1)
+    copies[5].start()
     for turn in range(3):
-        for copy in copies[2 * turn : 2 * turn + 2]:
-            copy.wait_recv()
+        copies[turn].wait_recv()
+        copies[3 + turn].wait_recv()
         total = total + taken_ref[turn].astype(F32)
     gain = gain_ref[...]
     valid = valid_ref[...]
@@ -294,7 +308,7 @@
         in_specs=[vmem] * 6,
         out_specs=[vmem] * 3,
         scratch_shapes=[
-            pltpu.VMEM((3, tok_count, width), BF16),
+            pltpu.VMEM((4, tok_count, width), BF16),
             pltpu.VMEM((3, tok_count, width), BF16),
             dma((3, 2)),
             dma((3, 2)),

time: 401 us -> 402 us (level)
  no operation moved by 1% of the time
where the time goes in v13:
time: 402 us; the launch traced here: 394 us
  Pallas kernels  309 us (77%)
  local copies, waits for them, and re-layouts  23.2 us (6%)
  matrix products  21.2 us (5%)
  between operations  15.5 us (4%)
  other arithmetic  15 us (4%)
  waiting for transfers between devices  9.72 us (2%)
    pallas_call x1, Pallas kernels, tail_round(): pl.pallas_call(functools.partial(tail_kernel, n_ctx), name='tail_round',...  60.5 us
    pallas_call x1, Pallas kernels, gather_weights(): pl.pallas_call(functools.partial(weights_kernel, n_batch, n_ctx), name='g...  48.3 us
    pallas_call x2, Pallas kernels, halo_call(): pl.pallas_call(kernel, out_shape=out_shape, in_specs=[vmem if i < in_vmem...  43 us
    pallas_call x2, Pallas kernels, square_gather(): pl.pallas_call(functools.partial(square_kernel, count), out_shape=[jax.Sh...  37.4 us
    pallas_call x1, Pallas kernels, turn_round(): pl.pallas_call(turn_kernel, name='turn_round', out_shape=(jax.ShapeDtypeS...  35.6 us
    pallas_call x1, Pallas kernels, hidden_back(): pl.pallas_call(back_kernel, name='hidden_back', grid=(count,), out_shape=...  21 us
    pallas_call x1, Pallas kernels, sum_back(): pl.pallas_call(functools.partial(sum_back_kernel, tile), name='sum_back',...  17.5 us
    pallas_call x1, Pallas kernels, batch_exchange(): pl.pallas_call(functools.partial(batch_kernel, size, kinds), out_shape=sh...  14.7 us
  transfers between devices with their start and end apart: 4, of which 2 were waited for; matrix products, arithmetic and copies ran while one was open for 13% of the time, Pallas kernels for 49%

profile of v13, /device:TPU:0, one launch (start us, length us, event | category | flops | bytes accessed | tf_op | source)
XLA Modules:
  0.0 394.4 jit_solution(17435536652001175886)
XLA Ops:
  7.2 3.9 pick_columns.1
  13.9 48.3 %gather_weights.1 = (bf16[4,8,144,384]{3,2,1,0:T(8,128)(2,1)}, bf16[8,4,32,1152]{3,2,1,0:T(8,128)(2,1)}, bf16[8,1,640]{2,1,0:T(2,128)(2,1)}) custom-call(bf16[4,144,384]{2,1,0:T(8,128)(2,1)} %bitcast.204, bf16[4,32,1152]{2,1,0:T(8,128)(2,1)} %bitcast.216, bf16[1,640]{1,0:T(2,128)(2,1)} %broadcast_in_dim.32.gain_ref), custom_call_target="tpu_custom_call" | custom-call | tf_op jit(solution)/shard_map/gather_weights/pallas_call | solution.py:1070
  63.3 2.3 fusion.91
  70.7 17.5 %shard_map.280 = bf16[4,128,512]{2,1,0:T(8,128)(2,1)} custom-call(bf16[128,512]{1,0:T(8,128)(2,1)} %pad_maximum_fusion.9.source_ref), custom_call_target="tpu_custom_call" | custom-call | tf_op jit(solution)/shard_map/pallas_call | solution.py:818
  88.4 1.1 maximum_maximum_fusion
  89.9 1.6 fusion.96
  91.5 0.9 convolution_convert_fusion.1
  93.3 2.3 multiply_reduce_fusion.6
  95.6 1.0 multiply_reduce_fusion.5
  97.5 16.0 %shard_map.281 = bf16[4,128,1152]{2,1,0:T(8,128)(2,1)} custom-call(bf16[128,1152]{1,0:T(8,128)(2,1)} %multiply_convert_fusion.1.refs_0_), custom_call_target="tpu_custom_call" | custom-call | tf_op jit(solution)/shard_map/pallas_call | solution.py:172
  113.6 2.4 copy.191
  118.0 12.0 %hidden_mix.1 = (f32[512,1792]{1,0:T(8,128)}, f32[512,1792]{1,0:T(8,128)}, bf16[512,1792]{1,0:T(8,128)(2,1)}, bf16[1792,512]{1,0:T(8,128)(2,1)}) custom-call(bf16[512,1152]{1,0:T(8,128)(2,1)} %bitcast.183, bf16[1152,3584]{1,0:T(8,128)(2,1)} %all-gather.3.cloned.1.call-done.w_gate_ref.w_up_ref, bf16[1152,3584]{1,0:T(8,128)(2,1)} %all-gather.3.cloned.1.call-done.w_gate_ref.w_up_ref), custom_call_target="tpu_custom_call" | custom-call | flops 4227858432 | bytes 25165824 | tf_op jit(solution)/shard_map/hidden_mix/pallas_call | solution.py:361
  130.0 21.4 %shard_map.282 = (bf16[4,128,1152]{2,1,0:T(8,128)(2,1)}, bf16[4,128,1024]{2,1,0:T(8,128)(2,1)}) custom-call(bf16[128,1152]{1,0:T(8,128)(2,1)} %get-tuple-element.64.refs_0_, bf16[128,1024]{1,0:T(8,128)(2,1)} %copy.190.refs_1_), custom_call_target="tpu_custom_call" | custom-call | tf_op jit(solution)/shard_map/pallas_call | solution.py:172
  151.4 8.4 %all-gather.5.cloned.1.call-done.down_ref = bf16[1792,1152]{1,0:T(8,128)(2,1)} async-done(((bf16[224,1152]{1,0:T(8,128)(2,1)}), bf16[1792,1152]{1,0:T(8,128)(2,1)}) %all-gather.5.cloned.1.call-update) | async-done | bytes 4128784 | tf_op jit(solution)/shard_map/all_gather | solution.py:1356
  159.8 35.6 %turn_round.1 = (bf16[128,1152]{1,0:T(8,128)(2,1)}, bf16[4,128,1152]{2,1,0:T(8,128)(2,1)}, f32[1,1152]{1,0:T(1,128)}) custom-call(bf16[512,1792]{1,0:T(8,128)(2,1)} %get-tuple-element.69.mixed_ref, bf16[1792,1152]{1,0:T(8,128)(2,1)} %all-gather.5.cloned.1.call-done.down_ref, f32[128,1152]{1,0:T(8,128)} %copy-done.3, bf16[128,1152]{1,0:T(8,128)(2,1)} %bitcast.215, ...), custom_call_target="tpu_custom_call" | custom-call | flops 2113929216 | bytes 8388608 | tf_op jit(solution)/shard_map/turn_round/pallas_call | solution.py:300
  195.5 6.3 %shard_map.283 = bf16[1792,1152]{1,0:T(8,128)(2,1)} custom-call(bf16[1792,512]{1,0:T(8,128)(2,1)} %get-tuple-element.71.left_ref, bf16[512,1152]{1,0:T(8,128)(2,1)} %bitcast.209), custom_call_target="tpu_custom_call" | custom-call | flops 2113929216 | bytes 8388608 | tf_op jit(solution)/shard_map/pallas_call | solution.py:330
  202.1 21.0 %hidden_back.1 = (bf16[512,1792]{1,0:T(8,128)(2,1)}, bf16[512,1792]{1,0:T(8,128)(2,1)}, bf16[512,1152]{1,0:T(8,128)(2,1)}) custom-call(bf16[512,1152]{1,0:T(8,128)(2,1)} %bitcast.210, bf16[1792,1152]{1,0:T(8,128)(2,1)} %all-gather.5.cloned.1.call-done.down_ref, f32[512,1792]{1,0:T(8,128)} %get-tuple-element.74.gate_ref, ...), custom_call_target="tpu_custom_call" | custom-call | flops 6341787648 | bytes 25165824 | tf_op jit(solution)/shard_map/hidden_back/pallas_call | solution.py:413
  223.1 17.5 %sum_back.1 = (f32[128,1152]{1,0:T(8,128)}, bf16[1152,2048]{1,0:T(8,128)(2,1)}) custom-call(bf16[4,128,1152]{2,1,0:T(8,128)(2,1)} %bitcast.223, bf16[1152,512]{1,0:T(8,128)(2,1)} %bitcast.194, bf16[512,1792]{1,0:T(8,128)(2,1)} %get-tuple-element.78.gate_ref, bf16[512,1792]{1,0:T(8,128)(2,1)} %get-tuple-element.79.up_ref), custom_call_target="tpu_custom_call" | custom-call | flops 2415919104 | bytes 12582912 | tf_op jit(solution)/shard_map/sum_back/pallas_call | solution.py:526
  241.7 1.3 multiply_reduce_fusion.1
  244.7 2.6 convolution_convert_fusion
  247.5 1.8 multiply_reduce_fusion
  252.9 3.0 convolution_bitcast_fusion.3
  258.9 1.2 convolution_add_fusion.2
  260.1 25.5 %shard_map.284 = (f32[128,512]{1,0:T(8,128)}, bf16[4,224,1152]{2,1,0:T(8,128)(2,1)}, bf16[1152,1536]{1,0:T(8,128)(2,1)}) custom-call(bf16[4,128,512]{2,1,0:T(8,128)(2,1)} %bitcast.203, bf16[224,1152]{1,0:T(8,128)(2,1)} %reduce-scatter.3.cloned.1.call-done.shard_ref, bf16[1152,512]{1,0:T(8,128)(2,1)} %bitcast.195, bf16[512,1792]{1,0:T(8,128)(2,1)} %get-tuple-element.79.up_ref), custom_call_target="tpu_custom_call" | custom-call | tf_op jit(solution)/shard_map/pallas_call | solution.py:818
  285.7 1.1 fusion.45
  292.5 14.7 %shard_map.285 = (f32[4,8,640]{2,1,0:T(8,128)}, bf16[4,128,384]{2,1,0:T(8,128)(2,1)}, bf16[4,128,288]{2,1,0:T(8,128)(2,1)}) custom-call(f32[8,640]{1,0:T(8,128)} %concatenate.54.refs_0_, bf16[4,128,384]{2,1,0:T(8,128)(2,1)} %bitcast.206, bf16[4,128,288]{2,1,0:T(8,128)(2,1)} %bitcast.208), custom_call_target="tpu_custom_call" | custom-call | tf_op jit(solution)/shard_map/pallas_call | solution.py:102
  307.3 1.9 fusion.11
  309.7 2.1 fusion.3
  311.8 1.8 fusion.6.attn_ref
  314.5 1.2 reduce-scatter.5.cloned.1.call-done.both_ref
  315.7 60.5 %tail_round.1 = (bf16[4,144,1792]{2,1,0:T(8,128)(2,1)}, bf16[4,144,1792]{2,1,0:T(8,128)(2,1)}, bf16[4,288,384]{2,1,0:T(8,128)(2,1)}) custom-call(bf16[144,2048]{1,0:T(8,128)(2,1)} %reduce-scatter.5.cloned.1.call-done.both_ref, bf16[8,144,1536]{2,1,0:T(8,128)(2,1)} %bitcast.200, bf16[8,288,384]{2,1,0:T(8,128)(2,1)} %fusion.6.attn_ref), custom_call_target="tpu_custom_call" | custom-call | tf_op jit(solution)/shard_map/tail_round/pallas_call | solution.py:1332
  376.3 8.9 %finish_round.1 = (f32[144,6912]{1,0:T(8,128)}, f32[144,6912]{1,0:T(8,128)}, f32[864,1152]{1,0:T(8,128)}, f32[144,1024]{1,0:T(8,128)}, f32[144,256]{1,0:T(8,128)...) custom-call(bf16[4,144,1792]{2,1,0:T(8,128)(2,1)} %get-tuple-element.91.gate_ref, ...), custom_call_target="tpu_custom_call" | custom-call | tf_op jit(solution)/shard_map/finish_round/pallas_call | solution.py:934
  (218 shorter events, 31.3 us)
Async XLA Ops:
  7.2 4.1 %copy-start = (bf16[864,1152]{1,0:T(8,128)(2,1)S(1)}, bf16[864,1152]{1,0:T(8,128)(2,1)}, u32[]{:S(2)}) copy-start(bf16[864,1152]{1,0:T(8,128)(2,1)} %param.32) | copy-start | bytes 5971972
  7.2 110.8 %all-gather.3.cloned.1.call-start = ((), (), s32[]{:S(2)}) async-start(), calls=%async_computation.2 | async-start | bytes 9289728 | tf_op jit(solution)/shard_map/all_gather | solution.py:1356
  11.2 148.6 %all-gather.5.cloned.1.call-start = ((), (), s32[]{:S(2)}) async-start(), calls=%async_computation.3 | async-start | bytes 4644864 | tf_op jit(solution)/shard_map/all_gather | solution.py:1356
  12.3 50.9 %copy-start.2 = (bf16[1,128,1152]{2,1,0:T(8,128)(2,1)S(1)}, bf16[1,128,1152]{2,1,0:T(8,128)(2,1)}, u32[]{:S(2)}) copy-start(bf16[1,128,1152]{2,1,0:T(8,128)(2,1)} %param.17) | copy-start | bytes 884740
  12.3 247.8 %reduce-scatter.3.cloned.1.call-start = ((), (), s32[]{:S(2)}) async-start(), calls=%async_computation.4 | async-start | bytes 4644864 | tf_op jit(solution)/shard_map/reduce_scatter | solution.py:1360
  63.3 2.3 copy-start.46
  68.9 19.3 %copy-start.42 = (f32[128]{0:T(128)}, f32[128]{0:T(128)S(1)}, u32[]{:S(2)}) copy-start(f32[128]{0:T(128)S(1)} %multiply_power_fusion) | copy-start | bytes 1540
  69.0 20.5 %copy-start.19 = (f32[128,256]{1,0:T(8,128)}, f32[128,256]{1,0:T(8,128)S(1)}, u32[]{:S(2)}) copy-start(f32[128,256]{1,0:T(8,128)S(1)} %get-tuple-element.117) | copy-start | bytes 393220
  69.5 18.7 %copy-start.35 = (f32[128]{0:T(128)}, f32[128]{0:T(128)S(1)}, u32[]{:S(2)}) copy-start(f32[128]{0:T(128)S(1)} %fusion.69) | copy-start | bytes 1540
  69.5 19.9 %copy-start.44 = (f32[128]{0:T(128)}, f32[128]{0:T(128)S(1)}, u32[]{:S(2)}) copy-start(f32[128]{0:T(128)S(1)} %bitcast_convert_fusion) | copy-start | bytes 1540
  89.5 2.0 copy-start.21
  89.6 1.9 copy-start.31
  91.5 157.8 %copy-start.40 = (f32[4,128]{1,0:T(4,128)}, f32[4,128]{1,0:T(4,128)S(1)}, u32[]{:S(2)}) copy-start(f32[4,128]{1,0:T(4,128)S(1)} %get-tuple-element.147) | copy-start | bytes 6148
  96.6 19.4 %copy-start.3 = (f32[128,1152]{1,0:T(8,128)}, f32[128,1152]{1,0:T(8,128)S(1)}, u32[]{:S(2)}) copy-start(f32[128,1152]{1,0:T(8,128)S(1)} %get-tuple-element.115.middle_ref) | copy-start | bytes 1769476
  201.8 113.9 %reduce-scatter.5.cloned.1.call-start = ((), (), s32[]{:S(2)}) async-start(), calls=%async_computation.5 | async-start | bytes 5308416 | tf_op jit(solution)/shard_map/reduce_scatter | solution.py:1360
  240.7 2.3 copy-start.17
  240.7 2.3 copy-start.26
  244.7 2.8 copy-start.22
  250.6 2.3 copy-start.41
  252.9 3.0 copy-start.12
  252.9 3.0 copy-start.25
  260.1 25.6 %copy-start.16 = (f32[640,256]{1,0:T(8,128)S(1)}, f32[640,256]{1,0:T(8,128)}, u32[]{:S(2)}) copy-start(f32[640,256]{1,0:T(8,128)} %convolution_bitcast_fusion.3) | copy-start | bytes 1966084
  285.7 2.2 copy-start.49
  286.8 3.8 copy-start.6
  286.8 3.8 copy-start.18
  307.2 2.3 copy-start.30
  307.3 2.4 copy-start.47
  307.3 2.4 copy-start.57
  309.6 2.1 copy-start.38
  311.8 1.8 copy-start.14
  376.3 10.9 %copy-start.28 = (bf16[128,1152]{1,0:T(8,128)(2,1)S(1)}, bf16[128,1152]{1,0:T(8,128)(2,1)}, u32[]{:S(2)}) copy-start(bf16[128,1152]{1,0:T(8,128)(2,1)} %get-tuple-element.70) | copy-start | bytes 884740
  376.3 11.6 %copy-start.1 = (bf16[864,1152]{1,0:T(8,128)(2,1)S(1)}, bf16[864,1152]{1,0:T(8,128)(2,1)}, u32[]{:S(2)}) copy-start(bf16[864,1152]{1,0:T(8,128)(2,1)} %param.32) | copy-start | bytes 5971972
  (30 other events, 35.7 us)
Sparse Core Ops, SparseCore 0:
  11.3 95.1 all-gather.2
  108.8 51.0 all-gather.4
  201.9 52.5 reduce-scatter.2
  256.7 58.9 reduce-scatter.4

commit v14 on v13

--- a/solution.py
+++ b/solution.py
@@ -51,66 +51,125 @@
     return jax.nn.gelu(gate_val, approximate=True) * up_val
 
 
-def batch_kernel(size, kinds, *refs):
-    count = len(kinds)
-    sources, results = refs[:count], refs[count : 2 * count]
-    send_sem, recv_sem, own_sem = refs[2 * count :]
+def spread_kernel(
+    n_chip,
+    gain_ref,
+    first_ref,
+    second_ref,
+    up_ref,
+    gain_out,
+    first_out,
+    second_out,
+    sums_ref,
+    own_ref,
+    taken_ref,
+    send_sem,
+    recv_sem,
+    own_sem,
+    pair_send,
+    pair_recv,
+    load_sem,
+):
     me = lax.axis_index("batch")
+    place_at = lax.axis_index("ctx")
+    core = lax.rem(place_at, 2)
+    near = {"ctx": place_at + 1 - 2 * core}
     barrier = pltpu.get_barrier_semaphore()
-    for step in range(1, size):
+    for step in range(1, 4):
         pl.semaphore_signal(
-            barrier, inc=1, device_id={"batch": lax.rem(me + step, size)}, device_id_type=MESH
+            barrier, inc=1, device_id={"batch": lax.rem(me + step, 4)}, device_id_type=MESH
         )
-    pl.semaphore_wait(barrier, size - 1)
+    pl.semaphore_signal(barrier, inc=1, device_id=near, device_id_type=MESH)
+    pl.semaphore_wait(barrier, 4)
+
+    def remote(source, target, send, recv, peer):
+        copy = pltpu.make_async_remote_copy(
+            src_ref=source,
+            dst_ref=target,
+            send_sem=send,
+            recv_sem=recv,
+            device_id=peer,
+            device_id_type=MESH,
+        )
+        copy.start()
+        return copy
+
+    items = ((gain_ref, gain_out), (first_ref, first_out), (second_ref, second_out))
     copies = []
-    for step in range(1, size):
-        peer = lax.rem(me + step, size)
-        for item in range(count):
-            source = sources[item].at[peer] if kinds[item] else sources[item]
+    for step in range(1, 4):
+        peer = lax.rem(me + step, 4)
+        for item, (source, target) in enumerate(items):
+            block = source.at[peer] if item else source
             copies.append(
-                pltpu.make_async_remote_copy(
-                    src_ref=source,
-                    dst_ref=results[item].at[me],
-                    send_sem=send_sem.at[item, step - 1],
-                    recv_sem=recv_sem.at[item, step - 1],
-                    device_id={"batch": peer},
-                    device_id_type=MESH,
+                remote(
+                    block,
+                    target.at[me],
+                    send_sem.at[item, step - 1],
+                    recv_sem.at[item, step - 1],
+                    {"batch": peer},
                 )
             )
-    for copy in copies:
-        copy.start()
-    own = []
-    for item in range(count):
-        source = sources[item].at[me] if kinds[item] else sources[item]
-        own.append(pltpu.make_async_copy(source, results[item].at[me], own_sem.at[item]))
+    pairs = [
+        remote(
+            up_ref.at[2 * place + 1 - core],
+            taken_ref.at[place],
+            pair_send.at[place],
+            pair_recv.at[place],
+            near,
+        )
+        for place in range(n_chip)
+    ]
+    own = [
+        pltpu.make_async_copy(
+            source.at[me] if item else source, target.at[me], own_sem.at[item]
+        )
+        for item, (source, target) in enumerate(items)
+    ]
+    own += [
+        pltpu.make_async_copy(up_ref.at[2 * place + core], own_ref.at[place], load_sem.at[place])
+        for place in range(n_chip)
+    ]
     for copy in own:
         copy.start()
     for copy in own:
         copy.wait()
+    for place in range(n_chip):
+        pairs[place].wait_recv()
+        sums_ref[place] = (own_ref[place].astype(F32) + taken_ref[place].astype(F32)).astype(BF16)
     for copy in copies:
         copy.wait()
-
-
-def batch_exchange(collective_id, size, whole=(), slots=()):
-    arrays = list(whole) + list(slots)
-    kinds = [0] * len(whole) + [1] * len(slots)
-    count = len(arrays)
-    shapes = [
-        jax.ShapeDtypeStruct(a.shape if k else (size, *a.shape), a.dtype)
-        for a, k in zip(arrays, kinds)
-    ]
+    for copy in pairs:
+        copy.wait_send()
+
+
+def spread_grads(n_ctx, gains, first, second, up):
+    n_chip = n_ctx // 2
+    dma = pltpu.SemaphoreType.DMA
+    vmem = pl.BlockSpec(memory_space=pltpu.VMEM)
+    half = (n_chip, *up.shape[1:])
     return pl.pallas_call(
-        functools.partial(batch_kernel, size, kinds),
-        out_shape=shapes,
-        in_specs=[pl.BlockSpec(memory_space=pltpu.VMEM)] * count,
-        out_specs=[pl.BlockSpec(memory_space=pltpu.VMEM)] * count,
+        functools.partial(spread_kernel, n_chip),
+        name="spread_grads",
+        out_shape=[
+            jax.ShapeDtypeStruct((4, *gains.shape), gains.dtype),
+            jax.ShapeDtypeStruct(first.shape, first.dtype),
+            jax.ShapeDtypeStruct(second.shape, second.dtype),
+            jax.ShapeDtypeStruct(half, up.dtype),
+        ],
+        in_specs=[vmem, vmem, vmem, pl.BlockSpec(memory_space=pl.ANY)],
+        out_specs=[vmem] * 4,
         scratch_shapes=[
-            pltpu.SemaphoreType.DMA((count, size - 1)),
-            pltpu.SemaphoreType.DMA((count, size - 1)),
-            pltpu.SemaphoreType.DMA((count,)),
+            pltpu.VMEM(half, up.dtype),
+            pltpu.VMEM(half, up.dtype),
+            dma((3, 3)),
+            dma((3, 3)),
+            dma((3,)),
+            dma((n_chip,)),
+            dma((n_chip,)),
+            dma((n_chip,)),
         ],
-        compiler_params=pltpu.CompilerParams(collective_id=collective_id, has_side_effects=True),
-    )(*arrays)
+        compiler_params=pltpu.CompilerParams(collective_id=7, has_side_effects=True),
+    )(gains, first, second, up)
 
 
 def square_kernel(count, *refs):
@@ -1098,7 +1157,6 @@
     gate_all,
     up_all,
     attn_all,
-    pair_up,
     pair_attn,
     way_up,
     way_attn,
@@ -1143,8 +1201,8 @@
     width = up_ref.shape[-1]
     cut = width // 256 * 128
     chains = (
-        (up_ref, pair_up, way_up, up_all, pl.ds(0, cut)),
-        (up_ref, pair_up, way_up, up_all, pl.ds(cut, width - cut)),
+        (None, up_ref, way_up, up_all, pl.ds(0, cut)),
+        (None, up_ref, way_up, up_all, pl.ds(cut, width - cut)),
         (attn_ref, pair_attn, way_attn, attn_all, pl.ds(0, attn_ref.shape[-1])),
     )
     gate_width = gate_all.shape[-1]
@@ -1157,8 +1215,8 @@
         return remote(
             source.at[2 * place + 1 - core, :, columns],
             pair.at[place, :, columns],
-            pair_send.at[number, place],
-            pair_recv.at[number, place],
+            pair_send.at[place],
+            pair_recv.at[place],
             near,
         )
 
@@ -1204,9 +1262,8 @@
             copies[-1].start()
         return copies
 
-    for number in numbers:
-        for place in range(n_chip):
-            pair_copy(number, place).start()
+    for place in range(n_chip):
+        pair_copy(2, place).start()
     early = (
         (both_ref.at[:, pl.ds(0, gate_width)], gate_all),
         (both_ref.at[:, pl.ds(gate_width, offset)], up_all),
@@ -1235,7 +1292,7 @@
 
     for number in numbers:
         source, pair, _, _, columns = chains[number]
-        for place in range(n_chip):
+        for place in range(n_chip if source is not None else 0):
             pair_copy(number, place).wait_recv()
             pair[place, :, columns] = (
                 pair[place, :, columns].astype(F32)
@@ -1312,8 +1369,8 @@
         for copy in firsts:
             copy.wait_send()
     for number in numbers:
-        _, pair, _, _, columns = chains[number]
-        for place in range(n_chip):
+        source, pair, _, _, columns = chains[number]
+        for place in range(n_chip if source is not None else 0):
             pair_copy(number, place).wait_send()
         for direction in range(2):
             for step in range(1, n_chip):
@@ -1336,12 +1393,11 @@
         in_specs=[vmem] * 3,
         out_specs=[vmem] * 3,
         scratch_shapes=[
-            pltpu.VMEM((n_chip, *up.shape[1:]), BF16),
             pltpu.VMEM((n_chip, *attn.shape[1:]), BF16),
             pltpu.VMEM((2, n_chip - 1, *up.shape[1:]), BF16),
             pltpu.VMEM((2, n_chip - 1, *attn.shape[1:]), BF16),
-            dma((3, n_chip)),
-            dma((3, n_chip)),
+            dma((n_chip,)),
+            dma((n_chip,)),
             dma((3, 2, n_chip - 1)),
             dma((3, 2, n_chip - 1)),
             dma((5, 4)),
@@ -1580,11 +1636,12 @@
         ],
         axis=1,
     )
-    gain_parts, qkv_slots, proj_slots = batch_exchange(
-        7,
-        n_batch,
-        whole=(gain_rows,),
-        slots=(column_slots(grad_qkv_low), column_slots(grad_proj_low)),
+    gain_parts, qkv_slots, proj_slots, up_sums = spread_grads(
+        n_ctx,
+        gain_rows,
+        column_slots(grad_qkv_low),
+        column_slots(grad_proj_low),
+        up_grad.reshape(n_ctx, width_shard, hidden_part - UP_FIRST),
     )
     proj_rows = w_output.shape[0]
     gain_count = gain_rows.shape[1]
@@ -1613,7 +1670,7 @@
         n_ctx,
         hidden_part,
         grad_w_both,
-        up_grad.reshape(n_ctx, width_shard, hidden_part - UP_FIRST),
+        up_sums,
         packed,
     )
     shapes = (

time: 402 us -> 399 us (level)
  transfers between devices with their start and end apart: 4 -> 4, of which waited for: 2 -> 2; matrix products, arithmetic and copies ran while one was open for 13% -> 13% of each run, Pallas kernels for 49% -> 50%
where the time goes in v14:
time: 399 us; the launch traced here: 392 us
  Pallas kernels  308 us (77%)
  local copies, waits for them, and re-layouts  23.2 us (6%)
  matrix products  21.2 us (5%)
  between operations  15.5 us (4%)
  other arithmetic  14.9 us (4%)
  waiting for transfers between devices  9.02 us (2%)
    pallas_call x1, Pallas kernels, tail_round(): pl.pallas_call(functools.partial(tail_kernel, n_ctx), name='tail_round',...  58.4 us
    pallas_call x1, Pallas kernels, gather_weights(): pl.pallas_call(functools.partial(weights_kernel, n_batch, n_ctx), name='g...  48.3 us
    pallas_call x2, Pallas kernels, halo_call(): pl.pallas_call(kernel, out_shape=out_shape, in_specs=[vmem if i < in_vmem...  43.1 us
    pallas_call x2, Pallas kernels, square_gather(): pl.pallas_call(functools.partial(square_kernel, count), out_shape=[jax.Sh...  37.4 us
    pallas_call x1, Pallas kernels, turn_round(): pl.pallas_call(turn_kernel, name='turn_round', out_shape=(jax.ShapeDtypeS...  35.6 us
    pallas_call x1, Pallas kernels, hidden_back(): pl.pallas_call(back_kernel, name='hidden_back', grid=(count,), out_shape=...  21 us
    pallas_call x1, Pallas kernels, sum_back(): pl.pallas_call(functools.partial(sum_back_kernel, tile), name='sum_back',...  17.5 us
    pallas_call x1, Pallas kernels, spread_grads(): pl.pallas_call(functools.partial(spread_kernel, n_chip), name='spread_gra...  15.4 us
  transfers between devices with their start and end apart: 4, of which 2 were waited for; matrix products, arithmetic and copies ran while one was open for 13% of the time, Pallas kernels for 50%

profile of v14, /device:TPU:0, one launch (start us, length us, event | category | flops | bytes accessed | tf_op | source)
XLA Modules:
  0.0 392.3 jit_solution(2521424501030783261)
XLA Ops:
  7.2 3.9 %pick_columns.1 = bf16[144,3584]{1,0:T(8,128)(2,1)} custom-call(bf16[144,6912]{1,0:T(8,128)(2,1)} %gate_ref.1, bf16[144,6912]{1,0:T(8,128)(2,1)} %up_ref.1), custom_call_target="tpu_custom_call" | custom-call | tf_op jit(solution)/shard_map/pick_columns/pallas_call | solution.py:935
  13.9 48.3 %gather_weights.1 = (bf16[4,8,144,384]{3,2,1,0:T(8,128)(2,1)}, bf16[8,4,32,1152]{3,2,1,0:T(8,128)(2,1)}, bf16[8,1,640]{2,1,0:T(2,128)(2,1)}) custom-call(bf16[4,144,384]{2,1,0:T(8,128)(2,1)} %bitcast.204, bf16[4,32,1152]{2,1,0:T(8,128)(2,1)} %bitcast.216, bf16[1,640]{1,0:T(2,128)(2,1)} %broadcast_in_dim.32.gain_ref), custom_call_target="tpu_custom_call" | custom-call | tf_op jit(solution)/shard_map/gather_weights/pallas_call | solution.py:1129
  63.3 2.3 fusion.91
  70.7 17.5 %shard_map.280 = bf16[4,128,512]{2,1,0:T(8,128)(2,1)} custom-call(bf16[128,512]{1,0:T(8,128)(2,1)} %pad_maximum_fusion.9.source_ref), custom_call_target="tpu_custom_call" | custom-call | tf_op jit(solution)/shard_map/pallas_call | solution.py:877
  88.4 1.1 maximum_maximum_fusion
  89.9 1.6 fusion.96
  91.5 0.9 convolution_convert_fusion.1
  93.3 2.3 multiply_reduce_fusion.6
  95.6 1.0 multiply_reduce_fusion.5
  97.5 16.0 %shard_map.281 = bf16[4,128,1152]{2,1,0:T(8,128)(2,1)} custom-call(bf16[128,1152]{1,0:T(8,128)(2,1)} %multiply_convert_fusion.1.refs_0_), custom_call_target="tpu_custom_call" | custom-call | tf_op jit(solution)/shard_map/pallas_call | solution.py:231
  113.6 2.4 copy.191
  118.0 12.0 %hidden_mix.1 = (f32[512,1792]{1,0:T(8,128)}, f32[512,1792]{1,0:T(8,128)}, bf16[512,1792]{1,0:T(8,128)(2,1)}, bf16[1792,512]{1,0:T(8,128)(2,1)}) custom-call(bf16[512,1152]{1,0:T(8,128)(2,1)} %bitcast.183, bf16[1152,3584]{1,0:T(8,128)(2,1)} %all-gather.3.cloned.1.call-done.w_gate_ref.w_up_ref, bf16[1152,3584]{1,0:T(8,128)(2,1)} %all-gather.3.cloned.1.call-done.w_gate_ref.w_up_ref), custom_call_target="tpu_custom_call" | custom-call | flops 4227858432 | bytes 25165824 | tf_op jit(solution)/shard_map/hidden_mix/pallas_call | solution.py:420
  130.0 21.4 %shard_map.282 = (bf16[4,128,1152]{2,1,0:T(8,128)(2,1)}, bf16[4,128,1024]{2,1,0:T(8,128)(2,1)}) custom-call(bf16[128,1152]{1,0:T(8,128)(2,1)} %get-tuple-element.65.refs_0_, bf16[128,1024]{1,0:T(8,128)(2,1)} %copy.190.refs_1_), custom_call_target="tpu_custom_call" | custom-call | tf_op jit(solution)/shard_map/pallas_call | solution.py:231
  151.4 8.4 %all-gather.5.cloned.1.call-done.down_ref = bf16[1792,1152]{1,0:T(8,128)(2,1)} async-done(((bf16[224,1152]{1,0:T(8,128)(2,1)}), bf16[1792,1152]{1,0:T(8,128)(2,1)}) %all-gather.5.cloned.1.call-update) | async-done | bytes 4128784 | tf_op jit(solution)/shard_map/all_gather | solution.py:1412
  159.8 35.6 %turn_round.1 = (bf16[128,1152]{1,0:T(8,128)(2,1)}, bf16[4,128,1152]{2,1,0:T(8,128)(2,1)}, f32[1,1152]{1,0:T(1,128)}) custom-call(bf16[512,1792]{1,0:T(8,128)(2,1)} %get-tuple-element.70.mixed_ref, bf16[1792,1152]{1,0:T(8,128)(2,1)} %all-gather.5.cloned.1.call-done.down_ref, f32[128,1152]{1,0:T(8,128)} %copy-done.3, bf16[128,1152]{1,0:T(8,128)(2,1)} %bitcast.215, ...), custom_call_target="tpu_custom_call" | custom-call | flops 2113929216 | bytes 8388608 | tf_op jit(solution)/shard_map/turn_round/pallas_call | solution.py:359
  195.5 6.3 %shard_map.283 = bf16[1792,1152]{1,0:T(8,128)(2,1)} custom-call(bf16[1792,512]{1,0:T(8,128)(2,1)} %get-tuple-element.72.left_ref, bf16[512,1152]{1,0:T(8,128)(2,1)} %bitcast.209), custom_call_target="tpu_custom_call" | custom-call | flops 2113929216 | bytes 8388608 | tf_op jit(solution)/shard_map/pallas_call | solution.py:389
  202.1 21.0 %hidden_back.1 = (bf16[512,1792]{1,0:T(8,128)(2,1)}, bf16[512,1792]{1,0:T(8,128)(2,1)}, bf16[512,1152]{1,0:T(8,128)(2,1)}) custom-call(bf16[512,1152]{1,0:T(8,128)(2,1)} %bitcast.210, bf16[1792,1152]{1,0:T(8,128)(2,1)} %all-gather.5.cloned.1.call-done.down_ref, f32[512,1792]{1,0:T(8,128)} %get-tuple-element.75.gate_ref, ...), custom_call_target="tpu_custom_call" | custom-call | flops 6341787648 | bytes 25165824 | tf_op jit(solution)/shard_map/hidden_back/pallas_call | solution.py:472
  223.1 17.5 %sum_back.1 = (f32[128,1152]{1,0:T(8,128)}, bf16[1152,2048]{1,0:T(8,128)(2,1)}) custom-call(bf16[4,128,1152]{2,1,0:T(8,128)(2,1)} %bitcast.223, bf16[1152,512]{1,0:T(8,128)(2,1)} %bitcast.194, bf16[512,1792]{1,0:T(8,128)(2,1)} %get-tuple-element.79.gate_ref, bf16[512,1792]{1,0:T(8,128)(2,1)} %get-tuple-element.80.up_ref), custom_call_target="tpu_custom_call" | custom-call | flops 2415919104 | bytes 12582912 | tf_op jit(solution)/shard_map/sum_back/pallas_call | solution.py:585
  241.7 1.3 multiply_reduce_fusion.1
  244.7 2.6 convolution_convert_fusion
  247.6 1.8 multiply_reduce_fusion
  253.0 3.0 convolution_bitcast_fusion.3
  258.9 1.2 convolution_add_fusion.2
  260.1 25.6 %shard_map.284 = (f32[128,512]{1,0:T(8,128)}, bf16[4,224,1152]{2,1,0:T(8,128)(2,1)}, bf16[1152,1536]{1,0:T(8,128)(2,1)}) custom-call(bf16[4,128,512]{2,1,0:T(8,128)(2,1)} %bitcast.203, bf16[224,1152]{1,0:T(8,128)(2,1)} %reduce-scatter.3.cloned.1.call-done.shard_ref, bf16[1152,512]{1,0:T(8,128)(2,1)} %bitcast.195, bf16[512,1792]{1,0:T(8,128)(2,1)} %get-tuple-element.80.up_ref), custom_call_target="tpu_custom_call" | custom-call | tf_op jit(solution)/shard_map/pallas_call | solution.py:877
  285.8 1.1 fusion.45
  289.8 0.9 copy.171
  292.6 15.4 %spread_grads.1 = (f32[4,8,640]{2,1,0:T(8,128)}, bf16[4,128,384]{2,1,0:T(8,128)(2,1)}, bf16[4,128,288]{2,1,0:T(8,128)(2,1)}, bf16[4,144,1536]{2,1,0:T(8,128)(2,1)}) custom-call(f32[8,640]{1,0:T(8,128)} %concatenate.54.gain_ref, bf16[4,128,384]{2,1,0:T(8,128)(2,1)} %bitcast.207, bf16[4,128,288]{2,1,0:T(8,128)(2,1)} %bitcast.206, bf16[8,144,1536]{2,1,0:T(8,128)(2,1)} %bitcast.200), custom_call_target="tpu_custom_call" | custom-call | tf_op jit(solution)/shard_map/spread_grads/pallas_call | solution.py:150
  308.0 1.9 fusion.11
  310.3 2.1 fusion.3
  312.5 1.8 fusion.6.attn_ref
  315.7 58.4 %tail_round.1 = (bf16[4,144,1792]{2,1,0:T(8,128)(2,1)}, bf16[4,144,1792]{2,1,0:T(8,128)(2,1)}, bf16[4,288,384]{2,1,0:T(8,128)(2,1)}) custom-call(bf16[144,2048]{1,0:T(8,128)(2,1)} %reduce-scatter.5.cloned.1.call-done.both_ref, bf16[4,144,1536]{2,1,0:T(8,128)(2,1)} %get-tuple-element.87.up_ref, bf16[8,288,384]{2,1,0:T(8,128)(2,1)} %fusion.6.attn_ref), custom_call_target="tpu_custom_call" | custom-call | tf_op jit(solution)/shard_map/tail_round/pallas_call | solution.py:1389
  374.2 8.9 %finish_round.1 = (f32[144,6912]{1,0:T(8,128)}, f32[144,6912]{1,0:T(8,128)}, f32[864,1152]{1,0:T(8,128)}, f32[144,1024]{1,0:T(8,128)}, f32[144,256]{1,0:T(8,128)...) custom-call(bf16[4,144,1792]{2,1,0:T(8,128)(2,1)} %get-tuple-element.93.gate_ref, ...), custom_call_target="tpu_custom_call" | custom-call | tf_op jit(solution)/shard_map/finish_round/pallas_call | solution.py:993
  (218 shorter events, 30.9 us)
Async XLA Ops:
  7.2 4.1 %copy-start = (bf16[864,1152]{1,0:T(8,128)(2,1)S(1)}, bf16[864,1152]{1,0:T(8,128)(2,1)}, u32[]{:S(2)}) copy-start(bf16[864,1152]{1,0:T(8,128)(2,1)} %param.32) | copy-start | bytes 5971972
  7.2 110.8 %all-gather.3.cloned.1.call-start = ((), (), s32[]{:S(2)}) async-start(), calls=%async_computation.2 | async-start | bytes 9289728 | tf_op jit(solution)/shard_map/all_gather | solution.py:1412
  11.2 148.6 %all-gather.5.cloned.1.call-start = ((), (), s32[]{:S(2)}) async-start(), calls=%async_computation.3 | async-start | bytes 4644864 | tf_op jit(solution)/shard_map/all_gather | solution.py:1412
  12.3 50.9 %copy-start.2 = (bf16[1,128,1152]{2,1,0:T(8,128)(2,1)S(1)}, bf16[1,128,1152]{2,1,0:T(8,128)(2,1)}, u32[]{:S(2)}) copy-start(bf16[1,128,1152]{2,1,0:T(8,128)(2,1)} %param.17) | copy-start | bytes 884740
  12.3 247.9 %reduce-scatter.3.cloned.1.call-start = ((), (), s32[]{:S(2)}) async-start(), calls=%async_computation.4 | async-start | bytes 4644864 | tf_op jit(solution)/shard_map/reduce_scatter | solution.py:1416
  63.3 2.3 copy-start.46
  68.9 19.3 %copy-start.42 = (f32[128]{0:T(128)}, f32[128]{0:T(128)S(1)}, u32[]{:S(2)}) copy-start(f32[128]{0:T(128)S(1)} %multiply_power_fusion) | copy-start | bytes 1540
  69.0 20.5 %copy-start.19 = (f32[128,256]{1,0:T(8,128)}, f32[128,256]{1,0:T(8,128)S(1)}, u32[]{:S(2)}) copy-start(f32[128,256]{1,0:T(8,128)S(1)} %get-tuple-element.119) | copy-start | bytes 393220
  69.5 18.7 %copy-start.35 = (f32[128]{0:T(128)}, f32[128]{0:T(128)S(1)}, u32[]{:S(2)}) copy-start(f32[128]{0:T(128)S(1)} %fusion.69) | copy-start | bytes 1540
  69.5 19.9 %copy-start.44 = (f32[128]{0:T(128)}, f32[128]{0:T(128)S(1)}, u32[]{:S(2)}) copy-start(f32[128]{0:T(128)S(1)} %bitcast_convert_fusion) | copy-start | bytes 1540
  89.5 2.0 copy-start.21
  89.6 1.9 copy-start.31
  91.5 157.8 %copy-start.40 = (f32[4,128]{1,0:T(4,128)}, f32[4,128]{1,0:T(4,128)S(1)}, u32[]{:S(2)}) copy-start(f32[4,128]{1,0:T(4,128)S(1)} %get-tuple-element.149) | copy-start | bytes 6148
  96.6 19.4 %copy-start.3 = (f32[128,1152]{1,0:T(8,128)}, f32[128,1152]{1,0:T(8,128)S(1)}, u32[]{:S(2)}) copy-start(f32[128,1152]{1,0:T(8,128)S(1)} %get-tuple-element.117.middle_ref) | copy-start | bytes 1769476
  201.8 113.9 %reduce-scatter.5.cloned.1.call-start = ((), (), s32[]{:S(2)}) async-start(), calls=%async_computation.5 | async-start | bytes 5308416 | tf_op jit(solution)/shard_map/reduce_scatter | solution.py:1416
  240.7 2.3 copy-start.17
  240.7 2.3 copy-start.26
  244.7 2.8 copy-start.22
  250.7 2.3 copy-start.41
  253.0 3.0 copy-start.12
  253.0 3.0 copy-start.25
  260.1 25.6 %copy-start.16 = (f32[640,256]{1,0:T(8,128)S(1)}, f32[640,256]{1,0:T(8,128)}, u32[]{:S(2)}) copy-start(f32[640,256]{1,0:T(8,128)} %convolution_bitcast_fusion.3) | copy-start | bytes 1966084
  285.8 2.2 copy-start.49
  286.9 3.8 copy-start.6
  286.9 3.8 copy-start.18
  307.9 2.3 copy-start.30
  307.9 2.3 copy-start.47
  308.0 2.3 copy-start.57
  310.3 2.1 copy-start.38
  312.5 1.8 copy-start.14
  374.1 10.9 %copy-start.28 = (bf16[128,1152]{1,0:T(8,128)(2,1)S(1)}, bf16[128,1152]{1,0:T(8,128)(2,1)}, u32[]{:S(2)}) copy-start(bf16[128,1152]{1,0:T(8,128)(2,1)} %get-tuple-element.71) | copy-start | bytes 884740
  374.2 11.6 %copy-start.1 = (bf16[864,1152]{1,0:T(8,128)(2,1)S(1)}, bf16[864,1152]{1,0:T(8,128)(2,1)}, u32[]{:S(2)}) copy-start(bf16[864,1152]{1,0:T(8,128)(2,1)} %param.32) | copy-start | bytes 5971972
  (30 other events, 35.7 us)
Sparse Core Ops, SparseCore 0:
  11.3 95.1 all-gather.2
  108.8 51.0 all-gather.4
  201.9 52.5 reduce-scatter.2
  256.7 58.9 reduce-scatter.4
